TPU v7x, 256 devices: a whole 4x4x8 slice. The times are simulated.
256 devices in a mesh: fsdp: 32 (over x_hi, z, core), ctx: 8 (over x_lo, y).
Axes of the slice: x: 4 (x_hi: 2, x_lo: 2; x = x_hi * 2 + x_lo), y: 4, z: 8, core: 2. Of those that a mesh axis runs over, the one named last changes fastest.
Arguments:
- hidden: bfloat16 [2048, 8192], P('ctx', 'fsdp'), may hold values from -6 to 6
- gain: bfloat16 [8192], replicated, may hold values from 0.25 to 1.75
- embed: bfloat16 [512, 8192], P(None, 'fsdp'), may hold values from -6 to 6
- qkv_weight: bfloat16 [8192, 12288], P('fsdp'), may hold values from -0.07164475 to 0.07164475
- out_weight: bfloat16 [4096, 8192], P('fsdp'), may hold values from -1 to 1
- ref_ids: int32 [2048], P('ctx'), may hold values from 0 to 511
- var_pos: int32 [128], P('ctx'), may hold values from 0 to 2047, as said below
- var_base: int32 [128], P('ctx'), may hold values from 0 to 511
Outputs:
- mixed: bfloat16 [2, 2048, 8192], P(None, 'ctx', 'fsdp')
Inputs may be any that keep to these rules, and one draw needn't show every extreme that they name: Each block of 256 consecutive positions holds exactly 16 distinct variant positions, and they are listed among that block's 16 entries of var_pos.
All inputs are finite; a program needn't handle non-finite values.
Results may differ from a plain program's by a relative error of at most 0.025.
Values may be sent and summed in bfloat16 or wider, within the bound.
No kernel may reach another device: no remote copies, remote signals or barrier semaphores. Data moves between devices by JAX's collectives and lax.ppermute only.
A program may use at most 128 MiB of HBM per device.

v0:
```python
import functools

import jax
import jax.numpy as jnp
from jax import lax
from jax.experimental import pallas as pl
from jax.experimental.pallas import tpu as pltpu
from jax.sharding import Mesh, PartitionSpec as P

epsilon = 1e-05
rope_base = 10000.0

X_HI, Z, CORE, X_LO, Y = 2, 8, 2, 2, 4
FSDP = ("x_hi", "z", "core")
CTX = ("x_lo", "y")
BLOCKS = X_LO * Y
HD = 128
QKV = 3 * HD
TOK = 256
VAR = 16
ROWS = TOK + VAR
SUM_ROWS = ROWS + 16
PAY = ROWS + VAR
bf16 = jnp.bfloat16
f32 = jnp.float32
MIB = 1024 * 1024


def shift(value, axis, size, distance):
    return lax.ppermute(value, axis, [(i, (i + distance) % size) for i in range(size)])


def vmem():
    return pl.BlockSpec(memory_space=pltpu.VMEM)


def anywhere():
    return pl.BlockSpec(memory_space=pl.ANY)


def limit(mib):
    return pltpu.CompilerParams(vmem_limit_bytes=mib * MIB)


def column_copies(w, out, sems, sister):
    z, core, x_hi = lax.axis_index("z"), lax.axis_index("core"), lax.axis_index("x_hi")
    whose = 1 - core if sister else core
    copies = []
    for k in range(Z):
        for xr in range(X_HI):
            head_pair = lax.rem(x_hi + xr, X_HI) * Z + lax.rem(z + k, Z)
            slot = k * X_HI + xr
            start = pl.multiple_of((head_pair * 2 + whose) * QKV, HD)
            copies.append(
                pltpu.make_async_copy(
                    w.at[:, pl.ds(start, QKV)],
                    out.at[:, pl.ds(slot * QKV, QKV)],
                    sems.at[slot],
                )
            )
    return copies


def pick_kernel(w, out, sems):
    copies = column_copies(w, out, sems, True)
    for copy in copies:
        copy.start()
    for copy in copies:
        copy.wait()


def pick_columns(w):
    return pl.pallas_call(
        pick_kernel,
        out_shape=jax.ShapeDtypeStruct((w.shape[0], Z * X_HI * QKV), bf16),
        in_specs=[anywhere()],
        out_specs=vmem(),
        scratch_shapes=[pltpu.SemaphoreType.DMA((Z * X_HI,))],
        compiler_params=limit(8),
    )(w)


def two_rows(row, width):
    high = row.astype(bf16)
    low = (row - high.astype(f32)).astype(bf16)
    line = lax.broadcasted_iota(jnp.int32, (16, width), 0)
    both = jnp.where(line == 0, high.astype(f32), jnp.where(line == 1, low.astype(f32), 0.0))
    return both.astype(bf16)


def one_row(rows):
    return jnp.sum(rows.astype(f32), axis=0, keepdims=True)


def partial_kernel(own, sis, gains, w, w_sis, out, up, down, w_own, sems):
    copies = column_copies(w, w_own, sems, False)
    for copy in copies:
        copy.start()
    width = X_HI * QKV
    own_rows, sis_rows = own[...].astype(f32), sis[...].astype(f32)
    x_own = (own_rows * gains[0:1, :]).astype(bf16)
    x_sis = (sis_rows * gains[1:2, :]).astype(bf16)
    squares = jnp.sum(own_rows * own_rows + sis_rows * sis_rows, axis=1, keepdims=True)
    line = lax.broadcasted_iota(jnp.int32, (ROWS, QKV), 0)
    lane = lax.broadcasted_iota(jnp.int32, (ROWS, QKV), 1)
    row = jnp.sum(jnp.where(line == lane, squares, 0.0), axis=0, keepdims=True)
    tail = two_rows(row, QKV)
    for copy in copies:
        copy.wait()

    def step(k, carry):
        cols = pl.ds(pl.multiple_of(k * width, width), width)
        acc = jnp.dot(x_own, w_own[:, cols], preferred_element_type=f32)
        acc = acc + jnp.dot(x_sis, w_sis[:, cols], preferred_element_type=f32)
        out[k, :ROWS, :] = acc.astype(bf16)
        out[k, ROWS:, :QKV] = tail
        out[k, ROWS:, QKV:] = tail
        return carry

    lax.fori_loop(0, Z, step, 0)
    up[...] = out[Z // 2, :, :QKV]
    down[...] = out[Z // 2, :, QKV:]


def partials(own, sis, gains, w, w_sis):
    half = jax.ShapeDtypeStruct((SUM_ROWS, QKV), bf16)
    return pl.pallas_call(
        partial_kernel,
        out_shape=(jax.ShapeDtypeStruct((Z, SUM_ROWS, X_HI * QKV), bf16), half, half),
        in_specs=[vmem(), vmem(), vmem(), anywhere(), vmem()],
        out_specs=(vmem(),) * 3,
        scratch_shapes=[
            pltpu.VMEM((w.shape[0], Z * X_HI * QKV), bf16),
            pltpu.SemaphoreType.DMA((Z * X_HI,)),
        ],
        compiler_params=limit(24),
    )(own, sis, gains, w, w_sis)


def store_sum(out, cols, terms):
    body = sum(term[:ROWS].astype(f32) for term in terms)
    row = sum(one_row(term[ROWS:]) for term in terms)
    out[:ROWS, cols] = body.astype(bf16)
    out[ROWS:, cols] = two_rows(row, row.shape[1])


def first_kernel(up, down, near_up, near_down, out_up, out_down):
    left, right = slice(0, QKV), slice(QKV, 2 * QKV)
    store_sum(out_up, left, [up[...], near_up[0, :, left]])
    out_up[:, right] = near_up[0, :, right]
    out_down[:, left] = near_down[0, :, left]
    store_sum(out_down, right, [down[...], near_down[0, :, right]])


def next_kernel(up, down, near_up, near_down, out_up, out_down):
    every = slice(0, 2 * QKV)
    store_sum(out_up, every, [up[...], near_up[0]])
    store_sum(out_down, every, [down[...], near_down[0]])


def part(k):
    return pl.BlockSpec((1, SUM_ROWS, X_HI * QKV), lambda i: (k, 0, 0))


def whole(shape):
    return pl.BlockSpec(shape, lambda i: (0, 0))


def ring_add(kernel, up, down, parts, k):
    shape = (SUM_ROWS, X_HI * QKV)
    out = jax.ShapeDtypeStruct(shape, bf16)
    return pl.pallas_call(
        kernel,
        grid=(1,),
        out_shape=(out, out),
        in_specs=[whole(up.shape), whole(down.shape), part(k), part(Z - k)],
        out_specs=(whole(shape), whole(shape)),
        compiler_params=limit(12),
    )(up, down, parts, parts)


def last_kernel(up, down, near, mine, other):
    own, far = slice(0, QKV), slice(QKV, 2 * QKV)
    terms = [up, down, near.at[0]]
    mine[:ROWS] = sum(term[:ROWS, own].astype(f32) for term in terms)
    row = sum(one_row(term[ROWS:, own]) for term in terms)
    mine[ROWS:] = jnp.broadcast_to(row, (8, QKV))
    store_sum(other, slice(0, QKV), [term[:, far] for term in terms])


def ring_last(up, down, parts):
    return pl.pallas_call(
        last_kernel,
        grid=(1,),
        out_shape=(
            jax.ShapeDtypeStruct((ROWS + 8, QKV), f32),
            jax.ShapeDtypeStruct((SUM_ROWS, QKV), bf16),
        ),
        in_specs=[whole(up.shape), whole(down.shape), part(0)],
        out_specs=(whole((ROWS + 8, QKV)), whole((SUM_ROWS, QKV))),
        compiler_params=limit(12),
    )(up, down, parts)


def rotated(x, cosine, sine):
    return x * cosine + pltpu.roll(x, HD // 2, 1) * sine


def finish_kernel(full_width, mine, other, cosine, sine, onehot, payload, queries):
    row = mine[ROWS : ROWS + 1, :] + one_row(other[ROWS:, :])
    line = lax.broadcasted_iota(jnp.int32, (ROWS, QKV), 0)
    lane = lax.broadcasted_iota(jnp.int32, (ROWS, QKV), 1)
    squares = jnp.sum(jnp.where(line == lane, row, 0.0), axis=1, keepdims=True)
    inv_rms = lax.rsqrt(squares / full_width + epsilon)
    proj = (mine[:ROWS, :] + other[:ROWS, :].astype(f32)) * inv_rms
    query = rotated(proj[:, :HD], cosine[...], sine[...]).astype(bf16)
    key = rotated(proj[:, HD : 2 * HD], cosine[...], sine[...]).astype(bf16)
    value = proj[:, 2 * HD :].astype(bf16)
    spots = onehot[...]

    def step(b, carry):
        payload[b, :ROWS, :HD] = key
        payload[b, :ROWS, HD:] = value
        payload[b, ROWS:, :] = spots
        return carry

    lax.fori_loop(0, BLOCKS, step, 0)
    contract = (((0,), (0,)), ((), ()))
    ones = jnp.ones((VAR, HD), bf16)
    changed = lax.dot_general(spots, ones, contract, preferred_element_type=f32)
    placed = lax.dot_general(spots, query[TOK:], contract, preferred_element_type=f32)
    base = query[:TOK]
    queries[:TOK] = base
    queries[TOK:] = jnp.where(changed > 0.5, placed, base.astype(f32)).astype(bf16)


def finish(full_width, mine, other, cosine, sine, onehot):
    return pl.pallas_call(
        functools.partial(finish_kernel, full_width),
        out_shape=(
            jax.ShapeDtypeStruct((BLOCKS, PAY, 2 * HD), bf16),
            jax.ShapeDtypeStruct((2 * TOK, HD), bf16),
        ),
        in_specs=[vmem()] * 5,
        out_specs=(vmem(), vmem()),
        compiler_params=limit(12),
    )(mine, other, cosine, sine, onehot)


def attend_kernel(queries, blocks, out, scores, peak, denom, total, var_kv, spots):
    my_block = lax.axis_index("x_lo") * Y + lax.axis_index("y")
    scale = 1.0 / HD**0.5
    by_cols = (((1,), (1,)), ((), ()))
    lowest = -jnp.inf
    query = queries[...]

    def score_block(j, own):
        score = lax.dot_general(
            query, blocks[j, :TOK, :HD], by_cols, preferred_element_type=f32
        ) * scale
        gone = jnp.sum(blocks[j, ROWS:, :].astype(f32), axis=0, keepdims=True) > 0.5
        line = lax.broadcasted_iota(jnp.int32, (2 * TOK, TOK), 0)
        hidden = (line >= TOK) & gone
        if own:
            lane = lax.broadcasted_iota(jnp.int32, (2 * TOK, TOK), 1)
            hidden = hidden | (lax.rem(line, TOK) < lane)
        return jnp.where(hidden, lowest, score)

    score = score_block(my_block, True)
    scores[my_block] = score
    peak[...] = jnp.maximum(score[:, :HD], score[:, HD:])

    def first(j, carry):
        score = score_block(j, False)
        scores[j] = score
        peak[...] = jnp.maximum(peak[...], jnp.maximum(score[:, :HD], score[:, HD:]))
        return carry

    lax.fori_loop(0, my_block, first, 0)

    for j in range(BLOCKS):
        var_kv[j * VAR : (j + 1) * VAR, :] = blocks[j, TOK:ROWS, :]
        spots[j * VAR : (j + 1) * VAR, :] = blocks[j, ROWS:, :]
    row = lax.broadcasted_iota(jnp.int32, (TOK, TOK), 0)
    col = lax.broadcasted_iota(jnp.int32, (TOK, TOK), 1)
    reached = lax.dot_general(
        jnp.where(row >= col, 1.0, 0.0).astype(bf16), spots[...], by_cols, preferred_element_type=f32
    )
    source = lax.broadcasted_iota(jnp.int32, (TOK, BLOCKS * VAR), 1) // VAR
    seen = (source < my_block) | ((source == my_block) & (reached > 0.5))
    more = lax.dot_general(
        query[TOK:], var_kv[:, :HD], by_cols, preferred_element_type=f32
    ) * scale
    more = jnp.where(seen, more, lowest)
    peak[TOK:, :] = jnp.maximum(peak[TOK:, :], more)
    top = jnp.max(peak[...], axis=1, keepdims=True)
    peak[...] = jnp.broadcast_to(top, (2 * TOK, HD))

    more = jnp.exp(more - top[TOK:])
    denom[:TOK, :] = jnp.zeros((TOK, HD), f32)
    denom[TOK:, :] = more
    total[:TOK, :] = jnp.zeros((TOK, HD), f32)
    total[TOK:, :] = jnp.dot(more.astype(bf16), var_kv[:, HD:], preferred_element_type=f32)

    def second(j, carry):
        best = peak[...]
        left = jnp.exp(scores[j, :, :HD] - best)
        right = jnp.exp(scores[j, :, HD:] - best)
        denom[...] = denom[...] + left + right
        probs = jnp.concatenate([left.astype(bf16), right.astype(bf16)], axis=1)
        total[...] = total[...] + jnp.dot(
            probs, blocks[j, :TOK, HD:], preferred_element_type=f32
        )
        return carry

    lax.fori_loop(0, my_block + 1, second, 0)
    out[...] = (total[...] / jnp.sum(denom[...], axis=1, keepdims=True)).astype(bf16)


def attend(queries, blocks):
    return pl.pallas_call(
        attend_kernel,
        out_shape=jax.ShapeDtypeStruct((2 * TOK, HD), bf16),
        in_specs=[vmem(), vmem()],
        out_specs=vmem(),
        scratch_shapes=[
            pltpu.VMEM((BLOCKS, 2 * TOK, TOK), f32),
            pltpu.VMEM((2 * TOK, HD), f32),
            pltpu.VMEM((2 * TOK, HD), f32),
            pltpu.VMEM((2 * TOK, HD), f32),
            pltpu.VMEM((BLOCKS * VAR, 2 * HD), bf16),
            pltpu.VMEM((BLOCKS * VAR, TOK), bf16),
        ],
        compiler_params=limit(16),
    )(queries, blocks)


def share_kernel(w, out, sems):
    my_block = lax.axis_index("x_lo") * Y + lax.axis_index("y")
    share, columns = out.shape[1], out.shape[2] // X_HI
    copies = []
    for k in range(Z):
        for x in range(X_HI):
            copies.append(
                pltpu.make_async_copy(
                    w.at[pl.ds(pl.multiple_of(my_block * share, share), share), pl.ds((x * Z + k) * columns, columns)],
                    out.at[k, :, pl.ds(x * columns, columns)],
                    sems.at[k, x],
                )
            )
    for copy in copies:
        copy.start()
    for copy in copies:
        copy.wait()


def share_rows(w):
    rows, columns = w.shape
    return pl.pallas_call(
        share_kernel,
        out_shape=jax.ShapeDtypeStruct((Z, rows // BLOCKS, columns // Z), bf16),
        in_specs=[anywhere()],
        out_specs=vmem(),
        scratch_shapes=[pltpu.SemaphoreType.DMA((Z, X_HI))],
        compiler_params=limit(4),
    )(w)


def project_kernel(w, *refs):
    shards, (keep, near, far), (joined, turned) = refs[:Z], refs[Z : Z + 3], refs[Z + 3 :]
    z, core, x_hi = lax.axis_index("z"), lax.axis_index("core"), lax.axis_index("x_hi")
    for d in range(Z):
        joined[:, d * HD : (d + 1) * HD] = shards[d][...]
        source = lax.rem(z + Z - d, Z)
        turned[d * HD : (d + 1) * HD, :] = w[source]

    def product(xr, cr, rows):
        column = (lax.rem(x_hi + xr, X_HI) * CORE + lax.rem(core + cr, CORE)) * TOK
        column = pl.ds(pl.multiple_of(column, TOK), TOK)
        return jnp.dot(joined[rows, :], turned[:, column], preferred_element_type=f32)

    size = 128

    def step(i, carry):
        rows = pl.ds(pl.multiple_of(i * size, size), size)
        for xr in range(X_HI):
            near[rows, xr * TOK : (xr + 1) * TOK] = product(xr, 1, rows).astype(bf16)
        keep[rows, :] = product(0, 0, rows)
        far[rows, :] = product(1, 0, rows)
        return carry

    lax.fori_loop(0, 2 * TOK // size, step, 0)


def project(w, shards):
    rows = shards[0].shape[0]
    return pl.pallas_call(
        project_kernel,
        out_shape=(
            jax.ShapeDtypeStruct((rows, TOK), f32),
            jax.ShapeDtypeStruct((rows, 2 * TOK), bf16),
            jax.ShapeDtypeStruct((rows, TOK), f32),
        ),
        in_specs=[vmem()] * (1 + Z),
        out_specs=(vmem(),) * 3,
        scratch_shapes=[
            pltpu.VMEM((rows, Z * HD), bf16),
            pltpu.VMEM((Z * HD, w.shape[2]), bf16),
        ],
        compiler_params=limit(16),
    )(w, *shards)


def shards(hidden, gain, embed, qkv_weight, out_weight, ref_ids, var_pos, var_base):
    tok_rows, width_part = hidden.shape
    vocab_size = embed.shape[0]
    full_width = out_weight.shape[1]
    x_hi, z, core = lax.axis_index("x_hi"), lax.axis_index("z"), lax.axis_index("core")
    my_block = lax.axis_index("x_lo") * Y + lax.axis_index("y")
    chip_slice = x_hi * Z + z

    with jax.named_scope("weights"):
        w_sis = shift(pick_columns(qkv_weight), "core", CORE, 1)

    with jax.named_scope("variant"):
        local_pos = var_pos - my_block * tok_rows
        var_spots = local_pos[:, None] == jnp.arange(tok_rows)[None, :]
        onehot = var_spots.astype(bf16)
        changed = jnp.any(var_spots, axis=0)
        ref_at = jnp.sum(jnp.where(var_spots, ref_ids[None, :], 0), axis=1)
        vocab_line = jnp.arange(vocab_size)[None, :]
        onehot_diff = (vocab_line == var_base[:, None]).astype(bf16) - (
            vocab_line == ref_at[:, None]
        ).astype(bf16)
        change = jnp.dot(onehot_diff, embed, preferred_element_type=f32)
        picked_rows = jnp.dot(onehot, hidden, preferred_element_type=f32)
        var_rows = (picked_rows + change).astype(bf16)
        rows = jnp.concatenate([hidden, var_rows], axis=0)
        rows_sis = shift(rows, "core", CORE, 1)
        gains = lax.dynamic_slice(gain, (chip_slice * 2 * width_part,), (2 * width_part,))
        gains = gains.astype(f32).reshape(2, width_part)
        gains = jnp.where(core == 0, gains, gains[::-1])

    with jax.named_scope("projection"):
        parts, up, down = partials(rows, rows_sis, gains, qkv_weight, w_sis)
        up, down = shift(up, "z", Z, 1), shift(down, "z", Z, -1)
        up, down = ring_add(first_kernel, up, down, parts, 3)
        for k in (2, 1):
            up, down = shift(up, "z", Z, 1), shift(down, "z", Z, -1)
            if k == 2:
                out_weight, up, down = lax.optimization_barrier((out_weight, up, down))
            up, down = ring_add(next_kernel, up, down, parts, k)
        up, down = shift(up, "z", Z, 1), shift(down, "z", Z, -1)
        mine, other = ring_last(up, down, parts)
        other = shift(other, "x_hi", X_HI, 1)

    with jax.named_scope("tables"):
        positions = jnp.concatenate([my_block * tok_rows + jnp.arange(tok_rows), var_pos])
        exponent = jnp.arange(HD // 2).astype(f32) * (-2.0 / HD)
        inv_freq = jnp.power(f32(rope_base), exponent)
        angle = positions.astype(f32)[:, None] * inv_freq[None, :]
        cosine, sine = jnp.cos(angle), jnp.sin(angle)
        cosine = jnp.concatenate([cosine, cosine], axis=1)
        sine = jnp.concatenate([-sine, sine], axis=1)

    with jax.named_scope("out_weights"):
        shared = lax.all_to_all(share_rows(out_weight), "z", 0, 0, tiled=True)
        out_w = lax.all_gather(shared, CTX, axis=1, tiled=True)

    with jax.named_scope("attention"):
        payload, queries = finish(full_width, mine, other, cosine, sine, onehot)
        blocks = lax.all_to_all(payload, CTX, 0, 0, tiled=True)
        attn = attend(queries, blocks)

    with jax.named_scope("output"):
        pieces = [None] * Z
        pieces[0] = attn
        for d in (4, 3, 5, 2, 6, 1, 7):
            pieces[d] = shift(attn, "z", Z, d)
        keep, near, far = project(out_w, pieces)
        near = shift(near, "core", CORE, 1).astype(f32)
        far = (far + near[:, width_part:]).astype(bf16)
        far = shift(far, "x_hi", X_HI, 1).astype(f32)
        branch = (keep + near[:, :width_part] + far).reshape(2, tok_rows, width_part)
        placed = jnp.dot(onehot.T, var_rows, preferred_element_type=f32)
        variant = jnp.where(changed[:, None], placed, hidden.astype(f32))
        seqs = jnp.stack([hidden.astype(f32), variant])
        return (seqs + branch).astype(bf16)


def solution(mesh):
    fine = Mesh(mesh.devices.reshape(X_HI, Z, CORE, X_LO, Y), (*FSDP, *CTX))
    in_specs = (
        P(CTX, FSDP),
        P(),
        P(None, FSDP),
        P(FSDP, None),
        P(FSDP, None),
        P(CTX),
        P(CTX),
        P(CTX),
    )
    out_specs = P(None, CTX, FSDP)
    return jax.shard_map(shards, mesh=fine, in_specs=in_specs, out_specs=out_specs, check_vma=False)
```

profile of v0, /device:TPU:6, one launch (start us, length us, event | category | flops | bytes accessed | tf_op | source)
XLA Modules:
  0.0 176.1 jit_solution(18040234555405379970)
XLA Ops:
  6.5 2.8 %copy-done.4 = bf16[256,12288]{1,0:T(8,128)(2,1)S(1)} copy-done((bf16[256,12288]{1,0:T(8,128)(2,1)S(1)}, bf16[256,12288]{1,0:T(8,128)(2,1)}, u32[]{:S(2)}) %copy-start.4) | copy-done | bytes 6291480
  9.4 2.5 %weights.1 = bf16[256,6144]{1,0:T(8,128)(2,1)} custom-call(bf16[256,12288]{1,0:T(8,128)(2,1)S(1)} %copy-done.4), custom_call_target="tpu_custom_call" | custom-call | tf_op jit(solution)/shard_map/weights/pallas_call | solution.py:73
  11.9 0.1 collective-permute-start.1
  12.0 0.2 select_reduce_fusion
  12.2 0.3 copy-done.10
  12.5 0.2 fusion.14
  12.7 0.2 fusion.1
  12.9 0.9 pad_maximum_fusion.own
  13.8 0.6 collective-permute-start
  14.4 1.3 dynamic-slice_convert_fusion
  15.7 1.3 reshape.38
  17.0 1.3 rev.3
  18.3 0.7 broadcast_select_fusion.gains
  19.0 2.8 %copy-done.5 = bf16[256,12288]{1,0:T(8,128)(2,1)S(1)} copy-done((bf16[256,12288]{1,0:T(8,128)(2,1)S(1)}, bf16[256,12288]{1,0:T(8,128)(2,1)}, u32[]{:S(2)}) %copy-start.5) | copy-done | bytes 6291480
  21.8 5.0 %projection.5 = (bf16[8,288,768]{2,1,0:T(8,128)(2,1)S(1)}, bf16[288,384]{1,0:T(8,128)(2,1)S(1)}, bf16[288,384]{1,0:T(8,128)(2,1)S(1)}) custom-call(bf16[272,256]{1,0:T(8,128)(2,1)S(1)} %pad_maximum_fusion.own, bf16[272,256]{1,0:T(8,128)(2,1)} %collective-permute-done.sis, f32[2,256]{1,0:T(2,128)S(1)} %broadcast_select_fusion.gains, ...), custom_call_target="tpu_custom_call" | custom-call | tf_op jit(solution)/shard_map/projection/pallas_call | solution.py:127
  26.8 2.0 %collective-permute-start.2 = (bf16[288,384]{1,0:T(8,128)(2,1)S(1)}, bf16[288,384]{1,0:T(8,128)(2,1)S(1)}, u32[]{:S(2)}, u32[]{:S(2)}) collective-permute-start(bf16[288,384]{1,0:T(8,128)(2,1)S(1)} %get-tuple-element.24), channel_id=1, source_target_pairs={{0,16},{16,32},{32,48},{48,64},{64,80},{80,96},{96,112},{112,0},{1... | collective-permute-start | bytes 663560 | tf_op jit(solution)/shard_map/projection/ppermute | solution.py:30
  28.8 4.0 %collective-permute-start.3 = (bf16[288,384]{1,0:T(8,128)(2,1)S(1)}, bf16[288,384]{1,0:T(8,128)(2,1)S(1)}, u32[]{:S(2)}, u32[]{:S(2)}) collective-permute-start(bf16[288,384]{1,0:T(8,128)(2,1)S(1)} %get-tuple-element.25), channel_id=1, source_target_pairs={{0,112},{16,0},{32,16},{48,32},{64,48},{80,64},{96,80},{112,96},{1... | collective-permute-start | bytes 663560 | tf_op jit(solution)/shard_map/projection/ppermute | solution.py:30
  32.8 5.5 %collective-permute-done.2.up = bf16[288,384]{1,0:T(8,128)(2,1)S(1)} collective-permute-done((bf16[288,384]{1,0:T(8,128)(2,1)S(1)}, bf16[288,384]{1,0:T(8,128)(2,1)S(1)}, u32[]{:S(2)}, u32[]{:S(2)}) %collective-permute-start.2) | collective-permute-done | bytes 221216 | tf_op jit(solution)/shard_map/projection/ppermute | solution.py:30
  38.2 0.2 projection.6
  38.4 0.1 collective-permute-start.4
  38.5 3.2 %collective-permute-start.5 = (bf16[288,768]{1,0:T(8,128)(2,1)S(1)}, bf16[288,768]{1,0:T(8,128)(2,1)S(1)}, u32[]{:S(2)}, u32[]{:S(2)}) collective-permute-start(bf16[288,768]{1,0:T(8,128)(2,1)S(1)} %get-tuple-element.28), channel_id=1, source_target_pairs={{0,112},{16,0},{32,16},{48,32},{64,48},{80,64},{96,80},{112,96},{1... | collective-permute-start | bytes 1327112 | tf_op jit(solution)/shard_map/projection/ppermute | solution.py:30
  41.7 9.5 %collective-permute-done.4.up = bf16[288,768]{1,0:T(8,128)(2,1)S(1)} collective-permute-done((bf16[288,768]{1,0:T(8,128)(2,1)S(1)}, bf16[288,768]{1,0:T(8,128)(2,1)S(1)}, u32[]{:S(2)}, u32[]{:S(2)}) %collective-permute-start.4) | collective-permute-done | bytes 442400 | tf_op jit(solution)/shard_map/projection/ppermute | solution.py:30
  51.2 0.3 out_weights.1
  51.5 15.9 %all_to_all.10 = bf16[8,16,1024]{2,1,0:T(8,128)(2,1)} all-to-all(bf16[8,16,1024]{2,1,0:T(8,128)(2,1)S(1)} %out_weights.1), channel_id=1, replica_groups=mesh['x_hi'=2,'z'=8,'core'=2,'x_lo'=2,'y'=4] {'z'}, dimensions={0} | all-to-all | bytes 524288 | tf_op jit(solution)/shard_map/out_weights/all_to_all | solution.py:467
  67.5 2.0 %copy-done.2 = bf16[8,288,768]{2,1,0:T(8,128)(2,1)S(1)} copy-done((bf16[8,288,768]{2,1,0:T(8,128)(2,1)S(1)}, bf16[8,288,768]{2,1,0:T(8,128)(2,1)}, u32[]{:S(2)}) %copy-start.2) | copy-done | bytes 3538968
  69.5 0.3 projection.7
  69.7 0.6 collective-permute-start.6
  70.4 2.7 %collective-permute-start.7 = (bf16[288,768]{1,0:T(8,128)(2,1)S(1)}, bf16[288,768]{1,0:T(8,128)(2,1)S(1)}, u32[]{:S(2)}, u32[]{:S(2)}) collective-permute-start(bf16[288,768]{1,0:T(8,128)(2,1)S(1)} %get-tuple-element.33), channel_id=1, source_target_pairs={{0,112},{16,0},{32,16},{48,32},{64,48},{80,64},{96,80},{112,96},{1... | collective-permute-start | bytes 1327112 | tf_op jit(solution)/shard_map/projection/ppermute | solution.py:30
  73.1 6.7 %collective-permute-done.6.up = bf16[288,768]{1,0:T(8,128)(2,1)S(1)} collective-permute-done((bf16[288,768]{1,0:T(8,128)(2,1)S(1)}, bf16[288,768]{1,0:T(8,128)(2,1)S(1)}, u32[]{:S(2)}, u32[]{:S(2)}) %collective-permute-start.6) | collective-permute-done | bytes 442400 | tf_op jit(solution)/shard_map/projection/ppermute | solution.py:30
  79.8 0.2 projection.8
  80.1 1.0 collective-permute-start.8
  81.0 2.4 %collective-permute-start.9 = (bf16[288,768]{1,0:T(8,128)(2,1)S(1)}, bf16[288,768]{1,0:T(8,128)(2,1)S(1)}, u32[]{:S(2)}, u32[]{:S(2)}) collective-permute-start(bf16[288,768]{1,0:T(8,128)(2,1)S(1)} %get-tuple-element.35), channel_id=1, source_target_pairs={{0,112},{16,0},{32,16},{48,32},{64,48},{80,64},{96,80},{112,96},{1... | collective-permute-start | bytes 1327112 | tf_op jit(solution)/shard_map/projection/ppermute | solution.py:30
  83.4 0.6 fusion.5
  84.0 0.1 pad_maximum_fusion.1
  84.1 5.5 %collective-permute-done.8.up = bf16[288,768]{1,0:T(8,128)(2,1)S(1)} collective-permute-done((bf16[288,768]{1,0:T(8,128)(2,1)S(1)}, bf16[288,768]{1,0:T(8,128)(2,1)S(1)}, u32[]{:S(2)}, u32[]{:S(2)}) %collective-permute-start.8) | collective-permute-done | bytes 442400 | tf_op jit(solution)/shard_map/projection/ppermute | solution.py:30
  89.7 0.2 projection.9
  89.9 1.6 collective-permute-start.10
  91.5 0.1 fusion.15
  91.6 10.4 %collective-permute-done.10.other = bf16[288,384]{1,0:T(8,128)(2,1)S(1)} collective-permute-done((bf16[288,384]{1,0:T(8,128)(2,1)S(1)}, bf16[288,384]{1,0:T(8,128)(2,1)S(1)}, u32[]{:S(2)}, u32[]{:S(2)}) %collective-permute-start.10) | collective-permute-done | bytes 221216 | tf_op jit(solution)/shard_map/projection/ppermute | solution.py:30
  102.0 0.6 attention.2
  102.6 16.4 %all_to_all.11.blocks = bf16[8,288,256]{2,1,0:T(8,128)(2,1)S(1)} all-to-all(bf16[8,288,256]{2,1,0:T(8,128)(2,1)S(1)} %get-tuple-element.39), channel_id=1, replica_groups=mesh['x_hi'=2,'z'=8,'core'=2,'x_lo'=2,'y'=4] {'x_lo','y'}, dimensions={0} | all-to-all | bytes 2359296 | tf_op jit(solution)/shard_map/attention/all_to_all | solution.py:472
  119.0 3.0 %attention.3.refs_0_ = bf16[512,128]{1,0:T(8,128)(2,1)S(1)} custom-call(bf16[512,128]{1,0:T(8,128)(2,1)S(1)} %get-tuple-element.38.queries, bf16[8,288,256]{2,1,0:T(8,128)(2,1)S(1)} %all_to_all.11.blocks), custom_call_target="tpu_custom_call" | custom-call | tf_op jit(solution)/shard_map/attention/pallas_call | solution.py:321
  122.0 0.8 collective-permute-start.11
  122.8 2.3 %collective-permute-start.12 = (bf16[512,128]{1,0:T(8,128)(2,1)S(1)}, bf16[512,128]{1,0:T(8,128)(2,1)S(1)}, u32[]{:S(2)}, u32[]{:S(2)}) collective-permute-start(bf16[512,128]{1,0:T(8,128)(2,1)S(1)} %attention.3.refs_0_), channel_id=1, source_target_pairs={{0,32},{16,48},{32,64},{48,80},{64,96},{80,112},{96,0},{112,16},{1... | collective-permute-start | bytes 393224 | tf_op jit(solution)/shard_map/output/ppermute | solution.py:30
  125.1 3.3 %collective-permute-start.13 = (bf16[512,128]{1,0:T(8,128)(2,1)S(1)}, bf16[512,128]{1,0:T(8,128)(2,1)S(1)}, u32[]{:S(2)}, u32[]{:S(2)}) collective-permute-start(bf16[512,128]{1,0:T(8,128)(2,1)S(1)} %attention.3.refs_0_), channel_id=1, source_target_pairs={{0,48},{16,64},{32,80},{48,96},{64,112},{80,0},{96,16},{112,32},{1... | collective-permute-start | bytes 393224 | tf_op jit(solution)/shard_map/output/ppermute | solution.py:30
  128.3 1.7 collective-permute-start.14
  130.0 4.0 %collective-permute-start.15 = (bf16[512,128]{1,0:T(8,128)(2,1)S(1)}, bf16[512,128]{1,0:T(8,128)(2,1)S(1)}, u32[]{:S(2)}, u32[]{:S(2)}) collective-permute-start(bf16[512,128]{1,0:T(8,128)(2,1)S(1)} %attention.3.refs_0_), channel_id=1, source_target_pairs={{0,80},{16,96},{32,112},{48,0},{64,16},{80,32},{96,48},{112,64},{1... | collective-permute-start | bytes 393224 | tf_op jit(solution)/shard_map/output/ppermute | solution.py:30
  134.0 2.6 %collective-permute-start.16 = (bf16[512,128]{1,0:T(8,128)(2,1)S(1)}, bf16[512,128]{1,0:T(8,128)(2,1)S(1)}, u32[]{:S(2)}, u32[]{:S(2)}) collective-permute-start(bf16[512,128]{1,0:T(8,128)(2,1)S(1)} %attention.3.refs_0_), channel_id=1, source_target_pairs={{0,96},{16,112},{32,0},{48,16},{64,32},{80,48},{96,64},{112,80},{1... | collective-permute-start | bytes 393224 | tf_op jit(solution)/shard_map/output/ppermute | solution.py:30
  136.6 1.4 collective-permute-done.12.refs_2_
  138.0 6.6 %collective-permute-done.14.refs_4_ = bf16[512,128]{1,0:T(8,128)(2,1)S(1)} collective-permute-done((bf16[512,128]{1,0:T(8,128)(2,1)S(1)}, bf16[512,128]{1,0:T(8,128)(2,1)S(1)}, u32[]{:S(2)}, u32[]{:S(2)}) %collective-permute-start.14) | collective-permute-done | bytes 131104 | tf_op jit(solution)/shard_map/output/ppermute | solution.py:30
  144.6 3.8 %collective-permute-done.15.refs_5_ = bf16[512,128]{1,0:T(8,128)(2,1)S(1)} collective-permute-done((bf16[512,128]{1,0:T(8,128)(2,1)S(1)}, bf16[512,128]{1,0:T(8,128)(2,1)S(1)}, u32[]{:S(2)}, u32[]{:S(2)}) %collective-permute-start.15) | collective-permute-done | bytes 131104 | tf_op jit(solution)/shard_map/output/ppermute | solution.py:30
  148.4 2.6 %collective-permute-done.16.refs_6_ = bf16[512,128]{1,0:T(8,128)(2,1)S(1)} collective-permute-done((bf16[512,128]{1,0:T(8,128)(2,1)S(1)}, bf16[512,128]{1,0:T(8,128)(2,1)S(1)}, u32[]{:S(2)}, u32[]{:S(2)}) %collective-permute-start.16) | collective-permute-done | bytes 131104 | tf_op jit(solution)/shard_map/output/ppermute | solution.py:30
  151.0 1.2 collective-permute-done.17.refs_7_
  152.3 1.6 copy-done.7
  153.9 2.3 %output.1 = (f32[512,256]{1,0:T(8,128)S(1)}, bf16[512,512]{1,0:T(8,128)(2,1)S(1)}, f32[512,256]{1,0:T(8,128)S(1)}) custom-call(bf16[8,128,1024]{2,1,0:T(8,128)(2,1)S(1)} %copy-done.7, bf16[512,128]{1,0:T(8,128)(2,1)S(1)} %attention.3.refs_0_, bf16[512,128]{1,0:T(8,128)(2,1)S(1)} %collective-permute-done.11.refs_1_, ...), custom_call_target="tpu_custom_call" | custom-call | tf_op jit(solution)/shard_map/output/pallas_call | solution.py:397
  156.2 0.1 collective-permute-start.18
  156.3 1.9 %collective-permute-done.18 = bf16[512,512]{1,0:T(8,128)(2,1)S(1)} collective-permute-done((bf16[512,512]{1,0:T(8,128)(2,1)S(1)}, bf16[512,512]{1,0:T(8,128)(2,1)S(1)}, u32[]{:S(2)}, u32[]{:S(2)}) %collective-permute-start.18) | collective-permute-done | bytes 524320 | tf_op jit(solution)/shard_map/output/ppermute | solution.py:30
  158.2 0.1 convert_element_type.50
  158.3 0.1 fusion.2
  158.4 1.0 collective-permute-start.19
  159.4 0.3 fusion
  159.7 8.6 %collective-permute-done.19 = bf16[512,256]{1,0:T(8,128)(2,1)S(1)} collective-permute-done((bf16[512,256]{1,0:T(8,128)(2,1)S(1)}, bf16[512,256]{1,0:T(8,128)(2,1)S(1)}, u32[]{:S(2)}, u32[]{:S(2)}) %collective-permute-start.19) | collective-permute-done | bytes 262176 | tf_op jit(solution)/shard_map/output/ppermute | solution.py:30
  168.4 0.1 fusion.3
  168.5 0.8 fusion.4
  (44 shorter events, 0.1 us)
Async XLA Ops:
  6.5 6.2 %copy-start = (bf16[512,256]{1,0:T(8,128)(2,1)S(1)}, bf16[512,256]{1,0:T(8,128)(2,1)}, u32[]{:S(2)}) copy-start(bf16[512,256]{1,0:T(8,128)(2,1)} %param.10) | copy-start | bytes 786436
  6.5 145.7 %all-gather.2.cloned.1.call-start = ((), (), s32[]{:S(2)}) async-start(), calls=%async_computation.2 | async-start | bytes 2359296 | tf_op jit(solution)/shard_map/out_weights/all_gather | solution.py:468
  6.5 2.8 %copy-start.4 = (bf16[256,12288]{1,0:T(8,128)(2,1)S(1)}, bf16[256,12288]{1,0:T(8,128)(2,1)}, u32[]{:S(2)}) copy-start(bf16[256,12288]{1,0:T(8,128)(2,1)} %w.3) | copy-start | bytes 18874372
  9.4 2.6 %copy-start.13 = (s32[16]{0:T(128)S(1)}, s32[16]{0:T(128)}, u32[]{:S(2)}) copy-start(s32[16]{0:T(128)} %param.14) | copy-start | bytes 196
  9.4 2.6 %copy-start.12 = (s32[256]{0:T(256)S(1)}, s32[256]{0:T(256)}, u32[]{:S(2)}) copy-start(s32[256]{0:T(256)} %param.13) | copy-start | bytes 3076
  9.4 3.2 %copy-start.8 = (bf16[256,256]{1,0:T(8,128)(2,1)S(1)}, bf16[256,256]{1,0:T(8,128)(2,1)}, u32[]{:S(2)}) copy-start(bf16[256,256]{1,0:T(8,128)(2,1)} %param.8) | copy-start | bytes 393220
  9.4 3.3 %copy-start.15 = (s32[16]{0:T(128)S(1)}, s32[16]{0:T(128)}, u32[]{:S(2)}) copy-start(s32[16]{0:T(128)} %param.15) | copy-start | bytes 196
  11.9 7.1 %collective-permute-start.1 = (bf16[256,6144]{1,0:T(8,128)(2,1)}, bf16[256,6144]{1,0:T(8,128)(2,1)S(1)}, u32[]{:S(2)}, u32[]{:S(2)}) collective-permute-start(bf16[256,6144]{1,0:T(8,128)(2,1)} %weights.1), channel_id=1, source_target_pairs={{0,8},{8,0},{1,9},{9,1},{2,10},{10,2},{3,11},{11,3},{4,12},{12,4},... | collective-permute-start | bytes 9437192 | tf_op jit(solution)/shard_map/weights/ppermute | solution.py:30
  12.0 0.5 copy-start.10
  13.8 5.1 %collective-permute-start = (bf16[272,256]{1,0:T(8,128)(2,1)S(1)}, bf16[272,256]{1,0:T(8,128)(2,1)}, u32[]{:S(2)}, u32[]{:S(2)}) collective-permute-start(bf16[272,256]{1,0:T(8,128)(2,1)S(1)} %pad_maximum_fusion.own), channel_id=1, source_target_pairs={{0,8},{8,0},{1,9},{9,1},{2,10},{10,2},{3,11},{11,3},{4,12},{12,4},... | collective-permute-start | bytes 417800 | tf_op jit(solution)/shard_map/variant/ppermute | solution.py:30
  19.0 2.8 %copy-start.5 = (bf16[256,12288]{1,0:T(8,128)(2,1)S(1)}, bf16[256,12288]{1,0:T(8,128)(2,1)}, u32[]{:S(2)}) copy-start(bf16[256,12288]{1,0:T(8,128)(2,1)} %w.3) | copy-start | bytes 18874372
  26.7 11.7 %copy-start.1 = (bf16[8,288,768]{2,1,0:T(8,128)(2,1)}, bf16[8,288,768]{2,1,0:T(8,128)(2,1)S(1)}, u32[]{:S(2)}) copy-start(bf16[8,288,768]{2,1,0:T(8,128)(2,1)S(1)} %get-tuple-element.26.near_up.near_down.near) | copy-start | bytes 10616836
  26.8 11.5 %collective-permute-start.2 = (bf16[288,384]{1,0:T(8,128)(2,1)S(1)}, bf16[288,384]{1,0:T(8,128)(2,1)S(1)}, u32[]{:S(2)}, u32[]{:S(2)}) collective-permute-start(bf16[288,384]{1,0:T(8,128)(2,1)S(1)} %get-tuple-element.24), channel_id=1, source_target_pairs={{0,16},{16,32},{32,48},{48,64},{64,80},{80,96},{96,112},{112,0},{1... | collective-permute-start | bytes 663560 | tf_op jit(solution)/shard_map/projection/ppermute | solution.py:30
  28.8 9.5 %collective-permute-start.3 = (bf16[288,384]{1,0:T(8,128)(2,1)S(1)}, bf16[288,384]{1,0:T(8,128)(2,1)S(1)}, u32[]{:S(2)}, u32[]{:S(2)}) collective-permute-start(bf16[288,384]{1,0:T(8,128)(2,1)S(1)} %get-tuple-element.25), channel_id=1, source_target_pairs={{0,112},{16,0},{32,16},{48,32},{64,48},{80,64},{96,80},{112,96},{1... | collective-permute-start | bytes 663560 | tf_op jit(solution)/shard_map/projection/ppermute | solution.py:30
  38.2 13.0 %copy-start.6 = (bf16[128,8192]{1,0:T(8,128)(2,1)S(1)}, bf16[128,8192]{1,0:T(8,128)(2,1)}, u32[]{:S(2)}) copy-start(bf16[128,8192]{1,0:T(8,128)(2,1)} %w.4) | copy-start | bytes 6291460
  38.4 12.8 %collective-permute-start.4 = (bf16[288,768]{1,0:T(8,128)(2,1)S(1)}, bf16[288,768]{1,0:T(8,128)(2,1)S(1)}, u32[]{:S(2)}, u32[]{:S(2)}) collective-permute-start(bf16[288,768]{1,0:T(8,128)(2,1)S(1)} %get-tuple-element.27), channel_id=1, source_target_pairs={{0,16},{16,32},{32,48},{48,64},{64,80},{80,96},{96,112},{112,0},{1... | collective-permute-start | bytes 1327112 | tf_op jit(solution)/shard_map/projection/ppermute | solution.py:30
  38.5 12.7 %collective-permute-start.5 = (bf16[288,768]{1,0:T(8,128)(2,1)S(1)}, bf16[288,768]{1,0:T(8,128)(2,1)S(1)}, u32[]{:S(2)}, u32[]{:S(2)}) collective-permute-start(bf16[288,768]{1,0:T(8,128)(2,1)S(1)} %get-tuple-element.28), channel_id=1, source_target_pairs={{0,112},{16,0},{32,16},{48,32},{64,48},{80,64},{96,80},{112,96},{1... | collective-permute-start | bytes 1327112 | tf_op jit(solution)/shard_map/projection/ppermute | solution.py:30
  67.5 2.0 %copy-start.2 = (bf16[8,288,768]{2,1,0:T(8,128)(2,1)S(1)}, bf16[8,288,768]{2,1,0:T(8,128)(2,1)}, u32[]{:S(2)}) copy-start(bf16[8,288,768]{2,1,0:T(8,128)(2,1)} %copy-done.1) | copy-start | bytes 10616836
  69.5 3.6 %copy-start.14 = (s32[16]{0:T(128)S(1)}, s32[16]{0:T(128)}, u32[]{:S(2)}) copy-start(s32[16]{0:T(128)} %param.14) | copy-start | bytes 196
  69.7 10.1 %collective-permute-start.6 = (bf16[288,768]{1,0:T(8,128)(2,1)S(1)}, bf16[288,768]{1,0:T(8,128)(2,1)S(1)}, u32[]{:S(2)}, u32[]{:S(2)}) collective-permute-start(bf16[288,768]{1,0:T(8,128)(2,1)S(1)} %get-tuple-element.32), channel_id=1, source_target_pairs={{0,16},{16,32},{32,48},{48,64},{64,80},{80,96},{96,112},{112,0},{1... | collective-permute-start | bytes 1327112 | tf_op jit(solution)/shard_map/projection/ppermute | solution.py:30
  70.4 9.4 %collective-permute-start.7 = (bf16[288,768]{1,0:T(8,128)(2,1)S(1)}, bf16[288,768]{1,0:T(8,128)(2,1)S(1)}, u32[]{:S(2)}, u32[]{:S(2)}) collective-permute-start(bf16[288,768]{1,0:T(8,128)(2,1)S(1)} %get-tuple-element.33), channel_id=1, source_target_pairs={{0,112},{16,0},{32,16},{48,32},{64,48},{80,64},{96,80},{112,96},{1... | collective-permute-start | bytes 1327112 | tf_op jit(solution)/shard_map/projection/ppermute | solution.py:30
  73.1 16.6 %copy-start.3 = (bf16[8,288,768]{2,1,0:T(8,128)(2,1)S(1)}, bf16[8,288,768]{2,1,0:T(8,128)(2,1)}, u32[]{:S(2)}) copy-start(bf16[8,288,768]{2,1,0:T(8,128)(2,1)} %copy-done.1) | copy-start | bytes 10616836
  80.1 11.4 %copy-start.11 = (s32[16]{0:T(128)S(1)}, s32[16]{0:T(128)}, u32[]{:S(2)}) copy-start(s32[16]{0:T(128)} %copy-done.10) | copy-start | bytes 196
  80.1 9.6 %collective-permute-start.8 = (bf16[288,768]{1,0:T(8,128)(2,1)S(1)}, bf16[288,768]{1,0:T(8,128)(2,1)S(1)}, u32[]{:S(2)}, u32[]{:S(2)}) collective-permute-start(bf16[288,768]{1,0:T(8,128)(2,1)S(1)} %get-tuple-element.34), channel_id=1, source_target_pairs={{0,16},{16,32},{32,48},{48,64},{64,80},{80,96},{96,112},{112,0},{1... | collective-permute-start | bytes 1327112 | tf_op jit(solution)/shard_map/projection/ppermute | solution.py:30
  81.0 8.6 %collective-permute-start.9 = (bf16[288,768]{1,0:T(8,128)(2,1)S(1)}, bf16[288,768]{1,0:T(8,128)(2,1)S(1)}, u32[]{:S(2)}, u32[]{:S(2)}) collective-permute-start(bf16[288,768]{1,0:T(8,128)(2,1)S(1)} %get-tuple-element.35), channel_id=1, source_target_pairs={{0,112},{16,0},{32,16},{48,32},{64,48},{80,64},{96,80},{112,96},{1... | collective-permute-start | bytes 1327112 | tf_op jit(solution)/shard_map/projection/ppermute | solution.py:30
  89.9 12.1 %collective-permute-start.10 = (bf16[288,384]{1,0:T(8,128)(2,1)S(1)}, bf16[288,384]{1,0:T(8,128)(2,1)S(1)}, u32[]{:S(2)}, u32[]{:S(2)}) collective-permute-start(bf16[288,384]{1,0:T(8,128)(2,1)S(1)} %get-tuple-element.37), channel_id=1, source_target_pairs={{0,128},{128,0},{1,129},{129,1},{2,130},{130,2},{3,131},{131,3},{4... | collective-permute-start | bytes 663560 | tf_op jit(solution)/shard_map/projection/ppermute | solution.py:30
  119.0 40.4 %copy-start.9 = (bf16[256,256]{1,0:T(8,128)(2,1)S(1)}, bf16[256,256]{1,0:T(8,128)(2,1)}, u32[]{:S(2)}) copy-start(bf16[256,256]{1,0:T(8,128)(2,1)} %param.8) | copy-start | bytes 393220
  122.0 12.0 %collective-permute-start.11 = (bf16[512,128]{1,0:T(8,128)(2,1)S(1)}, bf16[512,128]{1,0:T(8,128)(2,1)S(1)}, u32[]{:S(2)}, u32[]{:S(2)}) collective-permute-start(bf16[512,128]{1,0:T(8,128)(2,1)S(1)} %attention.3.refs_0_), channel_id=1, source_target_pairs={{0,16},{16,32},{32,48},{48,64},{64,80},{80,96},{96,112},{112,0},{1... | collective-permute-start | bytes 393224 | tf_op jit(solution)/shard_map/output/ppermute | solution.py:30
  122.8 15.2 %collective-permute-start.12 = (bf16[512,128]{1,0:T(8,128)(2,1)S(1)}, bf16[512,128]{1,0:T(8,128)(2,1)S(1)}, u32[]{:S(2)}, u32[]{:S(2)}) collective-permute-start(bf16[512,128]{1,0:T(8,128)(2,1)S(1)} %attention.3.refs_0_), channel_id=1, source_target_pairs={{0,32},{16,48},{32,64},{48,80},{64,96},{80,112},{96,0},{112,16},{1... | collective-permute-start | bytes 393224 | tf_op jit(solution)/shard_map/output/ppermute | solution.py:30
  125.1 12.9 %collective-permute-start.13 = (bf16[512,128]{1,0:T(8,128)(2,1)S(1)}, bf16[512,128]{1,0:T(8,128)(2,1)S(1)}, u32[]{:S(2)}, u32[]{:S(2)}) collective-permute-start(bf16[512,128]{1,0:T(8,128)(2,1)S(1)} %attention.3.refs_0_), channel_id=1, source_target_pairs={{0,48},{16,64},{32,80},{48,96},{64,112},{80,0},{96,16},{112,32},{1... | collective-permute-start | bytes 393224 | tf_op jit(solution)/shard_map/output/ppermute | solution.py:30
  128.3 16.3 %collective-permute-start.14 = (bf16[512,128]{1,0:T(8,128)(2,1)S(1)}, bf16[512,128]{1,0:T(8,128)(2,1)S(1)}, u32[]{:S(2)}, u32[]{:S(2)}) collective-permute-start(bf16[512,128]{1,0:T(8,128)(2,1)S(1)} %attention.3.refs_0_), channel_id=1, source_target_pairs={{0,64},{16,80},{32,96},{48,112},{64,0},{80,16},{96,32},{112,48},{1... | collective-permute-start | bytes 393224 | tf_op jit(solution)/shard_map/output/ppermute | solution.py:30
  130.0 18.4 %collective-permute-start.15 = (bf16[512,128]{1,0:T(8,128)(2,1)S(1)}, bf16[512,128]{1,0:T(8,128)(2,1)S(1)}, u32[]{:S(2)}, u32[]{:S(2)}) collective-permute-start(bf16[512,128]{1,0:T(8,128)(2,1)S(1)} %attention.3.refs_0_), channel_id=1, source_target_pairs={{0,80},{16,96},{32,112},{48,0},{64,16},{80,32},{96,48},{112,64},{1... | collective-permute-start | bytes 393224 | tf_op jit(solution)/shard_map/output/ppermute | solution.py:30
  134.0 17.0 %collective-permute-start.16 = (bf16[512,128]{1,0:T(8,128)(2,1)S(1)}, bf16[512,128]{1,0:T(8,128)(2,1)S(1)}, u32[]{:S(2)}, u32[]{:S(2)}) collective-permute-start(bf16[512,128]{1,0:T(8,128)(2,1)S(1)} %attention.3.refs_0_), channel_id=1, source_target_pairs={{0,96},{16,112},{32,0},{48,16},{64,32},{80,48},{96,64},{112,80},{1... | collective-permute-start | bytes 393224 | tf_op jit(solution)/shard_map/output/ppermute | solution.py:30
  138.0 14.3 %collective-permute-start.17 = (bf16[512,128]{1,0:T(8,128)(2,1)S(1)}, bf16[512,128]{1,0:T(8,128)(2,1)S(1)}, u32[]{:S(2)}, u32[]{:S(2)}) collective-permute-start(bf16[512,128]{1,0:T(8,128)(2,1)S(1)} %attention.3.refs_0_), channel_id=1, source_target_pairs={{0,112},{16,0},{32,16},{48,32},{64,48},{80,64},{96,80},{112,96},{1... | collective-permute-start | bytes 393224 | tf_op jit(solution)/shard_map/output/ppermute | solution.py:30
  152.3 1.6 copy-start.7
  156.2 2.0 %collective-permute-start.18 = (bf16[512,512]{1,0:T(8,128)(2,1)S(1)}, bf16[512,512]{1,0:T(8,128)(2,1)S(1)}, u32[]{:S(2)}, u32[]{:S(2)}) collective-permute-start(bf16[512,512]{1,0:T(8,128)(2,1)S(1)} %get-tuple-element.41), channel_id=1, source_target_pairs={{0,8},{8,0},{1,9},{9,1},{2,10},{10,2},{3,11},{11,3},{4,12},{12,4},... | collective-permute-start | bytes 1572872 | tf_op jit(solution)/shard_map/output/ppermute | solution.py:30
  158.4 9.9 %collective-permute-start.19 = (bf16[512,256]{1,0:T(8,128)(2,1)S(1)}, bf16[512,256]{1,0:T(8,128)(2,1)S(1)}, u32[]{:S(2)}, u32[]{:S(2)}) collective-permute-start(bf16[512,256]{1,0:T(8,128)(2,1)S(1)} %fusion.2), channel_id=1, source_target_pairs={{0,128},{128,0},{1,129},{129,1},{2,130},{130,2},{3,131},{131,3},{4... | collective-permute-start | bytes 786440 | tf_op jit(solution)/shard_map/output/ppermute | solution.py:30
Sparse Core Ops, SparseCore 0:
  67.6 41.0 all-gather.1
where the time goes:
time: 177 us; the launch traced here: 176 us
  waiting for transfers between devices  63.8 us (36%)
  starting transfers between devices  33.8 us (19%)
  blocking collectives  32.3 us (18%)
  Pallas kernels  14.6 us (8%)
  between operations  13.7 us (8%)
  local copies, waits for them, and re-layouts  12.1 us (7%)
  other arithmetic  5.06 us (3%)
    ppermute x20, waiting for transfers between devices, shift(): lax.ppermute(value, axis, [(i, (i + distance) % size) for i in range(size)])  63.8 us
    ppermute x20, starting transfers between devices, shift(): lax.ppermute(value, axis, [(i, (i + distance) % size) for i in range(size)])  33.8 us
    all_to_all x1, blocking collectives, shards(): blocks = lax.all_to_all(payload, CTX, 0, 0, tiled=True)  16.4 us
    all_to_all x1, blocking collectives, shards(): shared = lax.all_to_all(share_rows(out_weight), 'z', 0, 0, tiled=True)  15.9 us
    unnamed x32, local copies, waits for them, and re-layouts  9.57 us
    pallas_call x1, Pallas kernels, partials(): pl.pallas_call(partial_kernel, out_shape=(jax.ShapeDtypeStruct((Z, SUM_RO...  4.99 us
  transfers between devices with their start and end apart: 21, of which 12 were waited for; matrix products, arithmetic and copies ran while one was open for 4% of the time, Pallas kernels for 2%

commit v1 on v0

--- a/solution.py
+++ b/solution.py
@@ -38,31 +38,37 @@
     return pl.BlockSpec(memory_space=pl.ANY)
 
 
+def hbm():
+    return pl.BlockSpec(memory_space=pltpu.HBM)
+
+
 def limit(mib):
     return pltpu.CompilerParams(vmem_limit_bytes=mib * MIB)
 
 
-def column_copies(w, out, sems, sister):
+FIRST = (3, 4, 5)
+SECOND = (6, 7, 0, 1, 2)
+
+
+def pick_kernel(w, *refs):
+    sems = refs[-1]
     z, core, x_hi = lax.axis_index("z"), lax.axis_index("core"), lax.axis_index("x_hi")
-    whose = 1 - core if sister else core
     copies = []
-    for k in range(Z):
-        for xr in range(X_HI):
-            head_pair = lax.rem(x_hi + xr, X_HI) * Z + lax.rem(z + k, Z)
-            slot = k * X_HI + xr
-            start = pl.multiple_of((head_pair * 2 + whose) * QKV, HD)
-            copies.append(
-                pltpu.make_async_copy(
-                    w.at[:, pl.ds(start, QKV)],
-                    out.at[:, pl.ds(slot * QKV, QKV)],
-                    sems.at[slot],
+    for index, (whose, ks) in enumerate(
+        ((1 - core, FIRST), (1 - core, SECOND), (core, FIRST), (core, SECOND))
+    ):
+        for i, k in enumerate(ks):
+            for xr in range(X_HI):
+                head_pair = lax.rem(x_hi + xr, X_HI) * Z + lax.rem(z + k, Z)
+                slot = i * X_HI + xr
+                start = pl.multiple_of((head_pair * 2 + whose) * QKV, HD)
+                copies.append(
+                    pltpu.make_async_copy(
+                        w.at[:, pl.ds(start, QKV)],
+                        refs[index].at[:, slot * QKV : (slot + 1) * QKV],
+                        sems.at[index, slot],
+                    )
                 )
-            )
-    return copies
-
-
-def pick_kernel(w, out, sems):
-    copies = column_copies(w, out, sems, True)
     for copy in copies:
         copy.start()
     for copy in copies:
@@ -70,13 +76,15 @@
 
 
 def pick_columns(w):
+    first = jax.ShapeDtypeStruct((w.shape[0], len(FIRST) * X_HI * QKV), bf16)
+    second = jax.ShapeDtypeStruct((w.shape[0], len(SECOND) * X_HI * QKV), bf16)
     return pl.pallas_call(
         pick_kernel,
-        out_shape=jax.ShapeDtypeStruct((w.shape[0], Z * X_HI * QKV), bf16),
-        in_specs=[anywhere()],
-        out_specs=vmem(),
-        scratch_shapes=[pltpu.SemaphoreType.DMA((Z * X_HI,))],
-        compiler_params=limit(8),
+        out_shape=(first, second, first, second),
+        in_specs=[hbm()],
+        out_specs=(vmem(),) * 4,
+        scratch_shapes=[pltpu.SemaphoreType.DMA((4, len(SECOND) * X_HI))],
+        compiler_params=limit(12),
     )(w)
 
 
@@ -92,49 +100,55 @@
     return jnp.sum(rows.astype(f32), axis=0, keepdims=True)
 
 
-def partial_kernel(own, sis, gains, w, w_sis, out, up, down, w_own, sems):
-    copies = column_copies(w, w_own, sems, False)
-    for copy in copies:
-        copy.start()
+def partial_kernel(ks, own, sis, gains, w_own, w_sis, *outs):
     width = X_HI * QKV
+    core = lax.axis_index("core")
     own_rows, sis_rows = own[...].astype(f32), sis[...].astype(f32)
-    x_own = (own_rows * gains[0:1, :]).astype(bf16)
-    x_sis = (sis_rows * gains[1:2, :]).astype(bf16)
+    left, right = gains[:, :TOK].astype(f32), gains[:, TOK:].astype(f32)
+    x_own = (own_rows * jnp.where(core == 0, left, right)).astype(bf16)
+    x_sis = (sis_rows * jnp.where(core == 0, right, left)).astype(bf16)
     squares = jnp.sum(own_rows * own_rows + sis_rows * sis_rows, axis=1, keepdims=True)
     line = lax.broadcasted_iota(jnp.int32, (ROWS, QKV), 0)
     lane = lax.broadcasted_iota(jnp.int32, (ROWS, QKV), 1)
     row = jnp.sum(jnp.where(line == lane, squares, 0.0), axis=0, keepdims=True)
     tail = two_rows(row, QKV)
-    for copy in copies:
-        copy.wait()
-
-    def step(k, carry):
-        cols = pl.ds(pl.multiple_of(k * width, width), width)
+
+    def product(slot, count):
+        cols = slice(slot * QKV, (slot + count) * QKV)
         acc = jnp.dot(x_own, w_own[:, cols], preferred_element_type=f32)
         acc = acc + jnp.dot(x_sis, w_sis[:, cols], preferred_element_type=f32)
-        out[k, :ROWS, :] = acc.astype(bf16)
-        out[k, ROWS:, :QKV] = tail
-        out[k, ROWS:, QKV:] = tail
-        return carry
-
-    lax.fori_loop(0, Z, step, 0)
-    up[...] = out[Z // 2, :, :QKV]
-    down[...] = out[Z // 2, :, QKV:]
-
-
-def partials(own, sis, gains, w, w_sis):
+        return acc.astype(bf16)
+
+    outs = list(outs)
+    for i, k in enumerate(ks):
+        if k == Z // 2:
+            for xr in range(X_HI):
+                out = outs.pop(0)
+                out[:ROWS, :] = product(i * X_HI + xr, 1)
+                out[ROWS:, :] = tail
+        else:
+            out = outs.pop(0)
+            out[:ROWS, :] = product(i * X_HI, X_HI)
+            out[ROWS:, :QKV] = tail
+            out[ROWS:, QKV:] = tail
+
+
+def partials(ks, own, sis, gains, w_own, w_sis):
     half = jax.ShapeDtypeStruct((SUM_ROWS, QKV), bf16)
-    return pl.pallas_call(
-        partial_kernel,
-        out_shape=(jax.ShapeDtypeStruct((Z, SUM_ROWS, X_HI * QKV), bf16), half, half),
-        in_specs=[vmem(), vmem(), vmem(), anywhere(), vmem()],
-        out_specs=(vmem(),) * 3,
-        scratch_shapes=[
-            pltpu.VMEM((w.shape[0], Z * X_HI * QKV), bf16),
-            pltpu.SemaphoreType.DMA((Z * X_HI,)),
-        ],
-        compiler_params=limit(24),
-    )(own, sis, gains, w, w_sis)
+    full = jax.ShapeDtypeStruct((SUM_ROWS, X_HI * QKV), bf16)
+    shapes = []
+    for k in ks:
+        shapes += [half, half] if k == Z // 2 else [full]
+    return pl.pallas_call(
+        functools.partial(partial_kernel, ks),
+        out_shape=tuple(shapes),
+        in_specs=[vmem()] * 5,
+        out_specs=(vmem(),) * len(shapes),
+        compiler_params=limit(20),
+        cost_estimate=pl.CostEstimate(
+            flops=4 * ROWS * w_own.size, bytes_accessed=8 * w_own.size, transcendentals=0
+        ),
+    )(own, sis, gains, w_own, w_sis)
 
 
 def store_sum(out, cols, terms):
@@ -146,60 +160,49 @@
 
 def first_kernel(up, down, near_up, near_down, out_up, out_down):
     left, right = slice(0, QKV), slice(QKV, 2 * QKV)
-    store_sum(out_up, left, [up[...], near_up[0, :, left]])
-    out_up[:, right] = near_up[0, :, right]
-    out_down[:, left] = near_down[0, :, left]
-    store_sum(out_down, right, [down[...], near_down[0, :, right]])
+    store_sum(out_up, left, [up[...], near_up[:, left]])
+    out_up[:, right] = near_up[:, right]
+    out_down[:, left] = near_down[:, left]
+    store_sum(out_down, right, [down[...], near_down[:, right]])
 
 
 def next_kernel(up, down, near_up, near_down, out_up, out_down):
     every = slice(0, 2 * QKV)
-    store_sum(out_up, every, [up[...], near_up[0]])
-    store_sum(out_down, every, [down[...], near_down[0]])
-
-
-def part(k):
-    return pl.BlockSpec((1, SUM_ROWS, X_HI * QKV), lambda i: (k, 0, 0))
-
-
-def whole(shape):
-    return pl.BlockSpec(shape, lambda i: (0, 0))
-
-
-def ring_add(kernel, up, down, parts, k):
-    shape = (SUM_ROWS, X_HI * QKV)
-    out = jax.ShapeDtypeStruct(shape, bf16)
+    store_sum(out_up, every, [up[...], near_up[...]])
+    store_sum(out_down, every, [down[...], near_down[...]])
+
+
+def ring_add(kernel, up, down, near_up, near_down):
+    out = jax.ShapeDtypeStruct((SUM_ROWS, X_HI * QKV), bf16)
     return pl.pallas_call(
         kernel,
-        grid=(1,),
         out_shape=(out, out),
-        in_specs=[whole(up.shape), whole(down.shape), part(k), part(Z - k)],
-        out_specs=(whole(shape), whole(shape)),
-        compiler_params=limit(12),
-    )(up, down, parts, parts)
+        in_specs=[vmem()] * 4,
+        out_specs=(vmem(), vmem()),
+        compiler_params=limit(8),
+    )(up, down, near_up, near_down)
 
 
 def last_kernel(up, down, near, mine, other):
     own, far = slice(0, QKV), slice(QKV, 2 * QKV)
-    terms = [up, down, near.at[0]]
+    terms = [up, down, near]
     mine[:ROWS] = sum(term[:ROWS, own].astype(f32) for term in terms)
     row = sum(one_row(term[ROWS:, own]) for term in terms)
     mine[ROWS:] = jnp.broadcast_to(row, (8, QKV))
     store_sum(other, slice(0, QKV), [term[:, far] for term in terms])
 
 
-def ring_last(up, down, parts):
+def ring_last(up, down, near):
     return pl.pallas_call(
         last_kernel,
-        grid=(1,),
         out_shape=(
             jax.ShapeDtypeStruct((ROWS + 8, QKV), f32),
             jax.ShapeDtypeStruct((SUM_ROWS, QKV), bf16),
         ),
-        in_specs=[whole(up.shape), whole(down.shape), part(0)],
-        out_specs=(whole((ROWS + 8, QKV)), whole((SUM_ROWS, QKV))),
-        compiler_params=limit(12),
-    )(up, down, parts)
+        in_specs=[vmem()] * 3,
+        out_specs=(vmem(), vmem()),
+        compiler_params=limit(8),
+    )(up, down, near)
 
 
 def rotated(x, cosine, sine):
@@ -335,16 +338,18 @@
     )(queries, blocks)
 
 
-def share_kernel(w, out, sems):
+def share_kernel(w, out, buffer, sems, out_sem):
     my_block = lax.axis_index("x_lo") * Y + lax.axis_index("y")
-    share, columns = out.shape[1], out.shape[2] // X_HI
+    share, columns = buffer.shape[1], buffer.shape[2] // X_HI
+    rows = pl.ds(pl.multiple_of(my_block * share, share), share)
     copies = []
     for k in range(Z):
         for x in range(X_HI):
+            start = (x * Z + k) * columns
             copies.append(
                 pltpu.make_async_copy(
-                    w.at[pl.ds(pl.multiple_of(my_block * share, share), share), pl.ds((x * Z + k) * columns, columns)],
-                    out.at[k, :, pl.ds(x * columns, columns)],
+                    w.at[rows, start : start + columns],
+                    buffer.at[k, :, x * columns : (x + 1) * columns],
                     sems.at[k, x],
                 )
             )
@@ -352,16 +357,24 @@
         copy.start()
     for copy in copies:
         copy.wait()
+    copy = pltpu.make_async_copy(buffer, out, out_sem)
+    copy.start()
+    copy.wait()
 
 
 def share_rows(w):
     rows, columns = w.shape
+    shape = (Z, rows // BLOCKS, columns // Z)
     return pl.pallas_call(
         share_kernel,
-        out_shape=jax.ShapeDtypeStruct((Z, rows // BLOCKS, columns // Z), bf16),
-        in_specs=[anywhere()],
-        out_specs=vmem(),
-        scratch_shapes=[pltpu.SemaphoreType.DMA((Z, X_HI))],
+        out_shape=jax.ShapeDtypeStruct(shape, bf16),
+        in_specs=[hbm()],
+        out_specs=hbm(),
+        scratch_shapes=[
+            pltpu.VMEM(shape, bf16),
+            pltpu.SemaphoreType.DMA((Z, X_HI)),
+            pltpu.SemaphoreType.DMA(()),
+        ],
         compiler_params=limit(4),
     )(w)
 
@@ -420,7 +433,10 @@
     chip_slice = x_hi * Z + z
 
     with jax.named_scope("weights"):
-        w_sis = shift(pick_columns(qkv_weight), "core", CORE, 1)
+        send_first, send_second, own_first, own_second = pick_columns(
+            pltpu.with_memory_space_constraint(qkv_weight, pltpu.HBM)
+        )
+        sis_first = shift(send_first, "core", CORE, 1)
 
     with jax.named_scope("variant"):
         local_pos = var_pos - my_block * tok_rows
@@ -436,22 +452,30 @@
         picked_rows = jnp.dot(onehot, hidden, preferred_element_type=f32)
         var_rows = (picked_rows + change).astype(bf16)
         rows = jnp.concatenate([hidden, var_rows], axis=0)
+        rows, send_second = lax.optimization_barrier((rows, send_second))
         rows_sis = shift(rows, "core", CORE, 1)
-        gains = lax.dynamic_slice(gain, (chip_slice * 2 * width_part,), (2 * width_part,))
-        gains = gains.astype(f32).reshape(2, width_part)
-        gains = jnp.where(core == 0, gains, gains[::-1])
+        sis_second = shift(send_second, "core", CORE, 1)
+        start = chip_slice * 2 * width_part
+        gains = lax.dynamic_slice(gain.reshape(1, full_width), (0, start), (1, 2 * width_part))
 
     with jax.named_scope("projection"):
-        parts, up, down = partials(rows, rows_sis, gains, qkv_weight, w_sis)
+        near_up, up, down, near_down = partials(FIRST, rows, rows_sis, gains, own_first, sis_first)
         up, down = shift(up, "z", Z, 1), shift(down, "z", Z, -1)
-        up, down = ring_add(first_kernel, up, down, parts, 3)
-        for k in (2, 1):
-            up, down = shift(up, "z", Z, 1), shift(down, "z", Z, -1)
-            if k == 2:
-                out_weight, up, down = lax.optimization_barrier((out_weight, up, down))
-            up, down = ring_add(next_kernel, up, down, parts, k)
+        parts = partials(SECOND, rows, rows_sis, gains, own_second, sis_second)
+        up, down, parts = lax.optimization_barrier((up, down, parts))
+        up, down = ring_add(first_kernel, up, down, near_up, near_down)
+        up, down, out_weight = lax.optimization_barrier((up, down, out_weight))
+        parts = dict(zip(SECOND, parts))
         up, down = shift(up, "z", Z, 1), shift(down, "z", Z, -1)
-        mine, other = ring_last(up, down, parts)
+        share = share_rows(pltpu.with_memory_space_constraint(out_weight, pltpu.HBM))
+        shared = lax.all_to_all(share, "z", 0, 0, tiled=True)
+        up, down = ring_add(next_kernel, up, down, parts[2], parts[6])
+        up, down = shift(up, "z", Z, 1), shift(down, "z", Z, -1)
+        shared, up, down = lax.optimization_barrier((shared, up, down))
+        out_w = lax.all_gather(shared, CTX, axis=1, tiled=True)
+        up, down = ring_add(next_kernel, up, down, parts[1], parts[7])
+        up, down = shift(up, "z", Z, 1), shift(down, "z", Z, -1)
+        mine, other = ring_last(up, down, parts[0])
         other = shift(other, "x_hi", X_HI, 1)
 
     with jax.named_scope("tables"):
@@ -463,20 +487,18 @@
         cosine = jnp.concatenate([cosine, cosine], axis=1)
         sine = jnp.concatenate([-sine, sine], axis=1)
 
-    with jax.named_scope("out_weights"):
-        shared = lax.all_to_all(share_rows(out_weight), "z", 0, 0, tiled=True)
-        out_w = lax.all_gather(shared, CTX, axis=1, tiled=True)
-
     with jax.named_scope("attention"):
         payload, queries = finish(full_width, mine, other, cosine, sine, onehot)
         blocks = lax.all_to_all(payload, CTX, 0, 0, tiled=True)
         attn = attend(queries, blocks)
 
     with jax.named_scope("output"):
-        pieces = [None] * Z
-        pieces[0] = attn
-        for d in (4, 3, 5, 2, 6, 1, 7):
-            pieces[d] = shift(attn, "z", Z, d)
+        pieces = [attn] + [None] * (Z - 1)
+        for d in (1, 2, 3):
+            pieces[d] = shift(pieces[d - 1], "z", Z, 1)
+            pieces[Z - d] = shift(pieces[(Z - d + 1) % Z], "z", Z, -1)
+            if d == 1:
+                pieces[Z // 2] = shift(attn, "z", Z, Z // 2)
         keep, near, far = project(out_w, pieces)
         near = shift(near, "core", CORE, 1).astype(f32)
         far = (far + near[:, width_part:]).astype(bf16)

time: 177 us -> 170 us (0.960); the launches traced: 176 us -> 167 us
  waiting for transfers between devices: 63.8 us -> 48.3 us
  starting transfers between devices: 33.8 us -> 43.6 us
  local copies, waits for them, and re-layouts: 12.1 us -> 3.92 us
  Pallas kernels: 14.6 us -> 20.3 us
    ppermute x20 -> x21, waiting for transfers between devices: 63.8 us -> 47 us  [shift(): lax.ppermute(value, axis, [(i, (i + distance) % size) for i in range(size)])]
    all_to_all x1 -> x0, blocking collectives: 15.9 us -> none  [shards(): shared = lax.all_to_all(share_rows(out_weight), 'z', 0, 0, tiled=True)]
    all_to_all x1, blocking collectives: 16.4 us -> 30.7 us  [shards(): blocks = lax.all_to_all(payload, CTX, 0, 0, tiled=True)]
    unnamed x32 -> x26, local copies, waits for them, and re-layouts: 9.57 us -> 3.16 us
    pallas_call x7 -> x8, Pallas kernels: 8.65 us -> 14.4 us  [the longest x2 5.14 us: partials(): pl.pallas_call(functools.partial(partial_kernel, ks), out_shape=tuple(sha...]
    all_to_all x0 -> x1, starting transfers between devices: none -> 5.57 us  [shards(): shared = lax.all_to_all(share, 'z', 0, 0, tiled=True)]
    ppermute x20 -> x21, starting transfers between devices: 33.8 us -> 38 us  [shift(): lax.ppermute(value, axis, [(i, (i + distance) % size) for i in range(size)])]
  transfers between devices with their start and end apart: 21 -> 23, of which waited for: 12 -> 15; matrix products, arithmetic and copies ran while one was open for 4% -> 1% of each run, Pallas kernels for 2% -> 7%
where the time goes in v1:
time: 170 us; the launch traced here: 167 us
  waiting for transfers between devices  48.3 us (28%)
  starting transfers between devices  43.6 us (26%)
  blocking collectives  30.7 us (18%)
  Pallas kernels  20.3 us (12%)
  between operations  13.6 us (8%)
  other arithmetic  4.42 us (3%)
  local copies, waits for them, and re-layouts  3.92 us (2%)
  matrix products  2.23 us (1%)
    ppermute x21, waiting for transfers between devices, shift(): lax.ppermute(value, axis, [(i, (i + distance) % size) for i in range(size)])  47 us
    ppermute x21, starting transfers between devices, shift(): lax.ppermute(value, axis, [(i, (i + distance) % size) for i in range(size)])  38 us
    all_to_all x1, blocking collectives, shards(): blocks = lax.all_to_all(payload, CTX, 0, 0, tiled=True)  30.7 us
    all_to_all x1, starting transfers between devices, shards(): shared = lax.all_to_all(share, 'z', 0, 0, tiled=True)  5.57 us
    pallas_call x2, Pallas kernels, partials(): pl.pallas_call(functools.partial(partial_kernel, ks), out_shape=tuple(sha...  5.14 us
    pallas_call x1, Pallas kernels, pick_columns(): pl.pallas_call(pick_kernel, out_shape=(first, second, first, second), in_...  5 us
  transfers between devices with their start and end apart: 23, of which 15 were waited for; matrix products, arithmetic and copies ran while one was open for 1% of the time, Pallas kernels for 7%

profile of v1, /device:TPU:6, one launch (start us, length us, event | category | flops | bytes accessed | tf_op | source)
XLA Modules:
  0.0 167.1 jit_solution(2845830194174549175)
XLA Ops:
  6.5 0.7 broadcast_subtract_fusion
  7.2 1.1 fusion.14
  8.3 0.9 select_reduce_fusion
  9.2 0.8 fusion.1
  10.0 0.9 pad_maximum_fusion.own
  11.0 5.0 %weights.1 = (bf16[256,2304]{1,0:T(8,128)(2,1)}, bf16[256,3840]{1,0:T(8,128)(2,1)}, bf16[256,2304]{1,0:T(8,128)(2,1)S(1)}, bf16[256,3840]{1,0:T(8,128)(2,1)S(1)}) custom-call(bf16[256,12288]{1,0:T(8,128)(2,1)} %w.1), custom_call_target="tpu_custom_call" | custom-call | tf_op jit(solution)/shard_map/weights/pallas_call | solution.py:81
  16.0 0.1 collective-permute-start.4
  16.1 0.5 collective-permute-start.1
  16.6 0.1 collective-permute-start
  16.7 0.8 dynamic-slice.3
  17.4 3.1 %collective-permute-done.sis = bf16[272,256]{1,0:T(8,128)(2,1)} collective-permute-done((bf16[272,256]{1,0:T(8,128)(2,1)S(1)}, bf16[272,256]{1,0:T(8,128)(2,1)}, u32[]{:S(2)}, u32[]{:S(2)}) %collective-permute-start) | collective-permute-done | bytes 139296 | tf_op jit(solution)/shard_map/variant/ppermute | solution.py:30
  20.6 1.7 %collective-permute-done.1.w_sis = bf16[256,2304]{1,0:T(8,128)(2,1)} collective-permute-done((bf16[256,2304]{1,0:T(8,128)(2,1)}, bf16[256,2304]{1,0:T(8,128)(2,1)}, u32[]{:S(2)}, u32[]{:S(2)}) %collective-permute-start.1) | collective-permute-done | bytes 1179680 | tf_op jit(solution)/shard_map/weights/ppermute | solution.py:30
  22.3 2.3 %projection.7 = (bf16[288,768]{1,0:T(8,128)(2,1)S(1)}, bf16[288,384]{1,0:T(8,128)(2,1)S(1)}, bf16[288,384]{1,0:T(8,128)(2,1)S(1)}, bf16[288,768]{1,0:T(8,128)(2,1)S(1)}) custom-call(bf16[272,256]{1,0:T(8,128)(2,1)S(1)} %pad_maximum_fusion.own, bf16[272,256]{1,0:T(8,128)(2,1)} %collective-permute-done.sis, bf16[1,512]{1,0:T(2,128)(2,1)S(1)} %dynamic_slice.3.gains, ...), custom_call_target="tpu_custom_call" | custom-call | flops 641728512 | bytes 4718592 | tf_op jit(solution)/shard_map/projection/pallas_call | solution.py:142
  24.5 2.0 %collective-permute-start.2 = (bf16[288,384]{1,0:T(8,128)(2,1)S(1)}, bf16[288,384]{1,0:T(8,128)(2,1)S(1)}, u32[]{:S(2)}, u32[]{:S(2)}) collective-permute-start(bf16[288,384]{1,0:T(8,128)(2,1)S(1)} %get-tuple-element.50), channel_id=1, source_target_pairs={{0,16},{16,32},{32,48},{48,64},{64,80},{80,96},{96,112},{112,0},{1... | collective-permute-start | bytes 663560 | tf_op jit(solution)/shard_map/projection/ppermute | solution.py:30
  26.5 4.0 %collective-permute-start.3 = (bf16[288,384]{1,0:T(8,128)(2,1)S(1)}, bf16[288,384]{1,0:T(8,128)(2,1)S(1)}, u32[]{:S(2)}, u32[]{:S(2)}) collective-permute-start(bf16[288,384]{1,0:T(8,128)(2,1)S(1)} %get-tuple-element.51), channel_id=1, source_target_pairs={{0,112},{16,0},{32,16},{48,32},{64,48},{80,64},{96,80},{112,96},{1... | collective-permute-start | bytes 663560 | tf_op jit(solution)/shard_map/projection/ppermute | solution.py:30
  30.5 2.9 %projection.8 = (bf16[288,768]{1,0:T(8,128)(2,1)S(1)}, bf16[288,768]{1,0:T(8,128)(2,1)S(1)}, bf16[288,768]{1,0:T(8,128)(2,1)S(1)}, bf16[288,768]{1,0:T(8,128)(2,1)S(1)}, bf16[288,768]{1,0:T(8,128)(2,1)S(1)}) custom-call(bf16[272,256]{1,0:T(8,128)(2,1)S(1)} %pad_maximum_fusion.own, bf16[272,256]{1,0:T(8,128)(2,1)} %collective-permute-done.sis, ...), custom_call_target="tpu_custom_call" | custom-call | flops 1069547520 | bytes 7864320 | tf_op jit(solution)/shard_map/projection/pallas_call | solution.py:142
  33.4 0.8 copy-done.2
  34.2 0.8 copy-done.4
  35.0 1.2 collective-permute-done.2.up
  36.2 1.0 projection.9
  37.2 3.2 %collective-permute-start.6 = (bf16[288,768]{1,0:T(8,128)(2,1)}, bf16[288,768]{1,0:T(8,128)(2,1)S(1)}, u32[]{:S(2)}, u32[]{:S(2)}) collective-permute-start(bf16[288,768]{1,0:T(8,128)(2,1)} %get-tuple-element.67), channel_id=1, source_target_pairs={{0,112},{16,0},{32,16},{48,32},{64,48},{80,64},{96,80},{112,96},{1... | collective-permute-start | bytes 1327112 | tf_op jit(solution)/shard_map/projection/ppermute | solution.py:30
  40.4 1.7 %projection.10 = bf16[8,16,1024]{2,1,0:T(8,128)(2,1)} custom-call(bf16[128,8192]{1,0:T(8,128)(2,1)} %w.2), custom_call_target="tpu_custom_call" | custom-call | tf_op jit(solution)/shard_map/projection/pallas_call | solution.py:368
  42.2 5.6 %all-to-all-start = ((bf16[8,16,1024]{2,1,0:T(8,128)(2,1)}), bf16[8,16,1024]{2,1,0:T(8,128)(2,1)S(1)}, u32[]{:S(2)}, u32[]{:S(2)}) async-start(bf16[8,16,1024]{2,1,0:T(8,128)(2,1)} %projection.10), calls=%async_computation | async-start | bytes 524288 | tf_op jit(solution)/shard_map/projection/all_to_all | solution.py:471
  47.8 2.5 %collective-permute-done.5.up = bf16[288,768]{1,0:T(8,128)(2,1)S(1)} collective-permute-done((bf16[288,768]{1,0:T(8,128)(2,1)}, bf16[288,768]{1,0:T(8,128)(2,1)S(1)}, u32[]{:S(2)}, u32[]{:S(2)}) %collective-permute-start.5) | collective-permute-done | bytes 442400 | tf_op jit(solution)/shard_map/projection/ppermute | solution.py:30
  50.3 3.3 %collective-permute-done.6.down = bf16[288,768]{1,0:T(8,128)(2,1)S(1)} collective-permute-done((bf16[288,768]{1,0:T(8,128)(2,1)}, bf16[288,768]{1,0:T(8,128)(2,1)S(1)}, u32[]{:S(2)}, u32[]{:S(2)}) %collective-permute-start.6) | collective-permute-done | bytes 442400 | tf_op jit(solution)/shard_map/projection/ppermute | solution.py:30
  53.6 1.0 projection.11
  54.6 0.6 collective-permute-start.7
  55.3 3.2 %collective-permute-start.8 = (bf16[288,768]{1,0:T(8,128)(2,1)}, bf16[288,768]{1,0:T(8,128)(2,1)S(1)}, u32[]{:S(2)}, u32[]{:S(2)}) collective-permute-start(bf16[288,768]{1,0:T(8,128)(2,1)} %get-tuple-element.71), channel_id=1, source_target_pairs={{0,112},{16,0},{32,16},{48,32},{64,48},{80,64},{96,80},{112,96},{1... | collective-permute-start | bytes 1327112 | tf_op jit(solution)/shard_map/projection/ppermute | solution.py:30
  58.5 1.3 all-to-all-done
  59.8 5.9 %collective-permute-done.7.up = bf16[288,768]{1,0:T(8,128)(2,1)S(1)} collective-permute-done((bf16[288,768]{1,0:T(8,128)(2,1)}, bf16[288,768]{1,0:T(8,128)(2,1)S(1)}, u32[]{:S(2)}, u32[]{:S(2)}) %collective-permute-start.7) | collective-permute-done | bytes 442400 | tf_op jit(solution)/shard_map/projection/ppermute | solution.py:30
  65.8 0.2 projection.12
  66.1 1.8 %collective-permute-start.9 = (bf16[288,768]{1,0:T(8,128)(2,1)S(1)}, bf16[288,768]{1,0:T(8,128)(2,1)S(1)}, u32[]{:S(2)}, u32[]{:S(2)}) collective-permute-start(bf16[288,768]{1,0:T(8,128)(2,1)S(1)} %get-tuple-element.77), channel_id=1, source_target_pairs={{0,16},{16,32},{32,48},{48,64},{64,80},{80,96},{96,112},{112,0},{1... | collective-permute-start | bytes 1327112 | tf_op jit(solution)/shard_map/projection/ppermute | solution.py:30
  67.8 1.5 collective-permute-start.10
  69.4 0.6 fusion.5
  70.0 0.1 pad_maximum_fusion.1
  70.1 5.5 %collective-permute-done.9.up = bf16[288,768]{1,0:T(8,128)(2,1)S(1)} collective-permute-done((bf16[288,768]{1,0:T(8,128)(2,1)S(1)}, bf16[288,768]{1,0:T(8,128)(2,1)S(1)}, u32[]{:S(2)}, u32[]{:S(2)}) %collective-permute-start.9) | collective-permute-done | bytes 442400 | tf_op jit(solution)/shard_map/projection/ppermute | solution.py:30
  75.7 0.5 collective-permute-done.10.down
  76.2 0.2 projection.13
  76.4 1.5 collective-permute-start.11
  77.9 0.1 fusion.15
  78.0 6.0 %collective-permute-done.11.other = bf16[288,384]{1,0:T(8,128)(2,1)S(1)} collective-permute-done((bf16[288,384]{1,0:T(8,128)(2,1)S(1)}, bf16[288,384]{1,0:T(8,128)(2,1)S(1)}, u32[]{:S(2)}, u32[]{:S(2)}) %collective-permute-start.11) | collective-permute-done | bytes 221216 | tf_op jit(solution)/shard_map/projection/ppermute | solution.py:30
  83.9 0.6 attention.2
  84.6 30.7 %all_to_all.10.blocks = bf16[8,288,256]{2,1,0:T(8,128)(2,1)S(1)} all-to-all(bf16[8,288,256]{2,1,0:T(8,128)(2,1)S(1)} %get-tuple-element.83), channel_id=1, replica_groups=mesh['x_hi'=2,'z'=8,'core'=2,'x_lo'=2,'y'=4] {'x_lo','y'}, dimensions={0} | all-to-all | bytes 2359296 | tf_op jit(solution)/shard_map/attention/all_to_all | solution.py:492
  115.3 3.0 %attention.3.refs_0_ = bf16[512,128]{1,0:T(8,128)(2,1)S(1)} custom-call(bf16[512,128]{1,0:T(8,128)(2,1)S(1)} %get-tuple-element.82.queries, bf16[8,288,256]{2,1,0:T(8,128)(2,1)S(1)} %all_to_all.10.blocks), custom_call_target="tpu_custom_call" | custom-call | tf_op jit(solution)/shard_map/attention/pallas_call | solution.py:324
  118.3 1.6 collective-permute-start.12
  119.8 1.7 %collective-permute-start.16 = (bf16[512,128]{1,0:T(8,128)(2,1)S(1)}, bf16[512,128]{1,0:T(8,128)(2,1)S(1)}, u32[]{:S(2)}, u32[]{:S(2)}) collective-permute-start(bf16[512,128]{1,0:T(8,128)(2,1)S(1)} %attention.3.refs_0_), channel_id=1, source_target_pairs={{0,112},{16,0},{32,16},{48,32},{64,48},{80,64},{96,80},{112,96},{1... | collective-permute-start | bytes 393224 | tf_op jit(solution)/shard_map/output/ppermute | solution.py:30
  121.6 2.9 %collective-permute-done.12.refs_1_ = bf16[512,128]{1,0:T(8,128)(2,1)S(1)} collective-permute-done((bf16[512,128]{1,0:T(8,128)(2,1)S(1)}, bf16[512,128]{1,0:T(8,128)(2,1)S(1)}, u32[]{:S(2)}, u32[]{:S(2)}) %collective-permute-start.12) | collective-permute-done | bytes 131104 | tf_op jit(solution)/shard_map/output/ppermute | solution.py:30
  124.5 0.3 collective-permute-start.13
  124.8 2.9 %collective-permute-start.17 = (bf16[512,128]{1,0:T(8,128)(2,1)S(1)}, bf16[512,128]{1,0:T(8,128)(2,1)S(1)}, u32[]{:S(2)}, u32[]{:S(2)}) collective-permute-start(bf16[512,128]{1,0:T(8,128)(2,1)S(1)} %collective-permute-done.16.refs_7_), channel_id=1, source_target_pairs={{0,112},{16,0},{32,16},{48,32},{64,48},{80,64},{96,80},{112,96},{1... | collective-permute-start | bytes 393224 | tf_op jit(solution)/shard_map/output/ppermute | solution.py:30
  127.8 9.3 %collective-permute-start.15 = (bf16[512,128]{1,0:T(8,128)(2,1)S(1)}, bf16[512,128]{1,0:T(8,128)(2,1)S(1)}, u32[]{:S(2)}, u32[]{:S(2)}) collective-permute-start(bf16[512,128]{1,0:T(8,128)(2,1)S(1)} %attention.3.refs_0_), channel_id=1, source_target_pairs={{0,64},{16,80},{32,96},{48,112},{64,0},{80,16},{96,32},{112,48},{1... | collective-permute-start | bytes 393224 | tf_op jit(solution)/shard_map/output/ppermute | solution.py:30
  137.1 3.2 %collective-permute-start.18 = (bf16[512,128]{1,0:T(8,128)(2,1)S(1)}, bf16[512,128]{1,0:T(8,128)(2,1)S(1)}, u32[]{:S(2)}, u32[]{:S(2)}) collective-permute-start(bf16[512,128]{1,0:T(8,128)(2,1)S(1)} %collective-permute-done.17.refs_6_), channel_id=1, source_target_pairs={{0,112},{16,0},{32,16},{48,32},{64,48},{80,64},{96,80},{112,96},{1... | collective-permute-start | bytes 393224 | tf_op jit(solution)/shard_map/output/ppermute | solution.py:30
  140.3 0.8 collective-permute-done.15.refs_4_
  141.2 2.1 %collective-permute-done.14.refs_3_ = bf16[512,128]{1,0:T(8,128)(2,1)S(1)} collective-permute-done((bf16[512,128]{1,0:T(8,128)(2,1)S(1)}, bf16[512,128]{1,0:T(8,128)(2,1)S(1)}, u32[]{:S(2)}, u32[]{:S(2)}) %collective-permute-start.14) | collective-permute-done | bytes 131104 | tf_op jit(solution)/shard_map/output/ppermute | solution.py:30
  143.3 1.6 copy-done.1
  144.9 2.3 %output.1 = (f32[512,256]{1,0:T(8,128)S(1)}, bf16[512,512]{1,0:T(8,128)(2,1)S(1)}, f32[512,256]{1,0:T(8,128)S(1)}) custom-call(bf16[8,128,1024]{2,1,0:T(8,128)(2,1)S(1)} %copy-done.1, bf16[512,128]{1,0:T(8,128)(2,1)S(1)} %attention.3.refs_0_, bf16[512,128]{1,0:T(8,128)(2,1)S(1)} %collective-permute-done.12.refs_1_, ...), custom_call_target="tpu_custom_call" | custom-call | tf_op jit(solution)/shard_map/output/pallas_call | solution.py:410
  147.2 0.1 collective-permute-start.19
  147.3 1.9 %collective-permute-done.19 = bf16[512,512]{1,0:T(8,128)(2,1)S(1)} collective-permute-done((bf16[512,512]{1,0:T(8,128)(2,1)S(1)}, bf16[512,512]{1,0:T(8,128)(2,1)S(1)}, u32[]{:S(2)}, u32[]{:S(2)}) %collective-permute-start.19) | collective-permute-done | bytes 524320 | tf_op jit(solution)/shard_map/output/ppermute | solution.py:30
  149.2 0.1 convert_element_type.49
  149.3 0.1 fusion.2
  149.4 0.1 collective-permute-start.20
  149.6 0.3 fusion
  149.9 9.5 %collective-permute-done.20 = bf16[512,256]{1,0:T(8,128)(2,1)S(1)} collective-permute-done((bf16[512,256]{1,0:T(8,128)(2,1)S(1)}, bf16[512,256]{1,0:T(8,128)(2,1)S(1)}, u32[]{:S(2)}, u32[]{:S(2)}) %collective-permute-start.20) | collective-permute-done | bytes 262176 | tf_op jit(solution)/shard_map/output/ppermute | solution.py:30
  159.4 0.1 fusion.3
  159.5 0.8 fusion.4
  (40 shorter events, 0.2 us)
Async XLA Ops:
  6.5 2.7 %copy-start = (bf16[512,256]{1,0:T(8,128)(2,1)S(1)}, bf16[512,256]{1,0:T(8,128)(2,1)}, u32[]{:S(2)}) copy-start(bf16[512,256]{1,0:T(8,128)(2,1)} %param.10) | copy-start | bytes 786436
  7.2 2.8 %copy-start.10 = (s32[16]{0:T(128)}, s32[16]{0:T(128)S(1)}, u32[]{:S(2)}) copy-start(s32[16]{0:T(128)S(1)} %broadcast_subtract_fusion) | copy-start | bytes 196
  16.0 14.6 %collective-permute-start.4 = (bf16[256,3840]{1,0:T(8,128)(2,1)}, bf16[256,3840]{1,0:T(8,128)(2,1)}, u32[]{:S(2)}, u32[]{:S(2)}) collective-permute-start(bf16[256,3840]{1,0:T(8,128)(2,1)} %get-tuple-element.53), channel_id=1, source_target_pairs={{0,8},{8,0},{1,9},{9,1},{2,10},{10,2},{3,11},{11,3},{4,12},{12,4},... | collective-permute-start | bytes 5898248 | tf_op jit(solution)/shard_map/variant/ppermute | solution.py:30
  16.1 6.2 %collective-permute-start.1 = (bf16[256,2304]{1,0:T(8,128)(2,1)}, bf16[256,2304]{1,0:T(8,128)(2,1)}, u32[]{:S(2)}, u32[]{:S(2)}) collective-permute-start(bf16[256,2304]{1,0:T(8,128)(2,1)} %get-tuple-element.49), channel_id=1, source_target_pairs={{0,8},{8,0},{1,9},{9,1},{2,10},{10,2},{3,11},{11,3},{4,12},{12,4},... | collective-permute-start | bytes 3538952 | tf_op jit(solution)/shard_map/weights/ppermute | solution.py:30
  16.6 4.0 %collective-permute-start = (bf16[272,256]{1,0:T(8,128)(2,1)S(1)}, bf16[272,256]{1,0:T(8,128)(2,1)}, u32[]{:S(2)}, u32[]{:S(2)}) collective-permute-start(bf16[272,256]{1,0:T(8,128)(2,1)S(1)} %pad_maximum_fusion.own), channel_id=1, source_target_pairs={{0,8},{8,0},{1,9},{9,1},{2,10},{10,2},{3,11},{11,3},{4,12},{12,4},... | collective-permute-start | bytes 417800 | tf_op jit(solution)/shard_map/variant/ppermute | solution.py:30
  24.5 11.7 %collective-permute-start.2 = (bf16[288,384]{1,0:T(8,128)(2,1)S(1)}, bf16[288,384]{1,0:T(8,128)(2,1)S(1)}, u32[]{:S(2)}, u32[]{:S(2)}) collective-permute-start(bf16[288,384]{1,0:T(8,128)(2,1)S(1)} %get-tuple-element.50), channel_id=1, source_target_pairs={{0,16},{16,32},{32,48},{48,64},{64,80},{80,96},{96,112},{112,0},{1... | collective-permute-start | bytes 663560 | tf_op jit(solution)/shard_map/projection/ppermute | solution.py:30
  26.5 9.7 %collective-permute-start.3 = (bf16[288,384]{1,0:T(8,128)(2,1)S(1)}, bf16[288,384]{1,0:T(8,128)(2,1)S(1)}, u32[]{:S(2)}, u32[]{:S(2)}) collective-permute-start(bf16[288,384]{1,0:T(8,128)(2,1)S(1)} %get-tuple-element.51), channel_id=1, source_target_pairs={{0,112},{16,0},{32,16},{48,32},{64,48},{80,64},{96,80},{112,96},{1... | collective-permute-start | bytes 663560 | tf_op jit(solution)/shard_map/projection/ppermute | solution.py:30
  33.4 0.8 copy-start.2
  34.2 0.8 copy-start.4
  35.0 2.2 %copy-start.6 = (bf16[288,768]{1,0:T(8,128)(2,1)}, bf16[288,768]{1,0:T(8,128)(2,1)S(1)}, u32[]{:S(2)}) copy-start(bf16[288,768]{1,0:T(8,128)(2,1)S(1)} %get-tuple-element.79.near) | copy-start | bytes 1327108
  36.2 17.4 %copy-start.3 = (bf16[288,768]{1,0:T(8,128)(2,1)S(1)}, bf16[288,768]{1,0:T(8,128)(2,1)}, u32[]{:S(2)}) copy-start(bf16[288,768]{1,0:T(8,128)(2,1)} %copy-done.2) | copy-start | bytes 1327108
  36.2 17.4 %copy-start.5 = (bf16[288,768]{1,0:T(8,128)(2,1)S(1)}, bf16[288,768]{1,0:T(8,128)(2,1)}, u32[]{:S(2)}) copy-start(bf16[288,768]{1,0:T(8,128)(2,1)} %copy-done.4) | copy-start | bytes 1327108
  37.2 28.6 %copy-start.12 = (s32[16]{0:T(128)S(1)}, s32[16]{0:T(128)}, u32[]{:S(2)}) copy-start(s32[16]{0:T(128)} %param.14) | copy-start | bytes 196
  37.2 13.1 %collective-permute-start.5 = (bf16[288,768]{1,0:T(8,128)(2,1)}, bf16[288,768]{1,0:T(8,128)(2,1)S(1)}, u32[]{:S(2)}, u32[]{:S(2)}) collective-permute-start(bf16[288,768]{1,0:T(8,128)(2,1)} %get-tuple-element.66), channel_id=1, source_target_pairs={{0,16},{16,32},{32,48},{48,64},{64,80},{80,96},{96,112},{112,0},{1... | collective-permute-start | bytes 1327112 | tf_op jit(solution)/shard_map/projection/ppermute | solution.py:30
  37.2 16.4 %collective-permute-start.6 = (bf16[288,768]{1,0:T(8,128)(2,1)}, bf16[288,768]{1,0:T(8,128)(2,1)S(1)}, u32[]{:S(2)}, u32[]{:S(2)}) collective-permute-start(bf16[288,768]{1,0:T(8,128)(2,1)} %get-tuple-element.67), channel_id=1, source_target_pairs={{0,112},{16,0},{32,16},{48,32},{64,48},{80,64},{96,80},{112,96},{1... | collective-permute-start | bytes 1327112 | tf_op jit(solution)/shard_map/projection/ppermute | solution.py:30
  42.2 17.6 %all-to-all-start = ((bf16[8,16,1024]{2,1,0:T(8,128)(2,1)}), bf16[8,16,1024]{2,1,0:T(8,128)(2,1)S(1)}, u32[]{:S(2)}, u32[]{:S(2)}) async-start(bf16[8,16,1024]{2,1,0:T(8,128)(2,1)} %projection.10), calls=%async_computation | async-start | bytes 524288 | tf_op jit(solution)/shard_map/projection/all_to_all | solution.py:471
  47.8 95.5 %all-gather.2.cloned.1.call-start = ((), (), s32[]{:S(2)}) async-start(), calls=%async_computation.2 | async-start | bytes 2359296 | tf_op jit(solution)/shard_map/projection/all_gather | solution.py:475
  54.6 21.5 %copy-start.7 = (bf16[288,768]{1,0:T(8,128)(2,1)S(1)}, bf16[288,768]{1,0:T(8,128)(2,1)}, u32[]{:S(2)}) copy-start(bf16[288,768]{1,0:T(8,128)(2,1)} %copy-done.6) | copy-start | bytes 1327108
  54.6 11.1 %collective-permute-start.7 = (bf16[288,768]{1,0:T(8,128)(2,1)}, bf16[288,768]{1,0:T(8,128)(2,1)S(1)}, u32[]{:S(2)}, u32[]{:S(2)}) collective-permute-start(bf16[288,768]{1,0:T(8,128)(2,1)} %get-tuple-element.70), channel_id=1, source_target_pairs={{0,16},{16,32},{32,48},{48,64},{64,80},{80,96},{96,112},{112,0},{1... | collective-permute-start | bytes 1327112 | tf_op jit(solution)/shard_map/projection/ppermute | solution.py:30
  55.3 10.5 %collective-permute-start.8 = (bf16[288,768]{1,0:T(8,128)(2,1)}, bf16[288,768]{1,0:T(8,128)(2,1)S(1)}, u32[]{:S(2)}, u32[]{:S(2)}) collective-permute-start(bf16[288,768]{1,0:T(8,128)(2,1)} %get-tuple-element.71), channel_id=1, source_target_pairs={{0,112},{16,0},{32,16},{48,32},{64,48},{80,64},{96,80},{112,96},{1... | collective-permute-start | bytes 1327112 | tf_op jit(solution)/shard_map/projection/ppermute | solution.py:30
  59.8 5.9 %copy-start.9 = (bf16[8,16,1024]{2,1,0:T(8,128)(2,1)}, bf16[8,16,1024]{2,1,0:T(8,128)(2,1)S(1)}, u32[]{:S(2)}) copy-start(bf16[8,16,1024]{2,1,0:T(8,128)(2,1)S(1)} %all-to-all-done) | copy-start | bytes 786436
  65.8 12.1 %copy-start.11 = (s32[16]{0:T(128)S(1)}, s32[16]{0:T(128)}, u32[]{:S(2)}) copy-start(s32[16]{0:T(128)} %copy-done.10) | copy-start | bytes 196
  66.1 9.6 %collective-permute-start.9 = (bf16[288,768]{1,0:T(8,128)(2,1)S(1)}, bf16[288,768]{1,0:T(8,128)(2,1)S(1)}, u32[]{:S(2)}, u32[]{:S(2)}) collective-permute-start(bf16[288,768]{1,0:T(8,128)(2,1)S(1)} %get-tuple-element.77), channel_id=1, source_target_pairs={{0,16},{16,32},{32,48},{48,64},{64,80},{80,96},{96,112},{112,0},{1... | collective-permute-start | bytes 1327112 | tf_op jit(solution)/shard_map/projection/ppermute | solution.py:30
  67.8 8.3 %collective-permute-start.10 = (bf16[288,768]{1,0:T(8,128)(2,1)S(1)}, bf16[288,768]{1,0:T(8,128)(2,1)S(1)}, u32[]{:S(2)}, u32[]{:S(2)}) collective-permute-start(bf16[288,768]{1,0:T(8,128)(2,1)S(1)} %get-tuple-element.78), channel_id=1, source_target_pairs={{0,112},{16,0},{32,16},{48,32},{64,48},{80,64},{96,80},{112,96},{1... | collective-permute-start | bytes 1327112 | tf_op jit(solution)/shard_map/projection/ppermute | solution.py:30
  76.4 7.6 %collective-permute-start.11 = (bf16[288,384]{1,0:T(8,128)(2,1)S(1)}, bf16[288,384]{1,0:T(8,128)(2,1)S(1)}, u32[]{:S(2)}, u32[]{:S(2)}) collective-permute-start(bf16[288,384]{1,0:T(8,128)(2,1)S(1)} %get-tuple-element.81), channel_id=1, source_target_pairs={{0,128},{128,0},{1,129},{129,1},{2,130},{130,2},{3,131},{131,3},{4... | collective-permute-start | bytes 663560 | tf_op jit(solution)/shard_map/projection/ppermute | solution.py:30
  118.3 6.3 %collective-permute-start.12 = (bf16[512,128]{1,0:T(8,128)(2,1)S(1)}, bf16[512,128]{1,0:T(8,128)(2,1)S(1)}, u32[]{:S(2)}, u32[]{:S(2)}) collective-permute-start(bf16[512,128]{1,0:T(8,128)(2,1)S(1)} %attention.3.refs_0_), channel_id=1, source_target_pairs={{0,16},{16,32},{32,48},{48,64},{64,80},{80,96},{96,112},{112,0},{1... | collective-permute-start | bytes 393224 | tf_op jit(solution)/shard_map/output/ppermute | solution.py:30
  119.8 5.0 %collective-permute-start.16 = (bf16[512,128]{1,0:T(8,128)(2,1)S(1)}, bf16[512,128]{1,0:T(8,128)(2,1)S(1)}, u32[]{:S(2)}, u32[]{:S(2)}) collective-permute-start(bf16[512,128]{1,0:T(8,128)(2,1)S(1)} %attention.3.refs_0_), channel_id=1, source_target_pairs={{0,112},{16,0},{32,16},{48,32},{64,48},{80,64},{96,80},{112,96},{1... | collective-permute-start | bytes 393224 | tf_op jit(solution)/shard_map/output/ppermute | solution.py:30
  124.5 12.6 %collective-permute-start.13 = (bf16[512,128]{1,0:T(8,128)(2,1)S(1)}, bf16[512,128]{1,0:T(8,128)(2,1)S(1)}, u32[]{:S(2)}, u32[]{:S(2)}) collective-permute-start(bf16[512,128]{1,0:T(8,128)(2,1)S(1)} %collective-permute-done.12.refs_1_), channel_id=1, source_target_pairs={{0,16},{16,32},{32,48},{48,64},{64,80},{80,96},{96,112},{112,0},{1... | collective-permute-start | bytes 393224 | tf_op jit(solution)/shard_map/output/ppermute | solution.py:30
  124.8 12.3 %collective-permute-start.17 = (bf16[512,128]{1,0:T(8,128)(2,1)S(1)}, bf16[512,128]{1,0:T(8,128)(2,1)S(1)}, u32[]{:S(2)}, u32[]{:S(2)}) collective-permute-start(bf16[512,128]{1,0:T(8,128)(2,1)S(1)} %collective-permute-done.16.refs_7_), channel_id=1, source_target_pairs={{0,112},{16,0},{32,16},{48,32},{64,48},{80,64},{96,80},{112,96},{1... | collective-permute-start | bytes 393224 | tf_op jit(solution)/shard_map/output/ppermute | solution.py:30
  127.8 13.4 %collective-permute-start.15 = (bf16[512,128]{1,0:T(8,128)(2,1)S(1)}, bf16[512,128]{1,0:T(8,128)(2,1)S(1)}, u32[]{:S(2)}, u32[]{:S(2)}) collective-permute-start(bf16[512,128]{1,0:T(8,128)(2,1)S(1)} %attention.3.refs_0_), channel_id=1, source_target_pairs={{0,64},{16,80},{32,96},{48,112},{64,0},{80,16},{96,32},{112,48},{1... | collective-permute-start | bytes 393224 | tf_op jit(solution)/shard_map/output/ppermute | solution.py:30
  137.1 6.2 %collective-permute-start.14 = (bf16[512,128]{1,0:T(8,128)(2,1)S(1)}, bf16[512,128]{1,0:T(8,128)(2,1)S(1)}, u32[]{:S(2)}, u32[]{:S(2)}) collective-permute-start(bf16[512,128]{1,0:T(8,128)(2,1)S(1)} %collective-permute-done.13.refs_2_), channel_id=1, source_target_pairs={{0,16},{16,32},{32,48},{48,64},{64,80},{80,96},{96,112},{112,0},{1... | collective-permute-start | bytes 393224 | tf_op jit(solution)/shard_map/output/ppermute | solution.py:30
  137.1 6.2 %collective-permute-start.18 = (bf16[512,128]{1,0:T(8,128)(2,1)S(1)}, bf16[512,128]{1,0:T(8,128)(2,1)S(1)}, u32[]{:S(2)}, u32[]{:S(2)}) collective-permute-start(bf16[512,128]{1,0:T(8,128)(2,1)S(1)} %collective-permute-done.17.refs_6_), channel_id=1, source_target_pairs={{0,112},{16,0},{32,16},{48,32},{64,48},{80,64},{96,80},{112,96},{1... | collective-permute-start | bytes 393224 | tf_op jit(solution)/shard_map/output/ppermute | solution.py:30
  143.3 1.6 copy-start.1
  147.2 2.3 %copy-start.8 = (bf16[256,256]{1,0:T(8,128)(2,1)S(1)}, bf16[256,256]{1,0:T(8,128)(2,1)}, u32[]{:S(2)}) copy-start(bf16[256,256]{1,0:T(8,128)(2,1)} %param.8) | copy-start | bytes 393220
  147.2 2.0 %collective-permute-start.19 = (bf16[512,512]{1,0:T(8,128)(2,1)S(1)}, bf16[512,512]{1,0:T(8,128)(2,1)S(1)}, u32[]{:S(2)}, u32[]{:S(2)}) collective-permute-start(bf16[512,512]{1,0:T(8,128)(2,1)S(1)} %get-tuple-element.85), channel_id=1, source_target_pairs={{0,8},{8,0},{1,9},{9,1},{2,10},{10,2},{3,11},{11,3},{4,12},{12,4},... | collective-permute-start | bytes 1572872 | tf_op jit(solution)/shard_map/output/ppermute | solution.py:30
  149.4 9.9 %collective-permute-start.20 = (bf16[512,256]{1,0:T(8,128)(2,1)S(1)}, bf16[512,256]{1,0:T(8,128)(2,1)S(1)}, u32[]{:S(2)}, u32[]{:S(2)}) collective-permute-start(bf16[512,256]{1,0:T(8,128)(2,1)S(1)} %fusion.2), channel_id=1, source_target_pairs={{0,128},{128,0},{1,129},{129,1},{2,130},{130,2},{3,131},{131,3},{4... | collective-permute-start | bytes 786440 | tf_op jit(solution)/shard_map/output/ppermute | solution.py:30
Sparse Core Ops, SparseCore 0:
  65.9 49.8 all-gather.1

commit v2 on v1

--- a/solution.py
+++ b/solution.py
@@ -50,13 +50,55 @@
 SECOND = (6, 7, 0, 1, 2)
 
 
-def pick_kernel(w, *refs):
-    sems = refs[-1]
+def variant_kernel(pos, base, ids, hidden, embed, rows, onehot, variant):
+    first = (lax.axis_index("x_lo") * Y + lax.axis_index("y")) * TOK
+    vocab = embed.shape[0]
+    spot = lax.broadcasted_iota(jnp.int32, (VAR, TOK), 0)
+    lane = lax.broadcasted_iota(jnp.int32, (VAR, TOK), 1)
+    word_spot = lax.broadcasted_iota(jnp.int32, (VAR, vocab), 0)
+    word = lax.broadcasted_iota(jnp.int32, (VAR, vocab), 1)
+    places = jnp.zeros((VAR, TOK), f32)
+    words = jnp.zeros((VAR, vocab), f32)
+    for j in range(VAR):
+        place = pos[j] - first
+        places = jnp.where((spot == j) & (lane == place), 1.0, places)
+        new = jnp.where(word == base[j], 1.0, 0.0)
+        old = jnp.where(word == ids[place], 1.0, 0.0)
+        words = jnp.where(word_spot == j, new - old, words)
+    places = places.astype(bf16)
+    change = jnp.dot(words.astype(bf16), embed[...], preferred_element_type=f32)
+    picked = jnp.dot(places, hidden[...], preferred_element_type=f32)
+    changed_rows = (picked + change).astype(bf16)
+    rows[:TOK] = hidden[...]
+    rows[TOK:] = changed_rows
+    onehot[...] = places
+    contract = (((0,), (0,)), ((), ()))
+    placed = lax.dot_general(places, changed_rows, contract, preferred_element_type=f32)
+    ones = jnp.ones((VAR, hidden.shape[1]), bf16)
+    changed = lax.dot_general(places, ones, contract, preferred_element_type=f32)
+    variant[...] = jnp.where(changed > 0.5, placed, hidden[...].astype(f32)).astype(bf16)
+
+
+def make_variant(pos, base, ids, hidden, embed):
+    width = hidden.shape[1]
+    smem = pl.BlockSpec(memory_space=pltpu.SMEM)
+    return pl.pallas_call(
+        variant_kernel,
+        out_shape=(
+            jax.ShapeDtypeStruct((ROWS, width), bf16),
+            jax.ShapeDtypeStruct((VAR, TOK), bf16),
+            jax.ShapeDtypeStruct((TOK, width), bf16),
+        ),
+        in_specs=[smem, smem, smem, vmem(), vmem()],
+        out_specs=(vmem(),) * 3,
+        compiler_params=limit(4),
+    )(pos, base, ids, hidden, embed)
+
+
+def column_copies(ks, w, send, own, sems):
     z, core, x_hi = lax.axis_index("z"), lax.axis_index("core"), lax.axis_index("x_hi")
     copies = []
-    for index, (whose, ks) in enumerate(
-        ((1 - core, FIRST), (1 - core, SECOND), (core, FIRST), (core, SECOND))
-    ):
+    for index, (whose, out) in enumerate(((1 - core, send), (core, own))):
         for i, k in enumerate(ks):
             for xr in range(X_HI):
                 head_pair = lax.rem(x_hi + xr, X_HI) * Z + lax.rem(z + k, Z)
@@ -65,27 +107,80 @@
                 copies.append(
                     pltpu.make_async_copy(
                         w.at[:, pl.ds(start, QKV)],
-                        refs[index].at[:, slot * QKV : (slot + 1) * QKV],
+                        out.at[:, slot * QKV : (slot + 1) * QKV],
                         sems.at[index, slot],
                     )
                 )
+    return copies
+
+
+def first_columns_kernel(w, send, own, sems):
+    copies = column_copies(FIRST, w, send, own, sems)
     for copy in copies:
         copy.start()
     for copy in copies:
         copy.wait()
 
 
-def pick_columns(w):
-    first = jax.ShapeDtypeStruct((w.shape[0], len(FIRST) * X_HI * QKV), bf16)
-    second = jax.ShapeDtypeStruct((w.shape[0], len(SECOND) * X_HI * QKV), bf16)
-    return pl.pallas_call(
-        pick_kernel,
-        out_shape=(first, second, first, second),
+def first_columns(w):
+    columns = jax.ShapeDtypeStruct((w.shape[0], len(FIRST) * X_HI * QKV), bf16)
+    return pl.pallas_call(
+        first_columns_kernel,
+        out_shape=(columns, columns),
         in_specs=[hbm()],
-        out_specs=(vmem(),) * 4,
-        scratch_shapes=[pltpu.SemaphoreType.DMA((4, len(SECOND) * X_HI))],
+        out_specs=(vmem(), vmem()),
+        scratch_shapes=[pltpu.SemaphoreType.DMA((2, len(FIRST) * X_HI))],
+        compiler_params=limit(8),
+    )(pltpu.with_memory_space_constraint(w, pltpu.HBM))
+
+
+def second_columns_kernel(w, out_weight, send, own, share, buffer, sems, share_sems, out_sem):
+    my_block = lax.axis_index("x_lo") * Y + lax.axis_index("y")
+    size, width = buffer.shape[1], buffer.shape[2] // X_HI
+    share_copies = []
+    for k in range(Z):
+        for x in range(X_HI):
+            start = (x * Z + k) * width
+            share_copies.append(
+                pltpu.make_async_copy(
+                    out_weight.at[
+                        pl.ds(pl.multiple_of(my_block * size, size), size), start : start + width
+                    ],
+                    buffer.at[k, :, x * width : (x + 1) * width],
+                    share_sems.at[k, x],
+                )
+            )
+    copies = column_copies(SECOND, w, send, own, sems)
+    for copy in share_copies + copies:
+        copy.start()
+    for copy in share_copies:
+        copy.wait()
+    out_copy = pltpu.make_async_copy(buffer, share, out_sem)
+    out_copy.start()
+    for copy in copies:
+        copy.wait()
+    out_copy.wait()
+
+
+def second_columns(w, out_weight):
+    columns = jax.ShapeDtypeStruct((w.shape[0], len(SECOND) * X_HI * QKV), bf16)
+    shape = (Z, out_weight.shape[0] // BLOCKS, out_weight.shape[1] // Z)
+    return pl.pallas_call(
+        second_columns_kernel,
+        out_shape=(columns, columns, jax.ShapeDtypeStruct(shape, bf16)),
+        in_specs=[hbm(), hbm()],
+        out_specs=(vmem(), vmem(), hbm()),
+        scratch_shapes=[
+            pltpu.VMEM(shape, bf16),
+            pltpu.SemaphoreType.DMA((2, len(SECOND) * X_HI)),
+            pltpu.SemaphoreType.DMA((Z, X_HI)),
+            pltpu.SemaphoreType.DMA(()),
+        ],
         compiler_params=limit(12),
-    )(w)
+    )(
+        pltpu.with_memory_space_constraint(w, pltpu.HBM),
+        pltpu.with_memory_space_constraint(out_weight, pltpu.HBM),
+    )
 
 
 def two_rows(row, width):
@@ -338,47 +433,6 @@
     )(queries, blocks)
 
 
-def share_kernel(w, out, buffer, sems, out_sem):
-    my_block = lax.axis_index("x_lo") * Y + lax.axis_index("y")
-    share, columns = buffer.shape[1], buffer.shape[2] // X_HI
-    rows = pl.ds(pl.multiple_of(my_block * share, share), share)
-    copies = []
-    for k in range(Z):
-        for x in range(X_HI):
-            start = (x * Z + k) * columns
-            copies.append(
-                pltpu.make_async_copy(
-                    w.at[rows, start : start + columns],
-                    buffer.at[k, :, x * columns : (x + 1) * columns],
-                    sems.at[k, x],
-                )
-            )
-    for copy in copies:
-        copy.start()
-    for copy in copies:
-        copy.wait()
-    copy = pltpu.make_async_copy(buffer, out, out_sem)
-    copy.start()
-    copy.wait()
-
-
-def share_rows(w):
-    rows, columns = w.shape
-    shape = (Z, rows // BLOCKS, columns // Z)
-    return pl.pallas_call(
-        share_kernel,
-        out_shape=jax.ShapeDtypeStruct(shape, bf16),
-        in_specs=[hbm()],
-        out_specs=hbm(),
-        scratch_shapes=[
-            pltpu.VMEM(shape, bf16),
-            pltpu.SemaphoreType.DMA((Z, X_HI)),
-            pltpu.SemaphoreType.DMA(()),
-        ],
-        compiler_params=limit(4),
-    )(w)
-
-
 def project_kernel(w, *refs):
     shards, (keep, near, far), (joined, turned) = refs[:Z], refs[Z : Z + 3], refs[Z + 3 :]
     z, core, x_hi = lax.axis_index("z"), lax.axis_index("core"), lax.axis_index("x_hi")
@@ -426,53 +480,37 @@
 
 def shards(hidden, gain, embed, qkv_weight, out_weight, ref_ids, var_pos, var_base):
     tok_rows, width_part = hidden.shape
-    vocab_size = embed.shape[0]
     full_width = out_weight.shape[1]
     x_hi, z, core = lax.axis_index("x_hi"), lax.axis_index("z"), lax.axis_index("core")
     my_block = lax.axis_index("x_lo") * Y + lax.axis_index("y")
     chip_slice = x_hi * Z + z
 
-    with jax.named_scope("weights"):
-        send_first, send_second, own_first, own_second = pick_columns(
-            pltpu.with_memory_space_constraint(qkv_weight, pltpu.HBM)
-        )
+    with jax.named_scope("inputs"):
+        rows, onehot, variant = make_variant(var_pos, var_base, ref_ids, hidden, embed)
+        rows, qkv_weight = lax.optimization_barrier((rows, qkv_weight))
+        rows_sis = shift(rows, "core", CORE, 1)
+        send_first, own_first = first_columns(qkv_weight)
         sis_first = shift(send_first, "core", CORE, 1)
-
-    with jax.named_scope("variant"):
-        local_pos = var_pos - my_block * tok_rows
-        var_spots = local_pos[:, None] == jnp.arange(tok_rows)[None, :]
-        onehot = var_spots.astype(bf16)
-        changed = jnp.any(var_spots, axis=0)
-        ref_at = jnp.sum(jnp.where(var_spots, ref_ids[None, :], 0), axis=1)
-        vocab_line = jnp.arange(vocab_size)[None, :]
-        onehot_diff = (vocab_line == var_base[:, None]).astype(bf16) - (
-            vocab_line == ref_at[:, None]
-        ).astype(bf16)
-        change = jnp.dot(onehot_diff, embed, preferred_element_type=f32)
-        picked_rows = jnp.dot(onehot, hidden, preferred_element_type=f32)
-        var_rows = (picked_rows + change).astype(bf16)
-        rows = jnp.concatenate([hidden, var_rows], axis=0)
-        rows, send_second = lax.optimization_barrier((rows, send_second))
-        rows_sis = shift(rows, "core", CORE, 1)
+        rows_sis, send_first, qkv_weight = lax.optimization_barrier((rows_sis, send_first, qkv_weight))
+        send_second, own_second, share = second_columns(qkv_weight, out_weight)
         sis_second = shift(send_second, "core", CORE, 1)
+        shared = lax.all_to_all(share, "z", 0, 0, tiled=True)
         start = chip_slice * 2 * width_part
         gains = lax.dynamic_slice(gain.reshape(1, full_width), (0, start), (1, 2 * width_part))
 
     with jax.named_scope("projection"):
         near_up, up, down, near_down = partials(FIRST, rows, rows_sis, gains, own_first, sis_first)
         up, down = shift(up, "z", Z, 1), shift(down, "z", Z, -1)
+        up, down, shared = lax.optimization_barrier((up, down, shared))
+        out_w = lax.all_gather(shared, CTX, axis=1, tiled=True)
+        up, down = ring_add(first_kernel, up, down, near_up, near_down)
+        up, rows, down = lax.optimization_barrier((up, rows, down))
+        up, down = shift(up, "z", Z, 1), shift(down, "z", Z, -1)
         parts = partials(SECOND, rows, rows_sis, gains, own_second, sis_second)
         up, down, parts = lax.optimization_barrier((up, down, parts))
-        up, down = ring_add(first_kernel, up, down, near_up, near_down)
-        up, down, out_weight = lax.optimization_barrier((up, down, out_weight))
         parts = dict(zip(SECOND, parts))
-        up, down = shift(up, "z", Z, 1), shift(down, "z", Z, -1)
-        share = share_rows(pltpu.with_memory_space_constraint(out_weight, pltpu.HBM))
-        shared = lax.all_to_all(share, "z", 0, 0, tiled=True)
         up, down = ring_add(next_kernel, up, down, parts[2], parts[6])
         up, down = shift(up, "z", Z, 1), shift(down, "z", Z, -1)
-        shared, up, down = lax.optimization_barrier((shared, up, down))
-        out_w = lax.all_gather(shared, CTX, axis=1, tiled=True)
         up, down = ring_add(next_kernel, up, down, parts[1], parts[7])
         up, down = shift(up, "z", Z, 1), shift(down, "z", Z, -1)
         mine, other = ring_last(up, down, parts[0])
@@ -491,6 +529,7 @@
         payload, queries = finish(full_width, mine, other, cosine, sine, onehot)
         blocks = lax.all_to_all(payload, CTX, 0, 0, tiled=True)
         attn = attend(queries, blocks)
+        attn, out_w = lax.optimization_barrier((attn, out_w))
 
     with jax.named_scope("output"):
         pieces = [attn] + [None] * (Z - 1)
@@ -504,9 +543,7 @@
         far = (far + near[:, width_part:]).astype(bf16)
         far = shift(far, "x_hi", X_HI, 1).astype(f32)
         branch = (keep + near[:, :width_part] + far).reshape(2, tok_rows, width_part)
-        placed = jnp.dot(onehot.T, var_rows, preferred_element_type=f32)
-        variant = jnp.where(changed[:, None], placed, hidden.astype(f32))
-        seqs = jnp.stack([hidden.astype(f32), variant])
+        seqs = jnp.stack([hidden, variant]).astype(f32)
         return (seqs + branch).astype(bf16)
 
 

time: 170 us -> 163 us (0.959)
  blocking collectives: 30.7 us -> 18.2 us
  local copies, waits for them, and re-layouts: 3.92 us -> 11.7 us
  waiting for transfers between devices: 48.3 us -> 56 us
  starting transfers between devices: 43.6 us -> 39.2 us
  other arithmetic: 4.42 us -> 1.82 us
  matrix products: 2.23 us -> 0 us
    all_to_all x1, blocking collectives: 30.7 us -> 18.2 us  [shards(): blocks = lax.all_to_all(payload, CTX, 0, 0, tiled=True)]
    unnamed x26 -> x38, local copies, waits for them, and re-layouts: 3.16 us -> 11 us
    ppermute x21, starting transfers between devices: 38 us -> 30.7 us  [shift(): lax.ppermute(value, axis, [(i, (i + distance) % size) for i in range(size)])]
    ppermute x21, waiting for transfers between devices: 47 us -> 52.1 us  [shift(): lax.ppermute(value, axis, [(i, (i + distance) % size) for i in range(size)])]
    all_to_all x1, starting transfers between devices: 5.57 us -> 8.47 us  [shards(): shared = lax.all_to_all(share, 'z', 0, 0, tiled=True)]
    all_to_all x1, waiting for transfers between devices: 1.27 us -> 3.89 us  [shards(): shared = lax.all_to_all(share, 'z', 0, 0, tiled=True)]
    dot_general x3 -> x0, matrix products: 2.23 us -> none  [the longest x1 1.09 us: shards(): picked_rows = jnp.dot(onehot, hidden, preferred_element_type=f32)]
    pallas_call x2 -> x3, Pallas kernels: 6.74 us -> 7.85 us  [the longest x1 3.97 us: second_columns(): pl.pallas_call(second_columns_kernel, out_shape=(columns, columns, jax.Sh...]
  transfers between devices with their start and end apart: 23 -> 23, of which waited for: 15 -> 15; matrix products, arithmetic and copies ran while one was open for 1% -> 1% of each run, Pallas kernels for 7% -> 9%
where the time goes in v2:
time: 163 us; the launch traced here: 161 us
  waiting for transfers between devices  56 us (34%)
  starting transfers between devices  39.2 us (24%)
  Pallas kernels  20.2 us (12%)
  blocking collectives  18.2 us (11%)
  between operations  13.7 us (8%)
  local copies, waits for them, and re-layouts  11.7 us (7%)
  other arithmetic  1.82 us (1%)
    ppermute x21, waiting for transfers between devices, shift(): lax.ppermute(value, axis, [(i, (i + distance) % size) for i in range(size)])  52.1 us
    ppermute x21, starting transfers between devices, shift(): lax.ppermute(value, axis, [(i, (i + distance) % size) for i in range(size)])  30.7 us
    all_to_all x1, blocking collectives, shards(): blocks = lax.all_to_all(payload, CTX, 0, 0, tiled=True)  18.2 us
    unnamed x38, local copies, waits for them, and re-layouts  11 us
    all_to_all x1, starting transfers between devices, shards(): shared = lax.all_to_all(share, 'z', 0, 0, tiled=True)  8.47 us
    pallas_call x2, Pallas kernels, partials(): pl.pallas_call(functools.partial(partial_kernel, ks), out_shape=tuple(sha...  5.68 us
    pallas_call x1, Pallas kernels, second_columns(): pl.pallas_call(second_columns_kernel, out_shape=(columns, columns, jax.Sh...  3.97 us
    all_to_all x1, waiting for transfers between devices, shards(): shared = lax.all_to_all(share, 'z', 0, 0, tiled=True)  3.89 us
  transfers between devices with their start and end apart: 23, of which 15 were waited for; matrix products, arithmetic and copies ran while one was open for 1% of the time, Pallas kernels for 9%

profile of v2, /device:TPU:6, one launch (start us, length us, event | category | flops | bytes accessed | tf_op | source)
XLA Modules:
  0.0 160.8 jit_solution(10030160472172162680)
XLA Ops:
  6.5 0.9 copy-done.1
  7.4 0.9 copy-done.9
  8.4 0.7 copy-done.15
  9.0 0.7 copy-done.17
  9.7 0.7 copy-done.18
  10.4 1.0 inputs.3
  11.4 0.6 copy-done.13
  12.0 2.9 %inputs.4 = (bf16[256,2304]{1,0:T(8,128)(2,1)}, bf16[256,2304]{1,0:T(8,128)(2,1)S(1)}) custom-call(bf16[256,12288]{1,0:T(8,128)(2,1)} %w.1), custom_call_target="tpu_custom_call" | custom-call | tf_op jit(solution)/shard_map/inputs/pallas_call | solution.py:127
  15.0 0.5 collective-permute-start
  15.5 2.2 %collective-permute-done.sis = bf16[272,256]{1,0:T(8,128)(2,1)S(1)} collective-permute-done((bf16[272,256]{1,0:T(8,128)(2,1)S(1)}, bf16[272,256]{1,0:T(8,128)(2,1)S(1)}, u32[]{:S(2)}, u32[]{:S(2)}) %collective-permute-start) | collective-permute-done | bytes 139296 | tf_op jit(solution)/shard_map/inputs/ppermute | solution.py:30
  17.7 4.0 %inputs.5 = (bf16[256,3840]{1,0:T(8,128)(2,1)}, bf16[256,3840]{1,0:T(8,128)(2,1)S(1)}, bf16[8,16,1024]{2,1,0:T(8,128)(2,1)S(1)}) custom-call(bf16[256,12288]{1,0:T(8,128)(2,1)} %w.1, bf16[128,8192]{1,0:T(8,128)(2,1)} %out_weight.1), custom_call_target="tpu_custom_call" | custom-call | tf_op jit(solution)/shard_map/inputs/pallas_call | solution.py:168
  21.6 0.7 copy-done.10
  22.3 0.4 collective-permute-start.6
  22.7 8.5 %all-to-all-start = ((bf16[8,16,1024]{2,1,0:T(8,128)(2,1)}), bf16[8,16,1024]{2,1,0:T(8,128)(2,1)}, u32[]{:S(2)}, u32[]{:S(2)}) async-start(bf16[8,16,1024]{2,1,0:T(8,128)(2,1)} %copy-done.10), calls=%async_computation | async-start | bytes 524288 | tf_op jit(solution)/shard_map/inputs/all_to_all | solution.py:497
  31.2 0.8 dynamic-slice.3
  32.0 2.9 %projection.6 = (bf16[288,768]{1,0:T(8,128)(2,1)S(1)}, bf16[288,384]{1,0:T(8,128)(2,1)}, bf16[288,384]{1,0:T(8,128)(2,1)}, bf16[288,768]{1,0:T(8,128)(2,1)S(1)}) custom-call(bf16[272,256]{1,0:T(8,128)(2,1)S(1)} %get-tuple-element.73.own, bf16[272,256]{1,0:T(8,128)(2,1)S(1)} %collective-permute-done.sis, bf16[1,512]{1,0:T(2,128)(2,1)S(1)} %dynamic_slice.3.gains, ...), custom_call_target="tpu_custom_call" | custom-call | flops 641728512 | bytes 4718592 | tf_op jit(solution)/shard_map/projection/pallas_call | solution.py:237
  34.9 0.8 copy-done.5
  35.6 0.8 copy-done.7
  36.4 2.0 %collective-permute-start.2 = (bf16[288,384]{1,0:T(8,128)(2,1)}, bf16[288,384]{1,0:T(8,128)(2,1)S(1)}, u32[]{:S(2)}, u32[]{:S(2)}) collective-permute-start(bf16[288,384]{1,0:T(8,128)(2,1)} %get-tuple-element.61), channel_id=1, source_target_pairs={{0,16},{16,32},{32,48},{48,64},{64,80},{80,96},{96,112},{112,0},{1... | collective-permute-start | bytes 663560 | tf_op jit(solution)/shard_map/projection/ppermute | solution.py:30
  38.4 1.3 collective-permute-start.3
  39.6 3.9 %all-to-all-done = bf16[8,16,1024]{2,1,0:T(8,128)(2,1)} async-done(((bf16[8,16,1024]{2,1,0:T(8,128)(2,1)}), bf16[8,16,1024]{2,1,0:T(8,128)(2,1)}, u32[]{:S(2)}, u32[]{:S(2)}) %all-to-all-start) | async-done | bytes 262176 | tf_op jit(solution)/shard_map/inputs/all_to_all | solution.py:497
  43.5 2.5 %collective-permute-done.2.up = bf16[288,384]{1,0:T(8,128)(2,1)S(1)} collective-permute-done((bf16[288,384]{1,0:T(8,128)(2,1)}, bf16[288,384]{1,0:T(8,128)(2,1)S(1)}, u32[]{:S(2)}, u32[]{:S(2)}) %collective-permute-start.2) | collective-permute-done | bytes 221216 | tf_op jit(solution)/shard_map/projection/ppermute | solution.py:30
  46.1 1.0 copy-done.6
  47.1 1.0 copy-done.8
  48.1 0.2 projection.7
  48.3 1.4 collective-permute-start.4
  49.7 1.9 %collective-permute-start.5 = (bf16[288,768]{1,0:T(8,128)(2,1)S(1)}, bf16[288,768]{1,0:T(8,128)(2,1)S(1)}, u32[]{:S(2)}, u32[]{:S(2)}) collective-permute-start(bf16[288,768]{1,0:T(8,128)(2,1)S(1)} %get-tuple-element.72), channel_id=1, source_target_pairs={{0,112},{16,0},{32,16},{48,32},{64,48},{80,64},{96,80},{112,96},{1... | collective-permute-start | bytes 1327112 | tf_op jit(solution)/shard_map/projection/ppermute | solution.py:30
  51.6 0.7 copy-done.12
  52.3 2.8 %projection.8 = (bf16[288,768]{1,0:T(8,128)(2,1)S(1)}, bf16[288,768]{1,0:T(8,128)(2,1)S(1)}, bf16[288,768]{1,0:T(8,128)(2,1)S(1)}, bf16[288,768]{1,0:T(8,128)(2,1)S(1)}, bf16[288,768]{1,0:T(8,128)(2,1)S(1)}) custom-call(bf16[272,256]{1,0:T(8,128)(2,1)S(1)} %get-tuple-element.73.own, bf16[272,256]{1,0:T(8,128)(2,1)S(1)} %collective-permute-done.sis, ...), custom_call_target="tpu_custom_call" | custom-call | flops 1069547520 | bytes 7864320 | tf_op jit(solution)/shard_map/projection/pallas_call | solution.py:237
  55.1 6.0 %collective-permute-done.4.up = bf16[288,768]{1,0:T(8,128)(2,1)S(1)} collective-permute-done((bf16[288,768]{1,0:T(8,128)(2,1)S(1)}, bf16[288,768]{1,0:T(8,128)(2,1)S(1)}, u32[]{:S(2)}, u32[]{:S(2)}) %collective-permute-start.4) | collective-permute-done | bytes 442400 | tf_op jit(solution)/shard_map/projection/ppermute | solution.py:30
  61.1 0.2 projection.9
  61.3 1.7 %collective-permute-start.7 = (bf16[288,768]{1,0:T(8,128)(2,1)S(1)}, bf16[288,768]{1,0:T(8,128)(2,1)S(1)}, u32[]{:S(2)}, u32[]{:S(2)}) collective-permute-start(bf16[288,768]{1,0:T(8,128)(2,1)S(1)} %get-tuple-element.85), channel_id=1, source_target_pairs={{0,16},{16,32},{32,48},{48,64},{64,80},{80,96},{96,112},{112,0},{1... | collective-permute-start | bytes 1327112 | tf_op jit(solution)/shard_map/projection/ppermute | solution.py:30
  63.1 1.6 collective-permute-start.8
  64.7 8.6 %collective-permute-done.7.up = bf16[288,768]{1,0:T(8,128)(2,1)S(1)} collective-permute-done((bf16[288,768]{1,0:T(8,128)(2,1)S(1)}, bf16[288,768]{1,0:T(8,128)(2,1)S(1)}, u32[]{:S(2)}, u32[]{:S(2)}) %collective-permute-start.7) | collective-permute-done | bytes 442400 | tf_op jit(solution)/shard_map/projection/ppermute | solution.py:30
  73.2 0.2 projection.10
  73.5 1.0 collective-permute-start.9
  74.4 2.4 %collective-permute-start.10 = (bf16[288,768]{1,0:T(8,128)(2,1)S(1)}, bf16[288,768]{1,0:T(8,128)(2,1)S(1)}, u32[]{:S(2)}, u32[]{:S(2)}) collective-permute-start(bf16[288,768]{1,0:T(8,128)(2,1)S(1)} %get-tuple-element.90), channel_id=1, source_target_pairs={{0,112},{16,0},{32,16},{48,32},{64,48},{80,64},{96,80},{112,96},{1... | collective-permute-start | bytes 1327112 | tf_op jit(solution)/shard_map/projection/ppermute | solution.py:30
  76.8 7.6 %collective-permute-done.9.up = bf16[288,768]{1,0:T(8,128)(2,1)S(1)} collective-permute-done((bf16[288,768]{1,0:T(8,128)(2,1)S(1)}, bf16[288,768]{1,0:T(8,128)(2,1)S(1)}, u32[]{:S(2)}, u32[]{:S(2)}) %collective-permute-start.9) | collective-permute-done | bytes 442400 | tf_op jit(solution)/shard_map/projection/ppermute | solution.py:30
  84.4 0.2 projection.11
  84.6 1.8 %collective-permute-start.11 = (bf16[288,384]{1,0:T(8,128)(2,1)S(1)}, bf16[288,384]{1,0:T(8,128)(2,1)S(1)}, u32[]{:S(2)}, u32[]{:S(2)}) collective-permute-start(bf16[288,384]{1,0:T(8,128)(2,1)S(1)} %get-tuple-element.93), channel_id=1, source_target_pairs={{0,128},{128,0},{1,129},{129,1},{2,130},{130,2},{3,131},{131,3},{4... | collective-permute-start | bytes 663560 | tf_op jit(solution)/shard_map/projection/ppermute | solution.py:30
  86.4 0.6 fusion.2
  87.0 0.1 pad_maximum_fusion
  87.1 5.2 %collective-permute-done.11.other = bf16[288,384]{1,0:T(8,128)(2,1)S(1)} collective-permute-done((bf16[288,384]{1,0:T(8,128)(2,1)S(1)}, bf16[288,384]{1,0:T(8,128)(2,1)S(1)}, u32[]{:S(2)}, u32[]{:S(2)}) %collective-permute-start.11) | collective-permute-done | bytes 221216 | tf_op jit(solution)/shard_map/projection/ppermute | solution.py:30
  92.3 0.6 attention.2
  92.9 18.2 %all_to_all.10.blocks = bf16[8,288,256]{2,1,0:T(8,128)(2,1)S(1)} all-to-all(bf16[8,288,256]{2,1,0:T(8,128)(2,1)S(1)} %get-tuple-element.96), channel_id=1, replica_groups=mesh['x_hi'=2,'z'=8,'core'=2,'x_lo'=2,'y'=4] {'x_lo','y'}, dimensions={0} | all-to-all | bytes 2359296 | tf_op jit(solution)/shard_map/attention/all_to_all | solution.py:530
  111.1 3.0 %attention.3.refs_0_ = bf16[512,128]{1,0:T(8,128)(2,1)S(1)} custom-call(bf16[512,128]{1,0:T(8,128)(2,1)S(1)} %get-tuple-element.95.queries, bf16[8,288,256]{2,1,0:T(8,128)(2,1)S(1)} %all_to_all.10.blocks), custom_call_target="tpu_custom_call" | custom-call | tf_op jit(solution)/shard_map/attention/pallas_call | solution.py:419
  114.2 3.2 %collective-permute-start.16 = (bf16[512,128]{1,0:T(8,128)(2,1)S(1)}, bf16[512,128]{1,0:T(8,128)(2,1)S(1)}, u32[]{:S(2)}, u32[]{:S(2)}) collective-permute-start(bf16[512,128]{1,0:T(8,128)(2,1)S(1)} %attention.3.refs_0_), channel_id=1, source_target_pairs={{0,112},{16,0},{32,16},{48,32},{64,48},{80,64},{96,80},{112,96},{1... | collective-permute-start | bytes 393224 | tf_op jit(solution)/shard_map/output/ppermute | solution.py:30
  117.4 4.7 %collective-permute-done.12.refs_1_ = bf16[512,128]{1,0:T(8,128)(2,1)S(1)} collective-permute-done((bf16[512,128]{1,0:T(8,128)(2,1)S(1)}, bf16[512,128]{1,0:T(8,128)(2,1)S(1)}, u32[]{:S(2)}, u32[]{:S(2)}) %collective-permute-start.12) | collective-permute-done | bytes 131104 | tf_op jit(solution)/shard_map/output/ppermute | solution.py:30
  122.1 0.7 collective-permute-done.16.refs_7_
  122.8 3.7 %collective-permute-start.17 = (bf16[512,128]{1,0:T(8,128)(2,1)S(1)}, bf16[512,128]{1,0:T(8,128)(2,1)S(1)}, u32[]{:S(2)}, u32[]{:S(2)}) collective-permute-start(bf16[512,128]{1,0:T(8,128)(2,1)S(1)} %collective-permute-done.16.refs_7_), channel_id=1, source_target_pairs={{0,112},{16,0},{32,16},{48,32},{64,48},{80,64},{96,80},{112,96},{1... | collective-permute-start | bytes 393224 | tf_op jit(solution)/shard_map/output/ppermute | solution.py:30
  126.5 2.1 %collective-permute-start.15 = (bf16[512,128]{1,0:T(8,128)(2,1)S(1)}, bf16[512,128]{1,0:T(8,128)(2,1)S(1)}, u32[]{:S(2)}, u32[]{:S(2)}) collective-permute-start(bf16[512,128]{1,0:T(8,128)(2,1)S(1)} %attention.3.refs_0_), channel_id=1, source_target_pairs={{0,64},{16,80},{32,96},{48,112},{64,0},{80,16},{96,32},{112,48},{1... | collective-permute-start | bytes 393224 | tf_op jit(solution)/shard_map/output/ppermute | solution.py:30
  128.6 1.3 collective-permute-done.13.refs_2_
  129.9 0.4 collective-permute-done.17.refs_6_
  130.3 3.7 %collective-permute-start.18 = (bf16[512,128]{1,0:T(8,128)(2,1)S(1)}, bf16[512,128]{1,0:T(8,128)(2,1)S(1)}, u32[]{:S(2)}, u32[]{:S(2)}) collective-permute-start(bf16[512,128]{1,0:T(8,128)(2,1)S(1)} %collective-permute-done.17.refs_6_), channel_id=1, source_target_pairs={{0,112},{16,0},{32,16},{48,32},{64,48},{80,64},{96,80},{112,96},{1... | collective-permute-start | bytes 393224 | tf_op jit(solution)/shard_map/output/ppermute | solution.py:30
  134.0 1.7 %collective-permute-done.15.refs_4_ = bf16[512,128]{1,0:T(8,128)(2,1)S(1)} collective-permute-done((bf16[512,128]{1,0:T(8,128)(2,1)S(1)}, bf16[512,128]{1,0:T(8,128)(2,1)S(1)}, u32[]{:S(2)}, u32[]{:S(2)}) %collective-permute-start.15) | collective-permute-done | bytes 131104 | tf_op jit(solution)/shard_map/output/ppermute | solution.py:30
  135.7 1.3 collective-permute-done.14.refs_3_
  137.0 1.6 copy-done
  138.6 2.3 %output.1 = (f32[512,256]{1,0:T(8,128)S(1)}, bf16[512,512]{1,0:T(8,128)(2,1)S(1)}, f32[512,256]{1,0:T(8,128)S(1)}) custom-call(bf16[8,128,1024]{2,1,0:T(8,128)(2,1)S(1)} %copy-done, bf16[512,128]{1,0:T(8,128)(2,1)S(1)} %attention.3.refs_0_, bf16[512,128]{1,0:T(8,128)(2,1)S(1)} %collective-permute-done.12.refs_1_, ...), custom_call_target="tpu_custom_call" | custom-call | tf_op jit(solution)/shard_map/output/pallas_call | solution.py:464
  141.0 1.9 %collective-permute-done.19 = bf16[512,512]{1,0:T(8,128)(2,1)S(1)} collective-permute-done((bf16[512,512]{1,0:T(8,128)(2,1)S(1)}, bf16[512,512]{1,0:T(8,128)(2,1)S(1)}, u32[]{:S(2)}, u32[]{:S(2)}) %collective-permute-start.19) | collective-permute-done | bytes 524320 | tf_op jit(solution)/shard_map/output/ppermute | solution.py:30
  142.9 0.1 convert_element_type.32
  143.2 1.9 %collective-permute-start.20 = (bf16[512,256]{1,0:T(8,128)(2,1)S(1)}, bf16[512,256]{1,0:T(8,128)(2,1)S(1)}, u32[]{:S(2)}, u32[]{:S(2)}) collective-permute-start(bf16[512,256]{1,0:T(8,128)(2,1)S(1)} %fusion), channel_id=1, source_target_pairs={{0,128},{128,0},{1,129},{129,1},{2,130},{130,2},{3,131},{131,3},{4... | collective-permute-start | bytes 786440 | tf_op jit(solution)/shard_map/output/ppermute | solution.py:30
  145.1 8.0 %collective-permute-done.20 = bf16[512,256]{1,0:T(8,128)(2,1)S(1)} collective-permute-done((bf16[512,256]{1,0:T(8,128)(2,1)S(1)}, bf16[512,256]{1,0:T(8,128)(2,1)S(1)}, u32[]{:S(2)}, u32[]{:S(2)}) %collective-permute-start.20) | collective-permute-done | bytes 262176 | tf_op jit(solution)/shard_map/output/ppermute | solution.py:30
  153.1 0.1 fusion.1
  153.2 0.8 add_convert_fusion
  (45 shorter events, 0.5 us)
Async XLA Ops:
  6.5 0.9 copy-start.1
  7.4 0.9 copy-start.9
  8.4 0.7 copy-start.15
  9.0 0.7 copy-start.17
  9.7 0.7 copy-start.18
  11.4 0.6 copy-start.13
  14.9 17.1 %collective-permute-start.1 = (bf16[256,2304]{1,0:T(8,128)(2,1)}, bf16[256,2304]{1,0:T(8,128)(2,1)}, u32[]{:S(2)}, u32[]{:S(2)}) collective-permute-start(bf16[256,2304]{1,0:T(8,128)(2,1)} %get-tuple-element.58), channel_id=1, source_target_pairs={{0,8},{8,0},{1,9},{9,1},{2,10},{10,2},{3,11},{11,3},{4,12},{12,4},... | collective-permute-start | bytes 3538952 | tf_op jit(solution)/shard_map/inputs/ppermute | solution.py:30
  15.0 2.7 %collective-permute-start = (bf16[272,256]{1,0:T(8,128)(2,1)S(1)}, bf16[272,256]{1,0:T(8,128)(2,1)S(1)}, u32[]{:S(2)}, u32[]{:S(2)}) collective-permute-start(bf16[272,256]{1,0:T(8,128)(2,1)S(1)} %get-tuple-element.73.own), channel_id=1, source_target_pairs={{0,8},{8,0},{1,9},{9,1},{2,10},{10,2},{3,11},{11,3},{4,12},{12,4},... | collective-permute-start | bytes 417800 | tf_op jit(solution)/shard_map/inputs/ppermute | solution.py:30
  21.6 0.7 copy-start.10
  22.3 29.3 %collective-permute-start.6 = (bf16[256,3840]{1,0:T(8,128)(2,1)}, bf16[256,3840]{1,0:T(8,128)(2,1)}, u32[]{:S(2)}, u32[]{:S(2)}) collective-permute-start(bf16[256,3840]{1,0:T(8,128)(2,1)} %get-tuple-element.75), channel_id=1, source_target_pairs={{0,8},{8,0},{1,9},{9,1},{2,10},{10,2},{3,11},{11,3},{4,12},{12,4},... | collective-permute-start | bytes 5898248 | tf_op jit(solution)/shard_map/inputs/ppermute | solution.py:30
  22.7 20.8 %all-to-all-start = ((bf16[8,16,1024]{2,1,0:T(8,128)(2,1)}), bf16[8,16,1024]{2,1,0:T(8,128)(2,1)}, u32[]{:S(2)}, u32[]{:S(2)}) async-start(bf16[8,16,1024]{2,1,0:T(8,128)(2,1)} %copy-done.10), calls=%async_computation | async-start | bytes 524288 | tf_op jit(solution)/shard_map/inputs/all_to_all | solution.py:497
  31.2 82.9 %all-gather.2.cloned.1.call-start = ((), (), s32[]{:S(2)}) async-start(), calls=%async_computation.2 | async-start | bytes 2359296 | tf_op jit(solution)/shard_map/projection/all_gather | solution.py:505
  32.0 6.4 %copy-start.11 = (bf16[1,512]{1,0:T(2,128)(2,1)}, bf16[1,512]{1,0:T(2,128)(2,1)S(1)}, u32[]{:S(2)}) copy-start(bf16[1,512]{1,0:T(2,128)(2,1)S(1)} %dynamic_slice.3.gains) | copy-start | bytes 3076
  34.9 0.8 copy-start.5
  35.6 0.8 copy-start.7
  36.4 9.7 %collective-permute-start.2 = (bf16[288,384]{1,0:T(8,128)(2,1)}, bf16[288,384]{1,0:T(8,128)(2,1)S(1)}, u32[]{:S(2)}, u32[]{:S(2)}) collective-permute-start(bf16[288,384]{1,0:T(8,128)(2,1)} %get-tuple-element.61), channel_id=1, source_target_pairs={{0,16},{16,32},{32,48},{48,64},{64,80},{80,96},{96,112},{112,0},{1... | collective-permute-start | bytes 663560 | tf_op jit(solution)/shard_map/projection/ppermute | solution.py:30
  38.4 7.7 %collective-permute-start.3 = (bf16[288,384]{1,0:T(8,128)(2,1)}, bf16[288,384]{1,0:T(8,128)(2,1)S(1)}, u32[]{:S(2)}, u32[]{:S(2)}) collective-permute-start(bf16[288,384]{1,0:T(8,128)(2,1)} %get-tuple-element.62), channel_id=1, source_target_pairs={{0,112},{16,0},{32,16},{48,32},{64,48},{80,64},{96,80},{112,96},{1... | collective-permute-start | bytes 663560 | tf_op jit(solution)/shard_map/projection/ppermute | solution.py:30
  46.1 1.0 copy-start.6
  47.1 1.0 copy-start.8
  48.3 12.8 %collective-permute-start.4 = (bf16[288,768]{1,0:T(8,128)(2,1)S(1)}, bf16[288,768]{1,0:T(8,128)(2,1)S(1)}, u32[]{:S(2)}, u32[]{:S(2)}) collective-permute-start(bf16[288,768]{1,0:T(8,128)(2,1)S(1)} %get-tuple-element.71), channel_id=1, source_target_pairs={{0,16},{16,32},{32,48},{48,64},{64,80},{80,96},{96,112},{112,0},{1... | collective-permute-start | bytes 1327112 | tf_op jit(solution)/shard_map/projection/ppermute | solution.py:30
  49.7 11.4 %collective-permute-start.5 = (bf16[288,768]{1,0:T(8,128)(2,1)S(1)}, bf16[288,768]{1,0:T(8,128)(2,1)S(1)}, u32[]{:S(2)}, u32[]{:S(2)}) collective-permute-start(bf16[288,768]{1,0:T(8,128)(2,1)S(1)} %get-tuple-element.72), channel_id=1, source_target_pairs={{0,112},{16,0},{32,16},{48,32},{64,48},{80,64},{96,80},{112,96},{1... | collective-permute-start | bytes 1327112 | tf_op jit(solution)/shard_map/projection/ppermute | solution.py:30
  51.6 0.7 copy-start.12
  55.1 6.2 %copy-start.3 = (bf16[288,768]{1,0:T(8,128)(2,1)}, bf16[288,768]{1,0:T(8,128)(2,1)S(1)}, u32[]{:S(2)}) copy-start(bf16[288,768]{1,0:T(8,128)(2,1)S(1)} %get-tuple-element.91.near) | copy-start | bytes 1327108
  55.1 21.7 %copy-start.16 = (s32[16]{0:T(128)S(1)}, s32[16]{0:T(128)}, u32[]{:S(2)}) copy-start(s32[16]{0:T(128)} %pos.1) | copy-start | bytes 196
  61.3 23.1 %copy-start.4 = (bf16[288,768]{1,0:T(8,128)(2,1)S(1)}, bf16[288,768]{1,0:T(8,128)(2,1)}, u32[]{:S(2)}) copy-start(bf16[288,768]{1,0:T(8,128)(2,1)} %copy-done.3) | copy-start | bytes 1327108
  61.3 11.9 %collective-permute-start.7 = (bf16[288,768]{1,0:T(8,128)(2,1)S(1)}, bf16[288,768]{1,0:T(8,128)(2,1)S(1)}, u32[]{:S(2)}, u32[]{:S(2)}) collective-permute-start(bf16[288,768]{1,0:T(8,128)(2,1)S(1)} %get-tuple-element.85), channel_id=1, source_target_pairs={{0,16},{16,32},{32,48},{48,64},{64,80},{80,96},{96,112},{112,0},{1... | collective-permute-start | bytes 1327112 | tf_op jit(solution)/shard_map/projection/ppermute | solution.py:30
  63.1 29.3 %copy-start.14 = (bf16[16,256]{1,0:T(8,128)(2,1)S(1)}, bf16[16,256]{1,0:T(8,128)(2,1)}, u32[]{:S(2)}) copy-start(bf16[16,256]{1,0:T(8,128)(2,1)} %copy-done.13) | copy-start | bytes 24580
  63.1 10.1 %collective-permute-start.8 = (bf16[288,768]{1,0:T(8,128)(2,1)S(1)}, bf16[288,768]{1,0:T(8,128)(2,1)S(1)}, u32[]{:S(2)}, u32[]{:S(2)}) collective-permute-start(bf16[288,768]{1,0:T(8,128)(2,1)S(1)} %get-tuple-element.86), channel_id=1, source_target_pairs={{0,112},{16,0},{32,16},{48,32},{64,48},{80,64},{96,80},{112,96},{1... | collective-permute-start | bytes 1327112 | tf_op jit(solution)/shard_map/projection/ppermute | solution.py:30
  73.5 11.0 %collective-permute-start.9 = (bf16[288,768]{1,0:T(8,128)(2,1)S(1)}, bf16[288,768]{1,0:T(8,128)(2,1)S(1)}, u32[]{:S(2)}, u32[]{:S(2)}) collective-permute-start(bf16[288,768]{1,0:T(8,128)(2,1)S(1)} %get-tuple-element.89), channel_id=1, source_target_pairs={{0,16},{16,32},{32,48},{48,64},{64,80},{80,96},{96,112},{112,0},{1... | collective-permute-start | bytes 1327112 | tf_op jit(solution)/shard_map/projection/ppermute | solution.py:30
  74.4 10.0 %collective-permute-start.10 = (bf16[288,768]{1,0:T(8,128)(2,1)S(1)}, bf16[288,768]{1,0:T(8,128)(2,1)S(1)}, u32[]{:S(2)}, u32[]{:S(2)}) collective-permute-start(bf16[288,768]{1,0:T(8,128)(2,1)S(1)} %get-tuple-element.90), channel_id=1, source_target_pairs={{0,112},{16,0},{32,16},{48,32},{64,48},{80,64},{96,80},{112,96},{1... | collective-permute-start | bytes 1327112 | tf_op jit(solution)/shard_map/projection/ppermute | solution.py:30
  84.6 7.7 %collective-permute-start.11 = (bf16[288,384]{1,0:T(8,128)(2,1)S(1)}, bf16[288,384]{1,0:T(8,128)(2,1)S(1)}, u32[]{:S(2)}, u32[]{:S(2)}) collective-permute-start(bf16[288,384]{1,0:T(8,128)(2,1)S(1)} %get-tuple-element.93), channel_id=1, source_target_pairs={{0,128},{128,0},{1,129},{129,1},{2,130},{130,2},{3,131},{131,3},{4... | collective-permute-start | bytes 663560 | tf_op jit(solution)/shard_map/projection/ppermute | solution.py:30
  114.1 8.0 %collective-permute-start.12 = (bf16[512,128]{1,0:T(8,128)(2,1)S(1)}, bf16[512,128]{1,0:T(8,128)(2,1)S(1)}, u32[]{:S(2)}, u32[]{:S(2)}) collective-permute-start(bf16[512,128]{1,0:T(8,128)(2,1)S(1)} %attention.3.refs_0_), channel_id=1, source_target_pairs={{0,16},{16,32},{32,48},{48,64},{64,80},{80,96},{96,112},{112,0},{1... | collective-permute-start | bytes 393224 | tf_op jit(solution)/shard_map/output/ppermute | solution.py:30
  114.2 8.6 %collective-permute-start.16 = (bf16[512,128]{1,0:T(8,128)(2,1)S(1)}, bf16[512,128]{1,0:T(8,128)(2,1)S(1)}, u32[]{:S(2)}, u32[]{:S(2)}) collective-permute-start(bf16[512,128]{1,0:T(8,128)(2,1)S(1)} %attention.3.refs_0_), channel_id=1, source_target_pairs={{0,112},{16,0},{32,16},{48,32},{64,48},{80,64},{96,80},{112,96},{1... | collective-permute-start | bytes 393224 | tf_op jit(solution)/shard_map/output/ppermute | solution.py:30
  122.1 7.8 %collective-permute-start.13 = (bf16[512,128]{1,0:T(8,128)(2,1)S(1)}, bf16[512,128]{1,0:T(8,128)(2,1)S(1)}, u32[]{:S(2)}, u32[]{:S(2)}) collective-permute-start(bf16[512,128]{1,0:T(8,128)(2,1)S(1)} %collective-permute-done.12.refs_1_), channel_id=1, source_target_pairs={{0,16},{16,32},{32,48},{48,64},{64,80},{80,96},{96,112},{112,0},{1... | collective-permute-start | bytes 393224 | tf_op jit(solution)/shard_map/output/ppermute | solution.py:30
  122.8 7.5 %collective-permute-start.17 = (bf16[512,128]{1,0:T(8,128)(2,1)S(1)}, bf16[512,128]{1,0:T(8,128)(2,1)S(1)}, u32[]{:S(2)}, u32[]{:S(2)}) collective-permute-start(bf16[512,128]{1,0:T(8,128)(2,1)S(1)} %collective-permute-done.16.refs_7_), channel_id=1, source_target_pairs={{0,112},{16,0},{32,16},{48,32},{64,48},{80,64},{96,80},{112,96},{1... | collective-permute-start | bytes 393224 | tf_op jit(solution)/shard_map/output/ppermute | solution.py:30
  126.5 9.2 %collective-permute-start.15 = (bf16[512,128]{1,0:T(8,128)(2,1)S(1)}, bf16[512,128]{1,0:T(8,128)(2,1)S(1)}, u32[]{:S(2)}, u32[]{:S(2)}) collective-permute-start(bf16[512,128]{1,0:T(8,128)(2,1)S(1)} %attention.3.refs_0_), channel_id=1, source_target_pairs={{0,64},{16,80},{32,96},{48,112},{64,0},{80,16},{96,32},{112,48},{1... | collective-permute-start | bytes 393224 | tf_op jit(solution)/shard_map/output/ppermute | solution.py:30
  129.9 7.1 %collective-permute-start.14 = (bf16[512,128]{1,0:T(8,128)(2,1)S(1)}, bf16[512,128]{1,0:T(8,128)(2,1)S(1)}, u32[]{:S(2)}, u32[]{:S(2)}) collective-permute-start(bf16[512,128]{1,0:T(8,128)(2,1)S(1)} %collective-permute-done.13.refs_2_), channel_id=1, source_target_pairs={{0,16},{16,32},{32,48},{48,64},{64,80},{80,96},{96,112},{112,0},{1... | collective-permute-start | bytes 393224 | tf_op jit(solution)/shard_map/output/ppermute | solution.py:30
  130.3 6.7 %collective-permute-start.18 = (bf16[512,128]{1,0:T(8,128)(2,1)S(1)}, bf16[512,128]{1,0:T(8,128)(2,1)S(1)}, u32[]{:S(2)}, u32[]{:S(2)}) collective-permute-start(bf16[512,128]{1,0:T(8,128)(2,1)S(1)} %collective-permute-done.17.refs_6_), channel_id=1, source_target_pairs={{0,112},{16,0},{32,16},{48,32},{64,48},{80,64},{96,80},{112,96},{1... | collective-permute-start | bytes 393224 | tf_op jit(solution)/shard_map/output/ppermute | solution.py:30
  137.0 1.6 copy-start
  140.9 2.0 %collective-permute-start.19 = (bf16[512,512]{1,0:T(8,128)(2,1)S(1)}, bf16[512,512]{1,0:T(8,128)(2,1)S(1)}, u32[]{:S(2)}, u32[]{:S(2)}) collective-permute-start(bf16[512,512]{1,0:T(8,128)(2,1)S(1)} %get-tuple-element.101), channel_id=1, source_target_pairs={{0,8},{8,0},{1,9},{9,1},{2,10},{10,2},{3,11},{11,3},{4,12},{12,4},... | collective-permute-start | bytes 1572872 | tf_op jit(solution)/shard_map/output/ppermute | solution.py:30
  143.1 10.2 %copy-start.2 = (bf16[256,256]{1,0:T(8,128)(2,1)S(1)}, bf16[256,256]{1,0:T(8,128)(2,1)}, u32[]{:S(2)}) copy-start(bf16[256,256]{1,0:T(8,128)(2,1)} %hidden.1) | copy-start | bytes 393220
  143.2 9.9 %collective-permute-start.20 = (bf16[512,256]{1,0:T(8,128)(2,1)S(1)}, bf16[512,256]{1,0:T(8,128)(2,1)S(1)}, u32[]{:S(2)}, u32[]{:S(2)}) collective-permute-start(bf16[512,256]{1,0:T(8,128)(2,1)S(1)} %fusion), channel_id=1, source_target_pairs={{0,128},{128,0},{1,129},{129,1},{2,130},{130,2},{3,131},{131,3},{4... | collective-permute-start | bytes 786440 | tf_op jit(solution)/shard_map/output/ppermute | solution.py:30
Sparse Core Ops, SparseCore 0:
  46.2 44.1 all-gather.1

commit v3 on v2

--- a/solution.py
+++ b/solution.py
@@ -28,6 +28,13 @@
 
 def shift(value, axis, size, distance):
     return lax.ppermute(value, axis, [(i, (i + distance) % size) for i in range(size)])
+
+
+def shift_diagonal(value, distance):
+    route = [
+        (x * Z + z, (1 - x) * Z + (z + distance) % Z) for x in range(X_HI) for z in range(Z)
+    ]
+    return lax.ppermute(value, ("x_hi", "z"), route)
 
 
 def vmem():
@@ -92,7 +99,7 @@
         in_specs=[smem, smem, smem, vmem(), vmem()],
         out_specs=(vmem(),) * 3,
         compiler_params=limit(4),
-    )(pos, base, ids, hidden, embed)
+    )(*(pltpu.with_memory_space_constraint(v, pltpu.HBM) for v in (pos, base, ids, hidden, embed)))
 
 
 def column_copies(ks, w, send, own, sems):
@@ -114,73 +121,64 @@
     return copies
 
 
-def first_columns_kernel(w, send, own, sems):
-    copies = column_copies(FIRST, w, send, own, sems)
+def columns_kernel(ks, w, send, own, sems):
+    copies = column_copies(ks, w, send, own, sems)
     for copy in copies:
         copy.start()
     for copy in copies:
         copy.wait()
 
 
-def first_columns(w):
-    columns = jax.ShapeDtypeStruct((w.shape[0], len(FIRST) * X_HI * QKV), bf16)
-    return pl.pallas_call(
-        first_columns_kernel,
+def pick_columns(ks, w):
+    columns = jax.ShapeDtypeStruct((w.shape[0], len(ks) * X_HI * QKV), bf16)
+    return pl.pallas_call(
+        functools.partial(columns_kernel, ks),
         out_shape=(columns, columns),
         in_specs=[hbm()],
         out_specs=(vmem(), vmem()),
-        scratch_shapes=[pltpu.SemaphoreType.DMA((2, len(FIRST) * X_HI))],
+        scratch_shapes=[pltpu.SemaphoreType.DMA((2, len(ks) * X_HI))],
         compiler_params=limit(8),
     )(pltpu.with_memory_space_constraint(w, pltpu.HBM))
 
 
-def second_columns_kernel(w, out_weight, send, own, share, buffer, sems, share_sems, out_sem):
+def share_kernel(w, out, buffer, sems, out_sem):
     my_block = lax.axis_index("x_lo") * Y + lax.axis_index("y")
     size, width = buffer.shape[1], buffer.shape[2] // X_HI
-    share_copies = []
+    rows = pl.ds(pl.multiple_of(my_block * size, size), size)
+    copies = []
     for k in range(Z):
         for x in range(X_HI):
             start = (x * Z + k) * width
-            share_copies.append(
+            copies.append(
                 pltpu.make_async_copy(
-                    out_weight.at[
-                        pl.ds(pl.multiple_of(my_block * size, size), size), start : start + width
-                    ],
+                    w.at[rows, start : start + width],
                     buffer.at[k, :, x * width : (x + 1) * width],
-                    share_sems.at[k, x],
+                    sems.at[k, x],
                 )
             )
-    copies = column_copies(SECOND, w, send, own, sems)
-    for copy in share_copies + copies:
+    for copy in copies:
         copy.start()
-    for copy in share_copies:
-        copy.wait()
-    out_copy = pltpu.make_async_copy(buffer, share, out_sem)
-    out_copy.start()
     for copy in copies:
         copy.wait()
-    out_copy.wait()
-
-
-def second_columns(w, out_weight):
-    columns = jax.ShapeDtypeStruct((w.shape[0], len(SECOND) * X_HI * QKV), bf16)
-    shape = (Z, out_weight.shape[0] // BLOCKS, out_weight.shape[1] // Z)
-    return pl.pallas_call(
-        second_columns_kernel,
-        out_shape=(columns, columns, jax.ShapeDtypeStruct(shape, bf16)),
-        in_specs=[hbm(), hbm()],
-        out_specs=(vmem(), vmem(), hbm()),
+    copy = pltpu.make_async_copy(buffer, out, out_sem)
+    copy.start()
+    copy.wait()
+
+
+def share_rows(w):
+    shape = (Z, w.shape[0] // BLOCKS, w.shape[1] // Z)
+    return pl.pallas_call(
+        share_kernel,
+        out_shape=jax.ShapeDtypeStruct(shape, bf16),
+        in_specs=[hbm()],
+        out_specs=hbm(),
         scratch_shapes=[
             pltpu.VMEM(shape, bf16),
-            pltpu.SemaphoreType.DMA((2, len(SECOND) * X_HI)),
             pltpu.SemaphoreType.DMA((Z, X_HI)),
             pltpu.SemaphoreType.DMA(()),
         ],
-        compiler_params=limit(12),
-    )(
-        pltpu.with_memory_space_constraint(w, pltpu.HBM),
-        pltpu.with_memory_space_constraint(out_weight, pltpu.HBM),
-    )
+        compiler_params=limit(4),
+    )(pltpu.with_memory_space_constraint(w, pltpu.HBM))
 
 
 def two_rows(row, width):
@@ -195,8 +193,7 @@
     return jnp.sum(rows.astype(f32), axis=0, keepdims=True)
 
 
-def partial_kernel(ks, own, sis, gains, w_own, w_sis, *outs):
-    width = X_HI * QKV
+def partial_products(own, sis, gains, w_own, w_sis):
     core = lax.axis_index("core")
     own_rows, sis_rows = own[...].astype(f32), sis[...].astype(f32)
     left, right = gains[:, :TOK].astype(f32), gains[:, TOK:].astype(f32)
@@ -208,34 +205,41 @@
     row = jnp.sum(jnp.where(line == lane, squares, 0.0), axis=0, keepdims=True)
     tail = two_rows(row, QKV)
 
-    def product(slot, count):
-        cols = slice(slot * QKV, (slot + count) * QKV)
+    def product(slot, out):
+        cols = slice(slot * QKV, (slot + 1) * QKV)
         acc = jnp.dot(x_own, w_own[:, cols], preferred_element_type=f32)
         acc = acc + jnp.dot(x_sis, w_sis[:, cols], preferred_element_type=f32)
-        return acc.astype(bf16)
-
-    outs = list(outs)
-    for i, k in enumerate(ks):
-        if k == Z // 2:
-            for xr in range(X_HI):
-                out = outs.pop(0)
-                out[:ROWS, :] = product(i * X_HI + xr, 1)
-                out[ROWS:, :] = tail
-        else:
-            out = outs.pop(0)
-            out[:ROWS, :] = product(i * X_HI, X_HI)
-            out[ROWS:, :QKV] = tail
-            out[ROWS:, QKV:] = tail
-
-
-def partials(ks, own, sis, gains, w_own, w_sis):
-    half = jax.ShapeDtypeStruct((SUM_ROWS, QKV), bf16)
-    full = jax.ShapeDtypeStruct((SUM_ROWS, X_HI * QKV), bf16)
-    shapes = []
-    for k in ks:
-        shapes += [half, half] if k == Z // 2 else [full]
-    return pl.pallas_call(
-        functools.partial(partial_kernel, ks),
+        out[:ROWS, :] = acc.astype(bf16)
+        out[ROWS:, :] = tail
+
+    return product
+
+
+def first_partial_kernel(own, sis, gains, w_own, w_sis, up, down, near, near_far):
+    product = partial_products(own, sis, gains, w_own, w_sis)
+    slot = FIRST.index(4) * X_HI
+    product(slot, up)
+    product(slot + 1, down)
+    for i, k in enumerate((3, 5)):
+        slot = FIRST.index(k) * X_HI
+        product(slot, near.at[i])
+        product(slot + 1, near_far.at[i])
+
+
+def second_partial_kernel(own, sis, gains, w_own, w_sis, mid, mid_far, last, last_far):
+    product = partial_products(own, sis, gains, w_own, w_sis)
+    for ks, out, out_far in (((2, 6), mid, mid_far), ((1, 7, 0), last, last_far)):
+        for i, k in enumerate(ks):
+            slot = SECOND.index(k) * X_HI
+            product(slot, out.at[i])
+            product(slot + 1, out_far.at[i])
+
+
+def partials(kernel, counts, own, sis, gains, w_own, w_sis):
+    part = (SUM_ROWS, QKV)
+    shapes = [jax.ShapeDtypeStruct((n, *part) if n else part, bf16) for n in counts]
+    return pl.pallas_call(
+        kernel,
         out_shape=tuple(shapes),
         in_specs=[vmem()] * 5,
         out_specs=(vmem(),) * len(shapes),
@@ -246,71 +250,38 @@
     )(own, sis, gains, w_own, w_sis)
 
 
-def store_sum(out, cols, terms):
-    body = sum(term[:ROWS].astype(f32) for term in terms)
-    row = sum(one_row(term[ROWS:]) for term in terms)
-    out[:ROWS, cols] = body.astype(bf16)
-    out[ROWS:, cols] = two_rows(row, row.shape[1])
-
-
-def first_kernel(up, down, near_up, near_down, out_up, out_down):
-    left, right = slice(0, QKV), slice(QKV, 2 * QKV)
-    store_sum(out_up, left, [up[...], near_up[:, left]])
-    out_up[:, right] = near_up[:, right]
-    out_down[:, left] = near_down[:, left]
-    store_sum(out_down, right, [down[...], near_down[:, right]])
-
-
-def next_kernel(up, down, near_up, near_down, out_up, out_down):
-    every = slice(0, 2 * QKV)
-    store_sum(out_up, every, [up[...], near_up[...]])
-    store_sum(out_down, every, [down[...], near_down[...]])
-
-
-def ring_add(kernel, up, down, near_up, near_down):
-    out = jax.ShapeDtypeStruct((SUM_ROWS, X_HI * QKV), bf16)
-    return pl.pallas_call(
-        kernel,
+def add_kernel(up, down, near, far, out_up, out_down):
+    for i, (term, out) in enumerate(((up, out_up), (down, out_down))):
+        terms = (term, near.at[i], far.at[i])
+        body = sum(t[:ROWS].astype(f32) for t in terms)
+        row = sum(one_row(t[ROWS:]) for t in terms)
+        out[:ROWS] = body.astype(bf16)
+        out[ROWS:] = two_rows(row, QKV)
+
+
+def ring_add(up, down, near, far):
+    out = jax.ShapeDtypeStruct((SUM_ROWS, QKV), bf16)
+    return pl.pallas_call(
+        add_kernel,
         out_shape=(out, out),
         in_specs=[vmem()] * 4,
         out_specs=(vmem(), vmem()),
         compiler_params=limit(8),
-    )(up, down, near_up, near_down)
-
-
-def last_kernel(up, down, near, mine, other):
-    own, far = slice(0, QKV), slice(QKV, 2 * QKV)
-    terms = [up, down, near]
-    mine[:ROWS] = sum(term[:ROWS, own].astype(f32) for term in terms)
-    row = sum(one_row(term[ROWS:, own]) for term in terms)
-    mine[ROWS:] = jnp.broadcast_to(row, (8, QKV))
-    store_sum(other, slice(0, QKV), [term[:, far] for term in terms])
-
-
-def ring_last(up, down, near):
-    return pl.pallas_call(
-        last_kernel,
-        out_shape=(
-            jax.ShapeDtypeStruct((ROWS + 8, QKV), f32),
-            jax.ShapeDtypeStruct((SUM_ROWS, QKV), bf16),
-        ),
-        in_specs=[vmem()] * 3,
-        out_specs=(vmem(), vmem()),
-        compiler_params=limit(8),
-    )(up, down, near)
+    )(up, down, near, far)
 
 
 def rotated(x, cosine, sine):
     return x * cosine + pltpu.roll(x, HD // 2, 1) * sine
 
 
-def finish_kernel(full_width, mine, other, cosine, sine, onehot, payload, queries):
-    row = mine[ROWS : ROWS + 1, :] + one_row(other[ROWS:, :])
+def finish_kernel(full_width, up, down, near, far, cosine, sine, onehot, payload, queries):
+    terms = (up, down, near.at[2], far.at[2])
+    row = sum(one_row(t[ROWS:]) for t in terms)
     line = lax.broadcasted_iota(jnp.int32, (ROWS, QKV), 0)
     lane = lax.broadcasted_iota(jnp.int32, (ROWS, QKV), 1)
     squares = jnp.sum(jnp.where(line == lane, row, 0.0), axis=1, keepdims=True)
     inv_rms = lax.rsqrt(squares / full_width + epsilon)
-    proj = (mine[:ROWS, :] + other[:ROWS, :].astype(f32)) * inv_rms
+    proj = sum(t[:ROWS].astype(f32) for t in terms) * inv_rms
     query = rotated(proj[:, :HD], cosine[...], sine[...]).astype(bf16)
     key = rotated(proj[:, HD : 2 * HD], cosine[...], sine[...]).astype(bf16)
     value = proj[:, 2 * HD :].astype(bf16)
@@ -332,17 +303,17 @@
     queries[TOK:] = jnp.where(changed > 0.5, placed, base.astype(f32)).astype(bf16)
 
 
-def finish(full_width, mine, other, cosine, sine, onehot):
+def finish(full_width, up, down, near, far, cosine, sine, onehot):
     return pl.pallas_call(
         functools.partial(finish_kernel, full_width),
         out_shape=(
             jax.ShapeDtypeStruct((BLOCKS, PAY, 2 * HD), bf16),
             jax.ShapeDtypeStruct((2 * TOK, HD), bf16),
         ),
-        in_specs=[vmem()] * 5,
+        in_specs=[vmem()] * 7,
         out_specs=(vmem(), vmem()),
         compiler_params=limit(12),
-    )(mine, other, cosine, sine, onehot)
+    )(up, down, near, far, cosine, sine, onehot)
 
 
 def attend_kernel(queries, blocks, out, scores, peak, denom, total, var_kv, spots):
@@ -433,13 +404,36 @@
     )(queries, blocks)
 
 
-def project_kernel(w, *refs):
-    shards, (keep, near, far), (joined, turned) = refs[:Z], refs[Z : Z + 3], refs[Z + 3 :]
-    z, core, x_hi = lax.axis_index("z"), lax.axis_index("core"), lax.axis_index("x_hi")
+def arrange_kernel(w, out, sems):
+    z = lax.axis_index("z")
+    copies = []
+    for d in range(Z):
+        source = lax.rem(z + Z - d, Z)
+        copies.append(
+            pltpu.make_async_copy(w.at[source], out.at[d * HD : (d + 1) * HD, :], sems.at[d])
+        )
+    for copy in copies:
+        copy.start()
+    for copy in copies:
+        copy.wait()
+
+
+def arrange(w):
+    return pl.pallas_call(
+        arrange_kernel,
+        out_shape=jax.ShapeDtypeStruct((Z * HD, w.shape[2]), bf16),
+        in_specs=[hbm()],
+        out_specs=vmem(),
+        scratch_shapes=[pltpu.SemaphoreType.DMA((Z,))],
+        compiler_params=limit(4),
+    )(pltpu.with_memory_space_constraint(w, pltpu.HBM))
+
+
+def project_kernel(turned, *refs):
+    shards, (keep, near, far), joined = refs[:Z], refs[Z : Z + 3], refs[-1]
+    core, x_hi = lax.axis_index("core"), lax.axis_index("x_hi")
     for d in range(Z):
         joined[:, d * HD : (d + 1) * HD] = shards[d][...]
-        source = lax.rem(z + Z - d, Z)
-        turned[d * HD : (d + 1) * HD, :] = w[source]
 
     def product(xr, cr, rows):
         column = (lax.rem(x_hi + xr, X_HI) * CORE + lax.rem(core + cr, CORE)) * TOK
@@ -470,10 +464,7 @@
         ),
         in_specs=[vmem()] * (1 + Z),
         out_specs=(vmem(),) * 3,
-        scratch_shapes=[
-            pltpu.VMEM((rows, Z * HD), bf16),
-            pltpu.VMEM((Z * HD, w.shape[2]), bf16),
-        ],
+        scratch_shapes=[pltpu.VMEM((rows, Z * HD), bf16)],
         compiler_params=limit(16),
     )(w, *shards)
 
@@ -489,32 +480,40 @@
         rows, onehot, variant = make_variant(var_pos, var_base, ref_ids, hidden, embed)
         rows, qkv_weight = lax.optimization_barrier((rows, qkv_weight))
         rows_sis = shift(rows, "core", CORE, 1)
-        send_first, own_first = first_columns(qkv_weight)
+        send_first, own_first = pick_columns(FIRST, qkv_weight)
         sis_first = shift(send_first, "core", CORE, 1)
-        rows_sis, send_first, qkv_weight = lax.optimization_barrier((rows_sis, send_first, qkv_weight))
-        send_second, own_second, share = second_columns(qkv_weight, out_weight)
+        own_first, out_weight = lax.optimization_barrier((own_first, out_weight))
+        share = share_rows(out_weight)
+        shared = lax.all_to_all(share, "z", 0, 0, tiled=True)
+        rows_sis, sis_first, shared, qkv_weight = lax.optimization_barrier(
+            (rows_sis, sis_first, shared, qkv_weight)
+        )
+        out_w = lax.all_gather(shared, CTX, axis=1, tiled=True)
+        send_second, own_second = pick_columns(SECOND, qkv_weight)
+        own_first, own_second = lax.optimization_barrier((own_first, own_second))
         sis_second = shift(send_second, "core", CORE, 1)
-        shared = lax.all_to_all(share, "z", 0, 0, tiled=True)
         start = chip_slice * 2 * width_part
         gains = lax.dynamic_slice(gain.reshape(1, full_width), (0, start), (1, 2 * width_part))
 
     with jax.named_scope("projection"):
-        near_up, up, down, near_down = partials(FIRST, rows, rows_sis, gains, own_first, sis_first)
+        up, down, near, near_far = partials(
+            first_partial_kernel, (0, 0, 2, 2), rows, rows_sis, gains, own_first, sis_first
+        )
+        up = shift(up, "z", Z, 1)
+        down = shift_diagonal(down, -1)
+        near_far = shift(near_far, "x_hi", X_HI, 1)
+        mid, mid_far, last, last_far = partials(
+            second_partial_kernel, (2, 2, 3, 3), rows, rows_sis, gains, own_second, sis_second
+        )
+        mid_far = shift(mid_far, "x_hi", X_HI, 1)
+        last_far = shift(last_far, "x_hi", X_HI, 1)
+        up, down, near_far, mid = lax.optimization_barrier((up, down, near_far, mid))
+        up, down = ring_add(up, down, near, near_far)
         up, down = shift(up, "z", Z, 1), shift(down, "z", Z, -1)
-        up, down, shared = lax.optimization_barrier((up, down, shared))
-        out_w = lax.all_gather(shared, CTX, axis=1, tiled=True)
-        up, down = ring_add(first_kernel, up, down, near_up, near_down)
-        up, rows, down = lax.optimization_barrier((up, rows, down))
+        up, down = ring_add(up, down, mid, mid_far)
         up, down = shift(up, "z", Z, 1), shift(down, "z", Z, -1)
-        parts = partials(SECOND, rows, rows_sis, gains, own_second, sis_second)
-        up, down, parts = lax.optimization_barrier((up, down, parts))
-        parts = dict(zip(SECOND, parts))
-        up, down = ring_add(next_kernel, up, down, parts[2], parts[6])
+        up, down = ring_add(up, down, last, last_far)
         up, down = shift(up, "z", Z, 1), shift(down, "z", Z, -1)
-        up, down = ring_add(next_kernel, up, down, parts[1], parts[7])
-        up, down = shift(up, "z", Z, 1), shift(down, "z", Z, -1)
-        mine, other = ring_last(up, down, parts[0])
-        other = shift(other, "x_hi", X_HI, 1)
 
     with jax.named_scope("tables"):
         positions = jnp.concatenate([my_block * tok_rows + jnp.arange(tok_rows), var_pos])
@@ -526,7 +525,7 @@
         sine = jnp.concatenate([-sine, sine], axis=1)
 
     with jax.named_scope("attention"):
-        payload, queries = finish(full_width, mine, other, cosine, sine, onehot)
+        payload, queries = finish(full_width, up, down, last, last_far, cosine, sine, onehot)
         blocks = lax.all_to_all(payload, CTX, 0, 0, tiled=True)
         attn = attend(queries, blocks)
         attn, out_w = lax.optimization_barrier((attn, out_w))
@@ -538,6 +537,9 @@
             pieces[Z - d] = shift(pieces[(Z - d + 1) % Z], "z", Z, -1)
             if d == 1:
                 pieces[Z // 2] = shift(attn, "z", Z, Z // 2)
+                out_w, pieces[1], pieces[7] = lax.optimization_barrier(
+                    (arrange(out_w), pieces[1], pieces[7])
+                )
         keep, near, far = project(out_w, pieces)
         near = shift(near, "core", CORE, 1).astype(f32)
         far = (far + near[:, width_part:]).astype(bf16)

time: 163 us -> 183 us (1.12); the launches traced: 161 us -> 183 us
  waiting for transfers between devices: 56 us -> 78.1 us
  local copies, waits for them, and re-layouts: 11.7 us -> 5.45 us
  blocking collectives: 18.2 us -> 20.6 us
  starting transfers between devices: 39.2 us -> 41.5 us
    ppermute x21 -> x22, waiting for transfers between devices: 52.1 us -> 67 us  [shift(): lax.ppermute(value, axis, [(i, (i + distance) % size) for i in range(size)])]
    all_to_all x1, waiting for transfers between devices: 3.89 us -> 11.1 us  [shards(): shared = lax.all_to_all(share, 'z', 0, 0, tiled=True)]
    unnamed x38 -> x14, local copies, waits for them, and re-layouts: 11 us -> 4.69 us
    ppermute x0 -> x1, starting transfers between devices: none -> 4.25 us  [shift_diagonal(): return lax.ppermute(value, ('x_hi', 'z'), route)]
    all_to_all x1, blocking collectives: 18.2 us -> 20.6 us  [shards(): blocks = lax.all_to_all(payload, CTX, 0, 0, tiled=True)]
    ppermute x21 -> x22, starting transfers between devices: 30.7 us -> 28.7 us  [shift(): lax.ppermute(value, axis, [(i, (i + distance) % size) for i in range(size)])]
    pallas_call x8 -> x9, Pallas kernels: 13.3 us -> 14.6 us  [the longest x2 5.55 us: pick_columns(): pl.pallas_call(functools.partial(columns_kernel, ks), out_shape=(columns,...]
  transfers between devices with their start and end apart: 23 -> 25, of which waited for: 15 -> 14; matrix products, arithmetic and copies ran while one was open for 1% -> 1% of each run, Pallas kernels for 9% -> 7%
where the time goes in v3:
time: 183 us
  waiting for transfers between devices  78.1 us (43%)
  starting transfers between devices  41.5 us (23%)
  Pallas kernels  21.9 us (12%)
  blocking collectives  20.6 us (11%)
  between operations  13.6 us (7%)
  local copies, waits for them, and re-layouts  5.45 us (3%)
    ppermute x22, waiting for transfers between devices, shift(): lax.ppermute(value, axis, [(i, (i + distance) % size) for i in range(size)])  67 us
    ppermute x22, starting transfers between devices, shift(): lax.ppermute(value, axis, [(i, (i + distance) % size) for i in range(size)])  28.7 us
    all_to_all x1, blocking collectives, shards(): blocks = lax.all_to_all(payload, CTX, 0, 0, tiled=True)  20.6 us
    all_to_all x1, waiting for transfers between devices, shards(): shared = lax.all_to_all(share, 'z', 0, 0, tiled=True)  11.1 us
    all_to_all x1, starting transfers between devices, shards(): shared = lax.all_to_all(share, 'z', 0, 0, tiled=True)  8.48 us
    pallas_call x2, Pallas kernels, pick_columns(): pl.pallas_call(functools.partial(columns_kernel, ks), out_shape=(columns,...  5.55 us
    pallas_call x2, Pallas kernels, partials(): pl.pallas_call(kernel, out_shape=tuple(shapes), in_specs=[vmem()] * 5, ou...  5.17 us
    unnamed x14, local copies, waits for them, and re-layouts  4.69 us
  transfers between devices with their start and end apart: 25, of which 14 were waited for; matrix products, arithmetic and copies ran while one was open for 1% of the time, Pallas kernels for 7%

profile of v3, /device:TPU:6, one launch (start us, length us, event | category | flops | bytes accessed | tf_op | source)
XLA Modules:
  0.0 183.0 jit_solution(16030462718214886216)
XLA Ops:
  6.5 1.5 inputs.4
  8.1 1.8 %inputs.5 = (bf16[256,2304]{1,0:T(8,128)(2,1)S(1)}, bf16[256,2304]{1,0:T(8,128)(2,1)S(1)}) custom-call(bf16[256,12288]{1,0:T(8,128)(2,1)} %w.2), custom_call_target="tpu_custom_call" | custom-call | tf_op jit(solution)/shard_map/inputs/pallas_call | solution.py:134
  9.9 1.0 copy-done
  10.9 1.7 inputs.6
  12.7 8.5 %all-to-all-start = ((bf16[8,16,1024]{2,1,0:T(8,128)(2,1)}), bf16[8,16,1024]{2,1,0:T(8,128)(2,1)S(1)}, u32[]{:S(2)}, u32[]{:S(2)}) async-start(bf16[8,16,1024]{2,1,0:T(8,128)(2,1)} %inputs.6), calls=%async_computation | async-start | bytes 524288 | tf_op jit(solution)/shard_map/inputs/all_to_all | solution.py:487
  21.1 0.0 all-gather.2.cloned.1.call-start
  21.2 0.3 collective-permute-start
  21.5 1.1 collective-permute-done.sis
  22.6 11.1 %all-to-all-done = bf16[8,16,1024]{2,1,0:T(8,128)(2,1)S(1)} async-done(((bf16[8,16,1024]{2,1,0:T(8,128)(2,1)}), bf16[8,16,1024]{2,1,0:T(8,128)(2,1)S(1)}, u32[]{:S(2)}, u32[]{:S(2)}) %all-to-all-start) | async-done | bytes 262176 | tf_op jit(solution)/shard_map/inputs/all_to_all | solution.py:487
  33.7 1.1 copy-done.2
  34.8 3.7 %inputs.7 = (bf16[256,3840]{1,0:T(8,128)(2,1)}, bf16[256,3840]{1,0:T(8,128)(2,1)S(1)}) custom-call(bf16[256,12288]{1,0:T(8,128)(2,1)} %w.2), custom_call_target="tpu_custom_call" | custom-call | tf_op jit(solution)/shard_map/inputs/pallas_call | solution.py:134
  38.5 0.1 collective-permute-start.5
  38.7 0.0 all-gather.2.cloned.1.call-update
  38.7 0.8 dynamic-slice.3
  39.5 1.3 copy-done.1
  40.8 1.3 copy-done.3
  42.0 1.0 projection.5
  43.1 1.5 collective-permute-start.4
  44.6 0.5 collective-permute-start.2
  45.1 4.3 %collective-permute-start.3 = (bf16[288,384]{1,0:T(8,128)(2,1)S(1)}, bf16[288,384]{1,0:T(8,128)(2,1)S(1)}, u32[]{:S(2)}, u32[]{:S(2)}) collective-permute-start(bf16[288,384]{1,0:T(8,128)(2,1)S(1)} %get-tuple-element.64), channel_id=1, source_target_pairs={{0,240},{16,128},{32,144},{48,160},{64,176},{80,192},{96,208},{112... | collective-permute-start | bytes 663560 | tf_op jit(solution)/shard_map/projection/ppermute | solution.py:37
  49.4 4.1 %projection.6 = (bf16[2,288,384]{2,1,0:T(8,128)(2,1)S(1)}, bf16[2,288,384]{2,1,0:T(8,128)(2,1)}, bf16[3,288,384]{2,1,0:T(8,128)(2,1)S(1)}, bf16[3,288,384]{2,1,0:T(8,128)(2,1)}) custom-call(bf16[272,256]{1,0:T(8,128)(2,1)S(1)} %get-tuple-element.52.own, bf16[272,256]{1,0:T(8,128)(2,1)S(1)} %collective-permute-done.sis, ...), custom_call_target="tpu_custom_call" | custom-call | flops 1069547520 | bytes 7864320 | tf_op jit(solution)/shard_map/projection/pallas_call | solution.py:241
  53.5 1.4 collective-permute-start.8
  54.9 2.1 %collective-permute-start.11 = (bf16[3,288,384]{2,1,0:T(8,128)(2,1)}, bf16[3,288,384]{2,1,0:T(8,128)(2,1)S(1)}, u32[]{:S(2)}, u32[]{:S(2)}) collective-permute-start(bf16[3,288,384]{2,1,0:T(8,128)(2,1)} %get-tuple-element.80), channel_id=1, source_target_pairs={{0,128},{128,0},{1,129},{129,1},{2,130},{130,2},{3,131},{131,3},{4... | collective-permute-start | bytes 1990664 | tf_op jit(solution)/shard_map/projection/ppermute | solution.py:30
  57.0 14.6 %collective-permute-done.4.far = bf16[2,288,384]{2,1,0:T(8,128)(2,1)S(1)} collective-permute-done((bf16[2,288,384]{2,1,0:T(8,128)(2,1)S(1)}, bf16[2,288,384]{2,1,0:T(8,128)(2,1)S(1)}, u32[]{:S(2)}, u32[]{:S(2)}) %collective-permute-start.4) | collective-permute-done | bytes 442400 | tf_op jit(solution)/shard_map/projection/ppermute | solution.py:30
  71.6 0.2 projection.7
  71.8 0.1 collective-permute-start.6
  71.9 3.2 %collective-permute-start.7 = (bf16[288,384]{1,0:T(8,128)(2,1)S(1)}, bf16[288,384]{1,0:T(8,128)(2,1)S(1)}, u32[]{:S(2)}, u32[]{:S(2)}) collective-permute-start(bf16[288,384]{1,0:T(8,128)(2,1)S(1)} %get-tuple-element.74), channel_id=1, source_target_pairs={{0,112},{16,0},{32,16},{48,32},{64,48},{80,64},{96,80},{112,96},{1... | collective-permute-start | bytes 663560 | tf_op jit(solution)/shard_map/projection/ppermute | solution.py:30
  75.1 3.9 %collective-permute-done.6.up = bf16[288,384]{1,0:T(8,128)(2,1)S(1)} collective-permute-done((bf16[288,384]{1,0:T(8,128)(2,1)S(1)}, bf16[288,384]{1,0:T(8,128)(2,1)S(1)}, u32[]{:S(2)}, u32[]{:S(2)}) %collective-permute-start.6) | collective-permute-done | bytes 221216 | tf_op jit(solution)/shard_map/projection/ppermute | solution.py:30
  79.0 11.5 %collective-permute-done.8.far = bf16[2,288,384]{2,1,0:T(8,128)(2,1)S(1)} collective-permute-done((bf16[2,288,384]{2,1,0:T(8,128)(2,1)}, bf16[2,288,384]{2,1,0:T(8,128)(2,1)S(1)}, u32[]{:S(2)}, u32[]{:S(2)}) %collective-permute-start.8) | collective-permute-done | bytes 442400 | tf_op jit(solution)/shard_map/projection/ppermute | solution.py:30
  90.6 0.2 projection.8
  90.8 0.1 collective-permute-start.9
  90.9 3.2 %collective-permute-start.10 = (bf16[288,384]{1,0:T(8,128)(2,1)S(1)}, bf16[288,384]{1,0:T(8,128)(2,1)S(1)}, u32[]{:S(2)}, u32[]{:S(2)}) collective-permute-start(bf16[288,384]{1,0:T(8,128)(2,1)S(1)} %get-tuple-element.78), channel_id=1, source_target_pairs={{0,112},{16,0},{32,16},{48,32},{64,48},{80,64},{96,80},{112,96},{1... | collective-permute-start | bytes 663560 | tf_op jit(solution)/shard_map/projection/ppermute | solution.py:30
  94.1 11.2 %collective-permute-done.11.far = bf16[3,288,384]{2,1,0:T(8,128)(2,1)S(1)} collective-permute-done((bf16[3,288,384]{2,1,0:T(8,128)(2,1)}, bf16[3,288,384]{2,1,0:T(8,128)(2,1)S(1)}, u32[]{:S(2)}, u32[]{:S(2)}) %collective-permute-start.11) | collective-permute-done | bytes 663584 | tf_op jit(solution)/shard_map/projection/ppermute | solution.py:30
  105.3 0.2 projection.9
  105.5 0.8 collective-permute-start.12
  106.3 2.7 %collective-permute-start.13 = (bf16[288,384]{1,0:T(8,128)(2,1)S(1)}, bf16[288,384]{1,0:T(8,128)(2,1)S(1)}, u32[]{:S(2)}, u32[]{:S(2)}) collective-permute-start(bf16[288,384]{1,0:T(8,128)(2,1)S(1)} %get-tuple-element.82), channel_id=1, source_target_pairs={{0,112},{16,0},{32,16},{48,32},{64,48},{80,64},{96,80},{112,96},{1... | collective-permute-start | bytes 663560 | tf_op jit(solution)/shard_map/projection/ppermute | solution.py:30
  109.0 0.6 fusion.2
  109.6 0.1 pad_maximum_fusion
  109.7 4.3 %collective-permute-done.12.up = bf16[288,384]{1,0:T(8,128)(2,1)S(1)} collective-permute-done((bf16[288,384]{1,0:T(8,128)(2,1)S(1)}, bf16[288,384]{1,0:T(8,128)(2,1)S(1)}, u32[]{:S(2)}, u32[]{:S(2)}) %collective-permute-start.12) | collective-permute-done | bytes 221216 | tf_op jit(solution)/shard_map/projection/ppermute | solution.py:30
  114.0 0.6 attention.2
  114.7 20.6 %all_to_all.10.blocks = bf16[8,288,256]{2,1,0:T(8,128)(2,1)S(1)} all-to-all(bf16[8,288,256]{2,1,0:T(8,128)(2,1)S(1)} %get-tuple-element.85), channel_id=1, replica_groups=mesh['x_hi'=2,'z'=8,'core'=2,'x_lo'=2,'y'=4] {'x_lo','y'}, dimensions={0} | all-to-all | bytes 2359296 | tf_op jit(solution)/shard_map/attention/all_to_all | solution.py:529
  135.2 2.9 %attention.3.refs_0_ = bf16[512,128]{1,0:T(8,128)(2,1)S(1)} custom-call(bf16[512,128]{1,0:T(8,128)(2,1)S(1)} %get-tuple-element.84.queries, bf16[8,288,256]{2,1,0:T(8,128)(2,1)S(1)} %all_to_all.10.blocks), custom_call_target="tpu_custom_call" | custom-call | tf_op jit(solution)/shard_map/attention/pallas_call | solution.py:390
  138.2 0.0 all-gather.2.cloned.1.call-done.w
  138.2 0.1 collective-permute-start.14
  138.3 3.2 %collective-permute-start.15 = (bf16[512,128]{1,0:T(8,128)(2,1)S(1)}, bf16[512,128]{1,0:T(8,128)(2,1)S(1)}, u32[]{:S(2)}, u32[]{:S(2)}) collective-permute-start(bf16[512,128]{1,0:T(8,128)(2,1)S(1)} %attention.3.refs_0_), channel_id=1, source_target_pairs={{0,112},{16,0},{32,16},{48,32},{64,48},{80,64},{96,80},{112,96},{1... | collective-permute-start | bytes 393224 | tf_op jit(solution)/shard_map/output/ppermute | solution.py:30
  141.5 1.6 output.2.turned
  143.1 1.4 collective-permute-done.14.refs_1_
  144.5 3.5 %collective-permute-start.19 = (bf16[512,128]{1,0:T(8,128)(2,1)S(1)}, bf16[512,128]{1,0:T(8,128)(2,1)S(1)}, u32[]{:S(2)}, u32[]{:S(2)}) collective-permute-start(bf16[512,128]{1,0:T(8,128)(2,1)S(1)} %collective-permute-done.15.refs_7_), channel_id=1, source_target_pairs={{0,112},{16,0},{32,16},{48,32},{64,48},{80,64},{96,80},{112,96},{1... | collective-permute-start | bytes 393224 | tf_op jit(solution)/shard_map/output/ppermute | solution.py:30
  148.0 0.9 collective-permute-start.18
  148.8 4.9 %collective-permute-done.16.refs_2_ = bf16[512,128]{1,0:T(8,128)(2,1)S(1)} collective-permute-done((bf16[512,128]{1,0:T(8,128)(2,1)S(1)}, bf16[512,128]{1,0:T(8,128)(2,1)S(1)}, u32[]{:S(2)}, u32[]{:S(2)}) %collective-permute-start.16) | collective-permute-done | bytes 131104 | tf_op jit(solution)/shard_map/output/ppermute | solution.py:30
  153.7 0.7 collective-permute-done.19.refs_6_
  154.4 3.9 %collective-permute-start.20 = (bf16[512,128]{1,0:T(8,128)(2,1)S(1)}, bf16[512,128]{1,0:T(8,128)(2,1)S(1)}, u32[]{:S(2)}, u32[]{:S(2)}) collective-permute-start(bf16[512,128]{1,0:T(8,128)(2,1)S(1)} %collective-permute-done.19.refs_6_), channel_id=1, source_target_pairs={{0,112},{16,0},{32,16},{48,32},{64,48},{80,64},{96,80},{112,96},{1... | collective-permute-start | bytes 393224 | tf_op jit(solution)/shard_map/output/ppermute | solution.py:30
  158.3 1.6 collective-permute-done.17.refs_3_
  159.9 1.0 collective-permute-done.20.refs_5_
  160.8 2.2 %output.3 = (f32[512,256]{1,0:T(8,128)S(1)}, bf16[512,512]{1,0:T(8,128)(2,1)S(1)}, f32[512,256]{1,0:T(8,128)S(1)}) custom-call(bf16[1024,1024]{1,0:T(8,128)(2,1)S(1)} %output.2.turned, bf16[512,128]{1,0:T(8,128)(2,1)S(1)} %attention.3.refs_0_, bf16[512,128]{1,0:T(8,128)(2,1)S(1)} %collective-permute-done.14.refs_1_, ...), custom_call_target="tpu_custom_call" | custom-call | tf_op jit(solution)/shard_map/output/pallas_call | solution.py:458
  163.0 0.1 collective-permute-start.21
  163.1 1.9 %collective-permute-done.21 = bf16[512,512]{1,0:T(8,128)(2,1)S(1)} collective-permute-done((bf16[512,512]{1,0:T(8,128)(2,1)S(1)}, bf16[512,512]{1,0:T(8,128)(2,1)S(1)}, u32[]{:S(2)}, u32[]{:S(2)}) %collective-permute-start.21) | collective-permute-done | bytes 524320 | tf_op jit(solution)/shard_map/output/ppermute | solution.py:30
  165.0 0.1 convert_element_type.32
  165.2 0.0 copy-start.5
  165.2 0.1 fusion
  165.3 0.9 collective-permute-start.22
  166.2 9.0 %collective-permute-done.22 = bf16[512,256]{1,0:T(8,128)(2,1)S(1)} collective-permute-done((bf16[512,256]{1,0:T(8,128)(2,1)S(1)}, bf16[512,256]{1,0:T(8,128)(2,1)S(1)}, u32[]{:S(2)}, u32[]{:S(2)}) %collective-permute-start.22) | collective-permute-done | bytes 262176 | tf_op jit(solution)/shard_map/output/ppermute | solution.py:30
  175.2 0.1 fusion.1
  175.3 0.8 add_convert_fusion
  (26 shorter events, 0.1 us)
Async XLA Ops:
  9.9 1.0 copy-start
  10.9 22.8 %collective-permute-start.1 = (bf16[256,2304]{1,0:T(8,128)(2,1)S(1)}, bf16[256,2304]{1,0:T(8,128)(2,1)S(1)}, u32[]{:S(2)}, u32[]{:S(2)}) collective-permute-start(bf16[256,2304]{1,0:T(8,128)(2,1)S(1)} %get-tuple-element.54), channel_id=1, source_target_pairs={{0,8},{8,0},{1,9},{9,1},{2,10},{10,2},{3,11},{11,3},{4,12},{12,4},... | collective-permute-start | bytes 3538952 | tf_op jit(solution)/shard_map/inputs/ppermute | solution.py:30
  12.7 21.0 %all-to-all-start = ((bf16[8,16,1024]{2,1,0:T(8,128)(2,1)}), bf16[8,16,1024]{2,1,0:T(8,128)(2,1)S(1)}, u32[]{:S(2)}, u32[]{:S(2)}) async-start(bf16[8,16,1024]{2,1,0:T(8,128)(2,1)} %inputs.6), calls=%async_computation | async-start | bytes 524288 | tf_op jit(solution)/shard_map/inputs/all_to_all | solution.py:487
  21.1 117.0 %all-gather.2.cloned.1.call-start = ((), (), s32[]{:S(2)}) async-start(), calls=%async_computation.2 | async-start | bytes 2359296 | tf_op jit(solution)/shard_map/inputs/all_gather | solution.py:491
  21.2 1.4 collective-permute-start
  33.7 5.0 %copy-start.4 = (bf16[8,16,1024]{2,1,0:T(8,128)(2,1)}, bf16[8,16,1024]{2,1,0:T(8,128)(2,1)S(1)}, u32[]{:S(2)}) copy-start(bf16[8,16,1024]{2,1,0:T(8,128)(2,1)S(1)} %all-to-all-done) | copy-start | bytes 786436
  33.7 1.1 copy-start.2
  38.5 10.8 %collective-permute-start.5 = (bf16[256,3840]{1,0:T(8,128)(2,1)}, bf16[256,3840]{1,0:T(8,128)(2,1)}, u32[]{:S(2)}, u32[]{:S(2)}) collective-permute-start(bf16[256,3840]{1,0:T(8,128)(2,1)} %get-tuple-element.67), channel_id=1, source_target_pairs={{0,8},{8,0},{1,9},{9,1},{2,10},{10,2},{3,11},{11,3},{4,12},{12,4},... | collective-permute-start | bytes 5898248 | tf_op jit(solution)/shard_map/inputs/ppermute | solution.py:30
  39.5 1.3 copy-start.1
  40.8 1.3 copy-start.3
  43.1 28.6 %collective-permute-start.4 = (bf16[2,288,384]{2,1,0:T(8,128)(2,1)S(1)}, bf16[2,288,384]{2,1,0:T(8,128)(2,1)S(1)}, u32[]{:S(2)}, u32[]{:S(2)}) collective-permute-start(bf16[2,288,384]{2,1,0:T(8,128)(2,1)S(1)} %get-tuple-element.65), channel_id=1, source_target_pairs={{0,128},{128,0},{1,129},{129,1},{2,130},{130,2},{3,131},{131,3},{4... | collective-permute-start | bytes 1327112 | tf_op jit(solution)/shard_map/projection/ppermute | solution.py:30
  44.6 12.5 %collective-permute-start.2 = (bf16[288,384]{1,0:T(8,128)(2,1)S(1)}, bf16[288,384]{1,0:T(8,128)(2,1)S(1)}, u32[]{:S(2)}, u32[]{:S(2)}) collective-permute-start(bf16[288,384]{1,0:T(8,128)(2,1)S(1)} %get-tuple-element.63), channel_id=1, source_target_pairs={{0,16},{16,32},{32,48},{48,64},{64,80},{80,96},{96,112},{112,0},{1... | collective-permute-start | bytes 663560 | tf_op jit(solution)/shard_map/projection/ppermute | solution.py:30
  45.1 11.9 %collective-permute-start.3 = (bf16[288,384]{1,0:T(8,128)(2,1)S(1)}, bf16[288,384]{1,0:T(8,128)(2,1)S(1)}, u32[]{:S(2)}, u32[]{:S(2)}) collective-permute-start(bf16[288,384]{1,0:T(8,128)(2,1)S(1)} %get-tuple-element.64), channel_id=1, source_target_pairs={{0,240},{16,128},{32,144},{48,160},{64,176},{80,192},{96,208},{112... | collective-permute-start | bytes 663560 | tf_op jit(solution)/shard_map/projection/ppermute | solution.py:37
  53.5 40.6 %copy-start.6 = (s32[16]{0:T(128)S(1)}, s32[16]{0:T(128)}, u32[]{:S(2)}) copy-start(s32[16]{0:T(128)} %pos.1) | copy-start | bytes 196
  53.5 37.1 %collective-permute-start.8 = (bf16[2,288,384]{2,1,0:T(8,128)(2,1)}, bf16[2,288,384]{2,1,0:T(8,128)(2,1)S(1)}, u32[]{:S(2)}, u32[]{:S(2)}) collective-permute-start(bf16[2,288,384]{2,1,0:T(8,128)(2,1)} %get-tuple-element.76), channel_id=1, source_target_pairs={{0,128},{128,0},{1,129},{129,1},{2,130},{130,2},{3,131},{131,3},{4... | collective-permute-start | bytes 1327112 | tf_op jit(solution)/shard_map/projection/ppermute | solution.py:30
  54.9 50.4 %collective-permute-start.11 = (bf16[3,288,384]{2,1,0:T(8,128)(2,1)}, bf16[3,288,384]{2,1,0:T(8,128)(2,1)S(1)}, u32[]{:S(2)}, u32[]{:S(2)}) collective-permute-start(bf16[3,288,384]{2,1,0:T(8,128)(2,1)} %get-tuple-element.80), channel_id=1, source_target_pairs={{0,128},{128,0},{1,129},{129,1},{2,130},{130,2},{3,131},{131,3},{4... | collective-permute-start | bytes 1990664 | tf_op jit(solution)/shard_map/projection/ppermute | solution.py:30
  71.8 7.2 %collective-permute-start.6 = (bf16[288,384]{1,0:T(8,128)(2,1)S(1)}, bf16[288,384]{1,0:T(8,128)(2,1)S(1)}, u32[]{:S(2)}, u32[]{:S(2)}) collective-permute-start(bf16[288,384]{1,0:T(8,128)(2,1)S(1)} %get-tuple-element.73), channel_id=1, source_target_pairs={{0,16},{16,32},{32,48},{48,64},{64,80},{80,96},{96,112},{112,0},{1... | collective-permute-start | bytes 663560 | tf_op jit(solution)/shard_map/projection/ppermute | solution.py:30
  71.9 7.1 %collective-permute-start.7 = (bf16[288,384]{1,0:T(8,128)(2,1)S(1)}, bf16[288,384]{1,0:T(8,128)(2,1)S(1)}, u32[]{:S(2)}, u32[]{:S(2)}) collective-permute-start(bf16[288,384]{1,0:T(8,128)(2,1)S(1)} %get-tuple-element.74), channel_id=1, source_target_pairs={{0,112},{16,0},{32,16},{48,32},{64,48},{80,64},{96,80},{112,96},{1... | collective-permute-start | bytes 663560 | tf_op jit(solution)/shard_map/projection/ppermute | solution.py:30
  90.8 14.5 %collective-permute-start.9 = (bf16[288,384]{1,0:T(8,128)(2,1)S(1)}, bf16[288,384]{1,0:T(8,128)(2,1)S(1)}, u32[]{:S(2)}, u32[]{:S(2)}) collective-permute-start(bf16[288,384]{1,0:T(8,128)(2,1)S(1)} %get-tuple-element.77), channel_id=1, source_target_pairs={{0,16},{16,32},{32,48},{48,64},{64,80},{80,96},{96,112},{112,0},{1... | collective-permute-start | bytes 663560 | tf_op jit(solution)/shard_map/projection/ppermute | solution.py:30
  90.9 14.4 %collective-permute-start.10 = (bf16[288,384]{1,0:T(8,128)(2,1)S(1)}, bf16[288,384]{1,0:T(8,128)(2,1)S(1)}, u32[]{:S(2)}, u32[]{:S(2)}) collective-permute-start(bf16[288,384]{1,0:T(8,128)(2,1)S(1)} %get-tuple-element.78), channel_id=1, source_target_pairs={{0,112},{16,0},{32,16},{48,32},{64,48},{80,64},{96,80},{112,96},{1... | collective-permute-start | bytes 663560 | tf_op jit(solution)/shard_map/projection/ppermute | solution.py:30
  105.5 8.5 %collective-permute-start.12 = (bf16[288,384]{1,0:T(8,128)(2,1)S(1)}, bf16[288,384]{1,0:T(8,128)(2,1)S(1)}, u32[]{:S(2)}, u32[]{:S(2)}) collective-permute-start(bf16[288,384]{1,0:T(8,128)(2,1)S(1)} %get-tuple-element.81), channel_id=1, source_target_pairs={{0,16},{16,32},{32,48},{48,64},{64,80},{80,96},{96,112},{112,0},{1... | collective-permute-start | bytes 663560 | tf_op jit(solution)/shard_map/projection/ppermute | solution.py:30
  106.3 7.7 %collective-permute-start.13 = (bf16[288,384]{1,0:T(8,128)(2,1)S(1)}, bf16[288,384]{1,0:T(8,128)(2,1)S(1)}, u32[]{:S(2)}, u32[]{:S(2)}) collective-permute-start(bf16[288,384]{1,0:T(8,128)(2,1)S(1)} %get-tuple-element.82), channel_id=1, source_target_pairs={{0,112},{16,0},{32,16},{48,32},{64,48},{80,64},{96,80},{112,96},{1... | collective-permute-start | bytes 663560 | tf_op jit(solution)/shard_map/projection/ppermute | solution.py:30
  138.2 6.3 %collective-permute-start.14 = (bf16[512,128]{1,0:T(8,128)(2,1)S(1)}, bf16[512,128]{1,0:T(8,128)(2,1)S(1)}, u32[]{:S(2)}, u32[]{:S(2)}) collective-permute-start(bf16[512,128]{1,0:T(8,128)(2,1)S(1)} %attention.3.refs_0_), channel_id=1, source_target_pairs={{0,16},{16,32},{32,48},{48,64},{64,80},{80,96},{96,112},{112,0},{1... | collective-permute-start | bytes 393224 | tf_op jit(solution)/shard_map/output/ppermute | solution.py:30
  138.3 6.2 %collective-permute-start.15 = (bf16[512,128]{1,0:T(8,128)(2,1)S(1)}, bf16[512,128]{1,0:T(8,128)(2,1)S(1)}, u32[]{:S(2)}, u32[]{:S(2)}) collective-permute-start(bf16[512,128]{1,0:T(8,128)(2,1)S(1)} %attention.3.refs_0_), channel_id=1, source_target_pairs={{0,112},{16,0},{32,16},{48,32},{64,48},{80,64},{96,80},{112,96},{1... | collective-permute-start | bytes 393224 | tf_op jit(solution)/shard_map/output/ppermute | solution.py:30
  144.5 9.2 %collective-permute-start.16 = (bf16[512,128]{1,0:T(8,128)(2,1)S(1)}, bf16[512,128]{1,0:T(8,128)(2,1)S(1)}, u32[]{:S(2)}, u32[]{:S(2)}) collective-permute-start(bf16[512,128]{1,0:T(8,128)(2,1)S(1)} %collective-permute-done.14.refs_1_), channel_id=1, source_target_pairs={{0,16},{16,32},{32,48},{48,64},{64,80},{80,96},{96,112},{112,0},{1... | collective-permute-start | bytes 393224 | tf_op jit(solution)/shard_map/output/ppermute | solution.py:30
  144.5 10.0 %collective-permute-start.19 = (bf16[512,128]{1,0:T(8,128)(2,1)S(1)}, bf16[512,128]{1,0:T(8,128)(2,1)S(1)}, u32[]{:S(2)}, u32[]{:S(2)}) collective-permute-start(bf16[512,128]{1,0:T(8,128)(2,1)S(1)} %collective-permute-done.15.refs_7_), channel_id=1, source_target_pairs={{0,112},{16,0},{32,16},{48,32},{64,48},{80,64},{96,80},{112,96},{1... | collective-permute-start | bytes 393224 | tf_op jit(solution)/shard_map/output/ppermute | solution.py:30
  148.0 10.4 %collective-permute-start.18 = (bf16[512,128]{1,0:T(8,128)(2,1)S(1)}, bf16[512,128]{1,0:T(8,128)(2,1)S(1)}, u32[]{:S(2)}, u32[]{:S(2)}) collective-permute-start(bf16[512,128]{1,0:T(8,128)(2,1)S(1)} %attention.3.refs_0_), channel_id=1, source_target_pairs={{0,64},{16,80},{32,96},{48,112},{64,0},{80,16},{96,32},{112,48},{1... | collective-permute-start | bytes 393224 | tf_op jit(solution)/shard_map/output/ppermute | solution.py:30
  153.7 6.2 %collective-permute-start.17 = (bf16[512,128]{1,0:T(8,128)(2,1)S(1)}, bf16[512,128]{1,0:T(8,128)(2,1)S(1)}, u32[]{:S(2)}, u32[]{:S(2)}) collective-permute-start(bf16[512,128]{1,0:T(8,128)(2,1)S(1)} %collective-permute-done.16.refs_2_), channel_id=1, source_target_pairs={{0,16},{16,32},{32,48},{48,64},{64,80},{80,96},{96,112},{112,0},{1... | collective-permute-start | bytes 393224 | tf_op jit(solution)/shard_map/output/ppermute | solution.py:30
  154.4 6.4 %collective-permute-start.20 = (bf16[512,128]{1,0:T(8,128)(2,1)S(1)}, bf16[512,128]{1,0:T(8,128)(2,1)S(1)}, u32[]{:S(2)}, u32[]{:S(2)}) collective-permute-start(bf16[512,128]{1,0:T(8,128)(2,1)S(1)} %collective-permute-done.19.refs_6_), channel_id=1, source_target_pairs={{0,112},{16,0},{32,16},{48,32},{64,48},{80,64},{96,80},{112,96},{1... | collective-permute-start | bytes 393224 | tf_op jit(solution)/shard_map/output/ppermute | solution.py:30
  163.0 2.0 %collective-permute-start.21 = (bf16[512,512]{1,0:T(8,128)(2,1)S(1)}, bf16[512,512]{1,0:T(8,128)(2,1)S(1)}, u32[]{:S(2)}, u32[]{:S(2)}) collective-permute-start(bf16[512,512]{1,0:T(8,128)(2,1)S(1)} %get-tuple-element.93), channel_id=1, source_target_pairs={{0,8},{8,0},{1,9},{9,1},{2,10},{10,2},{3,11},{11,3},{4,12},{12,4},... | collective-permute-start | bytes 1572872 | tf_op jit(solution)/shard_map/output/ppermute | solution.py:30
  165.2 10.2 %copy-start.5 = (bf16[256,256]{1,0:T(8,128)(2,1)S(1)}, bf16[256,256]{1,0:T(8,128)(2,1)}, u32[]{:S(2)}) copy-start(bf16[256,256]{1,0:T(8,128)(2,1)} %hidden.1) | copy-start | bytes 393220
  165.3 9.9 %collective-permute-start.22 = (bf16[512,256]{1,0:T(8,128)(2,1)S(1)}, bf16[512,256]{1,0:T(8,128)(2,1)S(1)}, u32[]{:S(2)}, u32[]{:S(2)}) collective-permute-start(bf16[512,256]{1,0:T(8,128)(2,1)S(1)} %fusion), channel_id=1, source_target_pairs={{0,128},{128,0},{1,129},{129,1},{2,130},{130,2},{3,131},{131,3},{4... | collective-permute-start | bytes 786440 | tf_op jit(solution)/shard_map/output/ppermute | solution.py:30
Sparse Core Ops, SparseCore 0:
  38.8 55.7 all-gather.1

commit v4 on v2

--- a/solution.py
+++ b/solution.py
@@ -50,7 +50,9 @@
 SECOND = (6, 7, 0, 1, 2)
 
 
-def variant_kernel(pos, base, ids, hidden, embed, rows, onehot, variant):
+def variant_kernel(
+    pos, base, ids, hidden, embed, rows, onehot, variant, spots, block, sems
+):
     first = (lax.axis_index("x_lo") * Y + lax.axis_index("y")) * TOK
     vocab = embed.shape[0]
     spot = lax.broadcasted_iota(jnp.int32, (VAR, TOK), 0)
@@ -71,12 +73,18 @@
     changed_rows = (picked + change).astype(bf16)
     rows[:TOK] = hidden[...]
     rows[TOK:] = changed_rows
-    onehot[...] = places
+    spots[...] = places
+    first_copy = pltpu.make_async_copy(spots, onehot, sems.at[0])
+    first_copy.start()
     contract = (((0,), (0,)), ((), ()))
     placed = lax.dot_general(places, changed_rows, contract, preferred_element_type=f32)
     ones = jnp.ones((VAR, hidden.shape[1]), bf16)
     changed = lax.dot_general(places, ones, contract, preferred_element_type=f32)
-    variant[...] = jnp.where(changed > 0.5, placed, hidden[...].astype(f32)).astype(bf16)
+    block[...] = jnp.where(changed > 0.5, placed, hidden[...].astype(f32)).astype(bf16)
+    second_copy = pltpu.make_async_copy(block, variant, sems.at[1])
+    second_copy.start()
+    first_copy.wait()
+    second_copy.wait()
 
 
 def make_variant(pos, base, ids, hidden, embed):
@@ -86,13 +94,18 @@
         variant_kernel,
         out_shape=(
             jax.ShapeDtypeStruct((ROWS, width), bf16),
-            jax.ShapeDtypeStruct((VAR, TOK), bf16),
-            jax.ShapeDtypeStruct((TOK, width), bf16),
+            pltpu.HBM((VAR, TOK), bf16),
+            pltpu.HBM((TOK, width), bf16),
         ),
         in_specs=[smem, smem, smem, vmem(), vmem()],
-        out_specs=(vmem(),) * 3,
+        out_specs=(vmem(), hbm(), hbm()),
+        scratch_shapes=[
+            pltpu.VMEM((VAR, TOK), bf16),
+            pltpu.VMEM((TOK, width), bf16),
+            pltpu.SemaphoreType.DMA((2,)),
+        ],
         compiler_params=limit(4),
-    )(pos, base, ids, hidden, embed)
+    )(*(pltpu.with_memory_space_constraint(v, pltpu.HBM) for v in (pos, base, ids, hidden, embed)))
 
 
 def column_copies(ks, w, send, own, sems):
@@ -167,7 +180,7 @@
     shape = (Z, out_weight.shape[0] // BLOCKS, out_weight.shape[1] // Z)
     return pl.pallas_call(
         second_columns_kernel,
-        out_shape=(columns, columns, jax.ShapeDtypeStruct(shape, bf16)),
+        out_shape=(columns, columns, pltpu.HBM(shape, bf16)),
         in_specs=[hbm(), hbm()],
         out_specs=(vmem(), vmem(), hbm()),
         scratch_shapes=[
@@ -214,31 +227,43 @@
         acc = acc + jnp.dot(x_sis, w_sis[:, cols], preferred_element_type=f32)
         return acc.astype(bf16)
 
-    outs = list(outs)
-    for i, k in enumerate(ks):
-        if k == Z // 2:
-            for xr in range(X_HI):
-                out = outs.pop(0)
-                out[:ROWS, :] = product(i * X_HI + xr, 1)
-                out[ROWS:, :] = tail
-        else:
-            out = outs.pop(0)
-            out[:ROWS, :] = product(i * X_HI, X_HI)
-            out[ROWS:, :QKV] = tail
-            out[ROWS:, QKV:] = tail
+    def full(slot, out):
+        out[:ROWS, :] = product(slot, X_HI)
+        out[ROWS:, :QKV] = tail
+        out[ROWS:, QKV:] = tail
+
+    if ks == FIRST:
+        near_up, up, down, near_down, buffer, sems = outs
+        copies = []
+        for i, near in enumerate((near_up, near_down)):
+            full(FIRST.index((3, 5)[i]) * X_HI, buffer.at[i])
+            copies.append(pltpu.make_async_copy(buffer.at[i], near, sems.at[i]))
+            copies[i].start()
+        for xr, out in enumerate((up, down)):
+            out[:ROWS, :] = product(FIRST.index(Z // 2) * X_HI + xr, 1)
+            out[ROWS:, :] = tail
+        for copy in copies:
+            copy.wait()
+    else:
+        for i, out in enumerate(outs):
+            full(i * X_HI, out)
 
 
 def partials(ks, own, sis, gains, w_own, w_sis):
     half = jax.ShapeDtypeStruct((SUM_ROWS, QKV), bf16)
     full = jax.ShapeDtypeStruct((SUM_ROWS, X_HI * QKV), bf16)
-    shapes = []
-    for k in ks:
-        shapes += [half, half] if k == Z // 2 else [full]
+    if ks == FIRST:
+        away = pltpu.HBM(full.shape, bf16)
+        shapes, specs = (away, half, half, away), (hbm(), vmem(), vmem(), hbm())
+        scratch = [pltpu.VMEM((2, *full.shape), bf16), pltpu.SemaphoreType.DMA((2,))]
+    else:
+        shapes, specs, scratch = (full,) * len(ks), (vmem(),) * len(ks), []
     return pl.pallas_call(
         functools.partial(partial_kernel, ks),
-        out_shape=tuple(shapes),
+        out_shape=shapes,
         in_specs=[vmem()] * 5,
-        out_specs=(vmem(),) * len(shapes),
+        out_specs=specs,
+        scratch_shapes=scratch,
         compiler_params=limit(20),
         cost_estimate=pl.CostEstimate(
             flops=4 * ROWS * w_own.size, bytes_accessed=8 * w_own.size, transcendentals=0
@@ -342,7 +367,7 @@
         in_specs=[vmem()] * 5,
         out_specs=(vmem(), vmem()),
         compiler_params=limit(12),
-    )(mine, other, cosine, sine, onehot)
+    )(mine, other, cosine, sine, pltpu.with_memory_space_constraint(onehot, pltpu.HBM))
 
 
 def attend_kernel(queries, blocks, out, scores, peak, denom, total, var_kv, spots):
@@ -433,13 +458,36 @@
     )(queries, blocks)
 
 
-def project_kernel(w, *refs):
-    shards, (keep, near, far), (joined, turned) = refs[:Z], refs[Z : Z + 3], refs[Z + 3 :]
-    z, core, x_hi = lax.axis_index("z"), lax.axis_index("core"), lax.axis_index("x_hi")
+def arrange_kernel(w, out, sems):
+    z = lax.axis_index("z")
+    copies = []
+    for d in range(Z):
+        source = lax.rem(z + Z - d, Z)
+        copies.append(
+            pltpu.make_async_copy(w.at[source], out.at[d * HD : (d + 1) * HD, :], sems.at[d])
+        )
+    for copy in copies:
+        copy.start()
+    for copy in copies:
+        copy.wait()
+
+
+def arrange(w):
+    return pl.pallas_call(
+        arrange_kernel,
+        out_shape=jax.ShapeDtypeStruct((Z * HD, w.shape[2]), bf16),
+        in_specs=[hbm()],
+        out_specs=vmem(),
+        scratch_shapes=[pltpu.SemaphoreType.DMA((Z,))],
+        compiler_params=limit(4),
+    )(pltpu.with_memory_space_constraint(w, pltpu.HBM))
+
+
+def project_kernel(turned, *refs):
+    shards, (keep, near, far), joined = refs[:Z], refs[Z : Z + 3], refs[-1]
+    core, x_hi = lax.axis_index("core"), lax.axis_index("x_hi")
     for d in range(Z):
         joined[:, d * HD : (d + 1) * HD] = shards[d][...]
-        source = lax.rem(z + Z - d, Z)
-        turned[d * HD : (d + 1) * HD, :] = w[source]
 
     def product(xr, cr, rows):
         column = (lax.rem(x_hi + xr, X_HI) * CORE + lax.rem(core + cr, CORE)) * TOK
@@ -470,10 +518,7 @@
         ),
         in_specs=[vmem()] * (1 + Z),
         out_specs=(vmem(),) * 3,
-        scratch_shapes=[
-            pltpu.VMEM((rows, Z * HD), bf16),
-            pltpu.VMEM((Z * HD, w.shape[2]), bf16),
-        ],
+        scratch_shapes=[pltpu.VMEM((rows, Z * HD), bf16)],
         compiler_params=limit(16),
     )(w, *shards)
 
@@ -501,6 +546,8 @@
     with jax.named_scope("projection"):
         near_up, up, down, near_down = partials(FIRST, rows, rows_sis, gains, own_first, sis_first)
         up, down = shift(up, "z", Z, 1), shift(down, "z", Z, -1)
+        near_up = pltpu.with_memory_space_constraint(near_up, pltpu.HBM)
+        near_down = pltpu.with_memory_space_constraint(near_down, pltpu.HBM)
         up, down, shared = lax.optimization_barrier((up, down, shared))
         out_w = lax.all_gather(shared, CTX, axis=1, tiled=True)
         up, down = ring_add(first_kernel, up, down, near_up, near_down)
@@ -538,6 +585,9 @@
             pieces[Z - d] = shift(pieces[(Z - d + 1) % Z], "z", Z, -1)
             if d == 1:
                 pieces[Z // 2] = shift(attn, "z", Z, Z // 2)
+                out_w, pieces[1], pieces[7] = lax.optimization_barrier(
+                    (arrange(out_w), pieces[1], pieces[7])
+                )
         keep, near, far = project(out_w, pieces)
         near = shift(near, "core", CORE, 1).astype(f32)
         far = (far + near[:, width_part:]).astype(bf16)

time: 163 us -> 156 us (0.957)
  local copies, waits for them, and re-layouts: 11.7 us -> 0.79 us
  waiting for transfers between devices: 56 us -> 49.7 us
  Pallas kernels: 20.2 us -> 25.8 us
  starting transfers between devices: 39.2 us -> 43.8 us
    unnamed x38 -> x10, local copies, waits for them, and re-layouts: 11 us -> 0.03 us
    ppermute x21, waiting for transfers between devices: 52.1 us -> 44.7 us  [shift(): lax.ppermute(value, axis, [(i, (i + distance) % size) for i in range(size)])]
    ppermute x21, starting transfers between devices: 30.7 us -> 35.3 us  [shift(): lax.ppermute(value, axis, [(i, (i + distance) % size) for i in range(size)])]
    pallas_call x3 -> x4, Pallas kernels: 9.64 us -> 12.3 us  [the longest x2 6.33 us: partials(): pl.pallas_call(functools.partial(partial_kernel, ks), out_shape=shapes, i...]
  transfers between devices with their start and end apart: 23 -> 23, of which waited for: 15 -> 13; matrix products, arithmetic and copies ran while one was open for 1% -> 1% of each run, Pallas kernels for 9% -> 12%
where the time goes in v4:
time: 156 us; the launch traced here: 153 us
  waiting for transfers between devices  49.7 us (32%)
  starting transfers between devices  43.8 us (28%)
  Pallas kernels  25.8 us (17%)
  blocking collectives  17.9 us (11%)
  between operations  13.6 us (9%)
  other arithmetic  1.81 us (1%)
    ppermute x21, waiting for transfers between devices, shift(): lax.ppermute(value, axis, [(i, (i + distance) % size) for i in range(size)])  44.7 us
    ppermute x21, starting transfers between devices, shift(): lax.ppermute(value, axis, [(i, (i + distance) % size) for i in range(size)])  35.3 us
    all_to_all x1, blocking collectives, shards(): blocks = lax.all_to_all(payload, CTX, 0, 0, tiled=True)  17.9 us
    all_to_all x1, starting transfers between devices, shards(): shared = lax.all_to_all(share, 'z', 0, 0, tiled=True)  8.47 us
    pallas_call x2, Pallas kernels, partials(): pl.pallas_call(functools.partial(partial_kernel, ks), out_shape=shapes, i...  6.33 us
    all_to_all x1, waiting for transfers between devices, shards(): shared = lax.all_to_all(share, 'z', 0, 0, tiled=True)  4.9 us
    pallas_call x1, Pallas kernels, second_columns(): pl.pallas_call(second_columns_kernel, out_shape=(columns, columns, pltpu....  4.43 us
  transfers between devices with their start and end apart: 23, of which 13 were waited for; matrix products, arithmetic and copies ran while one was open for 1% of the time, Pallas kernels for 12%

profile of v4, /device:TPU:6, one launch (start us, length us, event | category | flops | bytes accessed | tf_op | source)
XLA Modules:
  0.0 153.5 jit_solution(6663392548028772728)
XLA Ops:
  6.5 2.2 %inputs.3 = (bf16[272,256]{1,0:T(8,128)(2,1)S(1)}, bf16[16,256]{1,0:T(8,128)(2,1)}, bf16[256,256]{1,0:T(8,128)(2,1)}) custom-call(s32[16]{0:T(128)} %pos.1, s32[16]{0:T(128)} %base.1, s32[256]{0:T(256)} %ids.1, bf16[256,256]{1,0:T(8,128)(2,1)} %hidden.1, bf16[512,256]{1,0:T(8,128)(2,1)} %embed.1), custom_call_target="tpu_custom_call" | custom-call | tf_op jit(solution)/shard_map/inputs/pallas_call | solution.py:93
  8.7 2.9 %inputs.4 = (bf16[256,2304]{1,0:T(8,128)(2,1)}, bf16[256,2304]{1,0:T(8,128)(2,1)S(1)}) custom-call(bf16[256,12288]{1,0:T(8,128)(2,1)} %w.1), custom_call_target="tpu_custom_call" | custom-call | tf_op jit(solution)/shard_map/inputs/pallas_call | solution.py:140
  11.6 0.1 collective-permute-start.1
  11.7 0.5 collective-permute-start
  12.2 2.2 %collective-permute-done.sis = bf16[272,256]{1,0:T(8,128)(2,1)S(1)} collective-permute-done((bf16[272,256]{1,0:T(8,128)(2,1)S(1)}, bf16[272,256]{1,0:T(8,128)(2,1)S(1)}, u32[]{:S(2)}, u32[]{:S(2)}) %collective-permute-start) | collective-permute-done | bytes 139296 | tf_op jit(solution)/shard_map/inputs/ppermute | solution.py:30
  14.4 4.4 %inputs.5 = (bf16[256,3840]{1,0:T(8,128)(2,1)}, bf16[256,3840]{1,0:T(8,128)(2,1)S(1)}, bf16[8,16,1024]{2,1,0:T(8,128)(2,1)}) custom-call(bf16[256,12288]{1,0:T(8,128)(2,1)} %w.1, bf16[128,8192]{1,0:T(8,128)(2,1)} %out_weight.1), custom_call_target="tpu_custom_call" | custom-call | tf_op jit(solution)/shard_map/inputs/pallas_call | solution.py:181
  18.8 0.5 collective-permute-start.6
  19.3 8.5 %all-to-all-start = ((bf16[8,16,1024]{2,1,0:T(8,128)(2,1)}), bf16[8,16,1024]{2,1,0:T(8,128)(2,1)}, u32[]{:S(2)}, u32[]{:S(2)}) async-start(bf16[8,16,1024]{2,1,0:T(8,128)(2,1)} %get-tuple-element.67), calls=%async_computation | async-start | bytes 524288 | tf_op jit(solution)/shard_map/inputs/all_to_all | solution.py:542
  27.7 0.0 all-gather.2.cloned.1.call-start
  27.8 0.8 dynamic-slice.3
  28.6 0.0 collective-permute-done.1.w_sis
  28.6 3.5 %projection.6 = (bf16[288,768]{1,0:T(8,128)(2,1)}, bf16[288,384]{1,0:T(8,128)(2,1)}, bf16[288,384]{1,0:T(8,128)(2,1)}, bf16[288,768]{1,0:T(8,128)(2,1)}) custom-call(bf16[272,256]{1,0:T(8,128)(2,1)S(1)} %get-tuple-element.76.own, bf16[272,256]{1,0:T(8,128)(2,1)S(1)} %collective-permute-done.sis, bf16[1,512]{1,0:T(2,128)(2,1)S(1)} %dynamic_slice.3.gains, ...), custom_call_target="tpu_custom_call" | custom-call | flops 641728512 | bytes 4718592 | tf_op jit(solution)/shard_map/projection/pallas_call | solution.py:261
  32.1 2.0 %collective-permute-start.2 = (bf16[288,384]{1,0:T(8,128)(2,1)}, bf16[288,384]{1,0:T(8,128)(2,1)S(1)}, u32[]{:S(2)}, u32[]{:S(2)}) collective-permute-start(bf16[288,384]{1,0:T(8,128)(2,1)} %get-tuple-element.64), channel_id=1, source_target_pairs={{0,16},{16,32},{32,48},{48,64},{64,80},{80,96},{96,112},{112,0},{1... | collective-permute-start | bytes 663560 | tf_op jit(solution)/shard_map/projection/ppermute | solution.py:30
  34.1 1.3 collective-permute-start.3
  35.5 4.9 %all-to-all-done = bf16[8,16,1024]{2,1,0:T(8,128)(2,1)} async-done(((bf16[8,16,1024]{2,1,0:T(8,128)(2,1)}), bf16[8,16,1024]{2,1,0:T(8,128)(2,1)}, u32[]{:S(2)}, u32[]{:S(2)}) %all-to-all-start) | async-done | bytes 262176 | tf_op jit(solution)/shard_map/inputs/all_to_all | solution.py:542
  40.4 1.7 %collective-permute-done.2.up = bf16[288,384]{1,0:T(8,128)(2,1)S(1)} collective-permute-done((bf16[288,384]{1,0:T(8,128)(2,1)}, bf16[288,384]{1,0:T(8,128)(2,1)S(1)}, u32[]{:S(2)}, u32[]{:S(2)}) %collective-permute-start.2) | collective-permute-done | bytes 221216 | tf_op jit(solution)/shard_map/projection/ppermute | solution.py:30
  42.1 0.0 all-gather.2.cloned.1.call-update
  42.1 1.3 projection.7
  43.4 1.3 collective-permute-start.4
  44.7 2.0 %collective-permute-start.5 = (bf16[288,768]{1,0:T(8,128)(2,1)S(1)}, bf16[288,768]{1,0:T(8,128)(2,1)S(1)}, u32[]{:S(2)}, u32[]{:S(2)}) collective-permute-start(bf16[288,768]{1,0:T(8,128)(2,1)S(1)} %get-tuple-element.75), channel_id=1, source_target_pairs={{0,112},{16,0},{32,16},{48,32},{64,48},{80,64},{96,80},{112,96},{1... | collective-permute-start | bytes 1327112 | tf_op jit(solution)/shard_map/projection/ppermute | solution.py:30
  46.7 2.8 %projection.8 = (bf16[288,768]{1,0:T(8,128)(2,1)S(1)}, bf16[288,768]{1,0:T(8,128)(2,1)S(1)}, bf16[288,768]{1,0:T(8,128)(2,1)S(1)}, bf16[288,768]{1,0:T(8,128)(2,1)S(1)}, bf16[288,768]{1,0:T(8,128)(2,1)S(1)}) custom-call(bf16[272,256]{1,0:T(8,128)(2,1)S(1)} %get-tuple-element.76.own, bf16[272,256]{1,0:T(8,128)(2,1)S(1)} %collective-permute-done.sis, ...), custom_call_target="tpu_custom_call" | custom-call | flops 1069547520 | bytes 7864320 | tf_op jit(solution)/shard_map/projection/pallas_call | solution.py:261
  49.5 0.0 copy-start.4
  49.5 6.5 %collective-permute-done.4.up = bf16[288,768]{1,0:T(8,128)(2,1)S(1)} collective-permute-done((bf16[288,768]{1,0:T(8,128)(2,1)S(1)}, bf16[288,768]{1,0:T(8,128)(2,1)S(1)}, u32[]{:S(2)}, u32[]{:S(2)}) %collective-permute-start.4) | collective-permute-done | bytes 442400 | tf_op jit(solution)/shard_map/projection/ppermute | solution.py:30
  56.0 0.0 collective-permute-done.5.down
  56.0 0.2 projection.9
  56.3 1.7 %collective-permute-start.7 = (bf16[288,768]{1,0:T(8,128)(2,1)S(1)}, bf16[288,768]{1,0:T(8,128)(2,1)S(1)}, u32[]{:S(2)}, u32[]{:S(2)}) collective-permute-start(bf16[288,768]{1,0:T(8,128)(2,1)S(1)} %get-tuple-element.88), channel_id=1, source_target_pairs={{0,16},{16,32},{32,48},{48,64},{64,80},{80,96},{96,112},{112,0},{1... | collective-permute-start | bytes 1327112 | tf_op jit(solution)/shard_map/projection/ppermute | solution.py:30
  58.0 1.7 %collective-permute-start.8 = (bf16[288,768]{1,0:T(8,128)(2,1)S(1)}, bf16[288,768]{1,0:T(8,128)(2,1)S(1)}, u32[]{:S(2)}, u32[]{:S(2)}) collective-permute-start(bf16[288,768]{1,0:T(8,128)(2,1)S(1)} %get-tuple-element.89), channel_id=1, source_target_pairs={{0,112},{16,0},{32,16},{48,32},{64,48},{80,64},{96,80},{112,96},{1... | collective-permute-start | bytes 1327112 | tf_op jit(solution)/shard_map/projection/ppermute | solution.py:30
  59.6 8.4 %collective-permute-done.7.up = bf16[288,768]{1,0:T(8,128)(2,1)S(1)} collective-permute-done((bf16[288,768]{1,0:T(8,128)(2,1)S(1)}, bf16[288,768]{1,0:T(8,128)(2,1)S(1)}, u32[]{:S(2)}, u32[]{:S(2)}) %collective-permute-start.7) | collective-permute-done | bytes 442400 | tf_op jit(solution)/shard_map/projection/ppermute | solution.py:30
  68.0 0.2 projection.10
  68.3 1.1 collective-permute-start.9
  69.3 2.3 %collective-permute-start.10 = (bf16[288,768]{1,0:T(8,128)(2,1)S(1)}, bf16[288,768]{1,0:T(8,128)(2,1)S(1)}, u32[]{:S(2)}, u32[]{:S(2)}) collective-permute-start(bf16[288,768]{1,0:T(8,128)(2,1)S(1)} %get-tuple-element.93), channel_id=1, source_target_pairs={{0,112},{16,0},{32,16},{48,32},{64,48},{80,64},{96,80},{112,96},{1... | collective-permute-start | bytes 1327112 | tf_op jit(solution)/shard_map/projection/ppermute | solution.py:30
  71.6 7.5 %collective-permute-done.9.up = bf16[288,768]{1,0:T(8,128)(2,1)S(1)} collective-permute-done((bf16[288,768]{1,0:T(8,128)(2,1)S(1)}, bf16[288,768]{1,0:T(8,128)(2,1)S(1)}, u32[]{:S(2)}, u32[]{:S(2)}) %collective-permute-start.9) | collective-permute-done | bytes 442400 | tf_op jit(solution)/shard_map/projection/ppermute | solution.py:30
  79.1 0.0 collective-permute-done.10.down
  79.1 0.2 projection.11
  79.3 1.7 %collective-permute-start.11 = (bf16[288,384]{1,0:T(8,128)(2,1)S(1)}, bf16[288,384]{1,0:T(8,128)(2,1)S(1)}, u32[]{:S(2)}, u32[]{:S(2)}) collective-permute-start(bf16[288,384]{1,0:T(8,128)(2,1)S(1)} %get-tuple-element.96), channel_id=1, source_target_pairs={{0,128},{128,0},{1,129},{129,1},{2,130},{130,2},{3,131},{131,3},{4... | collective-permute-start | bytes 663560 | tf_op jit(solution)/shard_map/projection/ppermute | solution.py:30
  80.9 0.6 fusion.2
  81.5 0.1 pad_maximum_fusion
  81.7 5.3 %collective-permute-done.11.other = bf16[288,384]{1,0:T(8,128)(2,1)S(1)} collective-permute-done((bf16[288,384]{1,0:T(8,128)(2,1)S(1)}, bf16[288,384]{1,0:T(8,128)(2,1)S(1)}, u32[]{:S(2)}, u32[]{:S(2)}) %collective-permute-start.11) | collective-permute-done | bytes 221216 | tf_op jit(solution)/shard_map/projection/ppermute | solution.py:30
  87.0 1.3 attention.2
  88.3 17.9 %all_to_all.10.blocks = bf16[8,288,256]{2,1,0:T(8,128)(2,1)S(1)} all-to-all(bf16[8,288,256]{2,1,0:T(8,128)(2,1)S(1)} %get-tuple-element.99), channel_id=1, replica_groups=mesh['x_hi'=2,'z'=8,'core'=2,'x_lo'=2,'y'=4] {'x_lo','y'}, dimensions={0} | all-to-all | bytes 2359296 | tf_op jit(solution)/shard_map/attention/all_to_all | solution.py:577
  106.2 2.9 %attention.3.refs_0_ = bf16[512,128]{1,0:T(8,128)(2,1)S(1)} custom-call(bf16[512,128]{1,0:T(8,128)(2,1)S(1)} %get-tuple-element.98.queries, bf16[8,288,256]{2,1,0:T(8,128)(2,1)S(1)} %all_to_all.10.blocks), custom_call_target="tpu_custom_call" | custom-call | tf_op jit(solution)/shard_map/attention/pallas_call | solution.py:444
  109.2 0.0 all-gather.2.cloned.1.call-done.w
  109.2 1.1 collective-permute-start.12
  110.3 2.2 %collective-permute-start.13 = (bf16[512,128]{1,0:T(8,128)(2,1)S(1)}, bf16[512,128]{1,0:T(8,128)(2,1)S(1)}, u32[]{:S(2)}, u32[]{:S(2)}) collective-permute-start(bf16[512,128]{1,0:T(8,128)(2,1)S(1)} %attention.3.refs_0_), channel_id=1, source_target_pairs={{0,112},{16,0},{32,16},{48,32},{64,48},{80,64},{96,80},{112,96},{1... | collective-permute-start | bytes 393224 | tf_op jit(solution)/shard_map/output/ppermute | solution.py:30
  112.5 1.6 %output.2.turned = bf16[1024,1024]{1,0:T(8,128)(2,1)S(1)} custom-call(bf16[8,128,1024]{2,1,0:T(8,128)(2,1)} %all-gather.2.cloned.1.call-done.w), custom_call_target="tpu_custom_call" | custom-call | tf_op jit(solution)/shard_map/output/pallas_call | solution.py:476
  114.1 1.4 collective-permute-done.12.refs_1_
  115.5 0.0 collective-permute-done.13.refs_7_
  115.5 2.1 %collective-permute-start.14 = (bf16[512,128]{1,0:T(8,128)(2,1)S(1)}, bf16[512,128]{1,0:T(8,128)(2,1)S(1)}, u32[]{:S(2)}, u32[]{:S(2)}) collective-permute-start(bf16[512,128]{1,0:T(8,128)(2,1)S(1)} %collective-permute-done.12.refs_1_), channel_id=1, source_target_pairs={{0,16},{16,32},{32,48},{48,64},{64,80},{80,96},{96,112},{112,0},{1... | collective-permute-start | bytes 393224 | tf_op jit(solution)/shard_map/output/ppermute | solution.py:30
  117.6 1.1 collective-permute-start.17
  118.8 5.9 %collective-permute-start.16 = (bf16[512,128]{1,0:T(8,128)(2,1)S(1)}, bf16[512,128]{1,0:T(8,128)(2,1)S(1)}, u32[]{:S(2)}, u32[]{:S(2)}) collective-permute-start(bf16[512,128]{1,0:T(8,128)(2,1)S(1)} %attention.3.refs_0_), channel_id=1, source_target_pairs={{0,64},{16,80},{32,96},{48,112},{64,0},{80,16},{96,32},{112,48},{1... | collective-permute-start | bytes 393224 | tf_op jit(solution)/shard_map/output/ppermute | solution.py:30
  124.7 3.2 %collective-permute-start.18 = (bf16[512,128]{1,0:T(8,128)(2,1)S(1)}, bf16[512,128]{1,0:T(8,128)(2,1)S(1)}, u32[]{:S(2)}, u32[]{:S(2)}) collective-permute-start(bf16[512,128]{1,0:T(8,128)(2,1)S(1)} %collective-permute-done.17.refs_6_), channel_id=1, source_target_pairs={{0,112},{16,0},{32,16},{48,32},{64,48},{80,64},{96,80},{112,96},{1... | collective-permute-start | bytes 393224 | tf_op jit(solution)/shard_map/output/ppermute | solution.py:30
  127.9 0.7 collective-permute-done.16.refs_4_
  128.7 2.2 %collective-permute-done.15.refs_3_ = bf16[512,128]{1,0:T(8,128)(2,1)S(1)} collective-permute-done((bf16[512,128]{1,0:T(8,128)(2,1)S(1)}, bf16[512,128]{1,0:T(8,128)(2,1)S(1)}, u32[]{:S(2)}, u32[]{:S(2)}) %collective-permute-start.15) | collective-permute-done | bytes 131104 | tf_op jit(solution)/shard_map/output/ppermute | solution.py:30
  130.9 0.3 collective-permute-done.18.refs_5_
  131.1 2.2 %output.3 = (f32[512,256]{1,0:T(8,128)S(1)}, bf16[512,512]{1,0:T(8,128)(2,1)S(1)}, f32[512,256]{1,0:T(8,128)S(1)}) custom-call(bf16[1024,1024]{1,0:T(8,128)(2,1)S(1)} %output.2.turned, bf16[512,128]{1,0:T(8,128)(2,1)S(1)} %attention.3.refs_0_, bf16[512,128]{1,0:T(8,128)(2,1)S(1)} %collective-permute-done.12.refs_1_, ...), custom_call_target="tpu_custom_call" | custom-call | tf_op jit(solution)/shard_map/output/pallas_call | solution.py:512
  133.3 0.1 collective-permute-start.19
  133.4 1.9 %collective-permute-done.19 = bf16[512,512]{1,0:T(8,128)(2,1)S(1)} collective-permute-done((bf16[512,512]{1,0:T(8,128)(2,1)S(1)}, bf16[512,512]{1,0:T(8,128)(2,1)S(1)}, u32[]{:S(2)}, u32[]{:S(2)}) %collective-permute-start.19) | collective-permute-done | bytes 524320 | tf_op jit(solution)/shard_map/output/ppermute | solution.py:30
  135.3 0.1 convert_element_type.32
  135.5 0.0 copy-start.2
  135.5 0.1 fusion
  135.6 3.5 %collective-permute-start.20 = (bf16[512,256]{1,0:T(8,128)(2,1)S(1)}, bf16[512,256]{1,0:T(8,128)(2,1)S(1)}, u32[]{:S(2)}, u32[]{:S(2)}) collective-permute-start(bf16[512,256]{1,0:T(8,128)(2,1)S(1)} %fusion), channel_id=1, source_target_pairs={{0,128},{128,0},{1,129},{129,1},{2,130},{130,2},{3,131},{131,3},{4... | collective-permute-start | bytes 786440 | tf_op jit(solution)/shard_map/output/ppermute | solution.py:30
  139.1 6.6 %collective-permute-done.20 = bf16[512,256]{1,0:T(8,128)(2,1)S(1)} collective-permute-done((bf16[512,256]{1,0:T(8,128)(2,1)S(1)}, bf16[512,256]{1,0:T(8,128)(2,1)S(1)}, u32[]{:S(2)}, u32[]{:S(2)}) %collective-permute-start.20) | collective-permute-done | bytes 262176 | tf_op jit(solution)/shard_map/output/ppermute | solution.py:30
  145.7 0.1 fusion.1
  145.9 0.8 add_convert_fusion
  (18 shorter events, 0.1 us)
Async XLA Ops:
  11.6 17.0 %collective-permute-start.1 = (bf16[256,2304]{1,0:T(8,128)(2,1)}, bf16[256,2304]{1,0:T(8,128)(2,1)}, u32[]{:S(2)}, u32[]{:S(2)}) collective-permute-start(bf16[256,2304]{1,0:T(8,128)(2,1)} %get-tuple-element.61), channel_id=1, source_target_pairs={{0,8},{8,0},{1,9},{9,1},{2,10},{10,2},{3,11},{11,3},{4,12},{12,4},... | collective-permute-start | bytes 3538952 | tf_op jit(solution)/shard_map/inputs/ppermute | solution.py:30
  11.7 2.7 %collective-permute-start = (bf16[272,256]{1,0:T(8,128)(2,1)S(1)}, bf16[272,256]{1,0:T(8,128)(2,1)S(1)}, u32[]{:S(2)}, u32[]{:S(2)}) collective-permute-start(bf16[272,256]{1,0:T(8,128)(2,1)S(1)} %get-tuple-element.76.own), channel_id=1, source_target_pairs={{0,8},{8,0},{1,9},{9,1},{2,10},{10,2},{3,11},{11,3},{4,12},{12,4},... | collective-permute-start | bytes 417800 | tf_op jit(solution)/shard_map/inputs/ppermute | solution.py:30
  18.8 27.9 %collective-permute-start.6 = (bf16[256,3840]{1,0:T(8,128)(2,1)}, bf16[256,3840]{1,0:T(8,128)(2,1)}, u32[]{:S(2)}, u32[]{:S(2)}) collective-permute-start(bf16[256,3840]{1,0:T(8,128)(2,1)} %get-tuple-element.78), channel_id=1, source_target_pairs={{0,8},{8,0},{1,9},{9,1},{2,10},{10,2},{3,11},{11,3},{4,12},{12,4},... | collective-permute-start | bytes 5898248 | tf_op jit(solution)/shard_map/inputs/ppermute | solution.py:30
  19.3 21.1 %all-to-all-start = ((bf16[8,16,1024]{2,1,0:T(8,128)(2,1)}), bf16[8,16,1024]{2,1,0:T(8,128)(2,1)}, u32[]{:S(2)}, u32[]{:S(2)}) async-start(bf16[8,16,1024]{2,1,0:T(8,128)(2,1)} %get-tuple-element.67), calls=%async_computation | async-start | bytes 524288 | tf_op jit(solution)/shard_map/inputs/all_to_all | solution.py:542
  27.7 81.4 %all-gather.2.cloned.1.call-start = ((), (), s32[]{:S(2)}) async-start(), calls=%async_computation.2 | async-start | bytes 2359296 | tf_op jit(solution)/shard_map/projection/all_gather | solution.py:552
  32.1 10.0 %collective-permute-start.2 = (bf16[288,384]{1,0:T(8,128)(2,1)}, bf16[288,384]{1,0:T(8,128)(2,1)S(1)}, u32[]{:S(2)}, u32[]{:S(2)}) collective-permute-start(bf16[288,384]{1,0:T(8,128)(2,1)} %get-tuple-element.64), channel_id=1, source_target_pairs={{0,16},{16,32},{32,48},{48,64},{64,80},{80,96},{96,112},{112,0},{1... | collective-permute-start | bytes 663560 | tf_op jit(solution)/shard_map/projection/ppermute | solution.py:30
  34.1 7.9 %collective-permute-start.3 = (bf16[288,384]{1,0:T(8,128)(2,1)}, bf16[288,384]{1,0:T(8,128)(2,1)S(1)}, u32[]{:S(2)}, u32[]{:S(2)}) collective-permute-start(bf16[288,384]{1,0:T(8,128)(2,1)} %get-tuple-element.65), channel_id=1, source_target_pairs={{0,112},{16,0},{32,16},{48,32},{64,48},{80,64},{96,80},{112,96},{1... | collective-permute-start | bytes 663560 | tf_op jit(solution)/shard_map/projection/ppermute | solution.py:30
  43.4 12.6 %collective-permute-start.4 = (bf16[288,768]{1,0:T(8,128)(2,1)S(1)}, bf16[288,768]{1,0:T(8,128)(2,1)S(1)}, u32[]{:S(2)}, u32[]{:S(2)}) collective-permute-start(bf16[288,768]{1,0:T(8,128)(2,1)S(1)} %get-tuple-element.74), channel_id=1, source_target_pairs={{0,16},{16,32},{32,48},{48,64},{64,80},{80,96},{96,112},{112,0},{1... | collective-permute-start | bytes 1327112 | tf_op jit(solution)/shard_map/projection/ppermute | solution.py:30
  44.7 11.4 %collective-permute-start.5 = (bf16[288,768]{1,0:T(8,128)(2,1)S(1)}, bf16[288,768]{1,0:T(8,128)(2,1)S(1)}, u32[]{:S(2)}, u32[]{:S(2)}) collective-permute-start(bf16[288,768]{1,0:T(8,128)(2,1)S(1)} %get-tuple-element.75), channel_id=1, source_target_pairs={{0,112},{16,0},{32,16},{48,32},{64,48},{80,64},{96,80},{112,96},{1... | collective-permute-start | bytes 1327112 | tf_op jit(solution)/shard_map/projection/ppermute | solution.py:30
  49.5 6.8 %copy-start = (bf16[288,768]{1,0:T(8,128)(2,1)}, bf16[288,768]{1,0:T(8,128)(2,1)S(1)}, u32[]{:S(2)}) copy-start(bf16[288,768]{1,0:T(8,128)(2,1)S(1)} %get-tuple-element.94.near) | copy-start | bytes 1327108
  49.5 22.1 %copy-start.4 = (s32[16]{0:T(128)S(1)}, s32[16]{0:T(128)}, u32[]{:S(2)}) copy-start(s32[16]{0:T(128)} %pos.1) | copy-start | bytes 196
  56.3 22.8 %copy-start.1 = (bf16[288,768]{1,0:T(8,128)(2,1)S(1)}, bf16[288,768]{1,0:T(8,128)(2,1)}, u32[]{:S(2)}) copy-start(bf16[288,768]{1,0:T(8,128)(2,1)} %copy-done) | copy-start | bytes 1327108
  56.3 11.7 %collective-permute-start.7 = (bf16[288,768]{1,0:T(8,128)(2,1)S(1)}, bf16[288,768]{1,0:T(8,128)(2,1)S(1)}, u32[]{:S(2)}, u32[]{:S(2)}) collective-permute-start(bf16[288,768]{1,0:T(8,128)(2,1)S(1)} %get-tuple-element.88), channel_id=1, source_target_pairs={{0,16},{16,32},{32,48},{48,64},{64,80},{80,96},{96,112},{112,0},{1... | collective-permute-start | bytes 1327112 | tf_op jit(solution)/shard_map/projection/ppermute | solution.py:30
  58.0 10.1 %collective-permute-start.8 = (bf16[288,768]{1,0:T(8,128)(2,1)S(1)}, bf16[288,768]{1,0:T(8,128)(2,1)S(1)}, u32[]{:S(2)}, u32[]{:S(2)}) collective-permute-start(bf16[288,768]{1,0:T(8,128)(2,1)S(1)} %get-tuple-element.89), channel_id=1, source_target_pairs={{0,112},{16,0},{32,16},{48,32},{64,48},{80,64},{96,80},{112,96},{1... | collective-permute-start | bytes 1327112 | tf_op jit(solution)/shard_map/projection/ppermute | solution.py:30
  68.3 10.8 %collective-permute-start.9 = (bf16[288,768]{1,0:T(8,128)(2,1)S(1)}, bf16[288,768]{1,0:T(8,128)(2,1)S(1)}, u32[]{:S(2)}, u32[]{:S(2)}) collective-permute-start(bf16[288,768]{1,0:T(8,128)(2,1)S(1)} %get-tuple-element.92), channel_id=1, source_target_pairs={{0,16},{16,32},{32,48},{48,64},{64,80},{80,96},{96,112},{112,0},{1... | collective-permute-start | bytes 1327112 | tf_op jit(solution)/shard_map/projection/ppermute | solution.py:30
  69.3 9.8 %collective-permute-start.10 = (bf16[288,768]{1,0:T(8,128)(2,1)S(1)}, bf16[288,768]{1,0:T(8,128)(2,1)S(1)}, u32[]{:S(2)}, u32[]{:S(2)}) collective-permute-start(bf16[288,768]{1,0:T(8,128)(2,1)S(1)} %get-tuple-element.93), channel_id=1, source_target_pairs={{0,112},{16,0},{32,16},{48,32},{64,48},{80,64},{96,80},{112,96},{1... | collective-permute-start | bytes 1327112 | tf_op jit(solution)/shard_map/projection/ppermute | solution.py:30
  79.3 7.7 %collective-permute-start.11 = (bf16[288,384]{1,0:T(8,128)(2,1)S(1)}, bf16[288,384]{1,0:T(8,128)(2,1)S(1)}, u32[]{:S(2)}, u32[]{:S(2)}) collective-permute-start(bf16[288,384]{1,0:T(8,128)(2,1)S(1)} %get-tuple-element.96), channel_id=1, source_target_pairs={{0,128},{128,0},{1,129},{129,1},{2,130},{130,2},{3,131},{131,3},{4... | collective-permute-start | bytes 663560 | tf_op jit(solution)/shard_map/projection/ppermute | solution.py:30
  109.2 6.3 %collective-permute-start.12 = (bf16[512,128]{1,0:T(8,128)(2,1)S(1)}, bf16[512,128]{1,0:T(8,128)(2,1)S(1)}, u32[]{:S(2)}, u32[]{:S(2)}) collective-permute-start(bf16[512,128]{1,0:T(8,128)(2,1)S(1)} %attention.3.refs_0_), channel_id=1, source_target_pairs={{0,16},{16,32},{32,48},{48,64},{64,80},{80,96},{96,112},{112,0},{1... | collective-permute-start | bytes 393224 | tf_op jit(solution)/shard_map/output/ppermute | solution.py:30
  110.3 5.3 %collective-permute-start.13 = (bf16[512,128]{1,0:T(8,128)(2,1)S(1)}, bf16[512,128]{1,0:T(8,128)(2,1)S(1)}, u32[]{:S(2)}, u32[]{:S(2)}) collective-permute-start(bf16[512,128]{1,0:T(8,128)(2,1)S(1)} %attention.3.refs_0_), channel_id=1, source_target_pairs={{0,112},{16,0},{32,16},{48,32},{64,48},{80,64},{96,80},{112,96},{1... | collective-permute-start | bytes 393224 | tf_op jit(solution)/shard_map/output/ppermute | solution.py:30
  115.5 9.1 %collective-permute-start.14 = (bf16[512,128]{1,0:T(8,128)(2,1)S(1)}, bf16[512,128]{1,0:T(8,128)(2,1)S(1)}, u32[]{:S(2)}, u32[]{:S(2)}) collective-permute-start(bf16[512,128]{1,0:T(8,128)(2,1)S(1)} %collective-permute-done.12.refs_1_), channel_id=1, source_target_pairs={{0,16},{16,32},{32,48},{48,64},{64,80},{80,96},{96,112},{112,0},{1... | collective-permute-start | bytes 393224 | tf_op jit(solution)/shard_map/output/ppermute | solution.py:30
  117.6 7.1 %collective-permute-start.17 = (bf16[512,128]{1,0:T(8,128)(2,1)S(1)}, bf16[512,128]{1,0:T(8,128)(2,1)S(1)}, u32[]{:S(2)}, u32[]{:S(2)}) collective-permute-start(bf16[512,128]{1,0:T(8,128)(2,1)S(1)} %collective-permute-done.13.refs_7_), channel_id=1, source_target_pairs={{0,112},{16,0},{32,16},{48,32},{64,48},{80,64},{96,80},{112,96},{1... | collective-permute-start | bytes 393224 | tf_op jit(solution)/shard_map/output/ppermute | solution.py:30
  118.8 9.9 %collective-permute-start.16 = (bf16[512,128]{1,0:T(8,128)(2,1)S(1)}, bf16[512,128]{1,0:T(8,128)(2,1)S(1)}, u32[]{:S(2)}, u32[]{:S(2)}) collective-permute-start(bf16[512,128]{1,0:T(8,128)(2,1)S(1)} %attention.3.refs_0_), channel_id=1, source_target_pairs={{0,64},{16,80},{32,96},{48,112},{64,0},{80,16},{96,32},{112,48},{1... | collective-permute-start | bytes 393224 | tf_op jit(solution)/shard_map/output/ppermute | solution.py:30
  124.7 6.2 %collective-permute-start.15 = (bf16[512,128]{1,0:T(8,128)(2,1)S(1)}, bf16[512,128]{1,0:T(8,128)(2,1)S(1)}, u32[]{:S(2)}, u32[]{:S(2)}) collective-permute-start(bf16[512,128]{1,0:T(8,128)(2,1)S(1)} %collective-permute-done.14.refs_2_), channel_id=1, source_target_pairs={{0,16},{16,32},{32,48},{48,64},{64,80},{80,96},{96,112},{112,0},{1... | collective-permute-start | bytes 393224 | tf_op jit(solution)/shard_map/output/ppermute | solution.py:30
  124.7 6.5 %collective-permute-start.18 = (bf16[512,128]{1,0:T(8,128)(2,1)S(1)}, bf16[512,128]{1,0:T(8,128)(2,1)S(1)}, u32[]{:S(2)}, u32[]{:S(2)}) collective-permute-start(bf16[512,128]{1,0:T(8,128)(2,1)S(1)} %collective-permute-done.17.refs_6_), channel_id=1, source_target_pairs={{0,112},{16,0},{32,16},{48,32},{64,48},{80,64},{96,80},{112,96},{1... | collective-permute-start | bytes 393224 | tf_op jit(solution)/shard_map/output/ppermute | solution.py:30
  133.3 2.0 %collective-permute-start.19 = (bf16[512,512]{1,0:T(8,128)(2,1)S(1)}, bf16[512,512]{1,0:T(8,128)(2,1)S(1)}, u32[]{:S(2)}, u32[]{:S(2)}) collective-permute-start(bf16[512,512]{1,0:T(8,128)(2,1)S(1)} %get-tuple-element.107), channel_id=1, source_target_pairs={{0,8},{8,0},{1,9},{9,1},{2,10},{10,2},{3,11},{11,3},{4,12},{12,4},... | collective-permute-start | bytes 1572872 | tf_op jit(solution)/shard_map/output/ppermute | solution.py:30
  135.5 10.4 %copy-start.2 = (bf16[256,256]{1,0:T(8,128)(2,1)S(1)}, bf16[256,256]{1,0:T(8,128)(2,1)}, u32[]{:S(2)}) copy-start(bf16[256,256]{1,0:T(8,128)(2,1)} %hidden.1) | copy-start | bytes 393220
  135.5 10.4 %copy-start.3 = (bf16[256,256]{1,0:T(8,128)(2,1)S(1)}, bf16[256,256]{1,0:T(8,128)(2,1)}, u32[]{:S(2)}) copy-start(bf16[256,256]{1,0:T(8,128)(2,1)} %get-tuple-element.57) | copy-start | bytes 393220
  135.6 10.1 %collective-permute-start.20 = (bf16[512,256]{1,0:T(8,128)(2,1)S(1)}, bf16[512,256]{1,0:T(8,128)(2,1)S(1)}, u32[]{:S(2)}, u32[]{:S(2)}) collective-permute-start(bf16[512,256]{1,0:T(8,128)(2,1)S(1)} %fusion), channel_id=1, source_target_pairs={{0,128},{128,0},{1,129},{129,1},{2,130},{130,2},{3,131},{131,3},{4... | collective-permute-start | bytes 786440 | tf_op jit(solution)/shard_map/output/ppermute | solution.py:30
Sparse Core Ops, SparseCore 0:
  42.2 44.3 all-gather.1

commit v5 on v4

--- a/solution.py
+++ b/solution.py
@@ -46,13 +46,29 @@
     return pltpu.CompilerParams(vmem_limit_bytes=mib * MIB)
 
 
-FIRST = (3, 4, 5)
-SECOND = (6, 7, 0, 1, 2)
+FIRST = (4,)
+SECOND = (3, 5, 2, 6, 1, 7, 0)
 
 
 def variant_kernel(
-    pos, base, ids, hidden, embed, rows, onehot, variant, spots, block, sems
+    pos, base, ids, hidden, embed, w, rows, onehot, variant, share, spots, block, buffer, sems, share_sems
 ):
+    my_block = lax.axis_index("x_lo") * Y + lax.axis_index("y")
+    size, half = buffer.shape[1], buffer.shape[2] // X_HI
+    share_rows = pl.ds(pl.multiple_of(my_block * size, size), size)
+    copies = []
+    for k in range(Z):
+        for x in range(X_HI):
+            start = (x * Z + k) * half
+            copies.append(
+                pltpu.make_async_copy(
+                    w.at[share_rows, start : start + half],
+                    buffer.at[k, :, x * half : (x + 1) * half],
+                    share_sems.at[k, x],
+                )
+            )
+    for copy in copies:
+        copy.start()
     first = (lax.axis_index("x_lo") * Y + lax.axis_index("y")) * TOK
     vocab = embed.shape[0]
     spot = lax.broadcasted_iota(jnp.int32, (VAR, TOK), 0)
@@ -74,6 +90,10 @@
     rows[:TOK] = hidden[...]
     rows[TOK:] = changed_rows
     spots[...] = places
+    for copy in copies:
+        copy.wait()
+    share_copy = pltpu.make_async_copy(buffer, share, sems.at[2])
+    share_copy.start()
     first_copy = pltpu.make_async_copy(spots, onehot, sems.at[0])
     first_copy.start()
     contract = (((0,), (0,)), ((), ()))
@@ -85,10 +105,13 @@
     second_copy.start()
     first_copy.wait()
     second_copy.wait()
-
-
-def make_variant(pos, base, ids, hidden, embed):
+    share_copy.wait()
+
+
+def make_variant(pos, base, ids, hidden, embed, w):
     width = hidden.shape[1]
+    shape = (Z, w.shape[0] // BLOCKS, w.shape[1] // Z)
+    args = (pos, base, ids, hidden, embed, w)
     smem = pl.BlockSpec(memory_space=pltpu.SMEM)
     return pl.pallas_call(
         variant_kernel,
@@ -96,16 +119,19 @@
             jax.ShapeDtypeStruct((ROWS, width), bf16),
             pltpu.HBM((VAR, TOK), bf16),
             pltpu.HBM((TOK, width), bf16),
+            pltpu.HBM(shape, bf16),
         ),
-        in_specs=[smem, smem, smem, vmem(), vmem()],
-        out_specs=(vmem(), hbm(), hbm()),
+        in_specs=[smem, smem, smem, vmem(), vmem(), hbm()],
+        out_specs=(vmem(), hbm(), hbm(), hbm()),
         scratch_shapes=[
             pltpu.VMEM((VAR, TOK), bf16),
             pltpu.VMEM((TOK, width), bf16),
-            pltpu.SemaphoreType.DMA((2,)),
+            pltpu.VMEM(shape, bf16),
+            pltpu.SemaphoreType.DMA((3,)),
+            pltpu.SemaphoreType.DMA((Z, X_HI)),
         ],
         compiler_params=limit(4),
-    )(*(pltpu.with_memory_space_constraint(v, pltpu.HBM) for v in (pos, base, ids, hidden, embed)))
+    )(*(pltpu.with_memory_space_constraint(v, pltpu.HBM) for v in args))
 
 
 def column_copies(ks, w, send, own, sems):
@@ -127,73 +153,24 @@
     return copies
 
 
-def first_columns_kernel(w, send, own, sems):
-    copies = column_copies(FIRST, w, send, own, sems)
+def columns_kernel(ks, w, send, own, sems):
+    copies = column_copies(ks, w, send, own, sems)
     for copy in copies:
         copy.start()
     for copy in copies:
         copy.wait()
 
 
-def first_columns(w):
-    columns = jax.ShapeDtypeStruct((w.shape[0], len(FIRST) * X_HI * QKV), bf16)
-    return pl.pallas_call(
-        first_columns_kernel,
+def pick_columns(ks, w):
+    columns = jax.ShapeDtypeStruct((w.shape[0], len(ks) * X_HI * QKV), bf16)
+    return pl.pallas_call(
+        functools.partial(columns_kernel, ks),
         out_shape=(columns, columns),
         in_specs=[hbm()],
         out_specs=(vmem(), vmem()),
-        scratch_shapes=[pltpu.SemaphoreType.DMA((2, len(FIRST) * X_HI))],
-        compiler_params=limit(8),
+        scratch_shapes=[pltpu.SemaphoreType.DMA((2, len(ks) * X_HI))],
+        compiler_params=limit(12),
     )(pltpu.with_memory_space_constraint(w, pltpu.HBM))
-
-
-def second_columns_kernel(w, out_weight, send, own, share, buffer, sems, share_sems, out_sem):
-    my_block = lax.axis_index("x_lo") * Y + lax.axis_index("y")
-    size, width = buffer.shape[1], buffer.shape[2] // X_HI
-    share_copies = []
-    for k in range(Z):
-        for x in range(X_HI):
-            start = (x * Z + k) * width
-            share_copies.append(
-                pltpu.make_async_copy(
-                    out_weight.at[
-                        pl.ds(pl.multiple_of(my_block * size, size), size), start : start + width
-                    ],
-                    buffer.at[k, :, x * width : (x + 1) * width],
-                    share_sems.at[k, x],
-                )
-            )
-    copies = column_copies(SECOND, w, send, own, sems)
-    for copy in share_copies + copies:
-        copy.start()
-    for copy in share_copies:
-        copy.wait()
-    out_copy = pltpu.make_async_copy(buffer, share, out_sem)
-    out_copy.start()
-    for copy in copies:
-        copy.wait()
-    out_copy.wait()
-
-
-def second_columns(w, out_weight):
-    columns = jax.ShapeDtypeStruct((w.shape[0], len(SECOND) * X_HI * QKV), bf16)
-    shape = (Z, out_weight.shape[0] // BLOCKS, out_weight.shape[1] // Z)
-    return pl.pallas_call(
-        second_columns_kernel,
-        out_shape=(columns, columns, pltpu.HBM(shape, bf16)),
-        in_specs=[hbm(), hbm()],
-        out_specs=(vmem(), vmem(), hbm()),
-        scratch_shapes=[
-            pltpu.VMEM(shape, bf16),
-            pltpu.SemaphoreType.DMA((2, len(SECOND) * X_HI)),
-            pltpu.SemaphoreType.DMA((Z, X_HI)),
-            pltpu.SemaphoreType.DMA(()),
-        ],
-        compiler_params=limit(12),
-    )(
-        pltpu.with_memory_space_constraint(w, pltpu.HBM),
-        pltpu.with_memory_space_constraint(out_weight, pltpu.HBM),
-    )
 
 
 def two_rows(row, width):
@@ -233,31 +210,28 @@
         out[ROWS:, QKV:] = tail
 
     if ks == FIRST:
-        near_up, up, down, near_down, buffer, sems = outs
+        for xr, out in enumerate(outs):
+            out[:ROWS, :] = product(xr, 1)
+            out[ROWS:, :] = tail
+    else:
+        outs, buffer, sems = outs[:-2], outs[-2], outs[-1]
         copies = []
-        for i, near in enumerate((near_up, near_down)):
-            full(FIRST.index((3, 5)[i]) * X_HI, buffer.at[i])
-            copies.append(pltpu.make_async_copy(buffer.at[i], near, sems.at[i]))
+        for i, out in enumerate(outs):
+            full(i * X_HI, buffer.at[i])
+            copies.append(pltpu.make_async_copy(buffer.at[i], out, sems.at[i]))
             copies[i].start()
-        for xr, out in enumerate((up, down)):
-            out[:ROWS, :] = product(FIRST.index(Z // 2) * X_HI + xr, 1)
-            out[ROWS:, :] = tail
         for copy in copies:
             copy.wait()
-    else:
-        for i, out in enumerate(outs):
-            full(i * X_HI, out)
 
 
 def partials(ks, own, sis, gains, w_own, w_sis):
     half = jax.ShapeDtypeStruct((SUM_ROWS, QKV), bf16)
     full = jax.ShapeDtypeStruct((SUM_ROWS, X_HI * QKV), bf16)
     if ks == FIRST:
-        away = pltpu.HBM(full.shape, bf16)
-        shapes, specs = (away, half, half, away), (hbm(), vmem(), vmem(), hbm())
-        scratch = [pltpu.VMEM((2, *full.shape), bf16), pltpu.SemaphoreType.DMA((2,))]
+        shapes, specs, scratch = (half, half), (vmem(), vmem()), []
     else:
-        shapes, specs, scratch = (full,) * len(ks), (vmem(),) * len(ks), []
+        shapes, specs = (pltpu.HBM(full.shape, bf16),) * len(ks), (hbm(),) * len(ks)
+        scratch = [pltpu.VMEM((len(ks), *full.shape), bf16), pltpu.SemaphoreType.DMA((len(ks),))]
     return pl.pallas_call(
         functools.partial(partial_kernel, ks),
         out_shape=shapes,
@@ -531,32 +505,37 @@
     chip_slice = x_hi * Z + z
 
     with jax.named_scope("inputs"):
-        rows, onehot, variant = make_variant(var_pos, var_base, ref_ids, hidden, embed)
+        rows, onehot, variant, share = make_variant(
+            var_pos, var_base, ref_ids, hidden, embed, out_weight
+        )
         rows, qkv_weight = lax.optimization_barrier((rows, qkv_weight))
         rows_sis = shift(rows, "core", CORE, 1)
-        send_first, own_first = first_columns(qkv_weight)
+        send_first, own_first = pick_columns(FIRST, qkv_weight)
         sis_first = shift(send_first, "core", CORE, 1)
-        rows_sis, send_first, qkv_weight = lax.optimization_barrier((rows_sis, send_first, qkv_weight))
-        send_second, own_second, share = second_columns(qkv_weight, out_weight)
+        rows_sis, sis_first, qkv_weight, share = lax.optimization_barrier(
+            (rows_sis, sis_first, qkv_weight, share)
+        )
+        send_second, own_second = pick_columns(SECOND, qkv_weight)
         sis_second = shift(send_second, "core", CORE, 1)
         shared = lax.all_to_all(share, "z", 0, 0, tiled=True)
         start = chip_slice * 2 * width_part
         gains = lax.dynamic_slice(gain.reshape(1, full_width), (0, start), (1, 2 * width_part))
 
     with jax.named_scope("projection"):
-        near_up, up, down, near_down = partials(FIRST, rows, rows_sis, gains, own_first, sis_first)
-        up, down = shift(up, "z", Z, 1), shift(down, "z", Z, -1)
-        near_up = pltpu.with_memory_space_constraint(near_up, pltpu.HBM)
-        near_down = pltpu.with_memory_space_constraint(near_down, pltpu.HBM)
-        up, down, shared = lax.optimization_barrier((up, down, shared))
-        out_w = lax.all_gather(shared, CTX, axis=1, tiled=True)
-        up, down = ring_add(first_kernel, up, down, near_up, near_down)
-        up, rows, down = lax.optimization_barrier((up, rows, down))
+        sis_first = pltpu.with_memory_space_constraint(sis_first, pltpu.HBM)
+        up, down = partials(FIRST, rows, rows_sis, gains, own_first, sis_first)
         up, down = shift(up, "z", Z, 1), shift(down, "z", Z, -1)
         parts = partials(SECOND, rows, rows_sis, gains, own_second, sis_second)
-        up, down, parts = lax.optimization_barrier((up, down, parts))
+        near_up = pltpu.with_memory_space_constraint(parts[0], pltpu.HBM)
+        near_down = pltpu.with_memory_space_constraint(parts[1], pltpu.HBM)
+        up, down, shared, near_up = lax.optimization_barrier((up, down, shared, near_up))
+        out_w = lax.all_gather(shared, CTX, axis=1, tiled=True)
         parts = dict(zip(SECOND, parts))
-        up, down = ring_add(next_kernel, up, down, parts[2], parts[6])
+        up, down = ring_add(first_kernel, up, down, near_up, near_down)
+        up, down = shift(up, "z", Z, 1), shift(down, "z", Z, -1)
+        near_up = pltpu.with_memory_space_constraint(parts[2], pltpu.HBM)
+        near_down = pltpu.with_memory_space_constraint(parts[6], pltpu.HBM)
+        up, down = ring_add(next_kernel, up, down, near_up, near_down)
         up, down = shift(up, "z", Z, 1), shift(down, "z", Z, -1)
         up, down = ring_add(next_kernel, up, down, parts[1], parts[7])
         up, down = shift(up, "z", Z, 1), shift(down, "z", Z, -1)

time: 156 us -> 156 us (level)
  waiting for transfers between devices: 49.7 us -> 54.7 us
  starting transfers between devices: 43.8 us -> 39.7 us
    ppermute x21, waiting for transfers between devices: 44.7 us -> 54.7 us  [shift(): lax.ppermute(value, axis, [(i, (i + distance) % size) for i in range(size)])]
    all_to_all x1, waiting for transfers between devices: 4.9 us -> 0.01 us  [shards(): shared = lax.all_to_all(share, 'z', 0, 0, tiled=True)]
    ppermute x21, starting transfers between devices: 35.3 us -> 31.2 us  [shift(): lax.ppermute(value, axis, [(i, (i + distance) % size) for i in range(size)])]
  transfers between devices with their start and end apart: 23 -> 23, of which waited for: 13 -> 13; matrix products, arithmetic and copies ran while one was open for 1% -> 1% of each run, Pallas kernels for 12% -> 10%
where the time goes in v5:
time: 156 us; the launch traced here: 155 us
  waiting for transfers between devices  54.7 us (35%)
  starting transfers between devices  39.7 us (25%)
  Pallas kernels  25.8 us (17%)
  blocking collectives  17.6 us (11%)
  between operations  13.7 us (9%)
  other arithmetic  1.81 us (1%)
  local copies, waits for them, and re-layouts  1.57 us (1%)
    ppermute x21, waiting for transfers between devices, shift(): lax.ppermute(value, axis, [(i, (i + distance) % size) for i in range(size)])  54.7 us
    ppermute x21, starting transfers between devices, shift(): lax.ppermute(value, axis, [(i, (i + distance) % size) for i in range(size)])  31.2 us
    all_to_all x1, blocking collectives, shards(): blocks = lax.all_to_all(payload, CTX, 0, 0, tiled=True)  17.6 us
    all_to_all x1, starting transfers between devices, shards(): shared = lax.all_to_all(share, 'z', 0, 0, tiled=True)  8.48 us
    pallas_call x2, Pallas kernels, pick_columns(): pl.pallas_call(functools.partial(columns_kernel, ks), out_shape=(columns,...  5.78 us
    pallas_call x2, Pallas kernels, partials(): pl.pallas_call(functools.partial(partial_kernel, ks), out_shape=shapes, i...  5.78 us
  transfers between devices with their start and end apart: 23, of which 13 were waited for; matrix products, arithmetic and copies ran while one was open for 1% of the time, Pallas kernels for 10%

profile of v5, /device:TPU:6, one launch (start us, length us, event | category | flops | bytes accessed | tf_op | source)
XLA Modules:
  0.0 154.9 jit_solution(11373972050192045579)
XLA Ops:
  6.5 3.1 %inputs.3 = (bf16[272,256]{1,0:T(8,128)(2,1)S(1)}, bf16[16,256]{1,0:T(8,128)(2,1)}, bf16[256,256]{1,0:T(8,128)(2,1)}, bf16[8,16,1024]{2,1,0:T(8,128)(2,1)}) custom-call(s32[16]{0:T(128)} %pos.1, s32[16]{0:T(128)} %base.1, s32[256]{0:T(256)} %ids.1, bf16[256,256]{1,0:T(8,128)(2,1)} %hidden.1, bf16[512,256]{1,0:T(8,128)(2,1)} %embed.1, bf16[128,8192]{1,0:T(8,128)(2,1)} %w.1), custom_call_target="tpu_custom_call" | custom-call | tf_op jit(solution)/shard_map/inputs/pallas_call | solution.py:116
  9.7 1.3 inputs.4
  10.9 0.1 collective-permute-start.1
  11.0 0.5 collective-permute-start
  11.5 1.4 collective-permute-done.sis
  13.0 0.8 copy-done.4
  13.7 4.5 %inputs.5 = (bf16[256,5376]{1,0:T(8,128)(2,1)}, bf16[256,5376]{1,0:T(8,128)(2,1)S(1)}) custom-call(bf16[256,12288]{1,0:T(8,128)(2,1)} %w.3), custom_call_target="tpu_custom_call" | custom-call | tf_op jit(solution)/shard_map/inputs/pallas_call | solution.py:166
  18.2 0.2 collective-permute-start.4
  18.5 8.5 %all-to-all-start = ((bf16[8,16,1024]{2,1,0:T(8,128)(2,1)}), bf16[8,16,1024]{2,1,0:T(8,128)(2,1)}, u32[]{:S(2)}, u32[]{:S(2)}) async-start(bf16[8,16,1024]{2,1,0:T(8,128)(2,1)} %get-tuple-element.61), calls=%async_computation | async-start | bytes 524288 | tf_op jit(solution)/shard_map/inputs/all_to_all | solution.py:520
  26.9 0.0 all-gather.2.cloned.1.call-start
  27.0 0.8 dynamic-slice.3
  27.8 1.5 projection.6
  29.2 2.0 %collective-permute-start.2 = (bf16[288,384]{1,0:T(8,128)(2,1)S(1)}, bf16[288,384]{1,0:T(8,128)(2,1)S(1)}, u32[]{:S(2)}, u32[]{:S(2)}) collective-permute-start(bf16[288,384]{1,0:T(8,128)(2,1)S(1)} %get-tuple-element.59), channel_id=1, source_target_pairs={{0,16},{16,32},{32,48},{48,64},{64,80},{80,96},{96,112},{112,0},{1... | collective-permute-start | bytes 663560 | tf_op jit(solution)/shard_map/projection/ppermute | solution.py:30
  31.3 1.3 collective-permute-start.3
  32.6 0.0 collective-permute-done.4.w_sis
  32.6 4.3 %projection.7 = (bf16[288,768]{1,0:T(8,128)(2,1)}, bf16[288,768]{1,0:T(8,128)(2,1)}, bf16[288,768]{1,0:T(8,128)(2,1)}, bf16[288,768]{1,0:T(8,128)(2,1)}, bf16[28...) custom-call(bf16[272,256]{1,0:T(8,128)(2,1)S(1)} %get-tuple-element.52.own, ...), custom_call_target="tpu_custom_call" | custom-call | flops 1497366528 | bytes 11010048 | tf_op jit(solution)/shard_map/projection/pallas_call | solution.py:235
  36.9 4.5 %collective-permute-done.2.up = bf16[288,384]{1,0:T(8,128)(2,1)S(1)} collective-permute-done((bf16[288,384]{1,0:T(8,128)(2,1)S(1)}, bf16[288,384]{1,0:T(8,128)(2,1)S(1)}, u32[]{:S(2)}, u32[]{:S(2)}) %collective-permute-start.2) | collective-permute-done | bytes 221216 | tf_op jit(solution)/shard_map/projection/ppermute | solution.py:30
  41.4 0.0 all-gather.2.cloned.1.call-update
  41.4 1.3 projection.8
  42.7 0.0 copy-start.6
  42.7 0.3 collective-permute-start.5
  43.1 3.0 %collective-permute-start.6 = (bf16[288,768]{1,0:T(8,128)(2,1)S(1)}, bf16[288,768]{1,0:T(8,128)(2,1)S(1)}, u32[]{:S(2)}, u32[]{:S(2)}) collective-permute-start(bf16[288,768]{1,0:T(8,128)(2,1)S(1)} %get-tuple-element.71), channel_id=1, source_target_pairs={{0,112},{16,0},{32,16},{48,32},{64,48},{80,64},{96,80},{112,96},{1... | collective-permute-start | bytes 1327112 | tf_op jit(solution)/shard_map/projection/ppermute | solution.py:30
  46.1 9.3 %collective-permute-done.5.up = bf16[288,768]{1,0:T(8,128)(2,1)S(1)} collective-permute-done((bf16[288,768]{1,0:T(8,128)(2,1)S(1)}, bf16[288,768]{1,0:T(8,128)(2,1)S(1)}, u32[]{:S(2)}, u32[]{:S(2)}) %collective-permute-start.5) | collective-permute-done | bytes 442400 | tf_op jit(solution)/shard_map/projection/ppermute | solution.py:30
  55.3 0.0 collective-permute-done.6.down
  55.3 1.4 projection.9
  56.7 1.6 %collective-permute-start.7 = (bf16[288,768]{1,0:T(8,128)(2,1)S(1)}, bf16[288,768]{1,0:T(8,128)(2,1)S(1)}, u32[]{:S(2)}, u32[]{:S(2)}) collective-permute-start(bf16[288,768]{1,0:T(8,128)(2,1)S(1)} %get-tuple-element.74), channel_id=1, source_target_pairs={{0,16},{16,32},{32,48},{48,64},{64,80},{80,96},{96,112},{112,0},{1... | collective-permute-start | bytes 1327112 | tf_op jit(solution)/shard_map/projection/ppermute | solution.py:30
  58.4 1.7 %collective-permute-start.8 = (bf16[288,768]{1,0:T(8,128)(2,1)S(1)}, bf16[288,768]{1,0:T(8,128)(2,1)S(1)}, u32[]{:S(2)}, u32[]{:S(2)}) collective-permute-start(bf16[288,768]{1,0:T(8,128)(2,1)S(1)} %get-tuple-element.75), channel_id=1, source_target_pairs={{0,112},{16,0},{32,16},{48,32},{64,48},{80,64},{96,80},{112,96},{1... | collective-permute-start | bytes 1327112 | tf_op jit(solution)/shard_map/projection/ppermute | solution.py:30
  60.0 8.8 %collective-permute-done.7.up = bf16[288,768]{1,0:T(8,128)(2,1)S(1)} collective-permute-done((bf16[288,768]{1,0:T(8,128)(2,1)S(1)}, bf16[288,768]{1,0:T(8,128)(2,1)S(1)}, u32[]{:S(2)}, u32[]{:S(2)}) %collective-permute-start.7) | collective-permute-done | bytes 442400 | tf_op jit(solution)/shard_map/projection/ppermute | solution.py:30
  68.8 0.2 projection.10
  69.1 1.8 %collective-permute-start.9 = (bf16[288,768]{1,0:T(8,128)(2,1)S(1)}, bf16[288,768]{1,0:T(8,128)(2,1)S(1)}, u32[]{:S(2)}, u32[]{:S(2)}) collective-permute-start(bf16[288,768]{1,0:T(8,128)(2,1)S(1)} %get-tuple-element.78), channel_id=1, source_target_pairs={{0,16},{16,32},{32,48},{48,64},{64,80},{80,96},{96,112},{112,0},{1... | collective-permute-start | bytes 1327112 | tf_op jit(solution)/shard_map/projection/ppermute | solution.py:30
  70.9 1.5 collective-permute-start.10
  72.4 7.9 %collective-permute-done.9.up = bf16[288,768]{1,0:T(8,128)(2,1)S(1)} collective-permute-done((bf16[288,768]{1,0:T(8,128)(2,1)S(1)}, bf16[288,768]{1,0:T(8,128)(2,1)S(1)}, u32[]{:S(2)}, u32[]{:S(2)}) %collective-permute-start.9) | collective-permute-done | bytes 442400 | tf_op jit(solution)/shard_map/projection/ppermute | solution.py:30
  80.3 0.2 projection.11
  80.5 1.7 %collective-permute-start.11 = (bf16[288,384]{1,0:T(8,128)(2,1)S(1)}, bf16[288,384]{1,0:T(8,128)(2,1)S(1)}, u32[]{:S(2)}, u32[]{:S(2)}) collective-permute-start(bf16[288,384]{1,0:T(8,128)(2,1)S(1)} %get-tuple-element.82), channel_id=1, source_target_pairs={{0,128},{128,0},{1,129},{129,1},{2,130},{130,2},{3,131},{131,3},{4... | collective-permute-start | bytes 663560 | tf_op jit(solution)/shard_map/projection/ppermute | solution.py:30
  82.2 0.6 fusion.2
  82.7 0.1 pad_maximum_fusion
  82.9 5.3 %collective-permute-done.11.other = bf16[288,384]{1,0:T(8,128)(2,1)S(1)} collective-permute-done((bf16[288,384]{1,0:T(8,128)(2,1)S(1)}, bf16[288,384]{1,0:T(8,128)(2,1)S(1)}, u32[]{:S(2)}, u32[]{:S(2)}) %collective-permute-start.11) | collective-permute-done | bytes 221216 | tf_op jit(solution)/shard_map/projection/ppermute | solution.py:30
  88.2 1.3 attention.2
  89.5 17.6 %all_to_all.10.blocks = bf16[8,288,256]{2,1,0:T(8,128)(2,1)S(1)} all-to-all(bf16[8,288,256]{2,1,0:T(8,128)(2,1)S(1)} %get-tuple-element.85), channel_id=1, replica_groups=mesh['x_hi'=2,'z'=8,'core'=2,'x_lo'=2,'y'=4] {'x_lo','y'}, dimensions={0} | all-to-all | bytes 2359296 | tf_op jit(solution)/shard_map/attention/all_to_all | solution.py:556
  107.1 3.0 %attention.3.refs_0_ = bf16[512,128]{1,0:T(8,128)(2,1)S(1)} custom-call(bf16[512,128]{1,0:T(8,128)(2,1)S(1)} %get-tuple-element.84.queries, bf16[8,288,256]{2,1,0:T(8,128)(2,1)S(1)} %all_to_all.10.blocks), custom_call_target="tpu_custom_call" | custom-call | tf_op jit(solution)/shard_map/attention/pallas_call | solution.py:418
  110.1 0.0 all-gather.2.cloned.1.call-done.w
  110.1 1.5 collective-permute-start.12
  111.6 1.9 %collective-permute-start.13 = (bf16[512,128]{1,0:T(8,128)(2,1)S(1)}, bf16[512,128]{1,0:T(8,128)(2,1)S(1)}, u32[]{:S(2)}, u32[]{:S(2)}) collective-permute-start(bf16[512,128]{1,0:T(8,128)(2,1)S(1)} %attention.3.refs_0_), channel_id=1, source_target_pairs={{0,112},{16,0},{32,16},{48,32},{64,48},{80,64},{96,80},{112,96},{1... | collective-permute-start | bytes 393224 | tf_op jit(solution)/shard_map/output/ppermute | solution.py:30
  113.4 1.6 %output.2.turned = bf16[1024,1024]{1,0:T(8,128)(2,1)S(1)} custom-call(bf16[8,128,1024]{2,1,0:T(8,128)(2,1)} %all-gather.2.cloned.1.call-done.w), custom_call_target="tpu_custom_call" | custom-call | tf_op jit(solution)/shard_map/output/pallas_call | solution.py:450
  115.0 1.4 collective-permute-done.12.refs_1_
  116.4 1.0 collective-permute-done.13.refs_7_
  117.4 1.4 collective-permute-start.14
  118.8 2.2 %collective-permute-start.17 = (bf16[512,128]{1,0:T(8,128)(2,1)S(1)}, bf16[512,128]{1,0:T(8,128)(2,1)S(1)}, u32[]{:S(2)}, u32[]{:S(2)}) collective-permute-start(bf16[512,128]{1,0:T(8,128)(2,1)S(1)} %collective-permute-done.13.refs_7_), channel_id=1, source_target_pairs={{0,112},{16,0},{32,16},{48,32},{64,48},{80,64},{96,80},{112,96},{1... | collective-permute-start | bytes 393224 | tf_op jit(solution)/shard_map/output/ppermute | solution.py:30
  121.0 3.9 %collective-permute-start.16 = (bf16[512,128]{1,0:T(8,128)(2,1)S(1)}, bf16[512,128]{1,0:T(8,128)(2,1)S(1)}, u32[]{:S(2)}, u32[]{:S(2)}) collective-permute-start(bf16[512,128]{1,0:T(8,128)(2,1)S(1)} %attention.3.refs_0_), channel_id=1, source_target_pairs={{0,64},{16,80},{32,96},{48,112},{64,0},{80,16},{96,32},{112,48},{1... | collective-permute-start | bytes 393224 | tf_op jit(solution)/shard_map/output/ppermute | solution.py:30
  125.0 0.4 collective-permute-start.15
  125.4 0.4 collective-permute-done.17.refs_6_
  125.8 2.4 %collective-permute-start.18 = (bf16[512,128]{1,0:T(8,128)(2,1)S(1)}, bf16[512,128]{1,0:T(8,128)(2,1)S(1)}, u32[]{:S(2)}, u32[]{:S(2)}) collective-permute-start(bf16[512,128]{1,0:T(8,128)(2,1)S(1)} %collective-permute-done.17.refs_6_), channel_id=1, source_target_pairs={{0,112},{16,0},{32,16},{48,32},{64,48},{80,64},{96,80},{112,96},{1... | collective-permute-start | bytes 393224 | tf_op jit(solution)/shard_map/output/ppermute | solution.py:30
  128.2 3.2 %collective-permute-done.16.refs_4_ = bf16[512,128]{1,0:T(8,128)(2,1)S(1)} collective-permute-done((bf16[512,128]{1,0:T(8,128)(2,1)S(1)}, bf16[512,128]{1,0:T(8,128)(2,1)S(1)}, u32[]{:S(2)}, u32[]{:S(2)}) %collective-permute-start.16) | collective-permute-done | bytes 131104 | tf_op jit(solution)/shard_map/output/ppermute | solution.py:30
  131.5 1.3 collective-permute-done.15.refs_3_
  132.7 2.2 %output.3 = (f32[512,256]{1,0:T(8,128)S(1)}, bf16[512,512]{1,0:T(8,128)(2,1)S(1)}, f32[512,256]{1,0:T(8,128)S(1)}) custom-call(bf16[1024,1024]{1,0:T(8,128)(2,1)S(1)} %output.2.turned, bf16[512,128]{1,0:T(8,128)(2,1)S(1)} %attention.3.refs_0_, bf16[512,128]{1,0:T(8,128)(2,1)S(1)} %collective-permute-done.12.refs_1_, ...), custom_call_target="tpu_custom_call" | custom-call | tf_op jit(solution)/shard_map/output/pallas_call | solution.py:486
  134.9 0.0 copy-start.3
  134.9 0.1 collective-permute-start.19
  135.0 1.9 %collective-permute-done.19 = bf16[512,512]{1,0:T(8,128)(2,1)S(1)} collective-permute-done((bf16[512,512]{1,0:T(8,128)(2,1)S(1)}, bf16[512,512]{1,0:T(8,128)(2,1)S(1)}, u32[]{:S(2)}, u32[]{:S(2)}) %collective-permute-start.19) | collective-permute-done | bytes 524320 | tf_op jit(solution)/shard_map/output/ppermute | solution.py:30
  136.9 0.1 convert_element_type.32
  137.1 0.1 fusion
  137.2 1.6 %collective-permute-start.20 = (bf16[512,256]{1,0:T(8,128)(2,1)S(1)}, bf16[512,256]{1,0:T(8,128)(2,1)S(1)}, u32[]{:S(2)}, u32[]{:S(2)}) collective-permute-start(bf16[512,256]{1,0:T(8,128)(2,1)S(1)} %fusion), channel_id=1, source_target_pairs={{0,128},{128,0},{1,129},{129,1},{2,130},{130,2},{3,131},{131,3},{4... | collective-permute-start | bytes 786440 | tf_op jit(solution)/shard_map/output/ppermute | solution.py:30
  138.8 8.3 %collective-permute-done.20 = bf16[512,256]{1,0:T(8,128)(2,1)S(1)} collective-permute-done((bf16[512,256]{1,0:T(8,128)(2,1)S(1)}, bf16[512,256]{1,0:T(8,128)(2,1)S(1)}, u32[]{:S(2)}, u32[]{:S(2)}) %collective-permute-start.20) | collective-permute-done | bytes 262176 | tf_op jit(solution)/shard_map/output/ppermute | solution.py:30
  147.1 0.1 fusion.1
  147.3 0.8 add_convert_fusion
  (22 shorter events, 0.1 us)
Async XLA Ops:
  10.9 2.0 %collective-permute-start.1 = (bf16[256,768]{1,0:T(8,128)(2,1)S(1)}, bf16[256,768]{1,0:T(8,128)(2,1)S(1)}, u32[]{:S(2)}, u32[]{:S(2)}) collective-permute-start(bf16[256,768]{1,0:T(8,128)(2,1)S(1)} %get-tuple-element.54), channel_id=1, source_target_pairs={{0,8},{8,0},{1,9},{9,1},{2,10},{10,2},{3,11},{11,3},{4,12},{12,4},... | collective-permute-start | bytes 1179656 | tf_op jit(solution)/shard_map/inputs/ppermute | solution.py:30
  11.0 1.9 %collective-permute-start = (bf16[272,256]{1,0:T(8,128)(2,1)S(1)}, bf16[272,256]{1,0:T(8,128)(2,1)S(1)}, u32[]{:S(2)}, u32[]{:S(2)}) collective-permute-start(bf16[272,256]{1,0:T(8,128)(2,1)S(1)} %get-tuple-element.52.own), channel_id=1, source_target_pairs={{0,8},{8,0},{1,9},{9,1},{2,10},{10,2},{3,11},{11,3},{4,12},{12,4},... | collective-permute-start | bytes 417800 | tf_op jit(solution)/shard_map/inputs/ppermute | solution.py:30
  13.0 0.8 copy-start.4
  18.2 14.3 %collective-permute-start.4 = (bf16[256,5376]{1,0:T(8,128)(2,1)}, bf16[256,5376]{1,0:T(8,128)(2,1)}, u32[]{:S(2)}, u32[]{:S(2)}) collective-permute-start(bf16[256,5376]{1,0:T(8,128)(2,1)} %get-tuple-element.64), channel_id=1, source_target_pairs={{0,8},{8,0},{1,9},{9,1},{2,10},{10,2},{3,11},{11,3},{4,12},{12,4},... | collective-permute-start | bytes 8257544 | tf_op jit(solution)/shard_map/inputs/ppermute | solution.py:30
  18.5 22.9 %all-to-all-start = ((bf16[8,16,1024]{2,1,0:T(8,128)(2,1)}), bf16[8,16,1024]{2,1,0:T(8,128)(2,1)}, u32[]{:S(2)}, u32[]{:S(2)}) async-start(bf16[8,16,1024]{2,1,0:T(8,128)(2,1)} %get-tuple-element.61), calls=%async_computation | async-start | bytes 524288 | tf_op jit(solution)/shard_map/inputs/all_to_all | solution.py:520
  26.9 83.2 %all-gather.2.cloned.1.call-start = ((), (), s32[]{:S(2)}) async-start(), calls=%async_computation.2 | async-start | bytes 2359296 | tf_op jit(solution)/shard_map/projection/all_gather | solution.py:532
  29.2 12.2 %collective-permute-start.2 = (bf16[288,384]{1,0:T(8,128)(2,1)S(1)}, bf16[288,384]{1,0:T(8,128)(2,1)S(1)}, u32[]{:S(2)}, u32[]{:S(2)}) collective-permute-start(bf16[288,384]{1,0:T(8,128)(2,1)S(1)} %get-tuple-element.59), channel_id=1, source_target_pairs={{0,16},{16,32},{32,48},{48,64},{64,80},{80,96},{96,112},{112,0},{1... | collective-permute-start | bytes 663560 | tf_op jit(solution)/shard_map/projection/ppermute | solution.py:30
  31.3 10.1 %collective-permute-start.3 = (bf16[288,384]{1,0:T(8,128)(2,1)S(1)}, bf16[288,384]{1,0:T(8,128)(2,1)S(1)}, u32[]{:S(2)}, u32[]{:S(2)}) collective-permute-start(bf16[288,384]{1,0:T(8,128)(2,1)S(1)} %get-tuple-element.60), channel_id=1, source_target_pairs={{0,112},{16,0},{32,16},{48,32},{64,48},{80,64},{96,80},{112,96},{1... | collective-permute-start | bytes 663560 | tf_op jit(solution)/shard_map/projection/ppermute | solution.py:30
  36.9 31.9 %copy-start = (bf16[288,768]{1,0:T(8,128)(2,1)S(1)}, bf16[288,768]{1,0:T(8,128)(2,1)}, u32[]{:S(2)}) copy-start(bf16[288,768]{1,0:T(8,128)(2,1)} %get-tuple-element.76.near_up) | copy-start | bytes 1327108
  36.9 31.9 %copy-start.1 = (bf16[288,768]{1,0:T(8,128)(2,1)S(1)}, bf16[288,768]{1,0:T(8,128)(2,1)}, u32[]{:S(2)}) copy-start(bf16[288,768]{1,0:T(8,128)(2,1)} %get-tuple-element.77.near_down) | copy-start | bytes 1327108
  42.7 29.7 %copy-start.6 = (s32[16]{0:T(128)S(1)}, s32[16]{0:T(128)}, u32[]{:S(2)}) copy-start(s32[16]{0:T(128)} %pos.1) | copy-start | bytes 196
  42.7 37.6 %copy-start.2 = (bf16[288,768]{1,0:T(8,128)(2,1)S(1)}, bf16[288,768]{1,0:T(8,128)(2,1)}, u32[]{:S(2)}) copy-start(bf16[288,768]{1,0:T(8,128)(2,1)} %get-tuple-element.80.near) | copy-start | bytes 1327108
  42.7 12.6 %collective-permute-start.5 = (bf16[288,768]{1,0:T(8,128)(2,1)S(1)}, bf16[288,768]{1,0:T(8,128)(2,1)S(1)}, u32[]{:S(2)}, u32[]{:S(2)}) collective-permute-start(bf16[288,768]{1,0:T(8,128)(2,1)S(1)} %get-tuple-element.70), channel_id=1, source_target_pairs={{0,16},{16,32},{32,48},{48,64},{64,80},{80,96},{96,112},{112,0},{1... | collective-permute-start | bytes 1327112 | tf_op jit(solution)/shard_map/projection/ppermute | solution.py:30
  43.1 12.3 %collective-permute-start.6 = (bf16[288,768]{1,0:T(8,128)(2,1)S(1)}, bf16[288,768]{1,0:T(8,128)(2,1)S(1)}, u32[]{:S(2)}, u32[]{:S(2)}) collective-permute-start(bf16[288,768]{1,0:T(8,128)(2,1)S(1)} %get-tuple-element.71), channel_id=1, source_target_pairs={{0,112},{16,0},{32,16},{48,32},{64,48},{80,64},{96,80},{112,96},{1... | collective-permute-start | bytes 1327112 | tf_op jit(solution)/shard_map/projection/ppermute | solution.py:30
  56.7 12.1 %collective-permute-start.7 = (bf16[288,768]{1,0:T(8,128)(2,1)S(1)}, bf16[288,768]{1,0:T(8,128)(2,1)S(1)}, u32[]{:S(2)}, u32[]{:S(2)}) collective-permute-start(bf16[288,768]{1,0:T(8,128)(2,1)S(1)} %get-tuple-element.74), channel_id=1, source_target_pairs={{0,16},{16,32},{32,48},{48,64},{64,80},{80,96},{96,112},{112,0},{1... | collective-permute-start | bytes 1327112 | tf_op jit(solution)/shard_map/projection/ppermute | solution.py:30
  58.4 10.5 %collective-permute-start.8 = (bf16[288,768]{1,0:T(8,128)(2,1)S(1)}, bf16[288,768]{1,0:T(8,128)(2,1)S(1)}, u32[]{:S(2)}, u32[]{:S(2)}) collective-permute-start(bf16[288,768]{1,0:T(8,128)(2,1)S(1)} %get-tuple-element.75), channel_id=1, source_target_pairs={{0,112},{16,0},{32,16},{48,32},{64,48},{80,64},{96,80},{112,96},{1... | collective-permute-start | bytes 1327112 | tf_op jit(solution)/shard_map/projection/ppermute | solution.py:30
  69.1 11.3 %collective-permute-start.9 = (bf16[288,768]{1,0:T(8,128)(2,1)S(1)}, bf16[288,768]{1,0:T(8,128)(2,1)S(1)}, u32[]{:S(2)}, u32[]{:S(2)}) collective-permute-start(bf16[288,768]{1,0:T(8,128)(2,1)S(1)} %get-tuple-element.78), channel_id=1, source_target_pairs={{0,16},{16,32},{32,48},{48,64},{64,80},{80,96},{96,112},{112,0},{1... | collective-permute-start | bytes 1327112 | tf_op jit(solution)/shard_map/projection/ppermute | solution.py:30
  70.9 9.4 %collective-permute-start.10 = (bf16[288,768]{1,0:T(8,128)(2,1)S(1)}, bf16[288,768]{1,0:T(8,128)(2,1)S(1)}, u32[]{:S(2)}, u32[]{:S(2)}) collective-permute-start(bf16[288,768]{1,0:T(8,128)(2,1)S(1)} %get-tuple-element.79), channel_id=1, source_target_pairs={{0,112},{16,0},{32,16},{48,32},{64,48},{80,64},{96,80},{112,96},{1... | collective-permute-start | bytes 1327112 | tf_op jit(solution)/shard_map/projection/ppermute | solution.py:30
  80.5 7.7 %collective-permute-start.11 = (bf16[288,384]{1,0:T(8,128)(2,1)S(1)}, bf16[288,384]{1,0:T(8,128)(2,1)S(1)}, u32[]{:S(2)}, u32[]{:S(2)}) collective-permute-start(bf16[288,384]{1,0:T(8,128)(2,1)S(1)} %get-tuple-element.82), channel_id=1, source_target_pairs={{0,128},{128,0},{1,129},{129,1},{2,130},{130,2},{3,131},{131,3},{4... | collective-permute-start | bytes 663560 | tf_op jit(solution)/shard_map/projection/ppermute | solution.py:30
  110.1 6.3 %collective-permute-start.12 = (bf16[512,128]{1,0:T(8,128)(2,1)S(1)}, bf16[512,128]{1,0:T(8,128)(2,1)S(1)}, u32[]{:S(2)}, u32[]{:S(2)}) collective-permute-start(bf16[512,128]{1,0:T(8,128)(2,1)S(1)} %attention.3.refs_0_), channel_id=1, source_target_pairs={{0,16},{16,32},{32,48},{48,64},{64,80},{80,96},{96,112},{112,0},{1... | collective-permute-start | bytes 393224 | tf_op jit(solution)/shard_map/output/ppermute | solution.py:30
  111.6 5.8 %collective-permute-start.13 = (bf16[512,128]{1,0:T(8,128)(2,1)S(1)}, bf16[512,128]{1,0:T(8,128)(2,1)S(1)}, u32[]{:S(2)}, u32[]{:S(2)}) collective-permute-start(bf16[512,128]{1,0:T(8,128)(2,1)S(1)} %attention.3.refs_0_), channel_id=1, source_target_pairs={{0,112},{16,0},{32,16},{48,32},{64,48},{80,64},{96,80},{112,96},{1... | collective-permute-start | bytes 393224 | tf_op jit(solution)/shard_map/output/ppermute | solution.py:30
  117.4 7.6 %collective-permute-start.14 = (bf16[512,128]{1,0:T(8,128)(2,1)S(1)}, bf16[512,128]{1,0:T(8,128)(2,1)S(1)}, u32[]{:S(2)}, u32[]{:S(2)}) collective-permute-start(bf16[512,128]{1,0:T(8,128)(2,1)S(1)} %collective-permute-done.12.refs_1_), channel_id=1, source_target_pairs={{0,16},{16,32},{32,48},{48,64},{64,80},{80,96},{96,112},{112,0},{1... | collective-permute-start | bytes 393224 | tf_op jit(solution)/shard_map/output/ppermute | solution.py:30
  118.8 7.1 %collective-permute-start.17 = (bf16[512,128]{1,0:T(8,128)(2,1)S(1)}, bf16[512,128]{1,0:T(8,128)(2,1)S(1)}, u32[]{:S(2)}, u32[]{:S(2)}) collective-permute-start(bf16[512,128]{1,0:T(8,128)(2,1)S(1)} %collective-permute-done.13.refs_7_), channel_id=1, source_target_pairs={{0,112},{16,0},{32,16},{48,32},{64,48},{80,64},{96,80},{112,96},{1... | collective-permute-start | bytes 393224 | tf_op jit(solution)/shard_map/output/ppermute | solution.py:30
  121.0 10.4 %collective-permute-start.16 = (bf16[512,128]{1,0:T(8,128)(2,1)S(1)}, bf16[512,128]{1,0:T(8,128)(2,1)S(1)}, u32[]{:S(2)}, u32[]{:S(2)}) collective-permute-start(bf16[512,128]{1,0:T(8,128)(2,1)S(1)} %attention.3.refs_0_), channel_id=1, source_target_pairs={{0,64},{16,80},{32,96},{48,112},{64,0},{80,16},{96,32},{112,48},{1... | collective-permute-start | bytes 393224 | tf_op jit(solution)/shard_map/output/ppermute | solution.py:30
  125.0 7.7 %collective-permute-start.15 = (bf16[512,128]{1,0:T(8,128)(2,1)S(1)}, bf16[512,128]{1,0:T(8,128)(2,1)S(1)}, u32[]{:S(2)}, u32[]{:S(2)}) collective-permute-start(bf16[512,128]{1,0:T(8,128)(2,1)S(1)} %collective-permute-done.14.refs_2_), channel_id=1, source_target_pairs={{0,16},{16,32},{32,48},{48,64},{64,80},{80,96},{96,112},{112,0},{1... | collective-permute-start | bytes 393224 | tf_op jit(solution)/shard_map/output/ppermute | solution.py:30
  125.8 6.9 %collective-permute-start.18 = (bf16[512,128]{1,0:T(8,128)(2,1)S(1)}, bf16[512,128]{1,0:T(8,128)(2,1)S(1)}, u32[]{:S(2)}, u32[]{:S(2)}) collective-permute-start(bf16[512,128]{1,0:T(8,128)(2,1)S(1)} %collective-permute-done.17.refs_6_), channel_id=1, source_target_pairs={{0,112},{16,0},{32,16},{48,32},{64,48},{80,64},{96,80},{112,96},{1... | collective-permute-start | bytes 393224 | tf_op jit(solution)/shard_map/output/ppermute | solution.py:30
  134.9 12.3 %copy-start.3 = (bf16[256,256]{1,0:T(8,128)(2,1)S(1)}, bf16[256,256]{1,0:T(8,128)(2,1)}, u32[]{:S(2)}) copy-start(bf16[256,256]{1,0:T(8,128)(2,1)} %hidden.1) | copy-start | bytes 393220
  134.9 12.3 %copy-start.5 = (bf16[256,256]{1,0:T(8,128)(2,1)S(1)}, bf16[256,256]{1,0:T(8,128)(2,1)}, u32[]{:S(2)}) copy-start(bf16[256,256]{1,0:T(8,128)(2,1)} %get-tuple-element.50) | copy-start | bytes 393220
  134.9 2.0 %collective-permute-start.19 = (bf16[512,512]{1,0:T(8,128)(2,1)S(1)}, bf16[512,512]{1,0:T(8,128)(2,1)S(1)}, u32[]{:S(2)}, u32[]{:S(2)}) collective-permute-start(bf16[512,512]{1,0:T(8,128)(2,1)S(1)} %get-tuple-element.93), channel_id=1, source_target_pairs={{0,8},{8,0},{1,9},{9,1},{2,10},{10,2},{3,11},{11,3},{4,12},{12,4},... | collective-permute-start | bytes 1572872 | tf_op jit(solution)/shard_map/output/ppermute | solution.py:30
  137.2 9.9 %collective-permute-start.20 = (bf16[512,256]{1,0:T(8,128)(2,1)S(1)}, bf16[512,256]{1,0:T(8,128)(2,1)S(1)}, u32[]{:S(2)}, u32[]{:S(2)}) collective-permute-start(bf16[512,256]{1,0:T(8,128)(2,1)S(1)} %fusion), channel_id=1, source_target_pairs={{0,128},{128,0},{1,129},{129,1},{2,130},{130,2},{3,131},{131,3},{4... | collective-permute-start | bytes 786440 | tf_op jit(solution)/shard_map/output/ppermute | solution.py:30
Sparse Core Ops, SparseCore 0:
  41.5 43.0 all-gather.1

commit v6 on v5

--- a/solution.py
+++ b/solution.py
@@ -28,6 +28,13 @@
 
 def shift(value, axis, size, distance):
     return lax.ppermute(value, axis, [(i, (i + distance) % size) for i in range(size)])
+
+
+def shift_diagonal(value, distance):
+    route = [
+        (x * Z + z, (1 - x) * Z + (z + distance) % Z) for x in range(X_HI) for z in range(Z)
+    ]
+    return lax.ppermute(value, ("x_hi", "z"), route)
 
 
 def vmem():
@@ -216,10 +223,16 @@
     else:
         outs, buffer, sems = outs[:-2], outs[-2], outs[-1]
         copies = []
-        for i, out in enumerate(outs):
+        last = len(ks) - 1
+        for i in range(last):
             full(i * X_HI, buffer.at[i])
-            copies.append(pltpu.make_async_copy(buffer.at[i], out, sems.at[i]))
+            copies.append(pltpu.make_async_copy(buffer.at[i], outs[i], sems.at[i]))
             copies[i].start()
+        full(last * X_HI, buffer.at[last])
+        for xr in range(X_HI):
+            half = buffer.at[last, :, xr * QKV : (xr + 1) * QKV]
+            copies.append(pltpu.make_async_copy(half, outs[last + xr], sems.at[last + xr]))
+            copies[last + xr].start()
         for copy in copies:
             copy.wait()
 
@@ -230,8 +243,12 @@
     if ks == FIRST:
         shapes, specs, scratch = (half, half), (vmem(), vmem()), []
     else:
-        shapes, specs = (pltpu.HBM(full.shape, bf16),) * len(ks), (hbm(),) * len(ks)
-        scratch = [pltpu.VMEM((len(ks), *full.shape), bf16), pltpu.SemaphoreType.DMA((len(ks),))]
+        shapes = (pltpu.HBM(full.shape, bf16),) * (len(ks) - 1) + (pltpu.HBM(half.shape, bf16),) * 2
+        specs = (hbm(),) * (len(ks) + 1)
+        scratch = [
+            pltpu.VMEM((len(ks), *full.shape), bf16),
+            pltpu.SemaphoreType.DMA((len(ks) + 1,)),
+        ]
     return pl.pallas_call(
         functools.partial(partial_kernel, ks),
         out_shape=shapes,
@@ -277,39 +294,37 @@
     )(up, down, near_up, near_down)
 
 
-def last_kernel(up, down, near, mine, other):
+def split_kernel(up, down, near_up, near_down, up_own, up_far, down_own, down_far):
     own, far = slice(0, QKV), slice(QKV, 2 * QKV)
-    terms = [up, down, near]
-    mine[:ROWS] = sum(term[:ROWS, own].astype(f32) for term in terms)
-    row = sum(one_row(term[ROWS:, own]) for term in terms)
-    mine[ROWS:] = jnp.broadcast_to(row, (8, QKV))
-    store_sum(other, slice(0, QKV), [term[:, far] for term in terms])
-
-
-def ring_last(up, down, near):
-    return pl.pallas_call(
-        last_kernel,
-        out_shape=(
-            jax.ShapeDtypeStruct((ROWS + 8, QKV), f32),
-            jax.ShapeDtypeStruct((SUM_ROWS, QKV), bf16),
-        ),
-        in_specs=[vmem()] * 3,
-        out_specs=(vmem(), vmem()),
+    every = slice(0, QKV)
+    store_sum(up_own, every, [up[:, own], near_up[:, own]])
+    store_sum(up_far, every, [up[:, far], near_up[:, far]])
+    store_sum(down_own, every, [down[:, own], near_down[:, own]])
+    store_sum(down_far, every, [down[:, far], near_down[:, far]])
+
+
+def ring_split(up, down, near_up, near_down):
+    return pl.pallas_call(
+        split_kernel,
+        out_shape=(jax.ShapeDtypeStruct((SUM_ROWS, QKV), bf16),) * 4,
+        in_specs=[vmem()] * 4,
+        out_specs=(vmem(),) * 4,
         compiler_params=limit(8),
-    )(up, down, near)
+    )(up, down, near_up, near_down)
 
 
 def rotated(x, cosine, sine):
     return x * cosine + pltpu.roll(x, HD // 2, 1) * sine
 
 
-def finish_kernel(full_width, mine, other, cosine, sine, onehot, payload, queries):
-    row = mine[ROWS : ROWS + 1, :] + one_row(other[ROWS:, :])
+def finish_kernel(full_width, *refs):
+    terms, (cosine, sine, onehot, payload, queries) = refs[:6], refs[6:]
+    row = sum(one_row(t[ROWS:]) for t in terms)
     line = lax.broadcasted_iota(jnp.int32, (ROWS, QKV), 0)
     lane = lax.broadcasted_iota(jnp.int32, (ROWS, QKV), 1)
     squares = jnp.sum(jnp.where(line == lane, row, 0.0), axis=1, keepdims=True)
     inv_rms = lax.rsqrt(squares / full_width + epsilon)
-    proj = (mine[:ROWS, :] + other[:ROWS, :].astype(f32)) * inv_rms
+    proj = sum(t[:ROWS].astype(f32) for t in terms) * inv_rms
     query = rotated(proj[:, :HD], cosine[...], sine[...]).astype(bf16)
     key = rotated(proj[:, HD : 2 * HD], cosine[...], sine[...]).astype(bf16)
     value = proj[:, 2 * HD :].astype(bf16)
@@ -331,17 +346,17 @@
     queries[TOK:] = jnp.where(changed > 0.5, placed, base.astype(f32)).astype(bf16)
 
 
-def finish(full_width, mine, other, cosine, sine, onehot):
+def finish(full_width, terms, cosine, sine, onehot):
     return pl.pallas_call(
         functools.partial(finish_kernel, full_width),
         out_shape=(
             jax.ShapeDtypeStruct((BLOCKS, PAY, 2 * HD), bf16),
             jax.ShapeDtypeStruct((2 * TOK, HD), bf16),
         ),
-        in_specs=[vmem()] * 5,
+        in_specs=[vmem()] * 9,
         out_specs=(vmem(), vmem()),
         compiler_params=limit(12),
-    )(mine, other, cosine, sine, pltpu.with_memory_space_constraint(onehot, pltpu.HBM))
+    )(*terms, cosine, sine, pltpu.with_memory_space_constraint(onehot, pltpu.HBM))
 
 
 def attend_kernel(queries, blocks, out, scores, peak, denom, total, var_kv, spots):
@@ -530,6 +545,8 @@
         near_down = pltpu.with_memory_space_constraint(parts[1], pltpu.HBM)
         up, down, shared, near_up = lax.optimization_barrier((up, down, shared, near_up))
         out_w = lax.all_gather(shared, CTX, axis=1, tiled=True)
+        own_term, far_term = parts[-2:]
+        far_term = shift(far_term, "x_hi", X_HI, 1)
         parts = dict(zip(SECOND, parts))
         up, down = ring_add(first_kernel, up, down, near_up, near_down)
         up, down = shift(up, "z", Z, 1), shift(down, "z", Z, -1)
@@ -537,10 +554,11 @@
         near_down = pltpu.with_memory_space_constraint(parts[6], pltpu.HBM)
         up, down = ring_add(next_kernel, up, down, near_up, near_down)
         up, down = shift(up, "z", Z, 1), shift(down, "z", Z, -1)
-        up, down = ring_add(next_kernel, up, down, parts[1], parts[7])
+        up, down, far_term = lax.optimization_barrier((up, down, far_term))
+        up, up_far, down, down_far = ring_split(up, down, parts[1], parts[7])
         up, down = shift(up, "z", Z, 1), shift(down, "z", Z, -1)
-        mine, other = ring_last(up, down, parts[0])
-        other = shift(other, "x_hi", X_HI, 1)
+        up_far, down_far = shift_diagonal(up_far, 1), shift_diagonal(down_far, -1)
+        terms = (up, down, up_far, down_far, own_term, far_term)
 
     with jax.named_scope("tables"):
         positions = jnp.concatenate([my_block * tok_rows + jnp.arange(tok_rows), var_pos])
@@ -552,7 +570,7 @@
         sine = jnp.concatenate([-sine, sine], axis=1)
 
     with jax.named_scope("attention"):
-        payload, queries = finish(full_width, mine, other, cosine, sine, onehot)
+        payload, queries = finish(full_width, terms, cosine, sine, onehot)
         blocks = lax.all_to_all(payload, CTX, 0, 0, tiled=True)
         attn = attend(queries, blocks)
         attn, out_w = lax.optimization_barrier((attn, out_w))

time: 156 us -> 158 us (1.013); the launches traced: 155 us -> 155 us
  waiting for transfers between devices: 54.7 us -> 49.8 us
  starting transfers between devices: 39.7 us -> 44.5 us
    ppermute x21, waiting for transfers between devices: 54.7 us -> 44.3 us  [shift(): lax.ppermute(value, axis, [(i, (i + distance) % size) for i in range(size)])]
    ppermute x0 -> x2, starting transfers between devices: none -> 5.64 us  [shift_diagonal(): return lax.ppermute(value, ('x_hi', 'z'), route)]
    ppermute x0 -> x2, waiting for transfers between devices: none -> 5.42 us  [shift_diagonal(): return lax.ppermute(value, ('x_hi', 'z'), route)]
  transfers between devices with their start and end apart: 23 -> 25, of which waited for: 13 -> 12; matrix products, arithmetic and copies ran while one was open for 1% -> 1% of each run, Pallas kernels for 10% -> 10%
where the time goes in v6:
time: 158 us; the launch traced here: 155 us
  waiting for transfers between devices  49.8 us (32%)
  starting transfers between devices  44.5 us (28%)
  Pallas kernels  25.8 us (16%)
  blocking collectives  17.7 us (11%)
  between operations  13.7 us (9%)
  other arithmetic  1.81 us (1%)
    ppermute x21, waiting for transfers between devices, shift(): lax.ppermute(value, axis, [(i, (i + distance) % size) for i in range(size)])  44.3 us
    ppermute x21, starting transfers between devices, shift(): lax.ppermute(value, axis, [(i, (i + distance) % size) for i in range(size)])  30.3 us
    all_to_all x1, blocking collectives, shards(): blocks = lax.all_to_all(payload, CTX, 0, 0, tiled=True)  17.7 us
    all_to_all x1, starting transfers between devices, shards(): shared = lax.all_to_all(share, 'z', 0, 0, tiled=True)  8.48 us
    pallas_call x2, Pallas kernels, partials(): pl.pallas_call(functools.partial(partial_kernel, ks), out_shape=shapes, i...  5.78 us
    pallas_call x2, Pallas kernels, pick_columns(): pl.pallas_call(functools.partial(columns_kernel, ks), out_shape=(columns,...  5.78 us
    ppermute x2, starting transfers between devices, shift_diagonal(): return lax.ppermute(value, ('x_hi', 'z'), route)  5.64 us
    ppermute x2, waiting for transfers between devices, shift_diagonal(): return lax.ppermute(value, ('x_hi', 'z'), route)  5.42 us
  transfers between devices with their start and end apart: 25, of which 12 were waited for; matrix products, arithmetic and copies ran while one was open for 1% of the time, Pallas kernels for 10%

profile of v6, /device:TPU:6, one launch (start us, length us, event | category | flops | bytes accessed | tf_op | source)
XLA Modules:
  0.0 154.7 jit_solution(1182351070614888403)
XLA Ops:
  6.5 3.1 %inputs.3 = (bf16[272,256]{1,0:T(8,128)(2,1)S(1)}, bf16[16,256]{1,0:T(8,128)(2,1)}, bf16[256,256]{1,0:T(8,128)(2,1)}, bf16[8,16,1024]{2,1,0:T(8,128)(2,1)}) custom-call(s32[16]{0:T(128)} %pos.1, s32[16]{0:T(128)} %base.1, s32[256]{0:T(256)} %ids.1, bf16[256,256]{1,0:T(8,128)(2,1)} %hidden.1, bf16[512,256]{1,0:T(8,128)(2,1)} %embed.1, bf16[128,8192]{1,0:T(8,128)(2,1)} %w.1), custom_call_target="tpu_custom_call" | custom-call | tf_op jit(solution)/shard_map/inputs/pallas_call | solution.py:123
  9.6 1.3 inputs.4
  10.9 0.1 collective-permute-start.1
  11.0 0.5 collective-permute-start
  11.5 1.4 collective-permute-done.sis
  12.9 0.0 collective-permute-done.1.w_sis
  12.9 0.8 copy-done.4
  13.7 4.5 %inputs.5 = (bf16[256,5376]{1,0:T(8,128)(2,1)}, bf16[256,5376]{1,0:T(8,128)(2,1)S(1)}) custom-call(bf16[256,12288]{1,0:T(8,128)(2,1)} %w.3), custom_call_target="tpu_custom_call" | custom-call | tf_op jit(solution)/shard_map/inputs/pallas_call | solution.py:173
  18.2 0.2 collective-permute-start.4
  18.4 8.5 %all-to-all-start = ((bf16[8,16,1024]{2,1,0:T(8,128)(2,1)}), bf16[8,16,1024]{2,1,0:T(8,128)(2,1)}, u32[]{:S(2)}, u32[]{:S(2)}) async-start(bf16[8,16,1024]{2,1,0:T(8,128)(2,1)} %get-tuple-element.65), calls=%async_computation | async-start | bytes 524288 | tf_op jit(solution)/shard_map/inputs/all_to_all | solution.py:535
  26.9 0.0 all-gather.2.cloned.1.call-start
  27.0 0.8 dynamic-slice.3
  27.7 1.5 projection.5
  29.2 2.0 %collective-permute-start.2 = (bf16[288,384]{1,0:T(8,128)(2,1)S(1)}, bf16[288,384]{1,0:T(8,128)(2,1)S(1)}, u32[]{:S(2)}, u32[]{:S(2)}) collective-permute-start(bf16[288,384]{1,0:T(8,128)(2,1)S(1)} %get-tuple-element.63), channel_id=1, source_target_pairs={{0,16},{16,32},{32,48},{48,64},{64,80},{80,96},{96,112},{112,0},{1... | collective-permute-start | bytes 663560 | tf_op jit(solution)/shard_map/projection/ppermute | solution.py:30
  31.2 1.3 collective-permute-start.3
  32.5 0.0 collective-permute-done.4.w_sis
  32.5 4.3 %projection.6 = (bf16[288,768]{1,0:T(8,128)(2,1)}, bf16[288,768]{1,0:T(8,128)(2,1)}, bf16[288,768]{1,0:T(8,128)(2,1)}, bf16[288,768]{1,0:T(8,128)(2,1)}, bf16[28...) custom-call(bf16[272,256]{1,0:T(8,128)(2,1)S(1)} %get-tuple-element.56.own, ...), custom_call_target="tpu_custom_call" | custom-call | flops 1497366528 | bytes 11010048 | tf_op jit(solution)/shard_map/projection/pallas_call | solution.py:252
  36.9 0.0 copy-start.6
  36.9 4.4 %collective-permute-done.2.up = bf16[288,384]{1,0:T(8,128)(2,1)S(1)} collective-permute-done((bf16[288,384]{1,0:T(8,128)(2,1)S(1)}, bf16[288,384]{1,0:T(8,128)(2,1)S(1)}, u32[]{:S(2)}, u32[]{:S(2)}) %collective-permute-start.2) | collective-permute-done | bytes 221216 | tf_op jit(solution)/shard_map/projection/ppermute | solution.py:30
  41.4 0.0 collective-permute-done.3.down
  41.4 0.0 all-to-all-done
  41.4 0.0 all-gather.2.cloned.1.call-update
  41.4 1.3 projection.7
  42.7 0.3 collective-permute-start.5
  43.0 3.0 %collective-permute-start.6 = (bf16[288,768]{1,0:T(8,128)(2,1)S(1)}, bf16[288,768]{1,0:T(8,128)(2,1)S(1)}, u32[]{:S(2)}, u32[]{:S(2)}) collective-permute-start(bf16[288,768]{1,0:T(8,128)(2,1)S(1)} %get-tuple-element.75), channel_id=1, source_target_pairs={{0,112},{16,0},{32,16},{48,32},{64,48},{80,64},{96,80},{112,96},{1... | collective-permute-start | bytes 1327112 | tf_op jit(solution)/shard_map/projection/ppermute | solution.py:30
  46.0 9.3 %collective-permute-done.5.up = bf16[288,768]{1,0:T(8,128)(2,1)S(1)} collective-permute-done((bf16[288,768]{1,0:T(8,128)(2,1)S(1)}, bf16[288,768]{1,0:T(8,128)(2,1)S(1)}, u32[]{:S(2)}, u32[]{:S(2)}) %collective-permute-start.5) | collective-permute-done | bytes 442400 | tf_op jit(solution)/shard_map/projection/ppermute | solution.py:30
  55.3 0.0 collective-permute-done.6.down
  55.3 1.5 projection.8
  56.8 1.6 %collective-permute-start.7 = (bf16[288,768]{1,0:T(8,128)(2,1)S(1)}, bf16[288,768]{1,0:T(8,128)(2,1)S(1)}, u32[]{:S(2)}, u32[]{:S(2)}) collective-permute-start(bf16[288,768]{1,0:T(8,128)(2,1)S(1)} %get-tuple-element.78), channel_id=1, source_target_pairs={{0,16},{16,32},{32,48},{48,64},{64,80},{80,96},{96,112},{112,0},{1... | collective-permute-start | bytes 1327112 | tf_op jit(solution)/shard_map/projection/ppermute | solution.py:30
  58.4 1.7 %collective-permute-start.8 = (bf16[288,768]{1,0:T(8,128)(2,1)S(1)}, bf16[288,768]{1,0:T(8,128)(2,1)S(1)}, u32[]{:S(2)}, u32[]{:S(2)}) collective-permute-start(bf16[288,768]{1,0:T(8,128)(2,1)S(1)} %get-tuple-element.79), channel_id=1, source_target_pairs={{0,112},{16,0},{32,16},{48,32},{64,48},{80,64},{96,80},{112,96},{1... | collective-permute-start | bytes 1327112 | tf_op jit(solution)/shard_map/projection/ppermute | solution.py:30
  60.1 1.4 collective-permute-start.9
  61.5 12.3 %collective-permute-done.9.refs_5_ = bf16[288,384]{1,0:T(8,128)(2,1)S(1)} collective-permute-done((bf16[288,384]{1,0:T(8,128)(2,1)}, bf16[288,384]{1,0:T(8,128)(2,1)S(1)}, u32[]{:S(2)}, u32[]{:S(2)}) %collective-permute-start.9) | collective-permute-done | bytes 221216 | tf_op jit(solution)/shard_map/projection/ppermute | solution.py:30
  73.8 0.2 projection.9
  74.1 0.4 collective-permute-start.10
  74.5 2.9 %collective-permute-start.11 = (bf16[288,384]{1,0:T(8,128)(2,1)S(1)}, bf16[288,384]{1,0:T(8,128)(2,1)S(1)}, u32[]{:S(2)}, u32[]{:S(2)}) collective-permute-start(bf16[288,384]{1,0:T(8,128)(2,1)S(1)} %get-tuple-element.86), channel_id=1, source_target_pairs={{0,112},{16,0},{32,16},{48,32},{64,48},{80,64},{96,80},{112,96},{1... | collective-permute-start | bytes 663560 | tf_op jit(solution)/shard_map/projection/ppermute | solution.py:30
  77.4 5.6 %collective-permute-start.13 = (bf16[288,384]{1,0:T(8,128)(2,1)S(1)}, bf16[288,384]{1,0:T(8,128)(2,1)S(1)}, u32[]{:S(2)}, u32[]{:S(2)}) collective-permute-start(bf16[288,384]{1,0:T(8,128)(2,1)S(1)} %get-tuple-element.88), channel_id=1, source_target_pairs={{0,240},{16,128},{32,144},{48,160},{64,176},{80,192},{96,208},{112... | collective-permute-start | bytes 663560 | tf_op jit(solution)/shard_map/projection/ppermute | solution.py:37
  83.0 0.6 fusion.2
  83.6 0.1 pad_maximum_fusion
  83.8 5.4 %collective-permute-done.12.refs_2_ = bf16[288,384]{1,0:T(8,128)(2,1)S(1)} collective-permute-done((bf16[288,384]{1,0:T(8,128)(2,1)S(1)}, bf16[288,384]{1,0:T(8,128)(2,1)S(1)}, u32[]{:S(2)}, u32[]{:S(2)}) %collective-permute-start.12) | collective-permute-done | bytes 221216 | tf_op jit(solution)/shard_map/projection/ppermute | solution.py:37
  89.1 0.1 collective-permute-done.13.refs_3_
  89.2 1.4 attention.2
  90.6 17.7 %all_to_all.10.blocks = bf16[8,288,256]{2,1,0:T(8,128)(2,1)S(1)} all-to-all(bf16[8,288,256]{2,1,0:T(8,128)(2,1)S(1)} %get-tuple-element.93), channel_id=1, replica_groups=mesh['x_hi'=2,'z'=8,'core'=2,'x_lo'=2,'y'=4] {'x_lo','y'}, dimensions={0} | all-to-all | bytes 2359296 | tf_op jit(solution)/shard_map/attention/all_to_all | solution.py:574
  108.3 2.9 %attention.3.refs_0_ = bf16[512,128]{1,0:T(8,128)(2,1)S(1)} custom-call(bf16[512,128]{1,0:T(8,128)(2,1)S(1)} %get-tuple-element.92.queries, bf16[8,288,256]{2,1,0:T(8,128)(2,1)S(1)} %all_to_all.10.blocks), custom_call_target="tpu_custom_call" | custom-call | tf_op jit(solution)/shard_map/attention/pallas_call | solution.py:433
  111.2 0.0 all-gather.2.cloned.1.call-done.w
  111.3 0.1 collective-permute-start.14
  111.4 3.2 %collective-permute-start.15 = (bf16[512,128]{1,0:T(8,128)(2,1)S(1)}, bf16[512,128]{1,0:T(8,128)(2,1)S(1)}, u32[]{:S(2)}, u32[]{:S(2)}) collective-permute-start(bf16[512,128]{1,0:T(8,128)(2,1)S(1)} %attention.3.refs_0_), channel_id=1, source_target_pairs={{0,112},{16,0},{32,16},{48,32},{64,48},{80,64},{96,80},{112,96},{1... | collective-permute-start | bytes 393224 | tf_op jit(solution)/shard_map/output/ppermute | solution.py:30
  114.6 1.6 %output.2.turned = bf16[1024,1024]{1,0:T(8,128)(2,1)S(1)} custom-call(bf16[8,128,1024]{2,1,0:T(8,128)(2,1)} %all-gather.2.cloned.1.call-done.w), custom_call_target="tpu_custom_call" | custom-call | tf_op jit(solution)/shard_map/output/pallas_call | solution.py:465
  116.2 2.2 %collective-permute-done.14.refs_1_ = bf16[512,128]{1,0:T(8,128)(2,1)S(1)} collective-permute-done((bf16[512,128]{1,0:T(8,128)(2,1)S(1)}, bf16[512,128]{1,0:T(8,128)(2,1)S(1)}, u32[]{:S(2)}, u32[]{:S(2)}) %collective-permute-start.14) | collective-permute-done | bytes 131104 | tf_op jit(solution)/shard_map/output/ppermute | solution.py:30
  118.3 3.2 %collective-permute-start.19 = (bf16[512,128]{1,0:T(8,128)(2,1)S(1)}, bf16[512,128]{1,0:T(8,128)(2,1)S(1)}, u32[]{:S(2)}, u32[]{:S(2)}) collective-permute-start(bf16[512,128]{1,0:T(8,128)(2,1)S(1)} %collective-permute-done.15.refs_7_), channel_id=1, source_target_pairs={{0,112},{16,0},{32,16},{48,32},{64,48},{80,64},{96,80},{112,96},{1... | collective-permute-start | bytes 393224 | tf_op jit(solution)/shard_map/output/ppermute | solution.py:30
  121.6 1.8 %collective-permute-start.18 = (bf16[512,128]{1,0:T(8,128)(2,1)S(1)}, bf16[512,128]{1,0:T(8,128)(2,1)S(1)}, u32[]{:S(2)}, u32[]{:S(2)}) collective-permute-start(bf16[512,128]{1,0:T(8,128)(2,1)S(1)} %attention.3.refs_0_), channel_id=1, source_target_pairs={{0,64},{16,80},{32,96},{48,112},{64,0},{80,16},{96,32},{112,48},{1... | collective-permute-start | bytes 393224 | tf_op jit(solution)/shard_map/output/ppermute | solution.py:30
  123.4 3.0 %collective-permute-done.16.refs_2_ = bf16[512,128]{1,0:T(8,128)(2,1)S(1)} collective-permute-done((bf16[512,128]{1,0:T(8,128)(2,1)S(1)}, bf16[512,128]{1,0:T(8,128)(2,1)S(1)}, u32[]{:S(2)}, u32[]{:S(2)}) %collective-permute-start.16) | collective-permute-done | bytes 131104 | tf_op jit(solution)/shard_map/output/ppermute | solution.py:30
  126.4 3.2 %collective-permute-start.20 = (bf16[512,128]{1,0:T(8,128)(2,1)S(1)}, bf16[512,128]{1,0:T(8,128)(2,1)S(1)}, u32[]{:S(2)}, u32[]{:S(2)}) collective-permute-start(bf16[512,128]{1,0:T(8,128)(2,1)S(1)} %collective-permute-done.19.refs_6_), channel_id=1, source_target_pairs={{0,112},{16,0},{32,16},{48,32},{64,48},{80,64},{96,80},{112,96},{1... | collective-permute-start | bytes 393224 | tf_op jit(solution)/shard_map/output/ppermute | solution.py:30
  129.7 1.3 collective-permute-done.18.refs_4_
  131.0 1.6 %collective-permute-done.17.refs_3_ = bf16[512,128]{1,0:T(8,128)(2,1)S(1)} collective-permute-done((bf16[512,128]{1,0:T(8,128)(2,1)S(1)}, bf16[512,128]{1,0:T(8,128)(2,1)S(1)}, u32[]{:S(2)}, u32[]{:S(2)}) %collective-permute-start.17) | collective-permute-done | bytes 131104 | tf_op jit(solution)/shard_map/output/ppermute | solution.py:30
  132.6 2.2 %output.3 = (f32[512,256]{1,0:T(8,128)S(1)}, bf16[512,512]{1,0:T(8,128)(2,1)S(1)}, f32[512,256]{1,0:T(8,128)S(1)}) custom-call(bf16[1024,1024]{1,0:T(8,128)(2,1)S(1)} %output.2.turned, bf16[512,128]{1,0:T(8,128)(2,1)S(1)} %attention.3.refs_0_, bf16[512,128]{1,0:T(8,128)(2,1)S(1)} %collective-permute-done.14.refs_1_, ...), custom_call_target="tpu_custom_call" | custom-call | tf_op jit(solution)/shard_map/output/pallas_call | solution.py:501
  134.8 0.0 copy-start.3
  134.8 0.1 collective-permute-start.21
  134.9 1.9 %collective-permute-done.21 = bf16[512,512]{1,0:T(8,128)(2,1)S(1)} collective-permute-done((bf16[512,512]{1,0:T(8,128)(2,1)S(1)}, bf16[512,512]{1,0:T(8,128)(2,1)S(1)}, u32[]{:S(2)}, u32[]{:S(2)}) %collective-permute-start.21) | collective-permute-done | bytes 524320 | tf_op jit(solution)/shard_map/output/ppermute | solution.py:30
  136.8 0.1 convert_element_type.32
  137.0 0.1 fusion
  137.1 3.1 %collective-permute-start.22 = (bf16[512,256]{1,0:T(8,128)(2,1)S(1)}, bf16[512,256]{1,0:T(8,128)(2,1)S(1)}, u32[]{:S(2)}, u32[]{:S(2)}) collective-permute-start(bf16[512,256]{1,0:T(8,128)(2,1)S(1)} %fusion), channel_id=1, source_target_pairs={{0,128},{128,0},{1,129},{129,1},{2,130},{130,2},{3,131},{131,3},{4... | collective-permute-start | bytes 786440 | tf_op jit(solution)/shard_map/output/ppermute | solution.py:30
  140.2 6.8 %collective-permute-done.22 = bf16[512,256]{1,0:T(8,128)(2,1)S(1)} collective-permute-done((bf16[512,256]{1,0:T(8,128)(2,1)S(1)}, bf16[512,256]{1,0:T(8,128)(2,1)S(1)}, u32[]{:S(2)}, u32[]{:S(2)}) %collective-permute-start.22) | collective-permute-done | bytes 262176 | tf_op jit(solution)/shard_map/output/ppermute | solution.py:30
  147.0 0.1 fusion.1
  147.1 0.8 add_convert_fusion
  (25 shorter events, 0.1 us)
Async XLA Ops:
  10.9 2.0 %collective-permute-start.1 = (bf16[256,768]{1,0:T(8,128)(2,1)S(1)}, bf16[256,768]{1,0:T(8,128)(2,1)S(1)}, u32[]{:S(2)}, u32[]{:S(2)}) collective-permute-start(bf16[256,768]{1,0:T(8,128)(2,1)S(1)} %get-tuple-element.58), channel_id=1, source_target_pairs={{0,8},{8,0},{1,9},{9,1},{2,10},{10,2},{3,11},{11,3},{4,12},{12,4},... | collective-permute-start | bytes 1179656 | tf_op jit(solution)/shard_map/inputs/ppermute | solution.py:30
  11.0 1.9 %collective-permute-start = (bf16[272,256]{1,0:T(8,128)(2,1)S(1)}, bf16[272,256]{1,0:T(8,128)(2,1)S(1)}, u32[]{:S(2)}, u32[]{:S(2)}) collective-permute-start(bf16[272,256]{1,0:T(8,128)(2,1)S(1)} %get-tuple-element.56.own), channel_id=1, source_target_pairs={{0,8},{8,0},{1,9},{9,1},{2,10},{10,2},{3,11},{11,3},{4,12},{12,4},... | collective-permute-start | bytes 417800 | tf_op jit(solution)/shard_map/inputs/ppermute | solution.py:30
  12.9 0.8 copy-start.4
  18.2 14.3 %collective-permute-start.4 = (bf16[256,5376]{1,0:T(8,128)(2,1)}, bf16[256,5376]{1,0:T(8,128)(2,1)}, u32[]{:S(2)}, u32[]{:S(2)}) collective-permute-start(bf16[256,5376]{1,0:T(8,128)(2,1)} %get-tuple-element.68), channel_id=1, source_target_pairs={{0,8},{8,0},{1,9},{9,1},{2,10},{10,2},{3,11},{11,3},{4,12},{12,4},... | collective-permute-start | bytes 8257544 | tf_op jit(solution)/shard_map/inputs/ppermute | solution.py:30
  18.4 22.9 %all-to-all-start = ((bf16[8,16,1024]{2,1,0:T(8,128)(2,1)}), bf16[8,16,1024]{2,1,0:T(8,128)(2,1)}, u32[]{:S(2)}, u32[]{:S(2)}) async-start(bf16[8,16,1024]{2,1,0:T(8,128)(2,1)} %get-tuple-element.65), calls=%async_computation | async-start | bytes 524288 | tf_op jit(solution)/shard_map/inputs/all_to_all | solution.py:535
  26.9 84.4 %all-gather.2.cloned.1.call-start = ((), (), s32[]{:S(2)}) async-start(), calls=%async_computation.2 | async-start | bytes 2359296 | tf_op jit(solution)/shard_map/projection/all_gather | solution.py:547
  29.2 12.2 %collective-permute-start.2 = (bf16[288,384]{1,0:T(8,128)(2,1)S(1)}, bf16[288,384]{1,0:T(8,128)(2,1)S(1)}, u32[]{:S(2)}, u32[]{:S(2)}) collective-permute-start(bf16[288,384]{1,0:T(8,128)(2,1)S(1)} %get-tuple-element.63), channel_id=1, source_target_pairs={{0,16},{16,32},{32,48},{48,64},{64,80},{80,96},{96,112},{112,0},{1... | collective-permute-start | bytes 663560 | tf_op jit(solution)/shard_map/projection/ppermute | solution.py:30
  31.2 10.1 %collective-permute-start.3 = (bf16[288,384]{1,0:T(8,128)(2,1)S(1)}, bf16[288,384]{1,0:T(8,128)(2,1)S(1)}, u32[]{:S(2)}, u32[]{:S(2)}) collective-permute-start(bf16[288,384]{1,0:T(8,128)(2,1)S(1)} %get-tuple-element.64), channel_id=1, source_target_pairs={{0,112},{16,0},{32,16},{48,32},{64,48},{80,64},{96,80},{112,96},{1... | collective-permute-start | bytes 663560 | tf_op jit(solution)/shard_map/projection/ppermute | solution.py:30
  36.9 24.6 %copy-start.6 = (s32[16]{0:T(128)S(1)}, s32[16]{0:T(128)}, u32[]{:S(2)}) copy-start(s32[16]{0:T(128)} %pos.1) | copy-start | bytes 196
  36.9 36.9 %copy-start = (bf16[288,768]{1,0:T(8,128)(2,1)S(1)}, bf16[288,768]{1,0:T(8,128)(2,1)}, u32[]{:S(2)}) copy-start(bf16[288,768]{1,0:T(8,128)(2,1)} %get-tuple-element.83.near_up) | copy-start | bytes 1327108
  36.9 36.9 %copy-start.1 = (bf16[288,768]{1,0:T(8,128)(2,1)S(1)}, bf16[288,768]{1,0:T(8,128)(2,1)}, u32[]{:S(2)}) copy-start(bf16[288,768]{1,0:T(8,128)(2,1)} %get-tuple-element.84.near_down) | copy-start | bytes 1327108
  42.7 12.6 %collective-permute-start.5 = (bf16[288,768]{1,0:T(8,128)(2,1)S(1)}, bf16[288,768]{1,0:T(8,128)(2,1)S(1)}, u32[]{:S(2)}, u32[]{:S(2)}) collective-permute-start(bf16[288,768]{1,0:T(8,128)(2,1)S(1)} %get-tuple-element.74), channel_id=1, source_target_pairs={{0,16},{16,32},{32,48},{48,64},{64,80},{80,96},{96,112},{112,0},{1... | collective-permute-start | bytes 1327112 | tf_op jit(solution)/shard_map/projection/ppermute | solution.py:30
  43.0 12.3 %collective-permute-start.6 = (bf16[288,768]{1,0:T(8,128)(2,1)S(1)}, bf16[288,768]{1,0:T(8,128)(2,1)S(1)}, u32[]{:S(2)}, u32[]{:S(2)}) collective-permute-start(bf16[288,768]{1,0:T(8,128)(2,1)S(1)} %get-tuple-element.75), channel_id=1, source_target_pairs={{0,112},{16,0},{32,16},{48,32},{64,48},{80,64},{96,80},{112,96},{1... | collective-permute-start | bytes 1327112 | tf_op jit(solution)/shard_map/projection/ppermute | solution.py:30
  55.3 33.9 %copy-start.2 = (bf16[288,384]{1,0:T(8,128)(2,1)S(1)}, bf16[288,384]{1,0:T(8,128)(2,1)}, u32[]{:S(2)}) copy-start(bf16[288,384]{1,0:T(8,128)(2,1)} %get-tuple-element.89.refs_4_) | copy-start | bytes 663556
  56.8 17.0 %collective-permute-start.7 = (bf16[288,768]{1,0:T(8,128)(2,1)S(1)}, bf16[288,768]{1,0:T(8,128)(2,1)S(1)}, u32[]{:S(2)}, u32[]{:S(2)}) collective-permute-start(bf16[288,768]{1,0:T(8,128)(2,1)S(1)} %get-tuple-element.78), channel_id=1, source_target_pairs={{0,16},{16,32},{32,48},{48,64},{64,80},{80,96},{96,112},{112,0},{1... | collective-permute-start | bytes 1327112 | tf_op jit(solution)/shard_map/projection/ppermute | solution.py:30
  58.4 15.4 %collective-permute-start.8 = (bf16[288,768]{1,0:T(8,128)(2,1)S(1)}, bf16[288,768]{1,0:T(8,128)(2,1)S(1)}, u32[]{:S(2)}, u32[]{:S(2)}) collective-permute-start(bf16[288,768]{1,0:T(8,128)(2,1)S(1)} %get-tuple-element.79), channel_id=1, source_target_pairs={{0,112},{16,0},{32,16},{48,32},{64,48},{80,64},{96,80},{112,96},{1... | collective-permute-start | bytes 1327112 | tf_op jit(solution)/shard_map/projection/ppermute | solution.py:30
  60.1 13.7 %collective-permute-start.9 = (bf16[288,384]{1,0:T(8,128)(2,1)}, bf16[288,384]{1,0:T(8,128)(2,1)S(1)}, u32[]{:S(2)}, u32[]{:S(2)}) collective-permute-start(bf16[288,384]{1,0:T(8,128)(2,1)} %get-tuple-element.80), channel_id=1, source_target_pairs={{0,128},{128,0},{1,129},{129,1},{2,130},{130,2},{3,131},{131,3},{4... | collective-permute-start | bytes 663560 | tf_op jit(solution)/shard_map/projection/ppermute | solution.py:30
  74.1 9.7 %collective-permute-start.10 = (bf16[288,384]{1,0:T(8,128)(2,1)S(1)}, bf16[288,384]{1,0:T(8,128)(2,1)S(1)}, u32[]{:S(2)}, u32[]{:S(2)}) collective-permute-start(bf16[288,384]{1,0:T(8,128)(2,1)S(1)} %get-tuple-element.85), channel_id=1, source_target_pairs={{0,16},{16,32},{32,48},{48,64},{64,80},{80,96},{96,112},{112,0},{1... | collective-permute-start | bytes 663560 | tf_op jit(solution)/shard_map/projection/ppermute | solution.py:30
  74.5 9.3 %collective-permute-start.11 = (bf16[288,384]{1,0:T(8,128)(2,1)S(1)}, bf16[288,384]{1,0:T(8,128)(2,1)S(1)}, u32[]{:S(2)}, u32[]{:S(2)}) collective-permute-start(bf16[288,384]{1,0:T(8,128)(2,1)S(1)} %get-tuple-element.86), channel_id=1, source_target_pairs={{0,112},{16,0},{32,16},{48,32},{64,48},{80,64},{96,80},{112,96},{1... | collective-permute-start | bytes 663560 | tf_op jit(solution)/shard_map/projection/ppermute | solution.py:30
  77.4 11.7 %collective-permute-start.12 = (bf16[288,384]{1,0:T(8,128)(2,1)S(1)}, bf16[288,384]{1,0:T(8,128)(2,1)S(1)}, u32[]{:S(2)}, u32[]{:S(2)}) collective-permute-start(bf16[288,384]{1,0:T(8,128)(2,1)S(1)} %get-tuple-element.87), channel_id=1, source_target_pairs={{0,144},{16,160},{32,176},{48,192},{64,208},{80,224},{96,240},{112... | collective-permute-start | bytes 663560 | tf_op jit(solution)/shard_map/projection/ppermute | solution.py:37
  77.4 11.8 %collective-permute-start.13 = (bf16[288,384]{1,0:T(8,128)(2,1)S(1)}, bf16[288,384]{1,0:T(8,128)(2,1)S(1)}, u32[]{:S(2)}, u32[]{:S(2)}) collective-permute-start(bf16[288,384]{1,0:T(8,128)(2,1)S(1)} %get-tuple-element.88), channel_id=1, source_target_pairs={{0,240},{16,128},{32,144},{48,160},{64,176},{80,192},{96,208},{112... | collective-permute-start | bytes 663560 | tf_op jit(solution)/shard_map/projection/ppermute | solution.py:37
  111.3 7.1 %collective-permute-start.14 = (bf16[512,128]{1,0:T(8,128)(2,1)S(1)}, bf16[512,128]{1,0:T(8,128)(2,1)S(1)}, u32[]{:S(2)}, u32[]{:S(2)}) collective-permute-start(bf16[512,128]{1,0:T(8,128)(2,1)S(1)} %attention.3.refs_0_), channel_id=1, source_target_pairs={{0,16},{16,32},{32,48},{48,64},{64,80},{80,96},{96,112},{112,0},{1... | collective-permute-start | bytes 393224 | tf_op jit(solution)/shard_map/output/ppermute | solution.py:30
  111.4 7.0 %collective-permute-start.15 = (bf16[512,128]{1,0:T(8,128)(2,1)S(1)}, bf16[512,128]{1,0:T(8,128)(2,1)S(1)}, u32[]{:S(2)}, u32[]{:S(2)}) collective-permute-start(bf16[512,128]{1,0:T(8,128)(2,1)S(1)} %attention.3.refs_0_), channel_id=1, source_target_pairs={{0,112},{16,0},{32,16},{48,32},{64,48},{80,64},{96,80},{112,96},{1... | collective-permute-start | bytes 393224 | tf_op jit(solution)/shard_map/output/ppermute | solution.py:30
  118.3 8.1 %collective-permute-start.16 = (bf16[512,128]{1,0:T(8,128)(2,1)S(1)}, bf16[512,128]{1,0:T(8,128)(2,1)S(1)}, u32[]{:S(2)}, u32[]{:S(2)}) collective-permute-start(bf16[512,128]{1,0:T(8,128)(2,1)S(1)} %collective-permute-done.14.refs_1_), channel_id=1, source_target_pairs={{0,16},{16,32},{32,48},{48,64},{64,80},{80,96},{96,112},{112,0},{1... | collective-permute-start | bytes 393224 | tf_op jit(solution)/shard_map/output/ppermute | solution.py:30
  118.3 8.1 %collective-permute-start.19 = (bf16[512,128]{1,0:T(8,128)(2,1)S(1)}, bf16[512,128]{1,0:T(8,128)(2,1)S(1)}, u32[]{:S(2)}, u32[]{:S(2)}) collective-permute-start(bf16[512,128]{1,0:T(8,128)(2,1)S(1)} %collective-permute-done.15.refs_7_), channel_id=1, source_target_pairs={{0,112},{16,0},{32,16},{48,32},{64,48},{80,64},{96,80},{112,96},{1... | collective-permute-start | bytes 393224 | tf_op jit(solution)/shard_map/output/ppermute | solution.py:30
  121.6 9.4 %collective-permute-start.18 = (bf16[512,128]{1,0:T(8,128)(2,1)S(1)}, bf16[512,128]{1,0:T(8,128)(2,1)S(1)}, u32[]{:S(2)}, u32[]{:S(2)}) collective-permute-start(bf16[512,128]{1,0:T(8,128)(2,1)S(1)} %attention.3.refs_0_), channel_id=1, source_target_pairs={{0,64},{16,80},{32,96},{48,112},{64,0},{80,16},{96,32},{112,48},{1... | collective-permute-start | bytes 393224 | tf_op jit(solution)/shard_map/output/ppermute | solution.py:30
  126.4 6.2 %collective-permute-start.17 = (bf16[512,128]{1,0:T(8,128)(2,1)S(1)}, bf16[512,128]{1,0:T(8,128)(2,1)S(1)}, u32[]{:S(2)}, u32[]{:S(2)}) collective-permute-start(bf16[512,128]{1,0:T(8,128)(2,1)S(1)} %collective-permute-done.16.refs_2_), channel_id=1, source_target_pairs={{0,16},{16,32},{32,48},{48,64},{64,80},{80,96},{96,112},{112,0},{1... | collective-permute-start | bytes 393224 | tf_op jit(solution)/shard_map/output/ppermute | solution.py:30
  126.4 6.2 %collective-permute-start.20 = (bf16[512,128]{1,0:T(8,128)(2,1)S(1)}, bf16[512,128]{1,0:T(8,128)(2,1)S(1)}, u32[]{:S(2)}, u32[]{:S(2)}) collective-permute-start(bf16[512,128]{1,0:T(8,128)(2,1)S(1)} %collective-permute-done.19.refs_6_), channel_id=1, source_target_pairs={{0,112},{16,0},{32,16},{48,32},{64,48},{80,64},{96,80},{112,96},{1... | collective-permute-start | bytes 393224 | tf_op jit(solution)/shard_map/output/ppermute | solution.py:30
  134.8 12.3 %copy-start.3 = (bf16[256,256]{1,0:T(8,128)(2,1)S(1)}, bf16[256,256]{1,0:T(8,128)(2,1)}, u32[]{:S(2)}) copy-start(bf16[256,256]{1,0:T(8,128)(2,1)} %hidden.1) | copy-start | bytes 393220
  134.8 12.3 %copy-start.5 = (bf16[256,256]{1,0:T(8,128)(2,1)S(1)}, bf16[256,256]{1,0:T(8,128)(2,1)}, u32[]{:S(2)}) copy-start(bf16[256,256]{1,0:T(8,128)(2,1)} %get-tuple-element.54) | copy-start | bytes 393220
  134.8 2.0 %collective-permute-start.21 = (bf16[512,512]{1,0:T(8,128)(2,1)S(1)}, bf16[512,512]{1,0:T(8,128)(2,1)S(1)}, u32[]{:S(2)}, u32[]{:S(2)}) collective-permute-start(bf16[512,512]{1,0:T(8,128)(2,1)S(1)} %get-tuple-element.101), channel_id=1, source_target_pairs={{0,8},{8,0},{1,9},{9,1},{2,10},{10,2},{3,11},{11,3},{4,12},{12,4},... | collective-permute-start | bytes 1572872 | tf_op jit(solution)/shard_map/output/ppermute | solution.py:30
  137.1 9.9 %collective-permute-start.22 = (bf16[512,256]{1,0:T(8,128)(2,1)S(1)}, bf16[512,256]{1,0:T(8,128)(2,1)S(1)}, u32[]{:S(2)}, u32[]{:S(2)}) collective-permute-start(bf16[512,256]{1,0:T(8,128)(2,1)S(1)} %fusion), channel_id=1, source_target_pairs={{0,128},{128,0},{1,129},{129,1},{2,130},{130,2},{3,131},{131,3},{4... | collective-permute-start | bytes 786440 | tf_op jit(solution)/shard_map/output/ppermute | solution.py:30
Sparse Core Ops, SparseCore 0:
  41.5 51.1 all-gather.1

commit v7 on v5

--- a/solution.py
+++ b/solution.py
@@ -458,10 +458,12 @@
 
 
 def project_kernel(turned, *refs):
-    shards, (keep, near, far), joined = refs[:Z], refs[Z : Z + 3], refs[-1]
+    shards, (rest, keep, near, far, joined) = refs[:Z], refs[Z:]
     core, x_hi = lax.axis_index("core"), lax.axis_index("x_hi")
     for d in range(Z):
-        joined[:, d * HD : (d + 1) * HD] = shards[d][...]
+        joined[: shards[d].shape[0], d * HD : (d + 1) * HD] = shards[d][...]
+    middle = slice(Z // 2 * HD, (Z // 2 + 1) * HD)
+    joined[rest.shape[0] :, middle] = rest[...]
 
     def product(xr, cr, rows):
         column = (lax.rem(x_hi + xr, X_HI) * CORE + lax.rem(core + cr, CORE)) * TOK
@@ -490,7 +492,7 @@
             jax.ShapeDtypeStruct((rows, 2 * TOK), bf16),
             jax.ShapeDtypeStruct((rows, TOK), f32),
         ),
-        in_specs=[vmem()] * (1 + Z),
+        in_specs=[vmem()] * (2 + Z),
         out_specs=(vmem(),) * 3,
         scratch_shapes=[pltpu.VMEM((rows, Z * HD), bf16)],
         compiler_params=limit(16),
@@ -563,10 +565,12 @@
             pieces[d] = shift(pieces[d - 1], "z", Z, 1)
             pieces[Z - d] = shift(pieces[(Z - d + 1) % Z], "z", Z, -1)
             if d == 1:
-                pieces[Z // 2] = shift(attn, "z", Z, Z // 2)
                 out_w, pieces[1], pieces[7] = lax.optimization_barrier(
                     (arrange(out_w), pieces[1], pieces[7])
                 )
+        first_half = shift(pieces[2][:tok_rows], "z", Z, 2)
+        pieces.append(shift(pieces[6][tok_rows:], "z", Z, -2))
+        pieces[Z // 2] = first_half
         keep, near, far = project(out_w, pieces)
         near = shift(near, "core", CORE, 1).astype(f32)
         far = (far + near[:, width_part:]).astype(bf16)

time: 156 us -> 159 us (1.019)
  waiting for transfers between devices: 54.7 us -> 57 us
    ppermute x21 -> x22, waiting for transfers between devices: 54.7 us -> 56.9 us  [shift(): lax.ppermute(value, axis, [(i, (i + distance) % size) for i in range(size)])]
    ppermute x21 -> x22, starting transfers between devices: 31.2 us -> 31 us  [shift(): lax.ppermute(value, axis, [(i, (i + distance) % size) for i in range(size)])]
  transfers between devices with their start and end apart: 23 -> 24, of which waited for: 13 -> 14; matrix products, arithmetic and copies ran while one was open for 1% -> 1% of each run, Pallas kernels for 10% -> 9%
where the time goes in v7:
time: 159 us; the launch traced here: 157 us
  waiting for transfers between devices  57 us (36%)
  starting transfers between devices  39.5 us (25%)
  Pallas kernels  25.8 us (16%)
  blocking collectives  17.6 us (11%)
  between operations  13.7 us (9%)
  other arithmetic  1.81 us (1%)
    ppermute x22, waiting for transfers between devices, shift(): lax.ppermute(value, axis, [(i, (i + distance) % size) for i in range(size)])  56.9 us
    ppermute x22, starting transfers between devices, shift(): lax.ppermute(value, axis, [(i, (i + distance) % size) for i in range(size)])  31 us
    all_to_all x1, blocking collectives, shards(): blocks = lax.all_to_all(payload, CTX, 0, 0, tiled=True)  17.6 us
    all_to_all x1, starting transfers between devices, shards(): shared = lax.all_to_all(share, 'z', 0, 0, tiled=True)  8.48 us
    pallas_call x2, Pallas kernels, pick_columns(): pl.pallas_call(functools.partial(columns_kernel, ks), out_shape=(columns,...  5.78 us
    pallas_call x2, Pallas kernels, partials(): pl.pallas_call(functools.partial(partial_kernel, ks), out_shape=shapes, i...  5.78 us
  transfers between devices with their start and end apart: 24, of which 14 were waited for; matrix products, arithmetic and copies ran while one was open for 1% of the time, Pallas kernels for 9%

profile of v7, /device:TPU:6, one launch (start us, length us, event | category | flops | bytes accessed | tf_op | source)
XLA Modules:
  0.0 156.9 jit_solution(5416863690958304089)
XLA Ops:
  6.5 3.1 %inputs.3 = (bf16[272,256]{1,0:T(8,128)(2,1)S(1)}, bf16[16,256]{1,0:T(8,128)(2,1)}, bf16[256,256]{1,0:T(8,128)(2,1)}, bf16[8,16,1024]{2,1,0:T(8,128)(2,1)}) custom-call(s32[16]{0:T(128)} %pos.1, s32[16]{0:T(128)} %base.1, s32[256]{0:T(256)} %ids.1, bf16[256,256]{1,0:T(8,128)(2,1)} %hidden.1, bf16[512,256]{1,0:T(8,128)(2,1)} %embed.1, bf16[128,8192]{1,0:T(8,128)(2,1)} %w.1), custom_call_target="tpu_custom_call" | custom-call | tf_op jit(solution)/shard_map/inputs/pallas_call | solution.py:116
  9.6 1.3 inputs.4
  10.9 0.1 collective-permute-start.1
  11.0 0.5 collective-permute-start
  11.5 1.4 collective-permute-done.sis
  12.9 0.8 copy-done.4
  13.7 4.5 %inputs.5 = (bf16[256,5376]{1,0:T(8,128)(2,1)}, bf16[256,5376]{1,0:T(8,128)(2,1)S(1)}) custom-call(bf16[256,12288]{1,0:T(8,128)(2,1)} %w.3), custom_call_target="tpu_custom_call" | custom-call | tf_op jit(solution)/shard_map/inputs/pallas_call | solution.py:166
  18.2 0.2 collective-permute-start.4
  18.4 8.5 %all-to-all-start = ((bf16[8,16,1024]{2,1,0:T(8,128)(2,1)}), bf16[8,16,1024]{2,1,0:T(8,128)(2,1)}, u32[]{:S(2)}, u32[]{:S(2)}) async-start(bf16[8,16,1024]{2,1,0:T(8,128)(2,1)} %get-tuple-element.61), calls=%async_computation | async-start | bytes 524288 | tf_op jit(solution)/shard_map/inputs/all_to_all | solution.py:522
  26.9 0.0 all-gather.2.cloned.1.call-start
  27.0 0.8 dynamic-slice.3
  27.7 1.5 projection.6
  29.2 2.0 %collective-permute-start.2 = (bf16[288,384]{1,0:T(8,128)(2,1)S(1)}, bf16[288,384]{1,0:T(8,128)(2,1)S(1)}, u32[]{:S(2)}, u32[]{:S(2)}) collective-permute-start(bf16[288,384]{1,0:T(8,128)(2,1)S(1)} %get-tuple-element.59), channel_id=1, source_target_pairs={{0,16},{16,32},{32,48},{48,64},{64,80},{80,96},{96,112},{112,0},{1... | collective-permute-start | bytes 663560 | tf_op jit(solution)/shard_map/projection/ppermute | solution.py:30
  31.2 1.3 collective-permute-start.3
  32.5 4.3 %projection.7 = (bf16[288,768]{1,0:T(8,128)(2,1)}, bf16[288,768]{1,0:T(8,128)(2,1)}, bf16[288,768]{1,0:T(8,128)(2,1)}, bf16[288,768]{1,0:T(8,128)(2,1)}, bf16[28...) custom-call(bf16[272,256]{1,0:T(8,128)(2,1)S(1)} %get-tuple-element.52.own, ...), custom_call_target="tpu_custom_call" | custom-call | flops 1497366528 | bytes 11010048 | tf_op jit(solution)/shard_map/projection/pallas_call | solution.py:235
  36.9 4.5 %collective-permute-done.2.up = bf16[288,384]{1,0:T(8,128)(2,1)S(1)} collective-permute-done((bf16[288,384]{1,0:T(8,128)(2,1)S(1)}, bf16[288,384]{1,0:T(8,128)(2,1)S(1)}, u32[]{:S(2)}, u32[]{:S(2)}) %collective-permute-start.2) | collective-permute-done | bytes 221216 | tf_op jit(solution)/shard_map/projection/ppermute | solution.py:30
  41.4 0.0 all-gather.2.cloned.1.call-update
  41.4 1.3 projection.8
  42.7 0.0 copy-start.6
  42.7 0.3 collective-permute-start.5
  43.0 3.0 %collective-permute-start.6 = (bf16[288,768]{1,0:T(8,128)(2,1)S(1)}, bf16[288,768]{1,0:T(8,128)(2,1)S(1)}, u32[]{:S(2)}, u32[]{:S(2)}) collective-permute-start(bf16[288,768]{1,0:T(8,128)(2,1)S(1)} %get-tuple-element.71), channel_id=1, source_target_pairs={{0,112},{16,0},{32,16},{48,32},{64,48},{80,64},{96,80},{112,96},{1... | collective-permute-start | bytes 1327112 | tf_op jit(solution)/shard_map/projection/ppermute | solution.py:30
  46.0 9.3 %collective-permute-done.5.up = bf16[288,768]{1,0:T(8,128)(2,1)S(1)} collective-permute-done((bf16[288,768]{1,0:T(8,128)(2,1)S(1)}, bf16[288,768]{1,0:T(8,128)(2,1)S(1)}, u32[]{:S(2)}, u32[]{:S(2)}) %collective-permute-start.5) | collective-permute-done | bytes 442400 | tf_op jit(solution)/shard_map/projection/ppermute | solution.py:30
  55.3 1.4 projection.9
  56.7 1.6 %collective-permute-start.7 = (bf16[288,768]{1,0:T(8,128)(2,1)S(1)}, bf16[288,768]{1,0:T(8,128)(2,1)S(1)}, u32[]{:S(2)}, u32[]{:S(2)}) collective-permute-start(bf16[288,768]{1,0:T(8,128)(2,1)S(1)} %get-tuple-element.74), channel_id=1, source_target_pairs={{0,16},{16,32},{32,48},{48,64},{64,80},{80,96},{96,112},{112,0},{1... | collective-permute-start | bytes 1327112 | tf_op jit(solution)/shard_map/projection/ppermute | solution.py:30
  58.3 1.7 %collective-permute-start.8 = (bf16[288,768]{1,0:T(8,128)(2,1)S(1)}, bf16[288,768]{1,0:T(8,128)(2,1)S(1)}, u32[]{:S(2)}, u32[]{:S(2)}) collective-permute-start(bf16[288,768]{1,0:T(8,128)(2,1)S(1)} %get-tuple-element.75), channel_id=1, source_target_pairs={{0,112},{16,0},{32,16},{48,32},{64,48},{80,64},{96,80},{112,96},{1... | collective-permute-start | bytes 1327112 | tf_op jit(solution)/shard_map/projection/ppermute | solution.py:30
  60.0 8.8 %collective-permute-done.7.up = bf16[288,768]{1,0:T(8,128)(2,1)S(1)} collective-permute-done((bf16[288,768]{1,0:T(8,128)(2,1)S(1)}, bf16[288,768]{1,0:T(8,128)(2,1)S(1)}, u32[]{:S(2)}, u32[]{:S(2)}) %collective-permute-start.7) | collective-permute-done | bytes 442400 | tf_op jit(solution)/shard_map/projection/ppermute | solution.py:30
  68.8 0.2 projection.10
  69.0 1.8 %collective-permute-start.9 = (bf16[288,768]{1,0:T(8,128)(2,1)S(1)}, bf16[288,768]{1,0:T(8,128)(2,1)S(1)}, u32[]{:S(2)}, u32[]{:S(2)}) collective-permute-start(bf16[288,768]{1,0:T(8,128)(2,1)S(1)} %get-tuple-element.78), channel_id=1, source_target_pairs={{0,16},{16,32},{32,48},{48,64},{64,80},{80,96},{96,112},{112,0},{1... | collective-permute-start | bytes 1327112 | tf_op jit(solution)/shard_map/projection/ppermute | solution.py:30
  70.9 1.5 collective-permute-start.10
  72.4 7.9 %collective-permute-done.9.up = bf16[288,768]{1,0:T(8,128)(2,1)S(1)} collective-permute-done((bf16[288,768]{1,0:T(8,128)(2,1)S(1)}, bf16[288,768]{1,0:T(8,128)(2,1)S(1)}, u32[]{:S(2)}, u32[]{:S(2)}) %collective-permute-start.9) | collective-permute-done | bytes 442400 | tf_op jit(solution)/shard_map/projection/ppermute | solution.py:30
  80.3 0.2 projection.11
  80.5 1.6 %collective-permute-start.11 = (bf16[288,384]{1,0:T(8,128)(2,1)S(1)}, bf16[288,384]{1,0:T(8,128)(2,1)S(1)}, u32[]{:S(2)}, u32[]{:S(2)}) collective-permute-start(bf16[288,384]{1,0:T(8,128)(2,1)S(1)} %get-tuple-element.82), channel_id=1, source_target_pairs={{0,128},{128,0},{1,129},{129,1},{2,130},{130,2},{3,131},{131,3},{4... | collective-permute-start | bytes 663560 | tf_op jit(solution)/shard_map/projection/ppermute | solution.py:30
  82.1 0.6 fusion.2
  82.7 0.1 pad_maximum_fusion
  82.9 5.3 %collective-permute-done.11.other = bf16[288,384]{1,0:T(8,128)(2,1)S(1)} collective-permute-done((bf16[288,384]{1,0:T(8,128)(2,1)S(1)}, bf16[288,384]{1,0:T(8,128)(2,1)S(1)}, u32[]{:S(2)}, u32[]{:S(2)}) %collective-permute-start.11) | collective-permute-done | bytes 221216 | tf_op jit(solution)/shard_map/projection/ppermute | solution.py:30
  88.2 1.3 attention.2
  89.5 17.6 %all_to_all.10.blocks = bf16[8,288,256]{2,1,0:T(8,128)(2,1)S(1)} all-to-all(bf16[8,288,256]{2,1,0:T(8,128)(2,1)S(1)} %get-tuple-element.85), channel_id=1, replica_groups=mesh['x_hi'=2,'z'=8,'core'=2,'x_lo'=2,'y'=4] {'x_lo','y'}, dimensions={0} | all-to-all | bytes 2359296 | tf_op jit(solution)/shard_map/attention/all_to_all | solution.py:558
  107.1 2.9 %attention.3.refs_0_ = bf16[512,128]{1,0:T(8,128)(2,1)S(1)} custom-call(bf16[512,128]{1,0:T(8,128)(2,1)S(1)} %get-tuple-element.84.queries, bf16[8,288,256]{2,1,0:T(8,128)(2,1)S(1)} %all_to_all.10.blocks), custom_call_target="tpu_custom_call" | custom-call | tf_op jit(solution)/shard_map/attention/pallas_call | solution.py:418
  110.1 0.0 all-gather.2.cloned.1.call-done.w
  110.1 1.5 collective-permute-start.12
  111.6 1.9 %collective-permute-start.13 = (bf16[512,128]{1,0:T(8,128)(2,1)S(1)}, bf16[512,128]{1,0:T(8,128)(2,1)S(1)}, u32[]{:S(2)}, u32[]{:S(2)}) collective-permute-start(bf16[512,128]{1,0:T(8,128)(2,1)S(1)} %attention.3.refs_0_), channel_id=1, source_target_pairs={{0,112},{16,0},{32,16},{48,32},{64,48},{80,64},{96,80},{112,96},{1... | collective-permute-start | bytes 393224 | tf_op jit(solution)/shard_map/output/ppermute | solution.py:30
  113.4 1.6 %output.2.turned = bf16[1024,1024]{1,0:T(8,128)(2,1)S(1)} custom-call(bf16[8,128,1024]{2,1,0:T(8,128)(2,1)} %all-gather.2.cloned.1.call-done.w), custom_call_target="tpu_custom_call" | custom-call | tf_op jit(solution)/shard_map/output/pallas_call | solution.py:450
  115.0 1.4 collective-permute-done.12.refs_1_
  116.4 0.2 collective-permute-done.13.refs_7_
  116.5 2.2 %collective-permute-start.14 = (bf16[512,128]{1,0:T(8,128)(2,1)S(1)}, bf16[512,128]{1,0:T(8,128)(2,1)S(1)}, u32[]{:S(2)}, u32[]{:S(2)}) collective-permute-start(bf16[512,128]{1,0:T(8,128)(2,1)S(1)} %collective-permute-done.12.refs_1_), channel_id=1, source_target_pairs={{0,16},{16,32},{32,48},{48,64},{64,80},{80,96},{96,112},{112,0},{1... | collective-permute-start | bytes 393224 | tf_op jit(solution)/shard_map/output/ppermute | solution.py:30
  118.7 1.0 collective-permute-start.17
  119.8 4.3 %collective-permute-done.14.refs_2_ = bf16[512,128]{1,0:T(8,128)(2,1)S(1)} collective-permute-done((bf16[512,128]{1,0:T(8,128)(2,1)S(1)}, bf16[512,128]{1,0:T(8,128)(2,1)S(1)}, u32[]{:S(2)}, u32[]{:S(2)}) %collective-permute-start.14) | collective-permute-done | bytes 131104 | tf_op jit(solution)/shard_map/output/ppermute | solution.py:30
  124.1 0.5 collective-permute-start.15
  124.6 0.5 collective-permute-done.17.refs_6_
  125.1 2.2 %collective-permute-start.18 = (bf16[512,128]{1,0:T(8,128)(2,1)S(1)}, bf16[512,128]{1,0:T(8,128)(2,1)S(1)}, u32[]{:S(2)}, u32[]{:S(2)}) collective-permute-start(bf16[512,128]{1,0:T(8,128)(2,1)S(1)} %collective-permute-done.17.refs_6_), channel_id=1, source_target_pairs={{0,112},{16,0},{32,16},{48,32},{64,48},{80,64},{96,80},{112,96},{1... | collective-permute-start | bytes 393224 | tf_op jit(solution)/shard_map/output/ppermute | solution.py:30
  127.4 0.4 collective-permute-start.16
  127.8 3.7 %collective-permute-start.19 = (bf16[256,128]{1,0:T(8,128)(2,1)S(1)}, bf16[256,128]{1,0:T(8,128)(2,1)S(1)}, u32[]{:S(2)}, u32[]{:S(2)}) collective-permute-start(bf16[256,128]{1,0:T(8,128)(2,1)S(1)} %slice.17), channel_id=1, source_target_pairs={{0,96},{16,112},{32,0},{48,16},{64,32},{80,48},{96,64},{112,80},{1... | collective-permute-start | bytes 196616 | tf_op jit(solution)/shard_map/output/ppermute | solution.py:30
  131.5 2.2 %collective-permute-done.16.refs_4_ = bf16[256,128]{1,0:T(8,128)(2,1)S(1)} collective-permute-done((bf16[256,128]{1,0:T(8,128)(2,1)S(1)}, bf16[256,128]{1,0:T(8,128)(2,1)S(1)}, u32[]{:S(2)}, u32[]{:S(2)}) %collective-permute-start.16) | collective-permute-done | bytes 65568 | tf_op jit(solution)/shard_map/output/ppermute | solution.py:30
  133.7 1.0 collective-permute-done.19.refs_8_
  134.7 2.2 %output.3 = (f32[512,256]{1,0:T(8,128)S(1)}, bf16[512,512]{1,0:T(8,128)(2,1)S(1)}, f32[512,256]{1,0:T(8,128)S(1)}) custom-call(bf16[1024,1024]{1,0:T(8,128)(2,1)S(1)} %output.2.turned, bf16[512,128]{1,0:T(8,128)(2,1)S(1)} %attention.3.refs_0_, bf16[512,128]{1,0:T(8,128)(2,1)S(1)} %collective-permute-done.12.refs_1_, ...), custom_call_target="tpu_custom_call" | custom-call | tf_op jit(solution)/shard_map/output/pallas_call | solution.py:488
  137.0 0.0 copy-start.3
  137.0 0.1 collective-permute-start.20
  137.1 1.9 %collective-permute-done.20 = bf16[512,512]{1,0:T(8,128)(2,1)S(1)} collective-permute-done((bf16[512,512]{1,0:T(8,128)(2,1)S(1)}, bf16[512,512]{1,0:T(8,128)(2,1)S(1)}, u32[]{:S(2)}, u32[]{:S(2)}) %collective-permute-start.20) | collective-permute-done | bytes 524320 | tf_op jit(solution)/shard_map/output/ppermute | solution.py:30
  139.0 0.1 convert_element_type.32
  139.1 0.1 fusion
  139.2 1.7 %collective-permute-start.21 = (bf16[512,256]{1,0:T(8,128)(2,1)S(1)}, bf16[512,256]{1,0:T(8,128)(2,1)S(1)}, u32[]{:S(2)}, u32[]{:S(2)}) collective-permute-start(bf16[512,256]{1,0:T(8,128)(2,1)S(1)} %fusion), channel_id=1, source_target_pairs={{0,128},{128,0},{1,129},{129,1},{2,130},{130,2},{3,131},{131,3},{4... | collective-permute-start | bytes 786440 | tf_op jit(solution)/shard_map/output/ppermute | solution.py:30
  140.9 8.2 %collective-permute-done.21 = bf16[512,256]{1,0:T(8,128)(2,1)S(1)} collective-permute-done((bf16[512,256]{1,0:T(8,128)(2,1)S(1)}, bf16[512,256]{1,0:T(8,128)(2,1)S(1)}, u32[]{:S(2)}, u32[]{:S(2)}) %collective-permute-start.21) | collective-permute-done | bytes 262176 | tf_op jit(solution)/shard_map/output/ppermute | solution.py:30
  149.2 0.1 fusion.1
  149.3 0.8 add_convert_fusion
  (26 shorter events, 0.1 us)
Async XLA Ops:
  10.9 2.0 %collective-permute-start.1 = (bf16[256,768]{1,0:T(8,128)(2,1)S(1)}, bf16[256,768]{1,0:T(8,128)(2,1)S(1)}, u32[]{:S(2)}, u32[]{:S(2)}) collective-permute-start(bf16[256,768]{1,0:T(8,128)(2,1)S(1)} %get-tuple-element.54), channel_id=1, source_target_pairs={{0,8},{8,0},{1,9},{9,1},{2,10},{10,2},{3,11},{11,3},{4,12},{12,4},... | collective-permute-start | bytes 1179656 | tf_op jit(solution)/shard_map/inputs/ppermute | solution.py:30
  11.0 1.9 %collective-permute-start = (bf16[272,256]{1,0:T(8,128)(2,1)S(1)}, bf16[272,256]{1,0:T(8,128)(2,1)S(1)}, u32[]{:S(2)}, u32[]{:S(2)}) collective-permute-start(bf16[272,256]{1,0:T(8,128)(2,1)S(1)} %get-tuple-element.52.own), channel_id=1, source_target_pairs={{0,8},{8,0},{1,9},{9,1},{2,10},{10,2},{3,11},{11,3},{4,12},{12,4},... | collective-permute-start | bytes 417800 | tf_op jit(solution)/shard_map/inputs/ppermute | solution.py:30
  12.9 0.8 copy-start.4
  18.2 14.3 %collective-permute-start.4 = (bf16[256,5376]{1,0:T(8,128)(2,1)}, bf16[256,5376]{1,0:T(8,128)(2,1)}, u32[]{:S(2)}, u32[]{:S(2)}) collective-permute-start(bf16[256,5376]{1,0:T(8,128)(2,1)} %get-tuple-element.64), channel_id=1, source_target_pairs={{0,8},{8,0},{1,9},{9,1},{2,10},{10,2},{3,11},{11,3},{4,12},{12,4},... | collective-permute-start | bytes 8257544 | tf_op jit(solution)/shard_map/inputs/ppermute | solution.py:30
  18.4 22.9 %all-to-all-start = ((bf16[8,16,1024]{2,1,0:T(8,128)(2,1)}), bf16[8,16,1024]{2,1,0:T(8,128)(2,1)}, u32[]{:S(2)}, u32[]{:S(2)}) async-start(bf16[8,16,1024]{2,1,0:T(8,128)(2,1)} %get-tuple-element.61), calls=%async_computation | async-start | bytes 524288 | tf_op jit(solution)/shard_map/inputs/all_to_all | solution.py:522
  26.9 83.2 %all-gather.2.cloned.1.call-start = ((), (), s32[]{:S(2)}) async-start(), calls=%async_computation.2 | async-start | bytes 2359296 | tf_op jit(solution)/shard_map/projection/all_gather | solution.py:534
  29.2 12.2 %collective-permute-start.2 = (bf16[288,384]{1,0:T(8,128)(2,1)S(1)}, bf16[288,384]{1,0:T(8,128)(2,1)S(1)}, u32[]{:S(2)}, u32[]{:S(2)}) collective-permute-start(bf16[288,384]{1,0:T(8,128)(2,1)S(1)} %get-tuple-element.59), channel_id=1, source_target_pairs={{0,16},{16,32},{32,48},{48,64},{64,80},{80,96},{96,112},{112,0},{1... | collective-permute-start | bytes 663560 | tf_op jit(solution)/shard_map/projection/ppermute | solution.py:30
  31.2 10.1 %collective-permute-start.3 = (bf16[288,384]{1,0:T(8,128)(2,1)S(1)}, bf16[288,384]{1,0:T(8,128)(2,1)S(1)}, u32[]{:S(2)}, u32[]{:S(2)}) collective-permute-start(bf16[288,384]{1,0:T(8,128)(2,1)S(1)} %get-tuple-element.60), channel_id=1, source_target_pairs={{0,112},{16,0},{32,16},{48,32},{64,48},{80,64},{96,80},{112,96},{1... | collective-permute-start | bytes 663560 | tf_op jit(solution)/shard_map/projection/ppermute | solution.py:30
  36.9 31.9 %copy-start = (bf16[288,768]{1,0:T(8,128)(2,1)S(1)}, bf16[288,768]{1,0:T(8,128)(2,1)}, u32[]{:S(2)}) copy-start(bf16[288,768]{1,0:T(8,128)(2,1)} %get-tuple-element.76.near_up) | copy-start | bytes 1327108
  36.9 31.9 %copy-start.1 = (bf16[288,768]{1,0:T(8,128)(2,1)S(1)}, bf16[288,768]{1,0:T(8,128)(2,1)}, u32[]{:S(2)}) copy-start(bf16[288,768]{1,0:T(8,128)(2,1)} %get-tuple-element.77.near_down) | copy-start | bytes 1327108
  42.7 29.7 %copy-start.6 = (s32[16]{0:T(128)S(1)}, s32[16]{0:T(128)}, u32[]{:S(2)}) copy-start(s32[16]{0:T(128)} %pos.1) | copy-start | bytes 196
  42.7 37.6 %copy-start.2 = (bf16[288,768]{1,0:T(8,128)(2,1)S(1)}, bf16[288,768]{1,0:T(8,128)(2,1)}, u32[]{:S(2)}) copy-start(bf16[288,768]{1,0:T(8,128)(2,1)} %get-tuple-element.80.near) | copy-start | bytes 1327108
  42.7 12.6 %collective-permute-start.5 = (bf16[288,768]{1,0:T(8,128)(2,1)S(1)}, bf16[288,768]{1,0:T(8,128)(2,1)S(1)}, u32[]{:S(2)}, u32[]{:S(2)}) collective-permute-start(bf16[288,768]{1,0:T(8,128)(2,1)S(1)} %get-tuple-element.70), channel_id=1, source_target_pairs={{0,16},{16,32},{32,48},{48,64},{64,80},{80,96},{96,112},{112,0},{1... | collective-permute-start | bytes 1327112 | tf_op jit(solution)/shard_map/projection/ppermute | solution.py:30
  43.0 12.3 %collective-permute-start.6 = (bf16[288,768]{1,0:T(8,128)(2,1)S(1)}, bf16[288,768]{1,0:T(8,128)(2,1)S(1)}, u32[]{:S(2)}, u32[]{:S(2)}) collective-permute-start(bf16[288,768]{1,0:T(8,128)(2,1)S(1)} %get-tuple-element.71), channel_id=1, source_target_pairs={{0,112},{16,0},{32,16},{48,32},{64,48},{80,64},{96,80},{112,96},{1... | collective-permute-start | bytes 1327112 | tf_op jit(solution)/shard_map/projection/ppermute | solution.py:30
  56.7 12.1 %collective-permute-start.7 = (bf16[288,768]{1,0:T(8,128)(2,1)S(1)}, bf16[288,768]{1,0:T(8,128)(2,1)S(1)}, u32[]{:S(2)}, u32[]{:S(2)}) collective-permute-start(bf16[288,768]{1,0:T(8,128)(2,1)S(1)} %get-tuple-element.74), channel_id=1, source_target_pairs={{0,16},{16,32},{32,48},{48,64},{64,80},{80,96},{96,112},{112,0},{1... | collective-permute-start | bytes 1327112 | tf_op jit(solution)/shard_map/projection/ppermute | solution.py:30
  58.3 10.5 %collective-permute-start.8 = (bf16[288,768]{1,0:T(8,128)(2,1)S(1)}, bf16[288,768]{1,0:T(8,128)(2,1)S(1)}, u32[]{:S(2)}, u32[]{:S(2)}) collective-permute-start(bf16[288,768]{1,0:T(8,128)(2,1)S(1)} %get-tuple-element.75), channel_id=1, source_target_pairs={{0,112},{16,0},{32,16},{48,32},{64,48},{80,64},{96,80},{112,96},{1... | collective-permute-start | bytes 1327112 | tf_op jit(solution)/shard_map/projection/ppermute | solution.py:30
  69.0 11.3 %collective-permute-start.9 = (bf16[288,768]{1,0:T(8,128)(2,1)S(1)}, bf16[288,768]{1,0:T(8,128)(2,1)S(1)}, u32[]{:S(2)}, u32[]{:S(2)}) collective-permute-start(bf16[288,768]{1,0:T(8,128)(2,1)S(1)} %get-tuple-element.78), channel_id=1, source_target_pairs={{0,16},{16,32},{32,48},{48,64},{64,80},{80,96},{96,112},{112,0},{1... | collective-permute-start | bytes 1327112 | tf_op jit(solution)/shard_map/projection/ppermute | solution.py:30
  70.9 9.4 %collective-permute-start.10 = (bf16[288,768]{1,0:T(8,128)(2,1)S(1)}, bf16[288,768]{1,0:T(8,128)(2,1)S(1)}, u32[]{:S(2)}, u32[]{:S(2)}) collective-permute-start(bf16[288,768]{1,0:T(8,128)(2,1)S(1)} %get-tuple-element.79), channel_id=1, source_target_pairs={{0,112},{16,0},{32,16},{48,32},{64,48},{80,64},{96,80},{112,96},{1... | collective-permute-start | bytes 1327112 | tf_op jit(solution)/shard_map/projection/ppermute | solution.py:30
  80.5 7.7 %collective-permute-start.11 = (bf16[288,384]{1,0:T(8,128)(2,1)S(1)}, bf16[288,384]{1,0:T(8,128)(2,1)S(1)}, u32[]{:S(2)}, u32[]{:S(2)}) collective-permute-start(bf16[288,384]{1,0:T(8,128)(2,1)S(1)} %get-tuple-element.82), channel_id=1, source_target_pairs={{0,128},{128,0},{1,129},{129,1},{2,130},{130,2},{3,131},{131,3},{4... | collective-permute-start | bytes 663560 | tf_op jit(solution)/shard_map/projection/ppermute | solution.py:30
  110.1 6.3 %collective-permute-start.12 = (bf16[512,128]{1,0:T(8,128)(2,1)S(1)}, bf16[512,128]{1,0:T(8,128)(2,1)S(1)}, u32[]{:S(2)}, u32[]{:S(2)}) collective-permute-start(bf16[512,128]{1,0:T(8,128)(2,1)S(1)} %attention.3.refs_0_), channel_id=1, source_target_pairs={{0,16},{16,32},{32,48},{48,64},{64,80},{80,96},{96,112},{112,0},{1... | collective-permute-start | bytes 393224 | tf_op jit(solution)/shard_map/output/ppermute | solution.py:30
  111.6 5.0 %collective-permute-start.13 = (bf16[512,128]{1,0:T(8,128)(2,1)S(1)}, bf16[512,128]{1,0:T(8,128)(2,1)S(1)}, u32[]{:S(2)}, u32[]{:S(2)}) collective-permute-start(bf16[512,128]{1,0:T(8,128)(2,1)S(1)} %attention.3.refs_0_), channel_id=1, source_target_pairs={{0,112},{16,0},{32,16},{48,32},{64,48},{80,64},{96,80},{112,96},{1... | collective-permute-start | bytes 393224 | tf_op jit(solution)/shard_map/output/ppermute | solution.py:30
  116.5 7.6 %collective-permute-start.14 = (bf16[512,128]{1,0:T(8,128)(2,1)S(1)}, bf16[512,128]{1,0:T(8,128)(2,1)S(1)}, u32[]{:S(2)}, u32[]{:S(2)}) collective-permute-start(bf16[512,128]{1,0:T(8,128)(2,1)S(1)} %collective-permute-done.12.refs_1_), channel_id=1, source_target_pairs={{0,16},{16,32},{32,48},{48,64},{64,80},{80,96},{96,112},{112,0},{1... | collective-permute-start | bytes 393224 | tf_op jit(solution)/shard_map/output/ppermute | solution.py:30
  118.7 6.4 %collective-permute-start.17 = (bf16[512,128]{1,0:T(8,128)(2,1)S(1)}, bf16[512,128]{1,0:T(8,128)(2,1)S(1)}, u32[]{:S(2)}, u32[]{:S(2)}) collective-permute-start(bf16[512,128]{1,0:T(8,128)(2,1)S(1)} %collective-permute-done.13.refs_7_), channel_id=1, source_target_pairs={{0,112},{16,0},{32,16},{48,32},{64,48},{80,64},{96,80},{112,96},{1... | collective-permute-start | bytes 393224 | tf_op jit(solution)/shard_map/output/ppermute | solution.py:30
  124.1 10.6 %collective-permute-start.15 = (bf16[512,128]{1,0:T(8,128)(2,1)S(1)}, bf16[512,128]{1,0:T(8,128)(2,1)S(1)}, u32[]{:S(2)}, u32[]{:S(2)}) collective-permute-start(bf16[512,128]{1,0:T(8,128)(2,1)S(1)} %collective-permute-done.14.refs_2_), channel_id=1, source_target_pairs={{0,16},{16,32},{32,48},{48,64},{64,80},{80,96},{96,112},{112,0},{1... | collective-permute-start | bytes 393224 | tf_op jit(solution)/shard_map/output/ppermute | solution.py:30
  125.1 9.6 %collective-permute-start.18 = (bf16[512,128]{1,0:T(8,128)(2,1)S(1)}, bf16[512,128]{1,0:T(8,128)(2,1)S(1)}, u32[]{:S(2)}, u32[]{:S(2)}) collective-permute-start(bf16[512,128]{1,0:T(8,128)(2,1)S(1)} %collective-permute-done.17.refs_6_), channel_id=1, source_target_pairs={{0,112},{16,0},{32,16},{48,32},{64,48},{80,64},{96,80},{112,96},{1... | collective-permute-start | bytes 393224 | tf_op jit(solution)/shard_map/output/ppermute | solution.py:30
  127.4 6.4 %collective-permute-start.16 = (bf16[256,128]{1,0:T(8,128)(2,1)S(1)}, bf16[256,128]{1,0:T(8,128)(2,1)S(1)}, u32[]{:S(2)}, u32[]{:S(2)}) collective-permute-start(bf16[256,128]{1,0:T(8,128)(2,1)S(1)} %slice.16), channel_id=1, source_target_pairs={{0,32},{16,48},{32,64},{48,80},{64,96},{80,112},{96,0},{112,16},{1... | collective-permute-start | bytes 196616 | tf_op jit(solution)/shard_map/output/ppermute | solution.py:30
  127.8 7.0 %collective-permute-start.19 = (bf16[256,128]{1,0:T(8,128)(2,1)S(1)}, bf16[256,128]{1,0:T(8,128)(2,1)S(1)}, u32[]{:S(2)}, u32[]{:S(2)}) collective-permute-start(bf16[256,128]{1,0:T(8,128)(2,1)S(1)} %slice.17), channel_id=1, source_target_pairs={{0,96},{16,112},{32,0},{48,16},{64,32},{80,48},{96,64},{112,80},{1... | collective-permute-start | bytes 196616 | tf_op jit(solution)/shard_map/output/ppermute | solution.py:30
  137.0 12.3 %copy-start.3 = (bf16[256,256]{1,0:T(8,128)(2,1)S(1)}, bf16[256,256]{1,0:T(8,128)(2,1)}, u32[]{:S(2)}) copy-start(bf16[256,256]{1,0:T(8,128)(2,1)} %hidden.1) | copy-start | bytes 393220
  137.0 12.3 %copy-start.5 = (bf16[256,256]{1,0:T(8,128)(2,1)S(1)}, bf16[256,256]{1,0:T(8,128)(2,1)}, u32[]{:S(2)}) copy-start(bf16[256,256]{1,0:T(8,128)(2,1)} %get-tuple-element.50) | copy-start | bytes 393220
  137.0 2.0 %collective-permute-start.20 = (bf16[512,512]{1,0:T(8,128)(2,1)S(1)}, bf16[512,512]{1,0:T(8,128)(2,1)S(1)}, u32[]{:S(2)}, u32[]{:S(2)}) collective-permute-start(bf16[512,512]{1,0:T(8,128)(2,1)S(1)} %get-tuple-element.93), channel_id=1, source_target_pairs={{0,8},{8,0},{1,9},{9,1},{2,10},{10,2},{3,11},{11,3},{4,12},{12,4},... | collective-permute-start | bytes 1572872 | tf_op jit(solution)/shard_map/output/ppermute | solution.py:30
  139.2 9.9 %collective-permute-start.21 = (bf16[512,256]{1,0:T(8,128)(2,1)S(1)}, bf16[512,256]{1,0:T(8,128)(2,1)S(1)}, u32[]{:S(2)}, u32[]{:S(2)}) collective-permute-start(bf16[512,256]{1,0:T(8,128)(2,1)S(1)} %fusion), channel_id=1, source_target_pairs={{0,128},{128,0},{1,129},{129,1},{2,130},{130,2},{3,131},{131,3},{4... | collective-permute-start | bytes 786440 | tf_op jit(solution)/shard_map/output/ppermute | solution.py:30
Sparse Core Ops, SparseCore 0:
  41.5 43.0 all-gather.1

commit v8 on v5

--- a/solution.py
+++ b/solution.py
@@ -457,11 +457,11 @@
     )(pltpu.with_memory_space_constraint(w, pltpu.HBM))
 
 
-def project_kernel(turned, *refs):
+def project_kernel(first, turned, *refs):
     shards, (keep, near, far), joined = refs[:Z], refs[Z : Z + 3], refs[-1]
     core, x_hi = lax.axis_index("core"), lax.axis_index("x_hi")
     for d in range(Z):
-        joined[:, d * HD : (d + 1) * HD] = shards[d][...]
+        joined[:, d * HD : (d + 1) * HD] = shards[d][first : first + TOK, :]
 
     def product(xr, cr, rows):
         column = (lax.rem(x_hi + xr, X_HI) * CORE + lax.rem(core + cr, CORE)) * TOK
@@ -478,13 +478,13 @@
         far[rows, :] = product(1, 0, rows)
         return carry
 
-    lax.fori_loop(0, 2 * TOK // size, step, 0)
-
-
-def project(w, shards):
-    rows = shards[0].shape[0]
-    return pl.pallas_call(
-        project_kernel,
+    lax.fori_loop(0, TOK // size, step, 0)
+
+
+def project(first, w, shards):
+    rows = TOK
+    return pl.pallas_call(
+        functools.partial(project_kernel, first),
         out_shape=(
             jax.ShapeDtypeStruct((rows, TOK), f32),
             jax.ShapeDtypeStruct((rows, 2 * TOK), bf16),
@@ -567,13 +567,15 @@
                 out_w, pieces[1], pieces[7] = lax.optimization_barrier(
                     (arrange(out_w), pieces[1], pieces[7])
                 )
-        keep, near, far = project(out_w, pieces)
-        near = shift(near, "core", CORE, 1).astype(f32)
-        far = (far + near[:, width_part:]).astype(bf16)
-        far = shift(far, "x_hi", X_HI, 1).astype(f32)
-        branch = (keep + near[:, :width_part] + far).reshape(2, tok_rows, width_part)
-        seqs = jnp.stack([hidden, variant]).astype(f32)
-        return (seqs + branch).astype(bf16)
+        mixed = []
+        for first, seq in ((0, hidden), (tok_rows, variant)):
+            keep, near, far = project(first, out_w, pieces)
+            near = shift(near, "core", CORE, 1).astype(f32)
+            far = (far + near[:, width_part:]).astype(bf16)
+            far = shift(far, "x_hi", X_HI, 1).astype(f32)
+            branch = keep + near[:, :width_part] + far
+            mixed.append((seq.astype(f32) + branch).astype(bf16))
+        return jnp.stack(mixed)
 
 
 def solution(mesh):

time: 156 us -> 154 us (0.987)
  waiting for transfers between devices: 54.7 us -> 50.3 us
  starting transfers between devices: 39.7 us -> 42.5 us
    ppermute x21 -> x23, waiting for transfers between devices: 54.7 us -> 50.3 us  [shift(): lax.ppermute(value, axis, [(i, (i + distance) % size) for i in range(size)])]
    ppermute x21 -> x23, starting transfers between devices: 31.2 us -> 34 us  [shift(): lax.ppermute(value, axis, [(i, (i + distance) % size) for i in range(size)])]
  transfers between devices with their start and end apart: 23 -> 25, of which waited for: 13 -> 13; matrix products, arithmetic and copies ran while one was open for 1% -> 1% of each run, Pallas kernels for 10% -> 10%
where the time goes in v8:
time: 154 us; the launch traced here: 153 us
  waiting for transfers between devices  50.3 us (33%)
  starting transfers between devices  42.5 us (28%)
  Pallas kernels  25.8 us (17%)
  blocking collectives  17.6 us (11%)
  between operations  13.7 us (9%)
  other arithmetic  1.78 us (1%)
  local copies, waits for them, and re-layouts  1.56 us (1%)
    ppermute x23, waiting for transfers between devices, shift(): lax.ppermute(value, axis, [(i, (i + distance) % size) for i in range(size)])  50.3 us
    ppermute x23, starting transfers between devices, shift(): lax.ppermute(value, axis, [(i, (i + distance) % size) for i in range(size)])  34 us
    all_to_all x1, blocking collectives, shards(): blocks = lax.all_to_all(payload, CTX, 0, 0, tiled=True)  17.6 us
    all_to_all x1, starting transfers between devices, shards(): shared = lax.all_to_all(share, 'z', 0, 0, tiled=True)  8.48 us
    pallas_call x2, Pallas kernels, pick_columns(): pl.pallas_call(functools.partial(columns_kernel, ks), out_shape=(columns,...  5.79 us
    pallas_call x2, Pallas kernels, partials(): pl.pallas_call(functools.partial(partial_kernel, ks), out_shape=shapes, i...  5.77 us
    pallas_call x1, Pallas kernels, make_variant(): pl.pallas_call(variant_kernel, out_shape=(jax.ShapeDtypeStruct((ROWS, wid...  3.09 us
  transfers between devices with their start and end apart: 25, of which 13 were waited for; matrix products, arithmetic and copies ran while one was open for 1% of the time, Pallas kernels for 10%

profile of v8, /device:TPU:6, one launch (start us, length us, event | category | flops | bytes accessed | tf_op | source)
XLA Modules:
  0.0 153.2 jit_solution(17445386377504358415)
XLA Ops:
  6.5 3.1 %inputs.3 = (bf16[272,256]{1,0:T(8,128)(2,1)S(1)}, bf16[16,256]{1,0:T(8,128)(2,1)}, bf16[256,256]{1,0:T(8,128)(2,1)}, bf16[8,16,1024]{2,1,0:T(8,128)(2,1)}) custom-call(s32[16]{0:T(128)} %pos.1, s32[16]{0:T(128)} %base.1, s32[256]{0:T(256)} %ids.1, bf16[256,256]{1,0:T(8,128)(2,1)} %hidden.1, bf16[512,256]{1,0:T(8,128)(2,1)} %embed.1, bf16[128,8192]{1,0:T(8,128)(2,1)} %w.1), custom_call_target="tpu_custom_call" | custom-call | tf_op jit(solution)/shard_map/inputs/pallas_call | solution.py:116
  9.6 1.3 inputs.4
  10.9 0.1 collective-permute-start.1
  11.0 0.5 collective-permute-start
  11.5 1.4 collective-permute-done.sis
  12.9 0.8 copy-done.4
  13.7 4.5 %inputs.5 = (bf16[256,5376]{1,0:T(8,128)(2,1)}, bf16[256,5376]{1,0:T(8,128)(2,1)S(1)}) custom-call(bf16[256,12288]{1,0:T(8,128)(2,1)} %w.3), custom_call_target="tpu_custom_call" | custom-call | tf_op jit(solution)/shard_map/inputs/pallas_call | solution.py:166
  18.2 0.2 collective-permute-start.4
  18.4 8.5 %all-to-all-start = ((bf16[8,16,1024]{2,1,0:T(8,128)(2,1)}), bf16[8,16,1024]{2,1,0:T(8,128)(2,1)}, u32[]{:S(2)}, u32[]{:S(2)}) async-start(bf16[8,16,1024]{2,1,0:T(8,128)(2,1)} %get-tuple-element.63), calls=%async_computation | async-start | bytes 524288 | tf_op jit(solution)/shard_map/inputs/all_to_all | solution.py:520
  26.9 0.0 all-gather.2.cloned.1.call-start
  27.0 0.8 dynamic-slice.3
  27.7 1.5 projection.6
  29.2 2.0 %collective-permute-start.2 = (bf16[288,384]{1,0:T(8,128)(2,1)S(1)}, bf16[288,384]{1,0:T(8,128)(2,1)S(1)}, u32[]{:S(2)}, u32[]{:S(2)}) collective-permute-start(bf16[288,384]{1,0:T(8,128)(2,1)S(1)} %get-tuple-element.61), channel_id=1, source_target_pairs={{0,16},{16,32},{32,48},{48,64},{64,80},{80,96},{96,112},{112,0},{1... | collective-permute-start | bytes 663560 | tf_op jit(solution)/shard_map/projection/ppermute | solution.py:30
  31.2 1.3 collective-permute-start.3
  32.6 4.3 %projection.7 = (bf16[288,768]{1,0:T(8,128)(2,1)}, bf16[288,768]{1,0:T(8,128)(2,1)}, bf16[288,768]{1,0:T(8,128)(2,1)}, bf16[288,768]{1,0:T(8,128)(2,1)}, bf16[28...) custom-call(bf16[272,256]{1,0:T(8,128)(2,1)S(1)} %get-tuple-element.54.own, ...), custom_call_target="tpu_custom_call" | custom-call | flops 1497366528 | bytes 11010048 | tf_op jit(solution)/shard_map/projection/pallas_call | solution.py:235
  36.9 4.5 %collective-permute-done.2.up = bf16[288,384]{1,0:T(8,128)(2,1)S(1)} collective-permute-done((bf16[288,384]{1,0:T(8,128)(2,1)S(1)}, bf16[288,384]{1,0:T(8,128)(2,1)S(1)}, u32[]{:S(2)}, u32[]{:S(2)}) %collective-permute-start.2) | collective-permute-done | bytes 221216 | tf_op jit(solution)/shard_map/projection/ppermute | solution.py:30
  41.4 0.0 all-gather.2.cloned.1.call-update
  41.4 1.3 projection.8
  42.7 0.0 copy-start.6
  42.7 0.3 collective-permute-start.5
  43.1 3.0 %collective-permute-start.6 = (bf16[288,768]{1,0:T(8,128)(2,1)S(1)}, bf16[288,768]{1,0:T(8,128)(2,1)S(1)}, u32[]{:S(2)}, u32[]{:S(2)}) collective-permute-start(bf16[288,768]{1,0:T(8,128)(2,1)S(1)} %get-tuple-element.73), channel_id=1, source_target_pairs={{0,112},{16,0},{32,16},{48,32},{64,48},{80,64},{96,80},{112,96},{1... | collective-permute-start | bytes 1327112 | tf_op jit(solution)/shard_map/projection/ppermute | solution.py:30
  46.0 9.3 %collective-permute-done.5.up = bf16[288,768]{1,0:T(8,128)(2,1)S(1)} collective-permute-done((bf16[288,768]{1,0:T(8,128)(2,1)S(1)}, bf16[288,768]{1,0:T(8,128)(2,1)S(1)}, u32[]{:S(2)}, u32[]{:S(2)}) %collective-permute-start.5) | collective-permute-done | bytes 442400 | tf_op jit(solution)/shard_map/projection/ppermute | solution.py:30
  55.3 1.4 projection.9
  56.7 1.6 %collective-permute-start.7 = (bf16[288,768]{1,0:T(8,128)(2,1)S(1)}, bf16[288,768]{1,0:T(8,128)(2,1)S(1)}, u32[]{:S(2)}, u32[]{:S(2)}) collective-permute-start(bf16[288,768]{1,0:T(8,128)(2,1)S(1)} %get-tuple-element.76), channel_id=1, source_target_pairs={{0,16},{16,32},{32,48},{48,64},{64,80},{80,96},{96,112},{112,0},{1... | collective-permute-start | bytes 1327112 | tf_op jit(solution)/shard_map/projection/ppermute | solution.py:30
  58.3 1.7 %collective-permute-start.8 = (bf16[288,768]{1,0:T(8,128)(2,1)S(1)}, bf16[288,768]{1,0:T(8,128)(2,1)S(1)}, u32[]{:S(2)}, u32[]{:S(2)}) collective-permute-start(bf16[288,768]{1,0:T(8,128)(2,1)S(1)} %get-tuple-element.77), channel_id=1, source_target_pairs={{0,112},{16,0},{32,16},{48,32},{64,48},{80,64},{96,80},{112,96},{1... | collective-permute-start | bytes 1327112 | tf_op jit(solution)/shard_map/projection/ppermute | solution.py:30
  60.0 8.8 %collective-permute-done.7.up = bf16[288,768]{1,0:T(8,128)(2,1)S(1)} collective-permute-done((bf16[288,768]{1,0:T(8,128)(2,1)S(1)}, bf16[288,768]{1,0:T(8,128)(2,1)S(1)}, u32[]{:S(2)}, u32[]{:S(2)}) %collective-permute-start.7) | collective-permute-done | bytes 442400 | tf_op jit(solution)/shard_map/projection/ppermute | solution.py:30
  68.8 0.2 projection.10
  69.0 1.8 %collective-permute-start.9 = (bf16[288,768]{1,0:T(8,128)(2,1)S(1)}, bf16[288,768]{1,0:T(8,128)(2,1)S(1)}, u32[]{:S(2)}, u32[]{:S(2)}) collective-permute-start(bf16[288,768]{1,0:T(8,128)(2,1)S(1)} %get-tuple-element.80), channel_id=1, source_target_pairs={{0,16},{16,32},{32,48},{48,64},{64,80},{80,96},{96,112},{112,0},{1... | collective-permute-start | bytes 1327112 | tf_op jit(solution)/shard_map/projection/ppermute | solution.py:30
  70.9 1.5 collective-permute-start.10
  72.4 7.9 %collective-permute-done.9.up = bf16[288,768]{1,0:T(8,128)(2,1)S(1)} collective-permute-done((bf16[288,768]{1,0:T(8,128)(2,1)S(1)}, bf16[288,768]{1,0:T(8,128)(2,1)S(1)}, u32[]{:S(2)}, u32[]{:S(2)}) %collective-permute-start.9) | collective-permute-done | bytes 442400 | tf_op jit(solution)/shard_map/projection/ppermute | solution.py:30
  80.3 0.2 projection.11
  80.5 1.7 %collective-permute-start.11 = (bf16[288,384]{1,0:T(8,128)(2,1)S(1)}, bf16[288,384]{1,0:T(8,128)(2,1)S(1)}, u32[]{:S(2)}, u32[]{:S(2)}) collective-permute-start(bf16[288,384]{1,0:T(8,128)(2,1)S(1)} %get-tuple-element.84), channel_id=1, source_target_pairs={{0,128},{128,0},{1,129},{129,1},{2,130},{130,2},{3,131},{131,3},{4... | collective-permute-start | bytes 663560 | tf_op jit(solution)/shard_map/projection/ppermute | solution.py:30
  82.1 0.6 fusion.10
  82.7 0.1 pad_maximum_fusion.1
  82.9 5.3 %collective-permute-done.11.other = bf16[288,384]{1,0:T(8,128)(2,1)S(1)} collective-permute-done((bf16[288,384]{1,0:T(8,128)(2,1)S(1)}, bf16[288,384]{1,0:T(8,128)(2,1)S(1)}, u32[]{:S(2)}, u32[]{:S(2)}) %collective-permute-start.11) | collective-permute-done | bytes 221216 | tf_op jit(solution)/shard_map/projection/ppermute | solution.py:30
  88.2 1.3 attention.2
  89.5 17.6 %all_to_all.10.blocks = bf16[8,288,256]{2,1,0:T(8,128)(2,1)S(1)} all-to-all(bf16[8,288,256]{2,1,0:T(8,128)(2,1)S(1)} %get-tuple-element.87), channel_id=1, replica_groups=mesh['x_hi'=2,'z'=8,'core'=2,'x_lo'=2,'y'=4] {'x_lo','y'}, dimensions={0} | all-to-all | bytes 2359296 | tf_op jit(solution)/shard_map/attention/all_to_all | solution.py:556
  107.1 2.9 %attention.3.refs_0_ = bf16[512,128]{1,0:T(8,128)(2,1)S(1)} custom-call(bf16[512,128]{1,0:T(8,128)(2,1)S(1)} %get-tuple-element.86.queries, bf16[8,288,256]{2,1,0:T(8,128)(2,1)S(1)} %all_to_all.10.blocks), custom_call_target="tpu_custom_call" | custom-call | tf_op jit(solution)/shard_map/attention/pallas_call | solution.py:418
  110.0 0.0 all-gather.2.cloned.1.call-done.w
  110.1 1.5 %collective-permute-start.12 = (bf16[512,128]{1,0:T(8,128)(2,1)S(1)}, bf16[512,128]{1,0:T(8,128)(2,1)S(1)}, u32[]{:S(2)}, u32[]{:S(2)}) collective-permute-start(bf16[512,128]{1,0:T(8,128)(2,1)S(1)} %attention.3.refs_0_), channel_id=1, source_target_pairs={{0,16},{16,32},{32,48},{48,64},{64,80},{80,96},{96,112},{112,0},{1... | collective-permute-start | bytes 393224 | tf_op jit(solution)/shard_map/output/ppermute | solution.py:30
  111.6 1.8 %collective-permute-start.13 = (bf16[512,128]{1,0:T(8,128)(2,1)S(1)}, bf16[512,128]{1,0:T(8,128)(2,1)S(1)}, u32[]{:S(2)}, u32[]{:S(2)}) collective-permute-start(bf16[512,128]{1,0:T(8,128)(2,1)S(1)} %attention.3.refs_0_), channel_id=1, source_target_pairs={{0,112},{16,0},{32,16},{48,32},{64,48},{80,64},{96,80},{112,96},{1... | collective-permute-start | bytes 393224 | tf_op jit(solution)/shard_map/output/ppermute | solution.py:30
  113.4 1.6 %output.3.turned = bf16[1024,1024]{1,0:T(8,128)(2,1)S(1)} custom-call(bf16[8,128,1024]{2,1,0:T(8,128)(2,1)} %all-gather.2.cloned.1.call-done.w), custom_call_target="tpu_custom_call" | custom-call | tf_op jit(solution)/shard_map/output/pallas_call | solution.py:450
  115.0 1.4 collective-permute-done.12.refs_1_
  116.3 1.0 collective-permute-done.13.refs_7_
  117.3 1.5 collective-permute-start.14
  118.8 2.2 %collective-permute-start.17 = (bf16[512,128]{1,0:T(8,128)(2,1)S(1)}, bf16[512,128]{1,0:T(8,128)(2,1)S(1)}, u32[]{:S(2)}, u32[]{:S(2)}) collective-permute-start(bf16[512,128]{1,0:T(8,128)(2,1)S(1)} %collective-permute-done.13.refs_7_), channel_id=1, source_target_pairs={{0,112},{16,0},{32,16},{48,32},{64,48},{80,64},{96,80},{112,96},{1... | collective-permute-start | bytes 393224 | tf_op jit(solution)/shard_map/output/ppermute | solution.py:30
  121.0 4.0 %collective-permute-start.16 = (bf16[512,128]{1,0:T(8,128)(2,1)S(1)}, bf16[512,128]{1,0:T(8,128)(2,1)S(1)}, u32[]{:S(2)}, u32[]{:S(2)}) collective-permute-start(bf16[512,128]{1,0:T(8,128)(2,1)S(1)} %attention.3.refs_0_), channel_id=1, source_target_pairs={{0,64},{16,80},{32,96},{48,112},{64,0},{80,16},{96,32},{112,48},{1... | collective-permute-start | bytes 393224 | tf_op jit(solution)/shard_map/output/ppermute | solution.py:30
  125.0 0.4 collective-permute-start.15
  125.4 0.4 collective-permute-done.17.refs_6_
  125.8 2.4 %collective-permute-start.18 = (bf16[512,128]{1,0:T(8,128)(2,1)S(1)}, bf16[512,128]{1,0:T(8,128)(2,1)S(1)}, u32[]{:S(2)}, u32[]{:S(2)}) collective-permute-start(bf16[512,128]{1,0:T(8,128)(2,1)S(1)} %collective-permute-done.17.refs_6_), channel_id=1, source_target_pairs={{0,112},{16,0},{32,16},{48,32},{64,48},{80,64},{96,80},{112,96},{1... | collective-permute-start | bytes 393224 | tf_op jit(solution)/shard_map/output/ppermute | solution.py:30
  128.2 3.2 %collective-permute-done.16.refs_4_ = bf16[512,128]{1,0:T(8,128)(2,1)S(1)} collective-permute-done((bf16[512,128]{1,0:T(8,128)(2,1)S(1)}, bf16[512,128]{1,0:T(8,128)(2,1)S(1)}, u32[]{:S(2)}, u32[]{:S(2)}) %collective-permute-start.16) | collective-permute-done | bytes 131104 | tf_op jit(solution)/shard_map/output/ppermute | solution.py:30
  131.4 1.3 collective-permute-done.15.refs_3_
  132.7 1.1 output.4
  133.8 0.1 collective-permute-start.19
  133.9 1.1 output.5
  135.0 0.0 copy-start.3
  135.0 0.6 collective-permute-start.21
  135.7 1.7 %collective-permute-start.20 = (bf16[256,256]{1,0:T(8,128)(2,1)S(1)}, bf16[256,256]{1,0:T(8,128)(2,1)S(1)}, u32[]{:S(2)}, u32[]{:S(2)}) collective-permute-start(bf16[256,256]{1,0:T(8,128)(2,1)S(1)} %fusion.4), channel_id=1, source_target_pairs={{0,128},{128,0},{1,129},{129,1},{2,130},{130,2},{3,131},{131,3},{4... | collective-permute-start | bytes 393224 | tf_op jit(solution)/shard_map/output/ppermute | solution.py:30
  137.5 2.1 %collective-permute-start.22 = (bf16[256,256]{1,0:T(8,128)(2,1)S(1)}, bf16[256,256]{1,0:T(8,128)(2,1)S(1)}, u32[]{:S(2)}, u32[]{:S(2)}) collective-permute-start(bf16[256,256]{1,0:T(8,128)(2,1)S(1)} %fusion), channel_id=1, source_target_pairs={{0,128},{128,0},{1,129},{129,1},{2,130},{130,2},{3,131},{131,3},{4... | collective-permute-start | bytes 393224 | tf_op jit(solution)/shard_map/output/ppermute | solution.py:30
  139.5 4.1 %collective-permute-done.20 = bf16[256,256]{1,0:T(8,128)(2,1)S(1)} collective-permute-done((bf16[256,256]{1,0:T(8,128)(2,1)S(1)}, bf16[256,256]{1,0:T(8,128)(2,1)S(1)}, u32[]{:S(2)}, u32[]{:S(2)}) %collective-permute-start.20) | collective-permute-done | bytes 131104 | tf_op jit(solution)/shard_map/output/ppermute | solution.py:30
  143.6 0.1 fusion.8
  143.7 1.8 %collective-permute-done.22 = bf16[256,256]{1,0:T(8,128)(2,1)S(1)} collective-permute-done((bf16[256,256]{1,0:T(8,128)(2,1)S(1)}, bf16[256,256]{1,0:T(8,128)(2,1)S(1)}, u32[]{:S(2)}, u32[]{:S(2)}) %collective-permute-start.22) | collective-permute-done | bytes 131104 | tf_op jit(solution)/shard_map/output/ppermute | solution.py:30
  145.5 0.1 fusion.9
  145.6 0.7 pad_maximum_fusion
  (30 shorter events, 0.3 us)
Async XLA Ops:
  10.9 2.0 %collective-permute-start.1 = (bf16[256,768]{1,0:T(8,128)(2,1)S(1)}, bf16[256,768]{1,0:T(8,128)(2,1)S(1)}, u32[]{:S(2)}, u32[]{:S(2)}) collective-permute-start(bf16[256,768]{1,0:T(8,128)(2,1)S(1)} %get-tuple-element.56), channel_id=1, source_target_pairs={{0,8},{8,0},{1,9},{9,1},{2,10},{10,2},{3,11},{11,3},{4,12},{12,4},... | collective-permute-start | bytes 1179656 | tf_op jit(solution)/shard_map/inputs/ppermute | solution.py:30
  11.0 1.9 %collective-permute-start = (bf16[272,256]{1,0:T(8,128)(2,1)S(1)}, bf16[272,256]{1,0:T(8,128)(2,1)S(1)}, u32[]{:S(2)}, u32[]{:S(2)}) collective-permute-start(bf16[272,256]{1,0:T(8,128)(2,1)S(1)} %get-tuple-element.54.own), channel_id=1, source_target_pairs={{0,8},{8,0},{1,9},{9,1},{2,10},{10,2},{3,11},{11,3},{4,12},{12,4},... | collective-permute-start | bytes 417800 | tf_op jit(solution)/shard_map/inputs/ppermute | solution.py:30
  12.9 0.8 copy-start.4
  18.2 14.3 %collective-permute-start.4 = (bf16[256,5376]{1,0:T(8,128)(2,1)}, bf16[256,5376]{1,0:T(8,128)(2,1)}, u32[]{:S(2)}, u32[]{:S(2)}) collective-permute-start(bf16[256,5376]{1,0:T(8,128)(2,1)} %get-tuple-element.66), channel_id=1, source_target_pairs={{0,8},{8,0},{1,9},{9,1},{2,10},{10,2},{3,11},{11,3},{4,12},{12,4},... | collective-permute-start | bytes 8257544 | tf_op jit(solution)/shard_map/inputs/ppermute | solution.py:30
  18.4 22.9 %all-to-all-start = ((bf16[8,16,1024]{2,1,0:T(8,128)(2,1)}), bf16[8,16,1024]{2,1,0:T(8,128)(2,1)}, u32[]{:S(2)}, u32[]{:S(2)}) async-start(bf16[8,16,1024]{2,1,0:T(8,128)(2,1)} %get-tuple-element.63), calls=%async_computation | async-start | bytes 524288 | tf_op jit(solution)/shard_map/inputs/all_to_all | solution.py:520
  26.9 83.1 %all-gather.2.cloned.1.call-start = ((), (), s32[]{:S(2)}) async-start(), calls=%async_computation.2 | async-start | bytes 2359296 | tf_op jit(solution)/shard_map/projection/all_gather | solution.py:532
  29.2 12.2 %collective-permute-start.2 = (bf16[288,384]{1,0:T(8,128)(2,1)S(1)}, bf16[288,384]{1,0:T(8,128)(2,1)S(1)}, u32[]{:S(2)}, u32[]{:S(2)}) collective-permute-start(bf16[288,384]{1,0:T(8,128)(2,1)S(1)} %get-tuple-element.61), channel_id=1, source_target_pairs={{0,16},{16,32},{32,48},{48,64},{64,80},{80,96},{96,112},{112,0},{1... | collective-permute-start | bytes 663560 | tf_op jit(solution)/shard_map/projection/ppermute | solution.py:30
  31.2 10.1 %collective-permute-start.3 = (bf16[288,384]{1,0:T(8,128)(2,1)S(1)}, bf16[288,384]{1,0:T(8,128)(2,1)S(1)}, u32[]{:S(2)}, u32[]{:S(2)}) collective-permute-start(bf16[288,384]{1,0:T(8,128)(2,1)S(1)} %get-tuple-element.62), channel_id=1, source_target_pairs={{0,112},{16,0},{32,16},{48,32},{64,48},{80,64},{96,80},{112,96},{1... | collective-permute-start | bytes 663560 | tf_op jit(solution)/shard_map/projection/ppermute | solution.py:30
  36.9 31.9 %copy-start = (bf16[288,768]{1,0:T(8,128)(2,1)S(1)}, bf16[288,768]{1,0:T(8,128)(2,1)}, u32[]{:S(2)}) copy-start(bf16[288,768]{1,0:T(8,128)(2,1)} %get-tuple-element.78.near_up) | copy-start | bytes 1327108
  36.9 31.9 %copy-start.1 = (bf16[288,768]{1,0:T(8,128)(2,1)S(1)}, bf16[288,768]{1,0:T(8,128)(2,1)}, u32[]{:S(2)}) copy-start(bf16[288,768]{1,0:T(8,128)(2,1)} %get-tuple-element.79.near_down) | copy-start | bytes 1327108
  42.7 29.7 %copy-start.6 = (s32[16]{0:T(128)S(1)}, s32[16]{0:T(128)}, u32[]{:S(2)}) copy-start(s32[16]{0:T(128)} %pos.1) | copy-start | bytes 196
  42.7 37.6 %copy-start.2 = (bf16[288,768]{1,0:T(8,128)(2,1)S(1)}, bf16[288,768]{1,0:T(8,128)(2,1)}, u32[]{:S(2)}) copy-start(bf16[288,768]{1,0:T(8,128)(2,1)} %get-tuple-element.82.near) | copy-start | bytes 1327108
  42.7 12.6 %collective-permute-start.5 = (bf16[288,768]{1,0:T(8,128)(2,1)S(1)}, bf16[288,768]{1,0:T(8,128)(2,1)S(1)}, u32[]{:S(2)}, u32[]{:S(2)}) collective-permute-start(bf16[288,768]{1,0:T(8,128)(2,1)S(1)} %get-tuple-element.72), channel_id=1, source_target_pairs={{0,16},{16,32},{32,48},{48,64},{64,80},{80,96},{96,112},{112,0},{1... | collective-permute-start | bytes 1327112 | tf_op jit(solution)/shard_map/projection/ppermute | solution.py:30
  43.1 12.3 %collective-permute-start.6 = (bf16[288,768]{1,0:T(8,128)(2,1)S(1)}, bf16[288,768]{1,0:T(8,128)(2,1)S(1)}, u32[]{:S(2)}, u32[]{:S(2)}) collective-permute-start(bf16[288,768]{1,0:T(8,128)(2,1)S(1)} %get-tuple-element.73), channel_id=1, source_target_pairs={{0,112},{16,0},{32,16},{48,32},{64,48},{80,64},{96,80},{112,96},{1... | collective-permute-start | bytes 1327112 | tf_op jit(solution)/shard_map/projection/ppermute | solution.py:30
  56.7 12.1 %collective-permute-start.7 = (bf16[288,768]{1,0:T(8,128)(2,1)S(1)}, bf16[288,768]{1,0:T(8,128)(2,1)S(1)}, u32[]{:S(2)}, u32[]{:S(2)}) collective-permute-start(bf16[288,768]{1,0:T(8,128)(2,1)S(1)} %get-tuple-element.76), channel_id=1, source_target_pairs={{0,16},{16,32},{32,48},{48,64},{64,80},{80,96},{96,112},{112,0},{1... | collective-permute-start | bytes 1327112 | tf_op jit(solution)/shard_map/projection/ppermute | solution.py:30
  58.3 10.5 %collective-permute-start.8 = (bf16[288,768]{1,0:T(8,128)(2,1)S(1)}, bf16[288,768]{1,0:T(8,128)(2,1)S(1)}, u32[]{:S(2)}, u32[]{:S(2)}) collective-permute-start(bf16[288,768]{1,0:T(8,128)(2,1)S(1)} %get-tuple-element.77), channel_id=1, source_target_pairs={{0,112},{16,0},{32,16},{48,32},{64,48},{80,64},{96,80},{112,96},{1... | collective-permute-start | bytes 1327112 | tf_op jit(solution)/shard_map/projection/ppermute | solution.py:30
  69.0 11.3 %collective-permute-start.9 = (bf16[288,768]{1,0:T(8,128)(2,1)S(1)}, bf16[288,768]{1,0:T(8,128)(2,1)S(1)}, u32[]{:S(2)}, u32[]{:S(2)}) collective-permute-start(bf16[288,768]{1,0:T(8,128)(2,1)S(1)} %get-tuple-element.80), channel_id=1, source_target_pairs={{0,16},{16,32},{32,48},{48,64},{64,80},{80,96},{96,112},{112,0},{1... | collective-permute-start | bytes 1327112 | tf_op jit(solution)/shard_map/projection/ppermute | solution.py:30
  70.9 9.4 %collective-permute-start.10 = (bf16[288,768]{1,0:T(8,128)(2,1)S(1)}, bf16[288,768]{1,0:T(8,128)(2,1)S(1)}, u32[]{:S(2)}, u32[]{:S(2)}) collective-permute-start(bf16[288,768]{1,0:T(8,128)(2,1)S(1)} %get-tuple-element.81), channel_id=1, source_target_pairs={{0,112},{16,0},{32,16},{48,32},{64,48},{80,64},{96,80},{112,96},{1... | collective-permute-start | bytes 1327112 | tf_op jit(solution)/shard_map/projection/ppermute | solution.py:30
  80.5 7.7 %collective-permute-start.11 = (bf16[288,384]{1,0:T(8,128)(2,1)S(1)}, bf16[288,384]{1,0:T(8,128)(2,1)S(1)}, u32[]{:S(2)}, u32[]{:S(2)}) collective-permute-start(bf16[288,384]{1,0:T(8,128)(2,1)S(1)} %get-tuple-element.84), channel_id=1, source_target_pairs={{0,128},{128,0},{1,129},{129,1},{2,130},{130,2},{3,131},{131,3},{4... | collective-permute-start | bytes 663560 | tf_op jit(solution)/shard_map/projection/ppermute | solution.py:30
  110.1 6.3 %collective-permute-start.12 = (bf16[512,128]{1,0:T(8,128)(2,1)S(1)}, bf16[512,128]{1,0:T(8,128)(2,1)S(1)}, u32[]{:S(2)}, u32[]{:S(2)}) collective-permute-start(bf16[512,128]{1,0:T(8,128)(2,1)S(1)} %attention.3.refs_0_), channel_id=1, source_target_pairs={{0,16},{16,32},{32,48},{48,64},{64,80},{80,96},{96,112},{112,0},{1... | collective-permute-start | bytes 393224 | tf_op jit(solution)/shard_map/output/ppermute | solution.py:30
  111.6 5.7 %collective-permute-start.13 = (bf16[512,128]{1,0:T(8,128)(2,1)S(1)}, bf16[512,128]{1,0:T(8,128)(2,1)S(1)}, u32[]{:S(2)}, u32[]{:S(2)}) collective-permute-start(bf16[512,128]{1,0:T(8,128)(2,1)S(1)} %attention.3.refs_0_), channel_id=1, source_target_pairs={{0,112},{16,0},{32,16},{48,32},{64,48},{80,64},{96,80},{112,96},{1... | collective-permute-start | bytes 393224 | tf_op jit(solution)/shard_map/output/ppermute | solution.py:30
  117.3 7.7 %collective-permute-start.14 = (bf16[512,128]{1,0:T(8,128)(2,1)S(1)}, bf16[512,128]{1,0:T(8,128)(2,1)S(1)}, u32[]{:S(2)}, u32[]{:S(2)}) collective-permute-start(bf16[512,128]{1,0:T(8,128)(2,1)S(1)} %collective-permute-done.12.refs_1_), channel_id=1, source_target_pairs={{0,16},{16,32},{32,48},{48,64},{64,80},{80,96},{96,112},{112,0},{1... | collective-permute-start | bytes 393224 | tf_op jit(solution)/shard_map/output/ppermute | solution.py:30
  118.8 7.0 %collective-permute-start.17 = (bf16[512,128]{1,0:T(8,128)(2,1)S(1)}, bf16[512,128]{1,0:T(8,128)(2,1)S(1)}, u32[]{:S(2)}, u32[]{:S(2)}) collective-permute-start(bf16[512,128]{1,0:T(8,128)(2,1)S(1)} %collective-permute-done.13.refs_7_), channel_id=1, source_target_pairs={{0,112},{16,0},{32,16},{48,32},{64,48},{80,64},{96,80},{112,96},{1... | collective-permute-start | bytes 393224 | tf_op jit(solution)/shard_map/output/ppermute | solution.py:30
  121.0 10.4 %collective-permute-start.16 = (bf16[512,128]{1,0:T(8,128)(2,1)S(1)}, bf16[512,128]{1,0:T(8,128)(2,1)S(1)}, u32[]{:S(2)}, u32[]{:S(2)}) collective-permute-start(bf16[512,128]{1,0:T(8,128)(2,1)S(1)} %attention.3.refs_0_), channel_id=1, source_target_pairs={{0,64},{16,80},{32,96},{48,112},{64,0},{80,16},{96,32},{112,48},{1... | collective-permute-start | bytes 393224 | tf_op jit(solution)/shard_map/output/ppermute | solution.py:30
  125.0 7.7 %collective-permute-start.15 = (bf16[512,128]{1,0:T(8,128)(2,1)S(1)}, bf16[512,128]{1,0:T(8,128)(2,1)S(1)}, u32[]{:S(2)}, u32[]{:S(2)}) collective-permute-start(bf16[512,128]{1,0:T(8,128)(2,1)S(1)} %collective-permute-done.14.refs_2_), channel_id=1, source_target_pairs={{0,16},{16,32},{32,48},{48,64},{64,80},{80,96},{96,112},{112,0},{1... | collective-permute-start | bytes 393224 | tf_op jit(solution)/shard_map/output/ppermute | solution.py:30
  125.8 6.8 %collective-permute-start.18 = (bf16[512,128]{1,0:T(8,128)(2,1)S(1)}, bf16[512,128]{1,0:T(8,128)(2,1)S(1)}, u32[]{:S(2)}, u32[]{:S(2)}) collective-permute-start(bf16[512,128]{1,0:T(8,128)(2,1)S(1)} %collective-permute-done.17.refs_6_), channel_id=1, source_target_pairs={{0,112},{16,0},{32,16},{48,32},{64,48},{80,64},{96,80},{112,96},{1... | collective-permute-start | bytes 393224 | tf_op jit(solution)/shard_map/output/ppermute | solution.py:30
  133.8 1.8 %collective-permute-start.19 = (bf16[256,512]{1,0:T(8,128)(2,1)S(1)}, bf16[256,512]{1,0:T(8,128)(2,1)S(1)}, u32[]{:S(2)}, u32[]{:S(2)}) collective-permute-start(bf16[256,512]{1,0:T(8,128)(2,1)S(1)} %get-tuple-element.95), channel_id=1, source_target_pairs={{0,8},{8,0},{1,9},{9,1},{2,10},{10,2},{3,11},{11,3},{4,12},{12,4},... | collective-permute-start | bytes 786440 | tf_op jit(solution)/shard_map/output/ppermute | solution.py:30
  135.0 8.7 %copy-start.3 = (bf16[256,256]{1,0:T(8,128)(2,1)S(1)}, bf16[256,256]{1,0:T(8,128)(2,1)}, u32[]{:S(2)}) copy-start(bf16[256,256]{1,0:T(8,128)(2,1)} %hidden.1) | copy-start | bytes 393220
  135.0 10.5 %copy-start.5 = (bf16[256,256]{1,0:T(8,128)(2,1)S(1)}, bf16[256,256]{1,0:T(8,128)(2,1)}, u32[]{:S(2)}) copy-start(bf16[256,256]{1,0:T(8,128)(2,1)} %get-tuple-element.97) | copy-start | bytes 393220
  135.0 2.4 %collective-permute-start.21 = (bf16[256,512]{1,0:T(8,128)(2,1)S(1)}, bf16[256,512]{1,0:T(8,128)(2,1)S(1)}, u32[]{:S(2)}, u32[]{:S(2)}) collective-permute-start(bf16[256,512]{1,0:T(8,128)(2,1)S(1)} %get-tuple-element.99), channel_id=1, source_target_pairs={{0,8},{8,0},{1,9},{9,1},{2,10},{10,2},{3,11},{11,3},{4,12},{12,4},... | collective-permute-start | bytes 786440 | tf_op jit(solution)/shard_map/output/ppermute | solution.py:30
  135.7 7.9 %collective-permute-start.20 = (bf16[256,256]{1,0:T(8,128)(2,1)S(1)}, bf16[256,256]{1,0:T(8,128)(2,1)S(1)}, u32[]{:S(2)}, u32[]{:S(2)}) collective-permute-start(bf16[256,256]{1,0:T(8,128)(2,1)S(1)} %fusion.4), channel_id=1, source_target_pairs={{0,128},{128,0},{1,129},{129,1},{2,130},{130,2},{3,131},{131,3},{4... | collective-permute-start | bytes 393224 | tf_op jit(solution)/shard_map/output/ppermute | solution.py:30
  137.5 8.1 %collective-permute-start.22 = (bf16[256,256]{1,0:T(8,128)(2,1)S(1)}, bf16[256,256]{1,0:T(8,128)(2,1)S(1)}, u32[]{:S(2)}, u32[]{:S(2)}) collective-permute-start(bf16[256,256]{1,0:T(8,128)(2,1)S(1)} %fusion), channel_id=1, source_target_pairs={{0,128},{128,0},{1,129},{129,1},{2,130},{130,2},{3,131},{131,3},{4... | collective-permute-start | bytes 393224 | tf_op jit(solution)/shard_map/output/ppermute | solution.py:30
Sparse Core Ops, SparseCore 0:
  41.5 43.0 all-gather.1

commit v9 on v8

--- a/solution.py
+++ b/solution.py
@@ -134,41 +134,45 @@
     )(*(pltpu.with_memory_space_constraint(v, pltpu.HBM) for v in args))
 
 
-def column_copies(ks, w, send, own, sems):
+def column_copies(ks, sister, w, out, sems):
     z, core, x_hi = lax.axis_index("z"), lax.axis_index("core"), lax.axis_index("x_hi")
+    whose = 1 - core if sister else core
     copies = []
-    for index, (whose, out) in enumerate(((1 - core, send), (core, own))):
-        for i, k in enumerate(ks):
-            for xr in range(X_HI):
-                head_pair = lax.rem(x_hi + xr, X_HI) * Z + lax.rem(z + k, Z)
-                slot = i * X_HI + xr
-                start = pl.multiple_of((head_pair * 2 + whose) * QKV, HD)
-                copies.append(
-                    pltpu.make_async_copy(
-                        w.at[:, pl.ds(start, QKV)],
-                        out.at[:, slot * QKV : (slot + 1) * QKV],
-                        sems.at[index, slot],
-                    )
+    for i, k in enumerate(ks):
+        for xr in range(X_HI):
+            head_pair = lax.rem(x_hi + xr, X_HI) * Z + lax.rem(z + k, Z)
+            slot = i * X_HI + xr
+            start = pl.multiple_of((head_pair * 2 + whose) * QKV, HD)
+            copies.append(
+                pltpu.make_async_copy(
+                    w.at[:, pl.ds(start, QKV)],
+                    out.at[:, slot * QKV : (slot + 1) * QKV],
+                    sems.at[slot],
                 )
+            )
     return copies
 
 
-def columns_kernel(ks, w, send, own, sems):
-    copies = column_copies(ks, w, send, own, sems)
+def columns_kernel(wanted, w, *refs):
+    outs, sems = refs[: len(wanted)], refs[len(wanted) :]
+    copies = []
+    for (ks, sister), out, sem in zip(wanted, outs, sems):
+        copies += column_copies(ks, sister, w, out, sem)
     for copy in copies:
         copy.start()
     for copy in copies:
         copy.wait()
 
 
-def pick_columns(ks, w):
-    columns = jax.ShapeDtypeStruct((w.shape[0], len(ks) * X_HI * QKV), bf16)
-    return pl.pallas_call(
-        functools.partial(columns_kernel, ks),
-        out_shape=(columns, columns),
+def pick_columns(wanted, w):
+    return pl.pallas_call(
+        functools.partial(columns_kernel, wanted),
+        out_shape=tuple(
+            jax.ShapeDtypeStruct((w.shape[0], len(ks) * X_HI * QKV), bf16) for ks, _ in wanted
+        ),
         in_specs=[hbm()],
-        out_specs=(vmem(), vmem()),
-        scratch_shapes=[pltpu.SemaphoreType.DMA((2, len(ks) * X_HI))],
+        out_specs=(vmem(),) * len(wanted),
+        scratch_shapes=[pltpu.SemaphoreType.DMA((len(ks) * X_HI,)) for ks, _ in wanted],
         compiler_params=limit(12),
     )(pltpu.with_memory_space_constraint(w, pltpu.HBM))
 
@@ -510,16 +514,18 @@
         )
         rows, qkv_weight = lax.optimization_barrier((rows, qkv_weight))
         rows_sis = shift(rows, "core", CORE, 1)
-        send_first, own_first = pick_columns(FIRST, qkv_weight)
+        (send_first,) = pick_columns(((FIRST, True),), qkv_weight)
         sis_first = shift(send_first, "core", CORE, 1)
-        rows_sis, sis_first, qkv_weight, share = lax.optimization_barrier(
-            (rows_sis, sis_first, qkv_weight, share)
+        start = chip_slice * 2 * width_part
+        gains = lax.dynamic_slice(gain.reshape(1, full_width), (0, start), (1, 2 * width_part))
+        rows_sis, sis_first, qkv_weight, share, gains = lax.optimization_barrier(
+            (rows_sis, sis_first, qkv_weight, share, gains)
         )
-        send_second, own_second = pick_columns(SECOND, qkv_weight)
+        send_second, own_first, own_second = pick_columns(
+            ((SECOND, True), (FIRST, False), (SECOND, False)), qkv_weight
+        )
         sis_second = shift(send_second, "core", CORE, 1)
         shared = lax.all_to_all(share, "z", 0, 0, tiled=True)
-        start = chip_slice * 2 * width_part
-        gains = lax.dynamic_slice(gain.reshape(1, full_width), (0, start), (1, 2 * width_part))
 
     with jax.named_scope("projection"):
         sis_first = pltpu.with_memory_space_constraint(sis_first, pltpu.HBM)

time: 154 us -> 155 us (level)
  transfers between devices with their start and end apart: 25 -> 25, of which waited for: 13 -> 15; matrix products, arithmetic and copies ran while one was open for 1% -> 1% of each run, Pallas kernels for 10% -> 10%
where the time goes in v9:
time: 155 us; the launch traced here: 153 us
  waiting for transfers between devices  51.6 us (33%)
  starting transfers between devices  41.5 us (27%)
  Pallas kernels  25.7 us (17%)
  blocking collectives  17.7 us (11%)
  between operations  13.6 us (9%)
  other arithmetic  1.78 us (1%)
  local copies, waits for them, and re-layouts  1.56 us (1%)
    ppermute x23, waiting for transfers between devices, shift(): lax.ppermute(value, axis, [(i, (i + distance) % size) for i in range(size)])  51.5 us
    ppermute x23, starting transfers between devices, shift(): lax.ppermute(value, axis, [(i, (i + distance) % size) for i in range(size)])  33 us
    all_to_all x1, blocking collectives, shards(): blocks = lax.all_to_all(payload, CTX, 0, 0, tiled=True)  17.7 us
    all_to_all x1, starting transfers between devices, shards(): shared = lax.all_to_all(share, 'z', 0, 0, tiled=True)  8.48 us
    pallas_call x2, Pallas kernels, partials(): pl.pallas_call(functools.partial(partial_kernel, ks), out_shape=shapes, i...  5.77 us
    pallas_call x2, Pallas kernels, pick_columns(): pl.pallas_call(functools.partial(columns_kernel, wanted), out_shape=tuple...  5.7 us
  transfers between devices with their start and end apart: 25, of which 15 were waited for; matrix products, arithmetic and copies ran while one was open for 1% of the time, Pallas kernels for 10%

profile of v9, /device:TPU:6, one launch (start us, length us, event | category | flops | bytes accessed | tf_op | source)
XLA Modules:
  0.0 153.5 jit_solution(4864247203638672311)
XLA Ops:
  6.5 3.1 %inputs.3 = (bf16[272,256]{1,0:T(8,128)(2,1)S(1)}, bf16[16,256]{1,0:T(8,128)(2,1)}, bf16[256,256]{1,0:T(8,128)(2,1)}, bf16[8,16,1024]{2,1,0:T(8,128)(2,1)}) custom-call(s32[16]{0:T(128)} %pos.1, s32[16]{0:T(128)} %base.1, s32[256]{0:T(256)} %ids.1, bf16[256,256]{1,0:T(8,128)(2,1)} %hidden.1, bf16[512,256]{1,0:T(8,128)(2,1)} %embed.1, bf16[128,8192]{1,0:T(8,128)(2,1)} %w.1), custom_call_target="tpu_custom_call" | custom-call | tf_op jit(solution)/shard_map/inputs/pallas_call | solution.py:116
  9.6 1.1 inputs.4
  10.7 0.1 collective-permute-start.1
  10.8 0.5 collective-permute-start
  11.3 0.8 dynamic-slice.3
  12.1 0.6 collective-permute-done.sis
  12.7 0.8 copy-done.4
  13.5 4.6 %inputs.5 = (bf16[256,5376]{1,0:T(8,128)(2,1)}, bf16[256,768]{1,0:T(8,128)(2,1)S(1)}, bf16[256,5376]{1,0:T(8,128)(2,1)S(1)}) custom-call(bf16[256,12288]{1,0:T(8,128)(2,1)} %w.3), custom_call_target="tpu_custom_call" | custom-call | tf_op jit(solution)/shard_map/inputs/pallas_call | solution.py:168
  18.1 0.2 collective-permute-start.4
  18.4 8.5 %all-to-all-start = ((bf16[8,16,1024]{2,1,0:T(8,128)(2,1)}), bf16[8,16,1024]{2,1,0:T(8,128)(2,1)}, u32[]{:S(2)}, u32[]{:S(2)}) async-start(bf16[8,16,1024]{2,1,0:T(8,128)(2,1)} %get-tuple-element.64), calls=%async_computation | async-start | bytes 524288 | tf_op jit(solution)/shard_map/inputs/all_to_all | solution.py:528
  26.8 0.0 all-gather.2.cloned.1.call-start
  26.9 1.5 projection.6
  28.4 2.0 %collective-permute-start.2 = (bf16[288,384]{1,0:T(8,128)(2,1)S(1)}, bf16[288,384]{1,0:T(8,128)(2,1)S(1)}, u32[]{:S(2)}, u32[]{:S(2)}) collective-permute-start(bf16[288,384]{1,0:T(8,128)(2,1)S(1)} %get-tuple-element.62), channel_id=1, source_target_pairs={{0,16},{16,32},{32,48},{48,64},{64,80},{80,96},{96,112},{112,0},{1... | collective-permute-start | bytes 663560 | tf_op jit(solution)/shard_map/projection/ppermute | solution.py:30
  30.4 1.3 collective-permute-start.3
  31.7 4.3 %projection.7 = (bf16[288,768]{1,0:T(8,128)(2,1)}, bf16[288,768]{1,0:T(8,128)(2,1)}, bf16[288,768]{1,0:T(8,128)(2,1)}, bf16[288,768]{1,0:T(8,128)(2,1)}, bf16[28...) custom-call(bf16[272,256]{1,0:T(8,128)(2,1)S(1)} %get-tuple-element.54.own, ...), custom_call_target="tpu_custom_call" | custom-call | flops 1497366528 | bytes 11010048 | tf_op jit(solution)/shard_map/projection/pallas_call | solution.py:239
  36.1 5.2 %collective-permute-done.2.up = bf16[288,384]{1,0:T(8,128)(2,1)S(1)} collective-permute-done((bf16[288,384]{1,0:T(8,128)(2,1)S(1)}, bf16[288,384]{1,0:T(8,128)(2,1)S(1)}, u32[]{:S(2)}, u32[]{:S(2)}) %collective-permute-start.2) | collective-permute-done | bytes 221216 | tf_op jit(solution)/shard_map/projection/ppermute | solution.py:30
  41.3 1.3 projection.8
  42.7 0.3 collective-permute-start.5
  43.0 3.0 %collective-permute-start.6 = (bf16[288,768]{1,0:T(8,128)(2,1)S(1)}, bf16[288,768]{1,0:T(8,128)(2,1)S(1)}, u32[]{:S(2)}, u32[]{:S(2)}) collective-permute-start(bf16[288,768]{1,0:T(8,128)(2,1)S(1)} %get-tuple-element.73), channel_id=1, source_target_pairs={{0,112},{16,0},{32,16},{48,32},{64,48},{80,64},{96,80},{112,96},{1... | collective-permute-start | bytes 1327112 | tf_op jit(solution)/shard_map/projection/ppermute | solution.py:30
  46.0 9.3 %collective-permute-done.5.up = bf16[288,768]{1,0:T(8,128)(2,1)S(1)} collective-permute-done((bf16[288,768]{1,0:T(8,128)(2,1)S(1)}, bf16[288,768]{1,0:T(8,128)(2,1)S(1)}, u32[]{:S(2)}, u32[]{:S(2)}) %collective-permute-start.5) | collective-permute-done | bytes 442400 | tf_op jit(solution)/shard_map/projection/ppermute | solution.py:30
  55.3 1.4 projection.9
  56.6 1.9 %collective-permute-start.7 = (bf16[288,768]{1,0:T(8,128)(2,1)S(1)}, bf16[288,768]{1,0:T(8,128)(2,1)S(1)}, u32[]{:S(2)}, u32[]{:S(2)}) collective-permute-start(bf16[288,768]{1,0:T(8,128)(2,1)S(1)} %get-tuple-element.76), channel_id=1, source_target_pairs={{0,16},{16,32},{32,48},{48,64},{64,80},{80,96},{96,112},{112,0},{1... | collective-permute-start | bytes 1327112 | tf_op jit(solution)/shard_map/projection/ppermute | solution.py:30
  58.5 1.4 collective-permute-start.8
  60.0 8.4 %collective-permute-done.7.up = bf16[288,768]{1,0:T(8,128)(2,1)S(1)} collective-permute-done((bf16[288,768]{1,0:T(8,128)(2,1)S(1)}, bf16[288,768]{1,0:T(8,128)(2,1)S(1)}, u32[]{:S(2)}, u32[]{:S(2)}) %collective-permute-start.7) | collective-permute-done | bytes 442400 | tf_op jit(solution)/shard_map/projection/ppermute | solution.py:30
  68.3 1.2 collective-permute-done.8.down
  69.5 0.2 projection.10
  69.7 1.5 collective-permute-start.9
  71.2 1.8 %collective-permute-start.10 = (bf16[288,768]{1,0:T(8,128)(2,1)S(1)}, bf16[288,768]{1,0:T(8,128)(2,1)S(1)}, u32[]{:S(2)}, u32[]{:S(2)}) collective-permute-start(bf16[288,768]{1,0:T(8,128)(2,1)S(1)} %get-tuple-element.81), channel_id=1, source_target_pairs={{0,112},{16,0},{32,16},{48,32},{64,48},{80,64},{96,80},{112,96},{1... | collective-permute-start | bytes 1327112 | tf_op jit(solution)/shard_map/projection/ppermute | solution.py:30
  73.1 8.1 %collective-permute-done.9.up = bf16[288,768]{1,0:T(8,128)(2,1)S(1)} collective-permute-done((bf16[288,768]{1,0:T(8,128)(2,1)S(1)}, bf16[288,768]{1,0:T(8,128)(2,1)S(1)}, u32[]{:S(2)}, u32[]{:S(2)}) %collective-permute-start.9) | collective-permute-done | bytes 442400 | tf_op jit(solution)/shard_map/projection/ppermute | solution.py:30
  81.2 0.2 projection.11
  81.4 1.7 %collective-permute-start.11 = (bf16[288,384]{1,0:T(8,128)(2,1)S(1)}, bf16[288,384]{1,0:T(8,128)(2,1)S(1)}, u32[]{:S(2)}, u32[]{:S(2)}) collective-permute-start(bf16[288,384]{1,0:T(8,128)(2,1)S(1)} %get-tuple-element.84), channel_id=1, source_target_pairs={{0,128},{128,0},{1,129},{129,1},{2,130},{130,2},{3,131},{131,3},{4... | collective-permute-start | bytes 663560 | tf_op jit(solution)/shard_map/projection/ppermute | solution.py:30
  83.0 0.6 fusion.10
  83.6 0.1 pad_maximum_fusion.1
  83.7 5.3 %collective-permute-done.11.other = bf16[288,384]{1,0:T(8,128)(2,1)S(1)} collective-permute-done((bf16[288,384]{1,0:T(8,128)(2,1)S(1)}, bf16[288,384]{1,0:T(8,128)(2,1)S(1)}, u32[]{:S(2)}, u32[]{:S(2)}) %collective-permute-start.11) | collective-permute-done | bytes 221216 | tf_op jit(solution)/shard_map/projection/ppermute | solution.py:30
  89.1 1.3 attention.2
  90.4 17.7 %all_to_all.10.blocks = bf16[8,288,256]{2,1,0:T(8,128)(2,1)S(1)} all-to-all(bf16[8,288,256]{2,1,0:T(8,128)(2,1)S(1)} %get-tuple-element.87), channel_id=1, replica_groups=mesh['x_hi'=2,'z'=8,'core'=2,'x_lo'=2,'y'=4] {'x_lo','y'}, dimensions={0} | all-to-all | bytes 2359296 | tf_op jit(solution)/shard_map/attention/all_to_all | solution.py:562
  108.1 3.0 %attention.3.refs_0_ = bf16[512,128]{1,0:T(8,128)(2,1)S(1)} custom-call(bf16[512,128]{1,0:T(8,128)(2,1)S(1)} %get-tuple-element.86.queries, bf16[8,288,256]{2,1,0:T(8,128)(2,1)S(1)} %all_to_all.10.blocks), custom_call_target="tpu_custom_call" | custom-call | tf_op jit(solution)/shard_map/attention/pallas_call | solution.py:422
  111.1 0.3 collective-permute-start.12
  111.4 3.0 %collective-permute-start.13 = (bf16[512,128]{1,0:T(8,128)(2,1)S(1)}, bf16[512,128]{1,0:T(8,128)(2,1)S(1)}, u32[]{:S(2)}, u32[]{:S(2)}) collective-permute-start(bf16[512,128]{1,0:T(8,128)(2,1)S(1)} %attention.3.refs_0_), channel_id=1, source_target_pairs={{0,112},{16,0},{32,16},{48,32},{64,48},{80,64},{96,80},{112,96},{1... | collective-permute-start | bytes 393224 | tf_op jit(solution)/shard_map/output/ppermute | solution.py:30
  114.4 1.6 %output.3.turned = bf16[1024,1024]{1,0:T(8,128)(2,1)S(1)} custom-call(bf16[8,128,1024]{2,1,0:T(8,128)(2,1)} %all-gather.2.cloned.1.call-done.w), custom_call_target="tpu_custom_call" | custom-call | tf_op jit(solution)/shard_map/output/pallas_call | solution.py:454
  116.0 1.4 collective-permute-done.12.refs_1_
  117.3 0.8 collective-permute-done.13.refs_7_
  118.1 0.4 collective-permute-start.14
  118.5 3.4 %collective-permute-start.17 = (bf16[512,128]{1,0:T(8,128)(2,1)S(1)}, bf16[512,128]{1,0:T(8,128)(2,1)S(1)}, u32[]{:S(2)}, u32[]{:S(2)}) collective-permute-start(bf16[512,128]{1,0:T(8,128)(2,1)S(1)} %collective-permute-done.13.refs_7_), channel_id=1, source_target_pairs={{0,112},{16,0},{32,16},{48,32},{64,48},{80,64},{96,80},{112,96},{1... | collective-permute-start | bytes 393224 | tf_op jit(solution)/shard_map/output/ppermute | solution.py:30
  121.8 2.8 %collective-permute-start.16 = (bf16[512,128]{1,0:T(8,128)(2,1)S(1)}, bf16[512,128]{1,0:T(8,128)(2,1)S(1)}, u32[]{:S(2)}, u32[]{:S(2)}) collective-permute-start(bf16[512,128]{1,0:T(8,128)(2,1)S(1)} %attention.3.refs_0_), channel_id=1, source_target_pairs={{0,64},{16,80},{32,96},{48,112},{64,0},{80,16},{96,32},{112,48},{1... | collective-permute-start | bytes 393224 | tf_op jit(solution)/shard_map/output/ppermute | solution.py:30
  124.7 0.1 collective-permute-done.14.refs_2_
  124.8 0.1 collective-permute-start.15
  124.9 0.3 collective-permute-done.17.refs_6_
  125.1 2.9 %collective-permute-start.18 = (bf16[512,128]{1,0:T(8,128)(2,1)S(1)}, bf16[512,128]{1,0:T(8,128)(2,1)S(1)}, u32[]{:S(2)}, u32[]{:S(2)}) collective-permute-start(bf16[512,128]{1,0:T(8,128)(2,1)S(1)} %collective-permute-done.17.refs_6_), channel_id=1, source_target_pairs={{0,112},{16,0},{32,16},{48,32},{64,48},{80,64},{96,80},{112,96},{1... | collective-permute-start | bytes 393224 | tf_op jit(solution)/shard_map/output/ppermute | solution.py:30
  128.0 2.9 %collective-permute-done.16.refs_4_ = bf16[512,128]{1,0:T(8,128)(2,1)S(1)} collective-permute-done((bf16[512,128]{1,0:T(8,128)(2,1)S(1)}, bf16[512,128]{1,0:T(8,128)(2,1)S(1)}, u32[]{:S(2)}, u32[]{:S(2)}) %collective-permute-start.16) | collective-permute-done | bytes 131104 | tf_op jit(solution)/shard_map/output/ppermute | solution.py:30
  130.9 2.0 %collective-permute-done.15.refs_3_ = bf16[512,128]{1,0:T(8,128)(2,1)S(1)} collective-permute-done((bf16[512,128]{1,0:T(8,128)(2,1)S(1)}, bf16[512,128]{1,0:T(8,128)(2,1)S(1)}, u32[]{:S(2)}, u32[]{:S(2)}) %collective-permute-start.15) | collective-permute-done | bytes 131104 | tf_op jit(solution)/shard_map/output/ppermute | solution.py:30
  133.0 1.1 output.4
  134.1 0.1 collective-permute-start.19
  134.2 1.1 output.5
  135.3 0.6 collective-permute-start.21
  135.9 0.1 convert_element_type.47
  136.0 2.1 %collective-permute-start.20 = (bf16[256,256]{1,0:T(8,128)(2,1)S(1)}, bf16[256,256]{1,0:T(8,128)(2,1)S(1)}, u32[]{:S(2)}, u32[]{:S(2)}) collective-permute-start(bf16[256,256]{1,0:T(8,128)(2,1)S(1)} %fusion.4), channel_id=1, source_target_pairs={{0,128},{128,0},{1,129},{129,1},{2,130},{130,2},{3,131},{131,3},{4... | collective-permute-start | bytes 393224 | tf_op jit(solution)/shard_map/output/ppermute | solution.py:30
  138.1 0.1 convert_element_type.52
  138.2 1.6 %collective-permute-start.22 = (bf16[256,256]{1,0:T(8,128)(2,1)S(1)}, bf16[256,256]{1,0:T(8,128)(2,1)S(1)}, u32[]{:S(2)}, u32[]{:S(2)}) collective-permute-start(bf16[256,256]{1,0:T(8,128)(2,1)S(1)} %fusion), channel_id=1, source_target_pairs={{0,128},{128,0},{1,129},{129,1},{2,130},{130,2},{3,131},{131,3},{4... | collective-permute-start | bytes 393224 | tf_op jit(solution)/shard_map/output/ppermute | solution.py:30
  139.8 4.1 %collective-permute-done.20 = bf16[256,256]{1,0:T(8,128)(2,1)S(1)} collective-permute-done((bf16[256,256]{1,0:T(8,128)(2,1)S(1)}, bf16[256,256]{1,0:T(8,128)(2,1)S(1)}, u32[]{:S(2)}, u32[]{:S(2)}) %collective-permute-start.20) | collective-permute-done | bytes 131104 | tf_op jit(solution)/shard_map/output/ppermute | solution.py:30
  143.9 0.1 fusion.8
  144.0 1.8 %collective-permute-done.22 = bf16[256,256]{1,0:T(8,128)(2,1)S(1)} collective-permute-done((bf16[256,256]{1,0:T(8,128)(2,1)S(1)}, bf16[256,256]{1,0:T(8,128)(2,1)S(1)}, u32[]{:S(2)}, u32[]{:S(2)}) %collective-permute-start.22) | collective-permute-done | bytes 131104 | tf_op jit(solution)/shard_map/output/ppermute | solution.py:30
  145.8 0.1 fusion.9
  145.9 0.7 pad_maximum_fusion
  (30 shorter events, 0.2 us)
Async XLA Ops:
  10.7 2.0 %collective-permute-start.1 = (bf16[256,768]{1,0:T(8,128)(2,1)S(1)}, bf16[256,768]{1,0:T(8,128)(2,1)S(1)}, u32[]{:S(2)}, u32[]{:S(2)}) collective-permute-start(bf16[256,768]{1,0:T(8,128)(2,1)S(1)} %inputs.4), channel_id=1, source_target_pairs={{0,8},{8,0},{1,9},{9,1},{2,10},{10,2},{3,11},{11,3},{4,12},{12,4},... | collective-permute-start | bytes 1179656 | tf_op jit(solution)/shard_map/inputs/ppermute | solution.py:30
  10.8 1.9 %collective-permute-start = (bf16[272,256]{1,0:T(8,128)(2,1)S(1)}, bf16[272,256]{1,0:T(8,128)(2,1)S(1)}, u32[]{:S(2)}, u32[]{:S(2)}) collective-permute-start(bf16[272,256]{1,0:T(8,128)(2,1)S(1)} %get-tuple-element.54.own), channel_id=1, source_target_pairs={{0,8},{8,0},{1,9},{9,1},{2,10},{10,2},{3,11},{11,3},{4,12},{12,4},... | collective-permute-start | bytes 417800 | tf_op jit(solution)/shard_map/inputs/ppermute | solution.py:30
  12.7 0.8 copy-start.4
  18.1 13.6 %collective-permute-start.4 = (bf16[256,5376]{1,0:T(8,128)(2,1)}, bf16[256,5376]{1,0:T(8,128)(2,1)}, u32[]{:S(2)}, u32[]{:S(2)}) collective-permute-start(bf16[256,5376]{1,0:T(8,128)(2,1)} %get-tuple-element.66), channel_id=1, source_target_pairs={{0,8},{8,0},{1,9},{9,1},{2,10},{10,2},{3,11},{11,3},{4,12},{12,4},... | collective-permute-start | bytes 8257544 | tf_op jit(solution)/shard_map/inputs/ppermute | solution.py:30
  18.4 22.9 %all-to-all-start = ((bf16[8,16,1024]{2,1,0:T(8,128)(2,1)}), bf16[8,16,1024]{2,1,0:T(8,128)(2,1)}, u32[]{:S(2)}, u32[]{:S(2)}) async-start(bf16[8,16,1024]{2,1,0:T(8,128)(2,1)} %get-tuple-element.64), calls=%async_computation | async-start | bytes 524288 | tf_op jit(solution)/shard_map/inputs/all_to_all | solution.py:528
  26.8 84.2 %all-gather.2.cloned.1.call-start = ((), (), s32[]{:S(2)}) async-start(), calls=%async_computation.2 | async-start | bytes 2359296 | tf_op jit(solution)/shard_map/projection/all_gather | solution.py:538
  28.4 12.9 %collective-permute-start.2 = (bf16[288,384]{1,0:T(8,128)(2,1)S(1)}, bf16[288,384]{1,0:T(8,128)(2,1)S(1)}, u32[]{:S(2)}, u32[]{:S(2)}) collective-permute-start(bf16[288,384]{1,0:T(8,128)(2,1)S(1)} %get-tuple-element.62), channel_id=1, source_target_pairs={{0,16},{16,32},{32,48},{48,64},{64,80},{80,96},{96,112},{112,0},{1... | collective-permute-start | bytes 663560 | tf_op jit(solution)/shard_map/projection/ppermute | solution.py:30
  30.4 10.9 %collective-permute-start.3 = (bf16[288,384]{1,0:T(8,128)(2,1)S(1)}, bf16[288,384]{1,0:T(8,128)(2,1)S(1)}, u32[]{:S(2)}, u32[]{:S(2)}) collective-permute-start(bf16[288,384]{1,0:T(8,128)(2,1)S(1)} %get-tuple-element.63), channel_id=1, source_target_pairs={{0,112},{16,0},{32,16},{48,32},{64,48},{80,64},{96,80},{112,96},{1... | collective-permute-start | bytes 663560 | tf_op jit(solution)/shard_map/projection/ppermute | solution.py:30
  36.0 33.5 %copy-start = (bf16[288,768]{1,0:T(8,128)(2,1)S(1)}, bf16[288,768]{1,0:T(8,128)(2,1)}, u32[]{:S(2)}) copy-start(bf16[288,768]{1,0:T(8,128)(2,1)} %get-tuple-element.78.near_up) | copy-start | bytes 1327108
  36.0 33.5 %copy-start.1 = (bf16[288,768]{1,0:T(8,128)(2,1)S(1)}, bf16[288,768]{1,0:T(8,128)(2,1)}, u32[]{:S(2)}) copy-start(bf16[288,768]{1,0:T(8,128)(2,1)} %get-tuple-element.79.near_down) | copy-start | bytes 1327108
  42.6 30.4 %copy-start.6 = (s32[16]{0:T(128)S(1)}, s32[16]{0:T(128)}, u32[]{:S(2)}) copy-start(s32[16]{0:T(128)} %pos.1) | copy-start | bytes 196
  42.6 38.5 %copy-start.2 = (bf16[288,768]{1,0:T(8,128)(2,1)S(1)}, bf16[288,768]{1,0:T(8,128)(2,1)}, u32[]{:S(2)}) copy-start(bf16[288,768]{1,0:T(8,128)(2,1)} %get-tuple-element.82.near) | copy-start | bytes 1327108
  42.7 12.6 %collective-permute-start.5 = (bf16[288,768]{1,0:T(8,128)(2,1)S(1)}, bf16[288,768]{1,0:T(8,128)(2,1)S(1)}, u32[]{:S(2)}, u32[]{:S(2)}) collective-permute-start(bf16[288,768]{1,0:T(8,128)(2,1)S(1)} %get-tuple-element.72), channel_id=1, source_target_pairs={{0,16},{16,32},{32,48},{48,64},{64,80},{80,96},{96,112},{112,0},{1... | collective-permute-start | bytes 1327112 | tf_op jit(solution)/shard_map/projection/ppermute | solution.py:30
  43.0 12.3 %collective-permute-start.6 = (bf16[288,768]{1,0:T(8,128)(2,1)S(1)}, bf16[288,768]{1,0:T(8,128)(2,1)S(1)}, u32[]{:S(2)}, u32[]{:S(2)}) collective-permute-start(bf16[288,768]{1,0:T(8,128)(2,1)S(1)} %get-tuple-element.73), channel_id=1, source_target_pairs={{0,112},{16,0},{32,16},{48,32},{64,48},{80,64},{96,80},{112,96},{1... | collective-permute-start | bytes 1327112 | tf_op jit(solution)/shard_map/projection/ppermute | solution.py:30
  56.6 11.7 %collective-permute-start.7 = (bf16[288,768]{1,0:T(8,128)(2,1)S(1)}, bf16[288,768]{1,0:T(8,128)(2,1)S(1)}, u32[]{:S(2)}, u32[]{:S(2)}) collective-permute-start(bf16[288,768]{1,0:T(8,128)(2,1)S(1)} %get-tuple-element.76), channel_id=1, source_target_pairs={{0,16},{16,32},{32,48},{48,64},{64,80},{80,96},{96,112},{112,0},{1... | collective-permute-start | bytes 1327112 | tf_op jit(solution)/shard_map/projection/ppermute | solution.py:30
  58.5 11.0 %collective-permute-start.8 = (bf16[288,768]{1,0:T(8,128)(2,1)S(1)}, bf16[288,768]{1,0:T(8,128)(2,1)S(1)}, u32[]{:S(2)}, u32[]{:S(2)}) collective-permute-start(bf16[288,768]{1,0:T(8,128)(2,1)S(1)} %get-tuple-element.77), channel_id=1, source_target_pairs={{0,112},{16,0},{32,16},{48,32},{64,48},{80,64},{96,80},{112,96},{1... | collective-permute-start | bytes 1327112 | tf_op jit(solution)/shard_map/projection/ppermute | solution.py:30
  69.7 11.4 %collective-permute-start.9 = (bf16[288,768]{1,0:T(8,128)(2,1)S(1)}, bf16[288,768]{1,0:T(8,128)(2,1)S(1)}, u32[]{:S(2)}, u32[]{:S(2)}) collective-permute-start(bf16[288,768]{1,0:T(8,128)(2,1)S(1)} %get-tuple-element.80), channel_id=1, source_target_pairs={{0,16},{16,32},{32,48},{48,64},{64,80},{80,96},{96,112},{112,0},{1... | collective-permute-start | bytes 1327112 | tf_op jit(solution)/shard_map/projection/ppermute | solution.py:30
  71.2 9.9 %collective-permute-start.10 = (bf16[288,768]{1,0:T(8,128)(2,1)S(1)}, bf16[288,768]{1,0:T(8,128)(2,1)S(1)}, u32[]{:S(2)}, u32[]{:S(2)}) collective-permute-start(bf16[288,768]{1,0:T(8,128)(2,1)S(1)} %get-tuple-element.81), channel_id=1, source_target_pairs={{0,112},{16,0},{32,16},{48,32},{64,48},{80,64},{96,80},{112,96},{1... | collective-permute-start | bytes 1327112 | tf_op jit(solution)/shard_map/projection/ppermute | solution.py:30
  81.4 7.7 %collective-permute-start.11 = (bf16[288,384]{1,0:T(8,128)(2,1)S(1)}, bf16[288,384]{1,0:T(8,128)(2,1)S(1)}, u32[]{:S(2)}, u32[]{:S(2)}) collective-permute-start(bf16[288,384]{1,0:T(8,128)(2,1)S(1)} %get-tuple-element.84), channel_id=1, source_target_pairs={{0,128},{128,0},{1,129},{129,1},{2,130},{130,2},{3,131},{131,3},{4... | collective-permute-start | bytes 663560 | tf_op jit(solution)/shard_map/projection/ppermute | solution.py:30
  111.1 6.3 %collective-permute-start.12 = (bf16[512,128]{1,0:T(8,128)(2,1)S(1)}, bf16[512,128]{1,0:T(8,128)(2,1)S(1)}, u32[]{:S(2)}, u32[]{:S(2)}) collective-permute-start(bf16[512,128]{1,0:T(8,128)(2,1)S(1)} %attention.3.refs_0_), channel_id=1, source_target_pairs={{0,16},{16,32},{32,48},{48,64},{64,80},{80,96},{96,112},{112,0},{1... | collective-permute-start | bytes 393224 | tf_op jit(solution)/shard_map/output/ppermute | solution.py:30
  111.4 6.7 %collective-permute-start.13 = (bf16[512,128]{1,0:T(8,128)(2,1)S(1)}, bf16[512,128]{1,0:T(8,128)(2,1)S(1)}, u32[]{:S(2)}, u32[]{:S(2)}) collective-permute-start(bf16[512,128]{1,0:T(8,128)(2,1)S(1)} %attention.3.refs_0_), channel_id=1, source_target_pairs={{0,112},{16,0},{32,16},{48,32},{64,48},{80,64},{96,80},{112,96},{1... | collective-permute-start | bytes 393224 | tf_op jit(solution)/shard_map/output/ppermute | solution.py:30
  118.1 6.7 %collective-permute-start.14 = (bf16[512,128]{1,0:T(8,128)(2,1)S(1)}, bf16[512,128]{1,0:T(8,128)(2,1)S(1)}, u32[]{:S(2)}, u32[]{:S(2)}) collective-permute-start(bf16[512,128]{1,0:T(8,128)(2,1)S(1)} %collective-permute-done.12.refs_1_), channel_id=1, source_target_pairs={{0,16},{16,32},{32,48},{48,64},{64,80},{80,96},{96,112},{112,0},{1... | collective-permute-start | bytes 393224 | tf_op jit(solution)/shard_map/output/ppermute | solution.py:30
  118.5 6.6 %collective-permute-start.17 = (bf16[512,128]{1,0:T(8,128)(2,1)S(1)}, bf16[512,128]{1,0:T(8,128)(2,1)S(1)}, u32[]{:S(2)}, u32[]{:S(2)}) collective-permute-start(bf16[512,128]{1,0:T(8,128)(2,1)S(1)} %collective-permute-done.13.refs_7_), channel_id=1, source_target_pairs={{0,112},{16,0},{32,16},{48,32},{64,48},{80,64},{96,80},{112,96},{1... | collective-permute-start | bytes 393224 | tf_op jit(solution)/shard_map/output/ppermute | solution.py:30
  121.8 9.1 %collective-permute-start.16 = (bf16[512,128]{1,0:T(8,128)(2,1)S(1)}, bf16[512,128]{1,0:T(8,128)(2,1)S(1)}, u32[]{:S(2)}, u32[]{:S(2)}) collective-permute-start(bf16[512,128]{1,0:T(8,128)(2,1)S(1)} %attention.3.refs_0_), channel_id=1, source_target_pairs={{0,64},{16,80},{32,96},{48,112},{64,0},{80,16},{96,32},{112,48},{1... | collective-permute-start | bytes 393224 | tf_op jit(solution)/shard_map/output/ppermute | solution.py:30
  124.8 8.2 %collective-permute-start.15 = (bf16[512,128]{1,0:T(8,128)(2,1)S(1)}, bf16[512,128]{1,0:T(8,128)(2,1)S(1)}, u32[]{:S(2)}, u32[]{:S(2)}) collective-permute-start(bf16[512,128]{1,0:T(8,128)(2,1)S(1)} %collective-permute-done.14.refs_2_), channel_id=1, source_target_pairs={{0,16},{16,32},{32,48},{48,64},{64,80},{80,96},{96,112},{112,0},{1... | collective-permute-start | bytes 393224 | tf_op jit(solution)/shard_map/output/ppermute | solution.py:30
  125.1 7.8 %collective-permute-start.18 = (bf16[512,128]{1,0:T(8,128)(2,1)S(1)}, bf16[512,128]{1,0:T(8,128)(2,1)S(1)}, u32[]{:S(2)}, u32[]{:S(2)}) collective-permute-start(bf16[512,128]{1,0:T(8,128)(2,1)S(1)} %collective-permute-done.17.refs_6_), channel_id=1, source_target_pairs={{0,112},{16,0},{32,16},{48,32},{64,48},{80,64},{96,80},{112,96},{1... | collective-permute-start | bytes 393224 | tf_op jit(solution)/shard_map/output/ppermute | solution.py:30
  134.1 1.8 %collective-permute-start.19 = (bf16[256,512]{1,0:T(8,128)(2,1)S(1)}, bf16[256,512]{1,0:T(8,128)(2,1)S(1)}, u32[]{:S(2)}, u32[]{:S(2)}) collective-permute-start(bf16[256,512]{1,0:T(8,128)(2,1)S(1)} %get-tuple-element.95), channel_id=1, source_target_pairs={{0,8},{8,0},{1,9},{9,1},{2,10},{10,2},{3,11},{11,3},{4,12},{12,4},... | collective-permute-start | bytes 786440 | tf_op jit(solution)/shard_map/output/ppermute | solution.py:30
  135.3 8.6 %copy-start.3 = (bf16[256,256]{1,0:T(8,128)(2,1)S(1)}, bf16[256,256]{1,0:T(8,128)(2,1)}, u32[]{:S(2)}) copy-start(bf16[256,256]{1,0:T(8,128)(2,1)} %hidden.1) | copy-start | bytes 393220
  135.3 10.5 %copy-start.5 = (bf16[256,256]{1,0:T(8,128)(2,1)S(1)}, bf16[256,256]{1,0:T(8,128)(2,1)}, u32[]{:S(2)}) copy-start(bf16[256,256]{1,0:T(8,128)(2,1)} %get-tuple-element.97) | copy-start | bytes 393220
  135.3 2.8 %collective-permute-start.21 = (bf16[256,512]{1,0:T(8,128)(2,1)S(1)}, bf16[256,512]{1,0:T(8,128)(2,1)S(1)}, u32[]{:S(2)}, u32[]{:S(2)}) collective-permute-start(bf16[256,512]{1,0:T(8,128)(2,1)S(1)} %get-tuple-element.99), channel_id=1, source_target_pairs={{0,8},{8,0},{1,9},{9,1},{2,10},{10,2},{3,11},{11,3},{4,12},{12,4},... | collective-permute-start | bytes 786440 | tf_op jit(solution)/shard_map/output/ppermute | solution.py:30
  136.0 7.9 %collective-permute-start.20 = (bf16[256,256]{1,0:T(8,128)(2,1)S(1)}, bf16[256,256]{1,0:T(8,128)(2,1)S(1)}, u32[]{:S(2)}, u32[]{:S(2)}) collective-permute-start(bf16[256,256]{1,0:T(8,128)(2,1)S(1)} %fusion.4), channel_id=1, source_target_pairs={{0,128},{128,0},{1,129},{129,1},{2,130},{130,2},{3,131},{131,3},{4... | collective-permute-start | bytes 393224 | tf_op jit(solution)/shard_map/output/ppermute | solution.py:30
  138.2 7.6 %collective-permute-start.22 = (bf16[256,256]{1,0:T(8,128)(2,1)S(1)}, bf16[256,256]{1,0:T(8,128)(2,1)S(1)}, u32[]{:S(2)}, u32[]{:S(2)}) collective-permute-start(bf16[256,256]{1,0:T(8,128)(2,1)S(1)} %fusion), channel_id=1, source_target_pairs={{0,128},{128,0},{1,129},{129,1},{2,130},{130,2},{3,131},{131,3},{4... | collective-permute-start | bytes 393224 | tf_op jit(solution)/shard_map/output/ppermute | solution.py:30
Sparse Core Ops, SparseCore 0:
  41.4 42.9 all-gather.1

commit v10 on v8

--- a/solution.py
+++ b/solution.py
@@ -468,7 +468,7 @@
         column = pl.ds(pl.multiple_of(column, TOK), TOK)
         return jnp.dot(joined[rows, :], turned[:, column], preferred_element_type=f32)
 
-    size = 128
+    size = TOK
 
     def step(i, carry):
         rows = pl.ds(pl.multiple_of(i * size, size), size)

time: 154 us -> 154 us (level)
  transfers between devices with their start and end apart: 25 -> 25, of which waited for: 13 -> 14; matrix products, arithmetic and copies ran while one was open for 1% -> 1% of each run, Pallas kernels for 10% -> 10%
where the time goes in v10:
time: 154 us; the launch traced here: 153 us
  waiting for transfers between devices  50.6 us (33%)
  starting transfers between devices  42.5 us (28%)
  Pallas kernels  25.1 us (16%)
  blocking collectives  17.6 us (11%)
  between operations  13.7 us (9%)
  other arithmetic  1.78 us (1%)
  local copies, waits for them, and re-layouts  1.56 us (1%)
    ppermute x23, waiting for transfers between devices, shift(): lax.ppermute(value, axis, [(i, (i + distance) % size) for i in range(size)])  50.6 us
    ppermute x23, starting transfers between devices, shift(): lax.ppermute(value, axis, [(i, (i + distance) % size) for i in range(size)])  33.9 us
    all_to_all x1, blocking collectives, shards(): blocks = lax.all_to_all(payload, CTX, 0, 0, tiled=True)  17.6 us
    all_to_all x1, starting transfers between devices, shards(): shared = lax.all_to_all(share, 'z', 0, 0, tiled=True)  8.48 us
    pallas_call x2, Pallas kernels, pick_columns(): pl.pallas_call(functools.partial(columns_kernel, ks), out_shape=(columns,...  5.79 us
    pallas_call x2, Pallas kernels, partials(): pl.pallas_call(functools.partial(partial_kernel, ks), out_shape=shapes, i...  5.77 us
    pallas_call x1, Pallas kernels, make_variant(): pl.pallas_call(variant_kernel, out_shape=(jax.ShapeDtypeStruct((ROWS, wid...  3.09 us
  transfers between devices with their start and end apart: 25, of which 14 were waited for; matrix products, arithmetic and copies ran while one was open for 1% of the time, Pallas kernels for 10%

profile of v10, /device:TPU:6, one launch (start us, length us, event | category | flops | bytes accessed | tf_op | source)
XLA Modules:
  0.0 152.8 jit_solution(17401950466525441595)
XLA Ops:
  6.5 3.1 %inputs.3 = (bf16[272,256]{1,0:T(8,128)(2,1)S(1)}, bf16[16,256]{1,0:T(8,128)(2,1)}, bf16[256,256]{1,0:T(8,128)(2,1)}, bf16[8,16,1024]{2,1,0:T(8,128)(2,1)}) custom-call(s32[16]{0:T(128)} %pos.1, s32[16]{0:T(128)} %base.1, s32[256]{0:T(256)} %ids.1, bf16[256,256]{1,0:T(8,128)(2,1)} %hidden.1, bf16[512,256]{1,0:T(8,128)(2,1)} %embed.1, bf16[128,8192]{1,0:T(8,128)(2,1)} %w.1), custom_call_target="tpu_custom_call" | custom-call | tf_op jit(solution)/shard_map/inputs/pallas_call | solution.py:116
  9.6 1.3 inputs.4
  10.9 0.1 collective-permute-start.1
  11.0 0.5 collective-permute-start
  11.5 1.4 collective-permute-done.sis
  12.9 0.8 copy-done.4
  13.7 4.5 %inputs.5 = (bf16[256,5376]{1,0:T(8,128)(2,1)}, bf16[256,5376]{1,0:T(8,128)(2,1)S(1)}) custom-call(bf16[256,12288]{1,0:T(8,128)(2,1)} %w.3), custom_call_target="tpu_custom_call" | custom-call | tf_op jit(solution)/shard_map/inputs/pallas_call | solution.py:166
  18.2 0.2 collective-permute-start.4
  18.4 8.5 %all-to-all-start = ((bf16[8,16,1024]{2,1,0:T(8,128)(2,1)}), bf16[8,16,1024]{2,1,0:T(8,128)(2,1)}, u32[]{:S(2)}, u32[]{:S(2)}) async-start(bf16[8,16,1024]{2,1,0:T(8,128)(2,1)} %get-tuple-element.63), calls=%async_computation | async-start | bytes 524288 | tf_op jit(solution)/shard_map/inputs/all_to_all | solution.py:520
  26.9 0.0 all-gather.2.cloned.1.call-start
  27.0 0.8 dynamic-slice.3
  27.7 1.5 projection.6
  29.2 2.0 %collective-permute-start.2 = (bf16[288,384]{1,0:T(8,128)(2,1)S(1)}, bf16[288,384]{1,0:T(8,128)(2,1)S(1)}, u32[]{:S(2)}, u32[]{:S(2)}) collective-permute-start(bf16[288,384]{1,0:T(8,128)(2,1)S(1)} %get-tuple-element.61), channel_id=1, source_target_pairs={{0,16},{16,32},{32,48},{48,64},{64,80},{80,96},{96,112},{112,0},{1... | collective-permute-start | bytes 663560 | tf_op jit(solution)/shard_map/projection/ppermute | solution.py:30
  31.2 1.3 collective-permute-start.3
  32.6 4.3 %projection.7 = (bf16[288,768]{1,0:T(8,128)(2,1)}, bf16[288,768]{1,0:T(8,128)(2,1)}, bf16[288,768]{1,0:T(8,128)(2,1)}, bf16[288,768]{1,0:T(8,128)(2,1)}, bf16[28...) custom-call(bf16[272,256]{1,0:T(8,128)(2,1)S(1)} %get-tuple-element.54.own, ...), custom_call_target="tpu_custom_call" | custom-call | flops 1497366528 | bytes 11010048 | tf_op jit(solution)/shard_map/projection/pallas_call | solution.py:235
  36.9 4.5 %collective-permute-done.2.up = bf16[288,384]{1,0:T(8,128)(2,1)S(1)} collective-permute-done((bf16[288,384]{1,0:T(8,128)(2,1)S(1)}, bf16[288,384]{1,0:T(8,128)(2,1)S(1)}, u32[]{:S(2)}, u32[]{:S(2)}) %collective-permute-start.2) | collective-permute-done | bytes 221216 | tf_op jit(solution)/shard_map/projection/ppermute | solution.py:30
  41.4 0.0 all-gather.2.cloned.1.call-update
  41.4 1.3 projection.8
  42.7 0.0 copy-start.6
  42.7 0.3 collective-permute-start.5
  43.1 3.0 %collective-permute-start.6 = (bf16[288,768]{1,0:T(8,128)(2,1)S(1)}, bf16[288,768]{1,0:T(8,128)(2,1)S(1)}, u32[]{:S(2)}, u32[]{:S(2)}) collective-permute-start(bf16[288,768]{1,0:T(8,128)(2,1)S(1)} %get-tuple-element.73), channel_id=1, source_target_pairs={{0,112},{16,0},{32,16},{48,32},{64,48},{80,64},{96,80},{112,96},{1... | collective-permute-start | bytes 1327112 | tf_op jit(solution)/shard_map/projection/ppermute | solution.py:30
  46.0 9.3 %collective-permute-done.5.up = bf16[288,768]{1,0:T(8,128)(2,1)S(1)} collective-permute-done((bf16[288,768]{1,0:T(8,128)(2,1)S(1)}, bf16[288,768]{1,0:T(8,128)(2,1)S(1)}, u32[]{:S(2)}, u32[]{:S(2)}) %collective-permute-start.5) | collective-permute-done | bytes 442400 | tf_op jit(solution)/shard_map/projection/ppermute | solution.py:30
  55.3 1.4 projection.9
  56.7 1.6 %collective-permute-start.7 = (bf16[288,768]{1,0:T(8,128)(2,1)S(1)}, bf16[288,768]{1,0:T(8,128)(2,1)S(1)}, u32[]{:S(2)}, u32[]{:S(2)}) collective-permute-start(bf16[288,768]{1,0:T(8,128)(2,1)S(1)} %get-tuple-element.76), channel_id=1, source_target_pairs={{0,16},{16,32},{32,48},{48,64},{64,80},{80,96},{96,112},{112,0},{1... | collective-permute-start | bytes 1327112 | tf_op jit(solution)/shard_map/projection/ppermute | solution.py:30
  58.3 1.7 %collective-permute-start.8 = (bf16[288,768]{1,0:T(8,128)(2,1)S(1)}, bf16[288,768]{1,0:T(8,128)(2,1)S(1)}, u32[]{:S(2)}, u32[]{:S(2)}) collective-permute-start(bf16[288,768]{1,0:T(8,128)(2,1)S(1)} %get-tuple-element.77), channel_id=1, source_target_pairs={{0,112},{16,0},{32,16},{48,32},{64,48},{80,64},{96,80},{112,96},{1... | collective-permute-start | bytes 1327112 | tf_op jit(solution)/shard_map/projection/ppermute | solution.py:30
  60.0 8.8 %collective-permute-done.7.up = bf16[288,768]{1,0:T(8,128)(2,1)S(1)} collective-permute-done((bf16[288,768]{1,0:T(8,128)(2,1)S(1)}, bf16[288,768]{1,0:T(8,128)(2,1)S(1)}, u32[]{:S(2)}, u32[]{:S(2)}) %collective-permute-start.7) | collective-permute-done | bytes 442400 | tf_op jit(solution)/shard_map/projection/ppermute | solution.py:30
  68.8 0.2 projection.10
  69.0 1.8 %collective-permute-start.9 = (bf16[288,768]{1,0:T(8,128)(2,1)S(1)}, bf16[288,768]{1,0:T(8,128)(2,1)S(1)}, u32[]{:S(2)}, u32[]{:S(2)}) collective-permute-start(bf16[288,768]{1,0:T(8,128)(2,1)S(1)} %get-tuple-element.80), channel_id=1, source_target_pairs={{0,16},{16,32},{32,48},{48,64},{64,80},{80,96},{96,112},{112,0},{1... | collective-permute-start | bytes 1327112 | tf_op jit(solution)/shard_map/projection/ppermute | solution.py:30
  70.9 1.5 collective-permute-start.10
  72.4 7.9 %collective-permute-done.9.up = bf16[288,768]{1,0:T(8,128)(2,1)S(1)} collective-permute-done((bf16[288,768]{1,0:T(8,128)(2,1)S(1)}, bf16[288,768]{1,0:T(8,128)(2,1)S(1)}, u32[]{:S(2)}, u32[]{:S(2)}) %collective-permute-start.9) | collective-permute-done | bytes 442400 | tf_op jit(solution)/shard_map/projection/ppermute | solution.py:30
  80.3 0.2 projection.11
  80.5 1.7 %collective-permute-start.11 = (bf16[288,384]{1,0:T(8,128)(2,1)S(1)}, bf16[288,384]{1,0:T(8,128)(2,1)S(1)}, u32[]{:S(2)}, u32[]{:S(2)}) collective-permute-start(bf16[288,384]{1,0:T(8,128)(2,1)S(1)} %get-tuple-element.84), channel_id=1, source_target_pairs={{0,128},{128,0},{1,129},{129,1},{2,130},{130,2},{3,131},{131,3},{4... | collective-permute-start | bytes 663560 | tf_op jit(solution)/shard_map/projection/ppermute | solution.py:30
  82.1 0.6 fusion.10
  82.7 0.1 pad_maximum_fusion.1
  82.9 5.3 %collective-permute-done.11.other = bf16[288,384]{1,0:T(8,128)(2,1)S(1)} collective-permute-done((bf16[288,384]{1,0:T(8,128)(2,1)S(1)}, bf16[288,384]{1,0:T(8,128)(2,1)S(1)}, u32[]{:S(2)}, u32[]{:S(2)}) %collective-permute-start.11) | collective-permute-done | bytes 221216 | tf_op jit(solution)/shard_map/projection/ppermute | solution.py:30
  88.2 1.3 attention.2
  89.5 17.6 %all_to_all.10.blocks = bf16[8,288,256]{2,1,0:T(8,128)(2,1)S(1)} all-to-all(bf16[8,288,256]{2,1,0:T(8,128)(2,1)S(1)} %get-tuple-element.87), channel_id=1, replica_groups=mesh['x_hi'=2,'z'=8,'core'=2,'x_lo'=2,'y'=4] {'x_lo','y'}, dimensions={0} | all-to-all | bytes 2359296 | tf_op jit(solution)/shard_map/attention/all_to_all | solution.py:556
  107.1 2.9 %attention.3.refs_0_ = bf16[512,128]{1,0:T(8,128)(2,1)S(1)} custom-call(bf16[512,128]{1,0:T(8,128)(2,1)S(1)} %get-tuple-element.86.queries, bf16[8,288,256]{2,1,0:T(8,128)(2,1)S(1)} %all_to_all.10.blocks), custom_call_target="tpu_custom_call" | custom-call | tf_op jit(solution)/shard_map/attention/pallas_call | solution.py:418
  110.0 0.0 all-gather.2.cloned.1.call-done.w
  110.1 1.5 %collective-permute-start.12 = (bf16[512,128]{1,0:T(8,128)(2,1)S(1)}, bf16[512,128]{1,0:T(8,128)(2,1)S(1)}, u32[]{:S(2)}, u32[]{:S(2)}) collective-permute-start(bf16[512,128]{1,0:T(8,128)(2,1)S(1)} %attention.3.refs_0_), channel_id=1, source_target_pairs={{0,16},{16,32},{32,48},{48,64},{64,80},{80,96},{96,112},{112,0},{1... | collective-permute-start | bytes 393224 | tf_op jit(solution)/shard_map/output/ppermute | solution.py:30
  111.6 1.8 %collective-permute-start.13 = (bf16[512,128]{1,0:T(8,128)(2,1)S(1)}, bf16[512,128]{1,0:T(8,128)(2,1)S(1)}, u32[]{:S(2)}, u32[]{:S(2)}) collective-permute-start(bf16[512,128]{1,0:T(8,128)(2,1)S(1)} %attention.3.refs_0_), channel_id=1, source_target_pairs={{0,112},{16,0},{32,16},{48,32},{64,48},{80,64},{96,80},{112,96},{1... | collective-permute-start | bytes 393224 | tf_op jit(solution)/shard_map/output/ppermute | solution.py:30
  113.4 1.6 %output.3.turned = bf16[1024,1024]{1,0:T(8,128)(2,1)S(1)} custom-call(bf16[8,128,1024]{2,1,0:T(8,128)(2,1)} %all-gather.2.cloned.1.call-done.w), custom_call_target="tpu_custom_call" | custom-call | tf_op jit(solution)/shard_map/output/pallas_call | solution.py:450
  115.0 1.4 collective-permute-done.12.refs_1_
  116.3 1.0 collective-permute-done.13.refs_7_
  117.3 1.5 collective-permute-start.14
  118.8 2.2 %collective-permute-start.17 = (bf16[512,128]{1,0:T(8,128)(2,1)S(1)}, bf16[512,128]{1,0:T(8,128)(2,1)S(1)}, u32[]{:S(2)}, u32[]{:S(2)}) collective-permute-start(bf16[512,128]{1,0:T(8,128)(2,1)S(1)} %collective-permute-done.13.refs_7_), channel_id=1, source_target_pairs={{0,112},{16,0},{32,16},{48,32},{64,48},{80,64},{96,80},{112,96},{1... | collective-permute-start | bytes 393224 | tf_op jit(solution)/shard_map/output/ppermute | solution.py:30
  121.0 4.0 %collective-permute-start.16 = (bf16[512,128]{1,0:T(8,128)(2,1)S(1)}, bf16[512,128]{1,0:T(8,128)(2,1)S(1)}, u32[]{:S(2)}, u32[]{:S(2)}) collective-permute-start(bf16[512,128]{1,0:T(8,128)(2,1)S(1)} %attention.3.refs_0_), channel_id=1, source_target_pairs={{0,64},{16,80},{32,96},{48,112},{64,0},{80,16},{96,32},{112,48},{1... | collective-permute-start | bytes 393224 | tf_op jit(solution)/shard_map/output/ppermute | solution.py:30
  125.0 0.4 collective-permute-start.15
  125.4 0.4 collective-permute-done.17.refs_6_
  125.8 2.4 %collective-permute-start.18 = (bf16[512,128]{1,0:T(8,128)(2,1)S(1)}, bf16[512,128]{1,0:T(8,128)(2,1)S(1)}, u32[]{:S(2)}, u32[]{:S(2)}) collective-permute-start(bf16[512,128]{1,0:T(8,128)(2,1)S(1)} %collective-permute-done.17.refs_6_), channel_id=1, source_target_pairs={{0,112},{16,0},{32,16},{48,32},{64,48},{80,64},{96,80},{112,96},{1... | collective-permute-start | bytes 393224 | tf_op jit(solution)/shard_map/output/ppermute | solution.py:30
  128.2 3.2 %collective-permute-done.16.refs_4_ = bf16[512,128]{1,0:T(8,128)(2,1)S(1)} collective-permute-done((bf16[512,128]{1,0:T(8,128)(2,1)S(1)}, bf16[512,128]{1,0:T(8,128)(2,1)S(1)}, u32[]{:S(2)}, u32[]{:S(2)}) %collective-permute-start.16) | collective-permute-done | bytes 131104 | tf_op jit(solution)/shard_map/output/ppermute | solution.py:30
  131.4 1.3 collective-permute-done.15.refs_3_
  132.7 0.8 output.4
  133.4 0.1 collective-permute-start.19
  133.5 0.8 output.5
  134.3 0.6 collective-permute-start.21
  134.9 0.2 collective-permute-done.19
  135.2 1.7 %collective-permute-start.20 = (bf16[256,256]{1,0:T(8,128)(2,1)S(1)}, bf16[256,256]{1,0:T(8,128)(2,1)S(1)}, u32[]{:S(2)}, u32[]{:S(2)}) collective-permute-start(bf16[256,256]{1,0:T(8,128)(2,1)S(1)} %fusion.4), channel_id=1, source_target_pairs={{0,128},{128,0},{1,129},{129,1},{2,130},{130,2},{3,131},{131,3},{4... | collective-permute-start | bytes 393224 | tf_op jit(solution)/shard_map/output/ppermute | solution.py:30
  136.9 2.0 %collective-permute-start.22 = (bf16[256,256]{1,0:T(8,128)(2,1)S(1)}, bf16[256,256]{1,0:T(8,128)(2,1)S(1)}, u32[]{:S(2)}, u32[]{:S(2)}) collective-permute-start(bf16[256,256]{1,0:T(8,128)(2,1)S(1)} %fusion), channel_id=1, source_target_pairs={{0,128},{128,0},{1,129},{129,1},{2,130},{130,2},{3,131},{131,3},{4... | collective-permute-start | bytes 393224 | tf_op jit(solution)/shard_map/output/ppermute | solution.py:30
  139.0 4.1 %collective-permute-done.20 = bf16[256,256]{1,0:T(8,128)(2,1)S(1)} collective-permute-done((bf16[256,256]{1,0:T(8,128)(2,1)S(1)}, bf16[256,256]{1,0:T(8,128)(2,1)S(1)}, u32[]{:S(2)}, u32[]{:S(2)}) %collective-permute-start.20) | collective-permute-done | bytes 131104 | tf_op jit(solution)/shard_map/output/ppermute | solution.py:30
  143.1 0.1 fusion.8
  143.2 1.9 %collective-permute-done.22 = bf16[256,256]{1,0:T(8,128)(2,1)S(1)} collective-permute-done((bf16[256,256]{1,0:T(8,128)(2,1)S(1)}, bf16[256,256]{1,0:T(8,128)(2,1)S(1)}, u32[]{:S(2)}, u32[]{:S(2)}) %collective-permute-start.22) | collective-permute-done | bytes 131104 | tf_op jit(solution)/shard_map/output/ppermute | solution.py:30
  145.1 0.1 fusion.9
  145.2 0.7 pad_maximum_fusion
  (30 shorter events, 0.3 us)
Async XLA Ops:
  10.9 2.0 %collective-permute-start.1 = (bf16[256,768]{1,0:T(8,128)(2,1)S(1)}, bf16[256,768]{1,0:T(8,128)(2,1)S(1)}, u32[]{:S(2)}, u32[]{:S(2)}) collective-permute-start(bf16[256,768]{1,0:T(8,128)(2,1)S(1)} %get-tuple-element.56), channel_id=1, source_target_pairs={{0,8},{8,0},{1,9},{9,1},{2,10},{10,2},{3,11},{11,3},{4,12},{12,4},... | collective-permute-start | bytes 1179656 | tf_op jit(solution)/shard_map/inputs/ppermute | solution.py:30
  11.0 1.9 %collective-permute-start = (bf16[272,256]{1,0:T(8,128)(2,1)S(1)}, bf16[272,256]{1,0:T(8,128)(2,1)S(1)}, u32[]{:S(2)}, u32[]{:S(2)}) collective-permute-start(bf16[272,256]{1,0:T(8,128)(2,1)S(1)} %get-tuple-element.54.own), channel_id=1, source_target_pairs={{0,8},{8,0},{1,9},{9,1},{2,10},{10,2},{3,11},{11,3},{4,12},{12,4},... | collective-permute-start | bytes 417800 | tf_op jit(solution)/shard_map/inputs/ppermute | solution.py:30
  12.9 0.8 copy-start.4
  18.2 14.3 %collective-permute-start.4 = (bf16[256,5376]{1,0:T(8,128)(2,1)}, bf16[256,5376]{1,0:T(8,128)(2,1)}, u32[]{:S(2)}, u32[]{:S(2)}) collective-permute-start(bf16[256,5376]{1,0:T(8,128)(2,1)} %get-tuple-element.66), channel_id=1, source_target_pairs={{0,8},{8,0},{1,9},{9,1},{2,10},{10,2},{3,11},{11,3},{4,12},{12,4},... | collective-permute-start | bytes 8257544 | tf_op jit(solution)/shard_map/inputs/ppermute | solution.py:30
  18.4 22.9 %all-to-all-start = ((bf16[8,16,1024]{2,1,0:T(8,128)(2,1)}), bf16[8,16,1024]{2,1,0:T(8,128)(2,1)}, u32[]{:S(2)}, u32[]{:S(2)}) async-start(bf16[8,16,1024]{2,1,0:T(8,128)(2,1)} %get-tuple-element.63), calls=%async_computation | async-start | bytes 524288 | tf_op jit(solution)/shard_map/inputs/all_to_all | solution.py:520
  26.9 83.1 %all-gather.2.cloned.1.call-start = ((), (), s32[]{:S(2)}) async-start(), calls=%async_computation.2 | async-start | bytes 2359296 | tf_op jit(solution)/shard_map/projection/all_gather | solution.py:532
  29.2 12.2 %collective-permute-start.2 = (bf16[288,384]{1,0:T(8,128)(2,1)S(1)}, bf16[288,384]{1,0:T(8,128)(2,1)S(1)}, u32[]{:S(2)}, u32[]{:S(2)}) collective-permute-start(bf16[288,384]{1,0:T(8,128)(2,1)S(1)} %get-tuple-element.61), channel_id=1, source_target_pairs={{0,16},{16,32},{32,48},{48,64},{64,80},{80,96},{96,112},{112,0},{1... | collective-permute-start | bytes 663560 | tf_op jit(solution)/shard_map/projection/ppermute | solution.py:30
  31.2 10.1 %collective-permute-start.3 = (bf16[288,384]{1,0:T(8,128)(2,1)S(1)}, bf16[288,384]{1,0:T(8,128)(2,1)S(1)}, u32[]{:S(2)}, u32[]{:S(2)}) collective-permute-start(bf16[288,384]{1,0:T(8,128)(2,1)S(1)} %get-tuple-element.62), channel_id=1, source_target_pairs={{0,112},{16,0},{32,16},{48,32},{64,48},{80,64},{96,80},{112,96},{1... | collective-permute-start | bytes 663560 | tf_op jit(solution)/shard_map/projection/ppermute | solution.py:30
  36.9 31.9 %copy-start = (bf16[288,768]{1,0:T(8,128)(2,1)S(1)}, bf16[288,768]{1,0:T(8,128)(2,1)}, u32[]{:S(2)}) copy-start(bf16[288,768]{1,0:T(8,128)(2,1)} %get-tuple-element.78.near_up) | copy-start | bytes 1327108
  36.9 31.9 %copy-start.1 = (bf16[288,768]{1,0:T(8,128)(2,1)S(1)}, bf16[288,768]{1,0:T(8,128)(2,1)}, u32[]{:S(2)}) copy-start(bf16[288,768]{1,0:T(8,128)(2,1)} %get-tuple-element.79.near_down) | copy-start | bytes 1327108
  42.7 29.7 %copy-start.6 = (s32[16]{0:T(128)S(1)}, s32[16]{0:T(128)}, u32[]{:S(2)}) copy-start(s32[16]{0:T(128)} %pos.1) | copy-start | bytes 196
  42.7 37.6 %copy-start.2 = (bf16[288,768]{1,0:T(8,128)(2,1)S(1)}, bf16[288,768]{1,0:T(8,128)(2,1)}, u32[]{:S(2)}) copy-start(bf16[288,768]{1,0:T(8,128)(2,1)} %get-tuple-element.82.near) | copy-start | bytes 1327108
  42.7 12.6 %collective-permute-start.5 = (bf16[288,768]{1,0:T(8,128)(2,1)S(1)}, bf16[288,768]{1,0:T(8,128)(2,1)S(1)}, u32[]{:S(2)}, u32[]{:S(2)}) collective-permute-start(bf16[288,768]{1,0:T(8,128)(2,1)S(1)} %get-tuple-element.72), channel_id=1, source_target_pairs={{0,16},{16,32},{32,48},{48,64},{64,80},{80,96},{96,112},{112,0},{1... | collective-permute-start | bytes 1327112 | tf_op jit(solution)/shard_map/projection/ppermute | solution.py:30
  43.1 12.3 %collective-permute-start.6 = (bf16[288,768]{1,0:T(8,128)(2,1)S(1)}, bf16[288,768]{1,0:T(8,128)(2,1)S(1)}, u32[]{:S(2)}, u32[]{:S(2)}) collective-permute-start(bf16[288,768]{1,0:T(8,128)(2,1)S(1)} %get-tuple-element.73), channel_id=1, source_target_pairs={{0,112},{16,0},{32,16},{48,32},{64,48},{80,64},{96,80},{112,96},{1... | collective-permute-start | bytes 1327112 | tf_op jit(solution)/shard_map/projection/ppermute | solution.py:30
  56.7 12.1 %collective-permute-start.7 = (bf16[288,768]{1,0:T(8,128)(2,1)S(1)}, bf16[288,768]{1,0:T(8,128)(2,1)S(1)}, u32[]{:S(2)}, u32[]{:S(2)}) collective-permute-start(bf16[288,768]{1,0:T(8,128)(2,1)S(1)} %get-tuple-element.76), channel_id=1, source_target_pairs={{0,16},{16,32},{32,48},{48,64},{64,80},{80,96},{96,112},{112,0},{1... | collective-permute-start | bytes 1327112 | tf_op jit(solution)/shard_map/projection/ppermute | solution.py:30
  58.3 10.5 %collective-permute-start.8 = (bf16[288,768]{1,0:T(8,128)(2,1)S(1)}, bf16[288,768]{1,0:T(8,128)(2,1)S(1)}, u32[]{:S(2)}, u32[]{:S(2)}) collective-permute-start(bf16[288,768]{1,0:T(8,128)(2,1)S(1)} %get-tuple-element.77), channel_id=1, source_target_pairs={{0,112},{16,0},{32,16},{48,32},{64,48},{80,64},{96,80},{112,96},{1... | collective-permute-start | bytes 1327112 | tf_op jit(solution)/shard_map/projection/ppermute | solution.py:30
  69.0 11.3 %collective-permute-start.9 = (bf16[288,768]{1,0:T(8,128)(2,1)S(1)}, bf16[288,768]{1,0:T(8,128)(2,1)S(1)}, u32[]{:S(2)}, u32[]{:S(2)}) collective-permute-start(bf16[288,768]{1,0:T(8,128)(2,1)S(1)} %get-tuple-element.80), channel_id=1, source_target_pairs={{0,16},{16,32},{32,48},{48,64},{64,80},{80,96},{96,112},{112,0},{1... | collective-permute-start | bytes 1327112 | tf_op jit(solution)/shard_map/projection/ppermute | solution.py:30
  70.9 9.4 %collective-permute-start.10 = (bf16[288,768]{1,0:T(8,128)(2,1)S(1)}, bf16[288,768]{1,0:T(8,128)(2,1)S(1)}, u32[]{:S(2)}, u32[]{:S(2)}) collective-permute-start(bf16[288,768]{1,0:T(8,128)(2,1)S(1)} %get-tuple-element.81), channel_id=1, source_target_pairs={{0,112},{16,0},{32,16},{48,32},{64,48},{80,64},{96,80},{112,96},{1... | collective-permute-start | bytes 1327112 | tf_op jit(solution)/shard_map/projection/ppermute | solution.py:30
  80.5 7.7 %collective-permute-start.11 = (bf16[288,384]{1,0:T(8,128)(2,1)S(1)}, bf16[288,384]{1,0:T(8,128)(2,1)S(1)}, u32[]{:S(2)}, u32[]{:S(2)}) collective-permute-start(bf16[288,384]{1,0:T(8,128)(2,1)S(1)} %get-tuple-element.84), channel_id=1, source_target_pairs={{0,128},{128,0},{1,129},{129,1},{2,130},{130,2},{3,131},{131,3},{4... | collective-permute-start | bytes 663560 | tf_op jit(solution)/shard_map/projection/ppermute | solution.py:30
  110.1 6.3 %collective-permute-start.12 = (bf16[512,128]{1,0:T(8,128)(2,1)S(1)}, bf16[512,128]{1,0:T(8,128)(2,1)S(1)}, u32[]{:S(2)}, u32[]{:S(2)}) collective-permute-start(bf16[512,128]{1,0:T(8,128)(2,1)S(1)} %attention.3.refs_0_), channel_id=1, source_target_pairs={{0,16},{16,32},{32,48},{48,64},{64,80},{80,96},{96,112},{112,0},{1... | collective-permute-start | bytes 393224 | tf_op jit(solution)/shard_map/output/ppermute | solution.py:30
  111.6 5.7 %collective-permute-start.13 = (bf16[512,128]{1,0:T(8,128)(2,1)S(1)}, bf16[512,128]{1,0:T(8,128)(2,1)S(1)}, u32[]{:S(2)}, u32[]{:S(2)}) collective-permute-start(bf16[512,128]{1,0:T(8,128)(2,1)S(1)} %attention.3.refs_0_), channel_id=1, source_target_pairs={{0,112},{16,0},{32,16},{48,32},{64,48},{80,64},{96,80},{112,96},{1... | collective-permute-start | bytes 393224 | tf_op jit(solution)/shard_map/output/ppermute | solution.py:30
  117.3 7.7 %collective-permute-start.14 = (bf16[512,128]{1,0:T(8,128)(2,1)S(1)}, bf16[512,128]{1,0:T(8,128)(2,1)S(1)}, u32[]{:S(2)}, u32[]{:S(2)}) collective-permute-start(bf16[512,128]{1,0:T(8,128)(2,1)S(1)} %collective-permute-done.12.refs_1_), channel_id=1, source_target_pairs={{0,16},{16,32},{32,48},{48,64},{64,80},{80,96},{96,112},{112,0},{1... | collective-permute-start | bytes 393224 | tf_op jit(solution)/shard_map/output/ppermute | solution.py:30
  118.8 7.0 %collective-permute-start.17 = (bf16[512,128]{1,0:T(8,128)(2,1)S(1)}, bf16[512,128]{1,0:T(8,128)(2,1)S(1)}, u32[]{:S(2)}, u32[]{:S(2)}) collective-permute-start(bf16[512,128]{1,0:T(8,128)(2,1)S(1)} %collective-permute-done.13.refs_7_), channel_id=1, source_target_pairs={{0,112},{16,0},{32,16},{48,32},{64,48},{80,64},{96,80},{112,96},{1... | collective-permute-start | bytes 393224 | tf_op jit(solution)/shard_map/output/ppermute | solution.py:30
  121.0 10.4 %collective-permute-start.16 = (bf16[512,128]{1,0:T(8,128)(2,1)S(1)}, bf16[512,128]{1,0:T(8,128)(2,1)S(1)}, u32[]{:S(2)}, u32[]{:S(2)}) collective-permute-start(bf16[512,128]{1,0:T(8,128)(2,1)S(1)} %attention.3.refs_0_), channel_id=1, source_target_pairs={{0,64},{16,80},{32,96},{48,112},{64,0},{80,16},{96,32},{112,48},{1... | collective-permute-start | bytes 393224 | tf_op jit(solution)/shard_map/output/ppermute | solution.py:30
  125.0 7.7 %collective-permute-start.15 = (bf16[512,128]{1,0:T(8,128)(2,1)S(1)}, bf16[512,128]{1,0:T(8,128)(2,1)S(1)}, u32[]{:S(2)}, u32[]{:S(2)}) collective-permute-start(bf16[512,128]{1,0:T(8,128)(2,1)S(1)} %collective-permute-done.14.refs_2_), channel_id=1, source_target_pairs={{0,16},{16,32},{32,48},{48,64},{64,80},{80,96},{96,112},{112,0},{1... | collective-permute-start | bytes 393224 | tf_op jit(solution)/shard_map/output/ppermute | solution.py:30
  125.8 6.8 %collective-permute-start.18 = (bf16[512,128]{1,0:T(8,128)(2,1)S(1)}, bf16[512,128]{1,0:T(8,128)(2,1)S(1)}, u32[]{:S(2)}, u32[]{:S(2)}) collective-permute-start(bf16[512,128]{1,0:T(8,128)(2,1)S(1)} %collective-permute-done.17.refs_6_), channel_id=1, source_target_pairs={{0,112},{16,0},{32,16},{48,32},{64,48},{80,64},{96,80},{112,96},{1... | collective-permute-start | bytes 393224 | tf_op jit(solution)/shard_map/output/ppermute | solution.py:30
  133.4 1.6 %collective-permute-start.19 = (bf16[256,512]{1,0:T(8,128)(2,1)S(1)}, bf16[256,512]{1,0:T(8,128)(2,1)S(1)}, u32[]{:S(2)}, u32[]{:S(2)}) collective-permute-start(bf16[256,512]{1,0:T(8,128)(2,1)S(1)} %get-tuple-element.95), channel_id=1, source_target_pairs={{0,8},{8,0},{1,9},{9,1},{2,10},{10,2},{3,11},{11,3},{4,12},{12,4},... | collective-permute-start | bytes 786440 | tf_op jit(solution)/shard_map/output/ppermute | solution.py:30
  134.3 8.8 %copy-start.3 = (bf16[256,256]{1,0:T(8,128)(2,1)S(1)}, bf16[256,256]{1,0:T(8,128)(2,1)}, u32[]{:S(2)}) copy-start(bf16[256,256]{1,0:T(8,128)(2,1)} %hidden.1) | copy-start | bytes 393220
  134.3 10.8 %copy-start.5 = (bf16[256,256]{1,0:T(8,128)(2,1)S(1)}, bf16[256,256]{1,0:T(8,128)(2,1)}, u32[]{:S(2)}) copy-start(bf16[256,256]{1,0:T(8,128)(2,1)} %get-tuple-element.97) | copy-start | bytes 393220
  134.3 2.5 %collective-permute-start.21 = (bf16[256,512]{1,0:T(8,128)(2,1)S(1)}, bf16[256,512]{1,0:T(8,128)(2,1)S(1)}, u32[]{:S(2)}, u32[]{:S(2)}) collective-permute-start(bf16[256,512]{1,0:T(8,128)(2,1)S(1)} %get-tuple-element.99), channel_id=1, source_target_pairs={{0,8},{8,0},{1,9},{9,1},{2,10},{10,2},{3,11},{11,3},{4,12},{12,4},... | collective-permute-start | bytes 786440 | tf_op jit(solution)/shard_map/output/ppermute | solution.py:30
  135.2 7.9 %collective-permute-start.20 = (bf16[256,256]{1,0:T(8,128)(2,1)S(1)}, bf16[256,256]{1,0:T(8,128)(2,1)S(1)}, u32[]{:S(2)}, u32[]{:S(2)}) collective-permute-start(bf16[256,256]{1,0:T(8,128)(2,1)S(1)} %fusion.4), channel_id=1, source_target_pairs={{0,128},{128,0},{1,129},{129,1},{2,130},{130,2},{3,131},{131,3},{4... | collective-permute-start | bytes 393224 | tf_op jit(solution)/shard_map/output/ppermute | solution.py:30
  136.9 8.2 %collective-permute-start.22 = (bf16[256,256]{1,0:T(8,128)(2,1)S(1)}, bf16[256,256]{1,0:T(8,128)(2,1)S(1)}, u32[]{:S(2)}, u32[]{:S(2)}) collective-permute-start(bf16[256,256]{1,0:T(8,128)(2,1)S(1)} %fusion), channel_id=1, source_target_pairs={{0,128},{128,0},{1,129},{129,1},{2,130},{130,2},{3,131},{131,3},{4... | collective-permute-start | bytes 393224 | tf_op jit(solution)/shard_map/output/ppermute | solution.py:30
Sparse Core Ops, SparseCore 0:
  41.5 43.0 all-gather.1
